TPU v7x, 32 devices: a whole 2x2x4 slice. The times are simulated.
32 devices in a mesh: pole: 4 (over x, core), row: 4 (over z), col: 2 (over y).
Axes of the slice: x: 2, y: 2, z: 4, core: 2. Of those that a mesh axis runs over, the one named last changes fastest.
Arguments:
- inverse: bfloat16 [4, 2, 4096, 4096], P('pole', None, 'row', 'col'), may hold values from -0.0625 to 0.0625
- factor: bfloat16 [4, 1, 2048, 1024], P('pole', None, ('row', 'col')), may hold values from -1.796875 to 1.796875
- dinv: float32 [512, 4, 1, 2, 512], P(('row', 'col'), 'pole'), may hold values from -6 to 6
- ancestors: int32 [1, 16], replicated, may hold values from 0 to 31, as said below
- owner: int32 [2048, 1], P(('row', 'col')), may hold values from 0 to 31; in each aligned block of 256 rows (0 to 255, 256 to 511, ...) at most 16 rows name the same one
- weight_table: float32 [2, 16], replicated, may hold values from -4 to 4
- pole_slot: int32 [4], P('pole'), may hold values from 0 to 15
Outputs:
- inverse_column: float32 [4096, 4, 1, 2, 512], P(('row', 'col'), 'pole')
- diag_inverse: float32 [512, 4, 1, 2, 512], P(('row', 'col'), 'pole')
- density_diag: float32 [512, 1, 512], P(('row', 'col'))
- tile_density: float32 [32, 8, 128], P(('pole', 'row', 'col'))
Inputs may be any that keep to these rules, and one draw needn't show every extreme that they name: `ancestors`: each row lists 16 distinct block numbers in increasing order. In the rows of one device (256 rows of owner) no tile is named more than 16 times.
All inputs are finite; a program needn't handle non-finite values.
Results may differ from a plain program's by a relative error of at most 0.0028.
Values may be sent and summed in bfloat16 or wider, within the bound.
No kernel may reach another device: no remote copies, remote signals or barrier semaphores. Data moves between devices by JAX's collectives and lax.ppermute only.
A program may use at most 64 MiB of HBM per device.

v0:
```python
import functools

import jax
import jax.numpy as jnp
from jax import lax
from jax.experimental import pallas as pl
from jax.experimental.pallas import tpu as pltpu
from jax.sharding import PartitionSpec as P


BS = 128
BR = 8
BC = 128
MIB = 1 << 20


def shift_pairs(rows, cols, step, valid):
    return [
        (r * cols + c, r * cols + (c + step) % cols)
        for r in range(rows)
        if valid(r)
        for c in range(cols)
    ]


def gather_stages(shard, rows, cols):
    grid = ("row", "col")
    if rows != 4:
        full = lax.all_gather(shard, grid, axis=0, tiled=True).reshape((rows, cols) + shard.shape)
        c = lax.axis_index("col")
        stages = []
        for row in range(rows):
            line = [lax.dynamic_index_in_dim(full[row], (c - step) % cols, 0, False) for step in range(cols)]
            stages.append([[piece] for piece in line])
        return stages, [[row] * rows for row in range(rows)]
    sources = [[0, 1, 2, 3], [1, 0, 3, 2], [2, 2, 1, 1], [3, 3, 0, 0]]
    outer = [(0, 1), (1, 0), (2, 3), (3, 2)]
    inner = [(1, 2), (2, 1)]
    r = lax.axis_index("row")
    middle = jnp.logical_or(r == 1, r == 2)
    height = shard.shape[0] // 2
    stages = [[[] for _ in range(cols)] for _ in range(rows)]
    for part in (0, 1):
        own = shard[part * height : (part + 1) * height]
        near = lax.ppermute(own, "row", outer)
        cross = lax.ppermute(own, "row", inner)
        cross_out = lax.ppermute(cross, "row", outer)
        far = lax.ppermute(near, "row", inner)
        far_out = lax.ppermute(far, "row", outer)
        line = [
            lambda: own,
            lambda: near,
            lambda: jnp.where(middle, cross, cross_out),
            lambda: jnp.where(middle, far, far_out),
        ]
        last = None
        opened = []
        for stage, make in enumerate(line):
            piece = make()
            stages[stage][0].append(piece)
            leaving = piece
            if last is not None:
                leaving, _ = lax.optimization_barrier((piece, last))
            for step in range(1, cols):
                if stage == 1 and part == 1:
                    relayed, _ = lax.optimization_barrier((opened[step - 1], far_out))
                    stages[stage][step].append(lax.ppermute(relayed, "row", outer))
                    continue
                pairs = shift_pairs(rows, cols, step, lambda r: True)
                last = lax.ppermute(leaving, grid, pairs)
                stages[stage][step].append(last)
                if stage == 0:
                    opened.append(last)
    return stages, sources


def counts_of(ancestors, inverse_rows, inverse_cols):
    r = lax.axis_index("row")
    c = lax.axis_index("col")

    def below(limit):
        total = jnp.int32(0)
        for i in range(ancestors.shape[0]):
            total = total + (ancestors[i] < limit).astype(jnp.int32)
        return total

    row_first, row_last = below(r * inverse_rows), below((r + 1) * inverse_rows)
    col_first, col_last = below(c * inverse_cols), below((c + 1) * inverse_cols)
    return row_first, row_last - row_first, col_first, col_last


def pick_kernel(stage_blocks, ancestors, inverse, picked, row_sem):
    row_blocks = inverse.shape[1] // BS
    col_blocks = inverse.shape[2] // BS
    r = lax.axis_index("row")
    c = lax.axis_index("col")
    row_first, row_count, col_first, col_last = counts_of(ancestors, row_blocks, col_blocks)

    def block_copy(i, k):
        row = pl.multiple_of((ancestors[row_first + i] - r * row_blocks) * BS, BS)
        col = pl.multiple_of((ancestors[k] - c * col_blocks) * BS, BS)
        return pltpu.make_async_copy(
            inverse.at[:, pl.ds(row, BS), pl.ds(col, BS)],
            picked.at[i, :, :, pl.ds(pl.multiple_of(k * BS, BS), BS)],
            row_sem.at[i],
        )

    @pl.loop(0, row_count)
    def _(i):
        @pl.loop(col_first, col_last)
        def _(k):
            block_copy(i, k).start()

    start = col_first // stage_blocks * stage_blocks
    end = (col_last + stage_blocks - 1) // stage_blocks * stage_blocks

    @pl.loop(0, row_count)
    def _(i):
        def clear(k):
            place = pl.ds(pl.multiple_of(k * BS, BS), BS)
            picked[i, :, :, place] = jnp.zeros((2, BS, BS), picked.dtype)

        pl.loop(start, col_first)(clear)
        pl.loop(col_last, end)(clear)

        @pl.loop(col_first, col_last)
        def _(k):
            block_copy(i, k).wait()


def source_row(sources, stage):
    r = lax.axis_index("row")
    total = jnp.int32(0)
    for row, source in enumerate(sources[stage]):
        total = total + jnp.where(r == row, source, 0)
    return total


def fill(full, pieces, sources, stage, cols):
    c = lax.axis_index("col")
    source = source_row(sources, stage)
    chunks = len(pieces) // cols
    height = pieces[0].shape[0]
    for step in range(cols):
        shard = source * cols + lax.rem(c - step + cols, cols)
        for chunk in range(chunks):
            start = pl.multiple_of((shard * chunks + chunk) * height, height)
            full[pl.ds(start, height), :] = pieces[step * chunks + chunk][...]


def multiply(acc, picked, full, i, source, stage_blocks, col_first, col_last):
    low = source * stage_blocks

    @pl.when(jnp.logical_and(low < col_last, low + stage_blocks > col_first))
    def _():
        size = stage_blocks * BS
        place = pl.ds(pl.multiple_of(low * BS, BS), size)
        left = picked[i, :, :, place].reshape(2 * BS, size)
        acc[...] += jnp.dot(left, full[place, :], preferred_element_type=jnp.float32)


def combine(acc):
    half = acc.shape[1] // 2
    return acc[:BS, :half] - acc[BS:, half:], acc[:BS, half:] + acc[BS:, :half]


def stage_kernel(sources, stages, added, rows, cols, total_blocks, ancestors, picked, *refs):
    early, full, acc = refs[-3:]
    before = refs[0] if added else None
    pieces = refs[1 if added else 0 : -3]
    each = len(pieces) // len(stages)
    stage_blocks = ancestors.shape[0] // rows
    half = acc.shape[1] // 2
    for n, stage in enumerate(stages):
        fill(full, pieces[n * each : (n + 1) * each], sources, stage, cols)
    _, row_count, col_first, col_last = counts_of(ancestors, early.shape[0], total_blocks // cols)

    @pl.loop(0, row_count)
    def _(i):
        if added:
            acc[:BS, :] = before[i]
            acc[BS:, :] = jnp.zeros((BS, 2 * half), jnp.float32)
        else:
            acc[...] = jnp.zeros_like(acc)
        for stage in stages:
            source = source_row(sources, stage)
            multiply(acc, picked, full, i, source, stage_blocks, col_first, col_last)
        real, imag = combine(acc)
        early[i, :, :half] = real
        early[i, :, half:] = imag


def last_kernel(sources, rows, cols, total_blocks, ancestors, table, slot, owner, picked, early, *refs):
    keep, send, diag_keep, diag_send, full, acc, diag, tiles = refs[-8:]
    pieces = refs[:-8]
    each = len(pieces) // rows
    stage_blocks = ancestors.shape[0] // rows
    wide = acc.shape[1]
    half = wide // 2
    row_blocks = early.shape[0]
    own_blocks = row_blocks // cols
    r = lax.axis_index("row")
    c = lax.axis_index("col")
    for stage in range(rows):
        fill(full, pieces[stage * each : (stage + 1) * each], sources, stage, cols)
    row_first, row_count, col_first, col_last = counts_of(ancestors, row_blocks, total_blocks // cols)
    diag[...] = jnp.zeros_like(diag)
    tiles[...] = jnp.zeros_like(tiles)
    weight_real = table[0, slot[0]]
    weight_imag = table[1, slot[0]]

    @pl.loop(0, row_count)
    def _(i):
        acc[:BS, :] = early[i]
        acc[BS:, :] = jnp.zeros((BS, wide), jnp.float32)
        source = source_row(sources, rows - 1)
        multiply(acc, picked, full, i, source, stage_blocks, col_first, col_last)
        real, imag = combine(acc)
        block = ancestors[row_first + i] - r * row_blocks
        place = block // own_blocks
        within = pl.multiple_of(lax.rem(block, own_blocks) * BS, BS)
        turn = lax.rem(place - c + cols, cols)

        @pl.when(turn == 0)
        def _():
            keep[pl.ds(within, BS), :half] = real
            keep[pl.ds(within, BS), half:] = imag

        @pl.when(turn > 0)
        def _():
            send[turn - 1, pl.ds(within, BS), :half] = real.astype(send.dtype)
            send[turn - 1, pl.ds(within, BS), half:] = imag.astype(send.dtype)

        mixed = -(weight_real * imag + weight_imag * real)
        across = half // BC
        per_device = own_blocks * (BS // BR) * across
        first = lax.rem(c - place + cols, cols) * per_device + lax.rem(block, own_blocks) * (
            BS // BR
        ) * across
        for group in range(BS // BR):
            for j in range(across):
                tile = owner[first + group * across + j]
                tiles[j, tile] += mixed[group * BR : (group + 1) * BR, j * BC : (j + 1) * BC]

        rows_of = full[pl.ds(pl.multiple_of((row_first + i) * BS, BS), BS), :]
        real_high = real.astype(jnp.bfloat16)
        imag_high = imag.astype(jnp.bfloat16)
        real_low = (real - real_high.astype(jnp.float32)).astype(jnp.bfloat16)
        imag_low = (imag - imag_high.astype(jnp.float32)).astype(jnp.bfloat16)
        left = jnp.concatenate([rows_of[:, :half], rows_of[:, half:]], axis=0)
        left = jnp.concatenate([left, left], axis=0)
        right = jnp.concatenate(
            [
                jnp.concatenate([real_high, imag_high], axis=1),
                jnp.concatenate([-imag_high, real_high], axis=1),
                jnp.concatenate([real_low, imag_low], axis=1),
                jnp.concatenate([-imag_low, real_low], axis=1),
            ],
            axis=0,
        )
        diag[...] += lax.dot_general(
            left, right, (((0,), (0,)), ((), ())), preferred_element_type=jnp.float32
        )

    part = half // (rows * cols)
    poles = tiles.shape[1] // (rows * cols)
    for row in range(rows):
        for step in range(cols):
            place = row * cols + lax.rem(c + step, cols)
            value = diag[pl.ds(pl.multiple_of(place * part, part), part), :]
            if step == 0:
                diag_keep[row, :part] = value
                diag_keep[row, part:] = jnp.zeros((BR, wide), jnp.float32)
            else:
                diag_send[step - 1, row, :part] = value.astype(diag_send.dtype)
                diag_send[step - 1, row, part:] = jnp.zeros((BR, wide), diag_send.dtype)
            for pole in range(poles):
                total = tiles[0, pole * rows * cols + place]
                for j in range(1, half // BC):
                    total = total + tiles[j, pole * rows * cols + place]
                if step == 0:
                    diag_keep[row, part:, 2 * pole * BC : (2 * pole + 1) * BC] = total
                else:
                    diag_send[step - 1, row, part:, 2 * pole * BC : 2 * (pole + 1) * BC] = halves(total)


def halves(value):
    high = value.astype(jnp.bfloat16)
    low = (value - high.astype(jnp.float32)).astype(jnp.bfloat16)
    return jnp.concatenate([high, low], axis=1)


def regroup_kernel(poles, rows, kept, *refs):
    *rounded, own = refs[-rows:]
    arrived = refs[:-rows]
    part = own.shape[0] - BR
    r = lax.axis_index("row")

    def total(row):
        value = kept[row]
        for ref in arrived:
            value = value + ref[row].astype(jnp.float32)
        return value

    own[...] = total(r)
    for step in range(1, rows):
        value = total(lax.rem(r + step, rows))
        out = rounded[step - 1]
        out[:part] = value[:part].astype(out.dtype)
        for pole in range(poles):
            first = 2 * pole * BC
            band = value[part:, first : first + BC] + value[part:, first + BC : first + 2 * BC]
            out[part:, first : first + 2 * BC] = halves(band)


def finish_kernel(poles, table, slot, flat_dinv, own, *refs):
    diag_out, message = refs[-2:]
    arrived = refs[:-2]
    part, wide = flat_dinv.shape
    half = wide // 2
    total = own[...]
    for ref in arrived:
        total = total + ref[...].astype(jnp.float32)
    block = flat_dinv[...] + total[:part]
    diag_out[...] = block
    weight_real = table[0, slot[0]]
    weight_imag = table[1, slot[0]]
    message[:part] = weight_real * block[:, half:] + weight_imag * block[:, :half]
    for pole in range(poles):
        first = 2 * pole * BC
        band = total[part:, first : first + BC] + total[part:, first + BC : first + 2 * BC]
        message[part:, pole * BC : (pole + 1) * BC] = band


def compute(inverse, factor, dinv, ancestors, owner, weight_table, pole_slot):
    rows = lax.axis_size("row")
    cols = lax.axis_size("col")
    poles = lax.axis_size("pole")
    r = lax.axis_index("row")
    c = lax.axis_index("col")
    grid = ("row", "col")
    tile_count = poles * rows * cols
    here = inverse[0]
    wide = factor.shape[3]
    half = wide // 2
    rows_here = here.shape[1] // cols
    row_blocks = here.shape[1] // BS
    col_blocks = here.shape[2] // BS
    selected = ancestors.shape[1]
    part = half // (rows * cols)
    everyone = lambda r: True

    owners = [owner[:, 0]]
    for step in range(1, cols):
        owners.append(lax.ppermute(owner[:, 0], grid, shift_pairs(rows, cols, step, everyone)))
    smem = pl.BlockSpec(memory_space=pltpu.SMEM)
    vmem = pl.BlockSpec(memory_space=pltpu.VMEM)
    whole = pl.BlockSpec(memory_space=pl.ANY)
    flat_dinv = lax.optimization_barrier(dinv.reshape(part, wide))
    stages, sources = gather_stages(factor[0, 0], rows, cols)
    stages = [[chunk for step in stage for chunk in step] for stage in stages]
    listed_blocks, _ = lax.optimization_barrier((ancestors[0], stages[1][0]))
    stage_blocks = selected // rows
    picked = pl.pallas_call(
        functools.partial(pick_kernel, stage_blocks),
        out_shape=jax.ShapeDtypeStruct((row_blocks, 2, BS, selected * BS), jnp.bfloat16),
        in_specs=[smem, pl.BlockSpec(memory_space=pltpu.HBM)],
        out_specs=vmem,
        scratch_shapes=[pltpu.SemaphoreType.DMA((row_blocks,))],
        compiler_params=pltpu.CompilerParams(vmem_limit_bytes=12 * MIB),
        cost_estimate=pl.CostEstimate(flops=0, bytes_accessed=8 * MIB, transcendentals=0),
        name="pick_blocks",
    )(listed_blocks, here)
    products = 2 * row_blocks * BS * 2 * wide * selected * BS // cols
    early = None
    for group in (tuple(range(rows - 2)), (rows - 2,)):
        added = early is not None
        group_pieces = [piece for stage in group for piece in stages[stage]]
        early = pl.pallas_call(
            functools.partial(stage_kernel, sources, group, added, rows, cols, col_blocks * cols),
            out_shape=jax.ShapeDtypeStruct((row_blocks, BS, wide), jnp.float32),
            in_specs=[smem, vmem] + [vmem] * (added + len(group_pieces)),
            out_specs=vmem,
            scratch_shapes=[
                pltpu.VMEM((selected * BS, wide), jnp.bfloat16),
                pltpu.VMEM((2 * BS, wide), jnp.float32),
            ],
            input_output_aliases={2: 0} if added else {},
            compiler_params=pltpu.CompilerParams(vmem_limit_bytes=32 * MIB),
            cost_estimate=pl.CostEstimate(
                flops=products * len(group) // rows, bytes_accessed=4 * MIB, transcendentals=0
            ),
            name="stage_products",
        )(ancestors[0], picked, *([early] if added else []), *group_pieces)
    all_pieces = [piece for stage in stages for piece in stage]
    others = max(1, cols - 1)
    keep, send, diag_keep, diag_send = pl.pallas_call(
        functools.partial(last_kernel, sources, rows, cols, col_blocks * cols),
        out_shape=(
            jax.ShapeDtypeStruct((rows_here, wide), jnp.float32),
            jax.ShapeDtypeStruct((others, rows_here, wide), jnp.bfloat16),
            jax.ShapeDtypeStruct((rows, part + BR, wide), jnp.float32),
            jax.ShapeDtypeStruct((others, rows, part + BR, wide), jnp.bfloat16),
        ),
        in_specs=[smem] * 4 + [vmem] * (2 + len(all_pieces)),
        out_specs=(vmem,) * 4,
        scratch_shapes=[
            pltpu.VMEM((selected * BS, wide), jnp.bfloat16),
            pltpu.VMEM((2 * BS, wide), jnp.float32),
            pltpu.VMEM((half, wide), jnp.float32),
            pltpu.VMEM((half // BC, tile_count, BR, BC), jnp.float32),
        ],
        compiler_params=pltpu.CompilerParams(vmem_limit_bytes=36 * MIB),
        cost_estimate=pl.CostEstimate(flops=products, bytes_accessed=8 * MIB, transcendentals=0),
        name="last_products",
    )(ancestors[0], weight_table, pole_slot, jnp.concatenate(owners), picked, early, *all_pieces)

    everyone_pairs = [shift_pairs(rows, cols, step, everyone) for step in range(cols)]
    arrived = [
        lax.ppermute(diag_send[step - 1], grid, everyone_pairs[step]) for step in range(1, cols)
    ]
    *rounded, own = pl.pallas_call(
        functools.partial(regroup_kernel, poles, rows),
        out_shape=(jax.ShapeDtypeStruct((part + BR, wide), jnp.bfloat16),) * (rows - 1)
        + (jax.ShapeDtypeStruct((part + BR, wide), jnp.float32),),
        in_specs=[vmem] * (1 + len(arrived)),
        out_specs=(vmem,) * rows,
        name="regroup",
    )(diag_keep, *arrived)
    parts = [
        lax.ppermute(rounded[step - 1], "row", [(i, (i + step) % rows) for i in range(rows)])
        for step in range(1, rows)
    ]
    flat_diag, message = pl.pallas_call(
        functools.partial(finish_kernel, poles),
        out_shape=(
            jax.ShapeDtypeStruct((part, wide), jnp.float32),
            jax.ShapeDtypeStruct((part + BR, half), jnp.float32),
        ),
        in_specs=[smem] * 2 + [vmem] * (2 + len(parts)),
        out_specs=(vmem,) * 2,
        name="finish",
    )(weight_table, pole_slot, flat_dinv, own, *parts)
    diag_inverse = flat_diag.reshape(dinv.shape)
    messages = [message]
    for step in range(1, poles):
        messages.append(lax.ppermute(message, "pole", [(i, i ^ step) for i in range(poles)]))
    while len(messages) > 1:
        messages = [a + b for a, b in zip(messages[::2], messages[1::2])]
    density_diag = messages[0][:part].reshape(part, 1, half)
    tile_sum = lax.dynamic_slice(messages[0], (part, lax.axis_index("pole") * BC), (BR, BC))[None]

    own_blocks = rows_here // BS
    listed = ((r * cols + c) * own_blocks + jnp.arange(own_blocks))[:, None] == ancestors[0][None]
    listed = jnp.repeat(jnp.any(listed, axis=1), BS * wide // BC)[:, None]

    def laid(value):
        value = value.reshape(rows_here, 2, half // BC, BC).transpose(0, 2, 1, 3)
        return lax.optimization_barrier(value.reshape(rows_here * wide // BC, BC))

    column = laid(keep)
    for step in range(1, cols):
        leaving = laid(send[step - 1])
        column = column + lax.ppermute(leaving, grid, everyone_pairs[step])
    column = jnp.where(listed, -column, 0.0)
    column = column.reshape(rows_here, half // BC, 2, BC).transpose(0, 2, 1, 3)
    column_out = column.reshape(rows_here, 1, 1, 2, half)
    return (column_out, diag_inverse, density_diag, tile_sum)


def solution(mesh):
    in_specs = (
        P("pole", None, "row", "col"),
        P("pole", None, ("row", "col"), None),
        P(("row", "col"), "pole", None, None, None),
        P(),
        P(("row", "col"), None),
        P(),
        P("pole"),
    )
    out_specs = (
        P(("row", "col"), "pole", None, None, None),
        P(("row", "col"), "pole", None, None, None),
        P(("row", "col"), None, None),
        P(("pole", "row", "col"), None, None),
    )
    return jax.shard_map(compute, mesh=mesh, in_specs=in_specs, out_specs=out_specs, check_vma=False)
```

profile of v0, /device:TPU:0, one launch (start us, length us, event | category | flops | bytes accessed | tf_op | source)
XLA Modules:
  0.0 125.4 jit_solution(15181799383501545348)
XLA Ops:
  0.6 1.1 slice_bitcast_fusion
  1.7 3.1 %collective-permute-start.4 = (bf16[128,1024]{1,0:T(8,128)(2,1)S(1)}, bf16[128,1024]{1,0:T(8,128)(2,1)S(1)}, u32[]{:S(2)}, u32[]{:S(2)}) collective-permute-start(bf16[128,1024]{1,0:T(8,128)(2,1)S(1)} %get-tuple-element.50.refs_1_), channel_id=1, source_target_pairs={{0,2},{2,0},{4,6},{6,4},{1,3},{3,1},{5,7},{7,5},{8,10},{10,8},{12,... | collective-permute-start | bytes 786440 | tf_op jit(solution)/shard_map/ppermute | solution.py:45
  5.5 4.4 %collective-permute-start.1 = (bf16[128,1024]{1,0:T(8,128)(2,1)S(1)}, bf16[128,1024]{1,0:T(8,128)(2,1)S(1)}, u32[]{:S(2)}, u32[]{:S(2)}) collective-permute-start(bf16[128,1024]{1,0:T(8,128)(2,1)S(1)} %get-tuple-element.51.refs_0_), channel_id=1, source_target_pairs={{0,2},{2,0},{4,6},{6,4},{1,3},{3,1},{5,7},{7,5},{8,10},{10,8},{12,... | collective-permute-start | bytes 786440 | tf_op jit(solution)/shard_map/ppermute | solution.py:45
  9.9 1.5 %collective-permute-start.2 = (bf16[128,1024]{1,0:T(8,128)(2,1)S(1)}, bf16[128,1024]{1,0:T(8,128)(2,1)S(1)}, u32[]{:S(2)}, u32[]{:S(2)}) collective-permute-start(bf16[128,1024]{1,0:T(8,128)(2,1)S(1)} %get-tuple-element.51.refs_0_), channel_id=1, source_target_pairs={{0,1},{1,0},{2,3},{3,2},{4,5},{5,4},{6,7},{7,6},{8,9},{9,8},{10,11... | collective-permute-start | bytes 786440 | tf_op jit(solution)/shard_map/ppermute | solution.py:70
  12.1 0.7 collective-permute-start.6
  12.8 4.7 %collective-permute-start.10 = (bf16[128,1024]{1,0:T(8,128)(2,1)S(1)}, bf16[128,1024]{1,0:T(8,128)(2,1)S(1)}, u32[]{:S(2)}, u32[]{:S(2)}) collective-permute-start(bf16[128,1024]{1,0:T(8,128)(2,1)S(1)} %collective-permute-done.9), channel_id=1, source_target_pairs={{0,2},{2,0},{4,6},{6,4},{1,3},{3,1},{5,7},{7,5},{8,10},{10,8},{12,... | collective-permute-start | bytes 786440 | tf_op jit(solution)/shard_map/ppermute | solution.py:47
  17.6 0.7 collective-permute-start.15
  18.2 1.9 %collective-permute-start = (s32[256]{0:T(256)}, s32[256]{0:T(256)S(1)}, u32[]{:S(2)}, u32[]{:S(2)}) collective-permute-start(s32[256]{0:T(256)} %bitcast.44), channel_id=1, source_target_pairs={{0,1},{1,0},{2,3},{3,2},{4,5},{5,4},{6,7},{7,6},{8,9},{9,8},{10,11... | collective-permute-start | bytes 3080 | tf_op jit(solution)/shard_map/ppermute | solution.py:355
  20.8 1.3 %collective-permute-done = s32[256]{0:T(256)S(1)} collective-permute-done((s32[256]{0:T(256)}, s32[256]{0:T(256)S(1)}, u32[]{:S(2)}, u32[]{:S(2)}) %collective-permute-start) | collective-permute-done | bytes 1056 | tf_op jit(solution)/shard_map/ppermute | solution.py:355
  22.1 1.8 %collective-permute-start.5 = (bf16[128,1024]{1,0:T(8,128)(2,1)S(1)}, bf16[128,1024]{1,0:T(8,128)(2,1)S(1)}, u32[]{:S(2)}, u32[]{:S(2)}) collective-permute-start(bf16[128,1024]{1,0:T(8,128)(2,1)S(1)} %collective-permute-done.1.refs_4_), channel_id=1, source_target_pairs={{0,1},{1,0},{2,3},{3,2},{4,5},{5,4},{6,7},{7,6},{8,9},{9,8},{10,11... | collective-permute-start | bytes 786440 | tf_op jit(solution)/shard_map/ppermute | solution.py:70
  23.9 4.6 %collective-permute-start.12 = (bf16[128,1024]{1,0:T(8,128)(2,1)S(1)}, bf16[128,1024]{1,0:T(8,128)(2,1)S(1)}, u32[]{:S(2)}, u32[]{:S(2)}) collective-permute-start(bf16[128,1024]{1,0:T(8,128)(2,1)S(1)} %collective-permute-done.11), channel_id=1, source_target_pairs={{0,2},{2,0},{4,6},{6,4},{1,3},{3,1},{5,7},{7,5},{8,10},{10,8},{12,... | collective-permute-start | bytes 786440 | tf_op jit(solution)/shard_map/ppermute | solution.py:47
  28.5 0.7 pad_add_fusion.owner
  29.2 3.4 %copy-done.1 = bf16[1,2,1024,2048]{3,2,1,0:T(8,128)(2,1)S(1)} copy-done((bf16[1,2,1024,2048]{3,2,1,0:T(8,128)(2,1)S(1)}, bf16[1,2,1024,2048]{3,2,1,0:T(8,128)(2,1)}, u32[]{:S(2)}) %copy-start.1) | copy-done | bytes 8388632
  33.2 1.5 %pick_blocks.1.picked = bf16[8,2,128,2048]{3,2,1,0:T(8,128)(2,1)S(1)} custom-call(s32[16]{0:T(128)S(1)} %bitcast.33, bf16[2,1024,2048]{2,1,0:T(8,128)(2,1)S(1)} %bitcast.32), custom_call_target="tpu_custom_call" | custom-call | bytes 8388608 | tf_op jit(solution)/shard_map/pick_blocks/pallas_call | solution.py:364
  34.7 1.0 collective-permute-start.3
  35.8 2.0 %collective-permute-start.16 = (bf16[128,1024]{1,0:T(8,128)(2,1)S(1)}, bf16[128,1024]{1,0:T(8,128)(2,1)S(1)}, u32[]{:S(2)}, u32[]{:S(2)}) collective-permute-start(bf16[128,1024]{1,0:T(8,128)(2,1)S(1)} %collective-permute-done.15), channel_id=1, source_target_pairs={{0,2},{2,0},{4,6},{6,4},{1,3},{3,1},{5,7},{7,5},{8,10},{10,8},{12,... | collective-permute-start | bytes 786440 | tf_op jit(solution)/shard_map/ppermute | solution.py:49
  37.8 1.1 collective-permute-start.13
  39.0 5.0 %collective-permute-done.3.refs_3_ = bf16[128,1024]{1,0:T(8,128)(2,1)S(1)} collective-permute-done((bf16[128,1024]{1,0:T(8,128)(2,1)S(1)}, bf16[128,1024]{1,0:T(8,128)(2,1)S(1)}, u32[]{:S(2)}, u32[]{:S(2)}) %collective-permute-start.3) | collective-permute-done | bytes 262176 | tf_op jit(solution)/shard_map/ppermute | solution.py:70
  44.0 0.9 collective-permute-start.14
  44.9 3.3 %collective-permute-done.16 = bf16[128,1024]{1,0:T(8,128)(2,1)S(1)} collective-permute-done((bf16[128,1024]{1,0:T(8,128)(2,1)S(1)}, bf16[128,1024]{1,0:T(8,128)(2,1)S(1)}, u32[]{:S(2)}, u32[]{:S(2)}) %collective-permute-start.16) | collective-permute-done | bytes 262176 | tf_op jit(solution)/shard_map/ppermute | solution.py:49
  48.3 1.3 %collective-permute-done.13.refs_3_.refs_10_ = bf16[128,1024]{1,0:T(8,128)(2,1)S(1)} collective-permute-done((bf16[128,1024]{1,0:T(8,128)(2,1)S(1)}, bf16[128,1024]{1,0:T(8,128)(2,1)S(1)}, u32[]{:S(2)}, u32[]{:S(2)}) %collective-permute-start.13) | collective-permute-done | bytes 262176 | tf_op jit(solution)/shard_map/ppermute | solution.py:70
  49.6 0.9 collective-permute-start.17
  50.6 4.6 %collective-permute-done.14.refs_4_.refs_11_ = bf16[128,1024]{1,0:T(8,128)(2,1)S(1)} collective-permute-done((bf16[128,1024]{1,0:T(8,128)(2,1)S(1)}, bf16[128,1024]{1,0:T(8,128)(2,1)S(1)}, u32[]{:S(2)}, u32[]{:S(2)}) %collective-permute-start.14) | collective-permute-done | bytes 262176 | tf_op jit(solution)/shard_map/ppermute | solution.py:70
  55.2 0.9 collective-permute-start.18
  56.2 3.8 %stage_products.2.refs_0_ = f32[8,128,1024]{2,1,0:T(8,128)S(1)} custom-call(s32[16]{0:T(128)S(1)} %bitcast.34, bf16[8,2,128,2048]{3,2,1,0:T(8,128)(2,1)S(1)} %pick_blocks.1.picked, bf16[128,1024]{1,0:T(8,128)(2,1)S(1)} %get-tuple-element.51.refs_0_, bf16[128,1024]{1,0:T(8,128)(2,1)S(1)} %get-tuple-element.50.refs_1_, ...), custom_call_target="tpu_custom_call" | custom-call | flops 2147483648 | bytes 4194304 | tf_op jit(solution)/shard_map/stage_products/pallas_call | solution.py:379
  60.0 1.0 stage_products.3.early
  61.6 7.6 %last_products.1 = (f32[512,1024]{1,0:T(8,128)S(1)}, bf16[1,512,1024]{2,1,0:T(8,128)(2,1)S(1)}, f32[4,72,1024]{2,1,0:T(8,128)S(1)}, bf16[1,4,72,1024]{3,2,1,0:T(8,128)(2,1)}) custom-call(s32[16]{0:T(128)S(1)} %bitcast.36, f32[2,16]{1,0:T(2,128)S(1)} %copy-done.8, s32[1]{0:T(128)S(6)} %copy.27.slot, s32[512]{0:T(512)S(1)} %pad_add_fusion.owner, ...), custom_call_target="tpu_custom_call" | custom-call | flops 4294967296 | bytes 8388608 | tf_op jit(solution)/shard_map/last_products/pallas_call | solution.py:397
  69.3 1.0 copy-done.2
  70.3 1.0 copy-done.5
  71.3 2.3 %collective-permute-start.20 = (bf16[4,72,1024]{2,1,0:T(8,128)(2,1)}, bf16[4,72,1024]{2,1,0:T(8,128)(2,1)}, u32[]{:S(2)}, u32[]{:S(2)}) collective-permute-start(bf16[4,72,1024]{2,1,0:T(8,128)(2,1)} %bitcast.12), channel_id=1, source_target_pairs={{0,1},{1,0},{2,3},{3,2},{4,5},{5,4},{6,7},{7,6},{8,9},{9,8},{10,11... | collective-permute-start | bytes 1769480 | tf_op jit(solution)/shard_map/ppermute | solution.py:420
  73.6 2.6 %reshape_squeeze.3 = bf16[512,2,4,128]{3,2,1,0:T(4,128)(2,1)} reshape(bf16[1,512,1024]{2,1,0:T(8,128)(2,1)} %copy-done.5) | data formatting | bytes 2097152 | tf_op jit(solution)/shard_map/reshape;squeeze | solution.py:458
  76.1 3.3 %copy.19 = bf16[512,2,4,128]{3,1,2,0:T(2,128)(2,1)} copy(bf16[512,2,4,128]{3,2,1,0:T(4,128)(2,1)} %reshape_squeeze.3) | data formatting | bytes 2097152 | tf_op jit(solution)/shard_map/reshape;squeeze | solution.py:458
  79.5 8.4 %collective-permute-done.20.refs_0_ = bf16[4,72,1024]{2,1,0:T(8,128)(2,1)} collective-permute-done((bf16[4,72,1024]{2,1,0:T(8,128)(2,1)}, bf16[4,72,1024]{2,1,0:T(8,128)(2,1)}, u32[]{:S(2)}, u32[]{:S(2)}) %collective-permute-start.20) | collective-permute-done | bytes 589856 | tf_op jit(solution)/shard_map/ppermute | solution.py:420
  87.9 2.4 %regroup.1 = (bf16[72,1024]{1,0:T(8,128)(2,1)}, bf16[72,1024]{1,0:T(8,128)(2,1)}, bf16[72,1024]{1,0:T(8,128)(2,1)}, f32[72,1024]{1,0:T(8,128)}) custom-call(f32[4,72,1024]{2,1,0:T(8,128)} %copy-done.2, bf16[4,72,1024]{2,1,0:T(8,128)(2,1)} %collective-permute-done.20.refs_0_), custom_call_target="tpu_custom_call" | custom-call | tf_op jit(solution)/shard_map/regroup/pallas_call | solution.py:422
  90.8 9.0 %collective-permute-start.22 = (bf16[72,1024]{1,0:T(8,128)(2,1)}, bf16[72,1024]{1,0:T(8,128)(2,1)S(1)}, u32[]{:S(2)}, u32[]{:S(2)}) collective-permute-start(bf16[72,1024]{1,0:T(8,128)(2,1)} %get-tuple-element.34), channel_id=1, source_target_pairs={{0,4},{2,6},{4,0},{6,2},{1,5},{3,7},{5,1},{7,3},{8,12},{10,14},{12... | collective-permute-start | bytes 442376 | tf_op jit(solution)/shard_map/ppermute | solution.py:431
  99.8 0.8 copy.23
  100.8 1.9 %collective-permute-done.21.refs_0_ = bf16[72,1024]{1,0:T(8,128)(2,1)S(1)} collective-permute-done((bf16[72,1024]{1,0:T(8,128)(2,1)}, bf16[72,1024]{1,0:T(8,128)(2,1)S(1)}, u32[]{:S(2)}, u32[]{:S(2)}) %collective-permute-start.21) | collective-permute-done | bytes 147488 | tf_op jit(solution)/shard_map/ppermute | solution.py:431
  102.7 3.2 %collective-permute-done.22.refs_1_ = bf16[72,1024]{1,0:T(8,128)(2,1)S(1)} collective-permute-done((bf16[72,1024]{1,0:T(8,128)(2,1)}, bf16[72,1024]{1,0:T(8,128)(2,1)S(1)}, u32[]{:S(2)}, u32[]{:S(2)}) %collective-permute-start.22) | collective-permute-done | bytes 147488 | tf_op jit(solution)/shard_map/ppermute | solution.py:431
  105.8 0.8 collective-permute-done.23.refs_2_
  107.3 2.0 %finish.1 = (f32[64,1024]{1,0:T(8,128)}, f32[72,512]{1,0:T(8,128)}) custom-call(f32[2,16]{1,0:T(2,128)} %table.3, s32[1]{0:T(128)S(6)} %copy.27.slot, f32[64,1024]{1,0:T(8,128)} %bitcast.40, f32[72,1024]{1,0:T(8,128)} %get-tuple-element.32.own, bf16[72,1024]{1,0:T(8,128)(2,1)} %copy-done.11, bf16[72,1024]{1,0:T(8,128)(2,1)} %copy-done.13, ...), custom_call_target="tpu_custom_call" | custom-call | tf_op jit(solution)/shard_map/finish/pallas_call | solution.py:434
  109.3 1.5 %collective-permute-start.25 = (f32[72,512]{1,0:T(8,128)}, f32[72,512]{1,0:T(8,128)S(1)}, u32[]{:S(2)}, u32[]{:S(2)}) collective-permute-start(f32[72,512]{1,0:T(8,128)} %get-tuple-element.37), channel_id=1, source_target_pairs={{0,16},{8,24},{16,0},{24,8},{1,17},{9,25},{17,1},{25,9},{2,18},{10... | collective-permute-start | bytes 442376 | tf_op jit(solution)/shard_map/ppermute | solution.py:447
  111.3 2.0 %reshape.39 = f32[512,2,4,128]{3,2,1,0:T(4,128)} reshape(f32[512,1024]{1,0:T(8,128)S(1)} %get-tuple-element.28) | data formatting | bytes 4194304 | tf_op jit(solution)/shard_map/reshape | solution.py:458
  113.3 2.7 %copy.18 = f32[512,2,4,128]{3,1,2,0:T(2,128)S(1)} copy(f32[512,2,4,128]{3,2,1,0:T(4,128)} %reshape.39) | data formatting | bytes 4194304 | tf_op jit(solution)/shard_map/reshape | solution.py:458
  116.0 0.9 reshape.45
  116.9 1.7 %collective-permute-done.26 = f32[72,512]{1,0:T(8,128)} collective-permute-done((f32[72,512]{1,0:T(8,128)}, f32[72,512]{1,0:T(8,128)}, u32[]{:S(2)}, u32[]{:S(2)}) %collective-permute-start.26) | collective-permute-done | bytes 147488 | tf_op jit(solution)/shard_map/ppermute | solution.py:447
  118.6 1.0 add_add_fusion
  119.6 0.8 copy.21
  121.0 4.4 %negate_select_fusion = f32[4096,128]{1,0:T(8,128)} fusion(f32[4096,128]{1,0:T(8,128)S(1)} %bitcast.38, bf16[4096,128]{1,0:T(8,128)(2,1)} %collective-permute-done.19, pred[4096]{0:T(1024)(128)(4,1)S(1)} %bitcast.43), kind=kLoop, calls=%fused_computation | loop fusion | flops 2097152 | bytes 5246976 | tf_op jit(solution)/shard_map/jit(_where)/select_n | solution.py:465
  (63 shorter events, 5.2 us)
Async XLA Ops:
  1.7 10.4 %collective-permute-start.4 = (bf16[128,1024]{1,0:T(8,128)(2,1)S(1)}, bf16[128,1024]{1,0:T(8,128)(2,1)S(1)}, u32[]{:S(2)}, u32[]{:S(2)}) collective-permute-start(bf16[128,1024]{1,0:T(8,128)(2,1)S(1)} %get-tuple-element.50.refs_1_), channel_id=1, source_target_pairs={{0,2},{2,0},{4,6},{6,4},{1,3},{3,1},{5,7},{7,5},{8,10},{10,8},{12,... | collective-permute-start | bytes 786440 | tf_op jit(solution)/shard_map/ppermute | solution.py:45
  4.8 8.0 %collective-permute-start.9 = (bf16[128,1024]{1,0:T(8,128)(2,1)S(1)}, bf16[128,1024]{1,0:T(8,128)(2,1)S(1)}, u32[]{:S(2)}, u32[]{:S(2)}) collective-permute-start(bf16[128,1024]{1,0:T(8,128)(2,1)S(1)} %get-tuple-element.51.refs_0_), channel_id=1, source_target_pairs={{2,4},{4,2},{3,5},{5,3},{10,12},{12,10},{11,13},{13,11},{18,20},{2... | collective-permute-start | bytes 786440 | tf_op jit(solution)/shard_map/ppermute | solution.py:46
  5.5 12.1 %collective-permute-start.1 = (bf16[128,1024]{1,0:T(8,128)(2,1)S(1)}, bf16[128,1024]{1,0:T(8,128)(2,1)S(1)}, u32[]{:S(2)}, u32[]{:S(2)}) collective-permute-start(bf16[128,1024]{1,0:T(8,128)(2,1)S(1)} %get-tuple-element.51.refs_0_), channel_id=1, source_target_pairs={{0,2},{2,0},{4,6},{6,4},{1,3},{3,1},{5,7},{7,5},{8,10},{10,8},{12,... | collective-permute-start | bytes 786440 | tf_op jit(solution)/shard_map/ppermute | solution.py:45
  9.9 8.3 %collective-permute-start.2 = (bf16[128,1024]{1,0:T(8,128)(2,1)S(1)}, bf16[128,1024]{1,0:T(8,128)(2,1)S(1)}, u32[]{:S(2)}, u32[]{:S(2)}) collective-permute-start(bf16[128,1024]{1,0:T(8,128)(2,1)S(1)} %get-tuple-element.51.refs_0_), channel_id=1, source_target_pairs={{0,1},{1,0},{2,3},{3,2},{4,5},{5,4},{6,7},{7,6},{8,9},{9,8},{10,11... | collective-permute-start | bytes 786440 | tf_op jit(solution)/shard_map/ppermute | solution.py:70
  11.5 12.4 %collective-permute-start.11 = (bf16[128,1024]{1,0:T(8,128)(2,1)S(1)}, bf16[128,1024]{1,0:T(8,128)(2,1)S(1)}, u32[]{:S(2)}, u32[]{:S(2)}) collective-permute-start(bf16[128,1024]{1,0:T(8,128)(2,1)S(1)} %get-tuple-element.50.refs_1_), channel_id=1, source_target_pairs={{2,4},{4,2},{3,5},{5,3},{10,12},{12,10},{11,13},{13,11},{18,20},{2... | collective-permute-start | bytes 786440 | tf_op jit(solution)/shard_map/ppermute | solution.py:46
  12.1 22.6 %collective-permute-start.6 = (bf16[128,1024]{1,0:T(8,128)(2,1)S(1)}, bf16[128,1024]{1,0:T(8,128)(2,1)S(1)}, u32[]{:S(2)}, u32[]{:S(2)}) collective-permute-start(bf16[128,1024]{1,0:T(8,128)(2,1)S(1)} %collective-permute-done.4.refs_5_), channel_id=1, source_target_pairs={{2,4},{4,2},{3,5},{5,3},{10,12},{12,10},{11,13},{13,11},{18,20},{2... | collective-permute-start | bytes 786440 | tf_op jit(solution)/shard_map/ppermute | solution.py:48
  12.8 22.9 %collective-permute-start.10 = (bf16[128,1024]{1,0:T(8,128)(2,1)S(1)}, bf16[128,1024]{1,0:T(8,128)(2,1)S(1)}, u32[]{:S(2)}, u32[]{:S(2)}) collective-permute-start(bf16[128,1024]{1,0:T(8,128)(2,1)S(1)} %collective-permute-done.9), channel_id=1, source_target_pairs={{0,2},{2,0},{4,6},{6,4},{1,3},{3,1},{5,7},{7,5},{8,10},{10,8},{12,... | collective-permute-start | bytes 786440 | tf_op jit(solution)/shard_map/ppermute | solution.py:47
  17.6 18.2 %collective-permute-start.15 = (bf16[128,1024]{1,0:T(8,128)(2,1)S(1)}, bf16[128,1024]{1,0:T(8,128)(2,1)S(1)}, u32[]{:S(2)}, u32[]{:S(2)}) collective-permute-start(bf16[128,1024]{1,0:T(8,128)(2,1)S(1)} %collective-permute-done.1.refs_4_), channel_id=1, source_target_pairs={{2,4},{4,2},{3,5},{5,3},{10,12},{12,10},{11,13},{13,11},{18,20},{2... | collective-permute-start | bytes 786440 | tf_op jit(solution)/shard_map/ppermute | solution.py:48
  18.2 37.9 %copy-start.3 = (bf16[128,1024]{1,0:T(8,128)(2,1)}, bf16[128,1024]{1,0:T(8,128)(2,1)S(1)}, u32[]{:S(2)}) copy-start(bf16[128,1024]{1,0:T(8,128)(2,1)S(1)} %collective-permute-done.2.refs_2_) | copy-start | bytes 786436
  18.2 3.9 %collective-permute-start = (s32[256]{0:T(256)}, s32[256]{0:T(256)S(1)}, u32[]{:S(2)}, u32[]{:S(2)}) collective-permute-start(s32[256]{0:T(256)} %bitcast.44), channel_id=1, source_target_pairs={{0,1},{1,0},{2,3},{3,2},{4,5},{5,4},{6,7},{7,6},{8,9},{9,8},{10,11... | collective-permute-start | bytes 3080 | tf_op jit(solution)/shard_map/ppermute | solution.py:355
  22.1 15.7 %collective-permute-start.5 = (bf16[128,1024]{1,0:T(8,128)(2,1)S(1)}, bf16[128,1024]{1,0:T(8,128)(2,1)S(1)}, u32[]{:S(2)}, u32[]{:S(2)}) collective-permute-start(bf16[128,1024]{1,0:T(8,128)(2,1)S(1)} %collective-permute-done.1.refs_4_), channel_id=1, source_target_pairs={{0,1},{1,0},{2,3},{3,2},{4,5},{5,4},{6,7},{7,6},{8,9},{9,8},{10,11... | collective-permute-start | bytes 786440 | tf_op jit(solution)/shard_map/ppermute | solution.py:70
  23.9 15.1 %collective-permute-start.12 = (bf16[128,1024]{1,0:T(8,128)(2,1)S(1)}, bf16[128,1024]{1,0:T(8,128)(2,1)S(1)}, u32[]{:S(2)}, u32[]{:S(2)}) collective-permute-start(bf16[128,1024]{1,0:T(8,128)(2,1)S(1)} %collective-permute-done.11), channel_id=1, source_target_pairs={{0,2},{2,0},{4,6},{6,4},{1,3},{3,1},{5,7},{7,5},{8,10},{10,8},{12,... | collective-permute-start | bytes 786440 | tf_op jit(solution)/shard_map/ppermute | solution.py:47
  29.2 3.4 %copy-start.1 = (bf16[1,2,1024,2048]{3,2,1,0:T(8,128)(2,1)S(1)}, bf16[1,2,1024,2048]{3,2,1,0:T(8,128)(2,1)}, u32[]{:S(2)}) copy-start(bf16[1,2,1024,2048]{3,2,1,0:T(8,128)(2,1)} %param.7) | copy-start | bytes 25165828
  32.6 0.7 copy-start.6
  34.7 25.2 %copy-start = (bf16[8,2,128,2048]{3,2,1,0:T(8,128)(2,1)}, bf16[8,2,128,2048]{3,2,1,0:T(8,128)(2,1)S(1)}, u32[]{:S(2)}) copy-start(bf16[8,2,128,2048]{3,2,1,0:T(8,128)(2,1)S(1)} %pick_blocks.1.picked) | copy-start | bytes 25165828
  34.7 21.5 %copy-start.7 = (s32[1,16]{1,0:T(1,128)S(1)}, s32[1,16]{1,0:T(1,128)}, u32[]{:S(2)}) copy-start(s32[1,16]{1,0:T(1,128)} %param.10) | copy-start | bytes 196
  34.7 9.2 %collective-permute-start.3 = (bf16[128,1024]{1,0:T(8,128)(2,1)S(1)}, bf16[128,1024]{1,0:T(8,128)(2,1)S(1)}, u32[]{:S(2)}, u32[]{:S(2)}) collective-permute-start(bf16[128,1024]{1,0:T(8,128)(2,1)S(1)} %get-tuple-element.50.refs_1_), channel_id=1, source_target_pairs={{0,1},{1,0},{2,3},{3,2},{4,5},{5,4},{6,7},{7,6},{8,9},{9,8},{10,11... | collective-permute-start | bytes 786440 | tf_op jit(solution)/shard_map/ppermute | solution.py:70
  35.8 9.2 %collective-permute-start.7 = (bf16[128,1024]{1,0:T(8,128)(2,1)S(1)}, bf16[128,1024]{1,0:T(8,128)(2,1)S(1)}, u32[]{:S(2)}, u32[]{:S(2)}) collective-permute-start(bf16[128,1024]{1,0:T(8,128)(2,1)S(1)} %collective-permute-done.6), channel_id=1, source_target_pairs={{0,2},{2,0},{4,6},{6,4},{1,3},{3,1},{5,7},{7,5},{8,10},{10,8},{12,... | collective-permute-start | bytes 786440 | tf_op jit(solution)/shard_map/ppermute | solution.py:49
  35.8 12.5 %collective-permute-start.16 = (bf16[128,1024]{1,0:T(8,128)(2,1)S(1)}, bf16[128,1024]{1,0:T(8,128)(2,1)S(1)}, u32[]{:S(2)}, u32[]{:S(2)}) collective-permute-start(bf16[128,1024]{1,0:T(8,128)(2,1)S(1)} %collective-permute-done.15), channel_id=1, source_target_pairs={{0,2},{2,0},{4,6},{6,4},{1,3},{3,1},{5,7},{7,5},{8,10},{10,8},{12,... | collective-permute-start | bytes 786440 | tf_op jit(solution)/shard_map/ppermute | solution.py:49
  37.8 11.8 %collective-permute-start.13 = (bf16[128,1024]{1,0:T(8,128)(2,1)S(1)}, bf16[128,1024]{1,0:T(8,128)(2,1)S(1)}, u32[]{:S(2)}, u32[]{:S(2)}) collective-permute-start(bf16[128,1024]{1,0:T(8,128)(2,1)S(1)} %broadcast_select_fusion.3.refs_1_.refs_8_), channel_id=1, source_target_pairs={{0,1},{1,0},{2,3},{3,2},{4,5},{5,4},{6,7},{7,6},{8,9},{9,8},{10,11... | collective-permute-start | bytes 786440 | tf_op jit(solution)/shard_map/ppermute | solution.py:70
  44.0 11.2 %collective-permute-start.14 = (bf16[128,1024]{1,0:T(8,128)(2,1)S(1)}, bf16[128,1024]{1,0:T(8,128)(2,1)S(1)}, u32[]{:S(2)}, u32[]{:S(2)}) collective-permute-start(bf16[128,1024]{1,0:T(8,128)(2,1)S(1)} %broadcast_select_fusion.2.refs_2_.refs_9_), channel_id=1, source_target_pairs={{0,1},{1,0},{2,3},{3,2},{4,5},{5,4},{6,7},{7,6},{8,9},{9,8},{10,11... | collective-permute-start | bytes 786440 | tf_op jit(solution)/shard_map/ppermute | solution.py:70
  44.9 11.2 %collective-permute-start.8 = (bf16[128,1024]{1,0:T(8,128)(2,1)S(1)}, bf16[128,1024]{1,0:T(8,128)(2,1)S(1)}, u32[]{:S(2)}, u32[]{:S(2)}) collective-permute-start(bf16[128,1024]{1,0:T(8,128)(2,1)S(1)} %collective-permute-done.3.refs_3_), channel_id=1, source_target_pairs={{0,2},{2,0},{4,6},{6,4},{1,3},{3,1},{5,7},{7,5},{8,10},{10,8},{12,... | collective-permute-start | bytes 786440 | tf_op jit(solution)/shard_map/ppermute | solution.py:67
  49.6 11.4 %collective-permute-start.17 = (bf16[128,1024]{1,0:T(8,128)(2,1)S(1)}, bf16[128,1024]{1,0:T(8,128)(2,1)S(1)}, u32[]{:S(2)}, u32[]{:S(2)}) collective-permute-start(bf16[128,1024]{1,0:T(8,128)(2,1)S(1)} %broadcast_select_fusion.1.refs_12_), channel_id=1, source_target_pairs={{0,1},{1,0},{2,3},{3,2},{4,5},{5,4},{6,7},{7,6},{8,9},{9,8},{10,11... | collective-permute-start | bytes 786440 | tf_op jit(solution)/shard_map/ppermute | solution.py:70
  55.2 6.4 %collective-permute-start.18 = (bf16[128,1024]{1,0:T(8,128)(2,1)S(1)}, bf16[128,1024]{1,0:T(8,128)(2,1)S(1)}, u32[]{:S(2)}, u32[]{:S(2)}) collective-permute-start(bf16[128,1024]{1,0:T(8,128)(2,1)S(1)} %broadcast_select_fusion.refs_13_), channel_id=1, source_target_pairs={{0,1},{1,0},{2,3},{3,2},{4,5},{5,4},{6,7},{7,6},{8,9},{9,8},{10,11... | collective-permute-start | bytes 786440 | tf_op jit(solution)/shard_map/ppermute | solution.py:70
  59.9 1.7 %copy-start.4 = (bf16[128,1024]{1,0:T(8,128)(2,1)S(1)}, bf16[128,1024]{1,0:T(8,128)(2,1)}, u32[]{:S(2)}) copy-start(bf16[128,1024]{1,0:T(8,128)(2,1)} %copy-done.3) | copy-start | bytes 786436
  60.0 1.7 %copy-start.8 = (f32[2,16]{1,0:T(2,128)S(1)}, f32[2,16]{1,0:T(2,128)}, u32[]{:S(2)}) copy-start(f32[2,16]{1,0:T(2,128)} %table.3) | copy-start | bytes 388
  69.3 1.0 copy-start.2
  70.3 1.0 copy-start.5
  71.3 16.6 %collective-permute-start.20 = (bf16[4,72,1024]{2,1,0:T(8,128)(2,1)}, bf16[4,72,1024]{2,1,0:T(8,128)(2,1)}, u32[]{:S(2)}, u32[]{:S(2)}) collective-permute-start(bf16[4,72,1024]{2,1,0:T(8,128)(2,1)} %bitcast.12), channel_id=1, source_target_pairs={{0,1},{1,0},{2,3},{3,2},{4,5},{5,4},{6,7},{7,6},{8,9},{9,8},{10,11... | collective-permute-start | bytes 1769480 | tf_op jit(solution)/shard_map/ppermute | solution.py:420
  76.1 23.7 %copy-start.9 = (f32[64,1,1,2,512]{4,3,2,1,0:T(2,128)S(1)}, f32[64,1,1,2,512]{4,3,2,1,0:T(2,128)}, u32[]{:S(2)}) copy-start(f32[64,1,1,2,512]{4,3,2,1,0:T(2,128)} %param.9) | copy-start | bytes 786436
  79.5 41.5 %collective-permute-start.19 = (bf16[4096,128]{1,0:T(8,128)(2,1)}, bf16[4096,128]{1,0:T(8,128)(2,1)}, u32[]{:S(2)}, u32[]{:S(2)}) collective-permute-start(bf16[4096,128]{1,0:T(8,128)(2,1)} %bitcast.8), channel_id=1, source_target_pairs={{0,1},{1,0},{2,3},{3,2},{4,5},{5,4},{6,7},{7,6},{8,9},{9,8},{10,11... | collective-permute-start | bytes 3145736 | tf_op jit(solution)/shard_map/ppermute | solution.py:464
  90.3 12.4 %collective-permute-start.21 = (bf16[72,1024]{1,0:T(8,128)(2,1)}, bf16[72,1024]{1,0:T(8,128)(2,1)S(1)}, u32[]{:S(2)}, u32[]{:S(2)}) collective-permute-start(bf16[72,1024]{1,0:T(8,128)(2,1)} %get-tuple-element.33), channel_id=1, source_target_pairs={{0,2},{2,4},{4,6},{6,0},{1,3},{3,5},{5,7},{7,1},{8,10},{10,12},{12... | collective-permute-start | bytes 442376 | tf_op jit(solution)/shard_map/ppermute | solution.py:431
  90.8 15.0 %collective-permute-start.22 = (bf16[72,1024]{1,0:T(8,128)(2,1)}, bf16[72,1024]{1,0:T(8,128)(2,1)S(1)}, u32[]{:S(2)}, u32[]{:S(2)}) collective-permute-start(bf16[72,1024]{1,0:T(8,128)(2,1)} %get-tuple-element.34), channel_id=1, source_target_pairs={{0,4},{2,6},{4,0},{6,2},{1,5},{3,7},{5,1},{7,3},{8,12},{10,14},{12... | collective-permute-start | bytes 442376 | tf_op jit(solution)/shard_map/ppermute | solution.py:431
  99.8 6.8 %collective-permute-start.23 = (bf16[72,1024]{1,0:T(8,128)(2,1)}, bf16[72,1024]{1,0:T(8,128)(2,1)S(1)}, u32[]{:S(2)}, u32[]{:S(2)}) collective-permute-start(bf16[72,1024]{1,0:T(8,128)(2,1)} %get-tuple-element.35), channel_id=1, source_target_pairs={{0,6},{2,0},{4,2},{6,4},{1,7},{3,1},{5,3},{7,5},{8,14},{10,8},{12,... | collective-permute-start | bytes 442376 | tf_op jit(solution)/shard_map/ppermute | solution.py:431
  102.7 4.0 %copy-start.11 = (bf16[72,1024]{1,0:T(8,128)(2,1)}, bf16[72,1024]{1,0:T(8,128)(2,1)S(1)}, u32[]{:S(2)}) copy-start(bf16[72,1024]{1,0:T(8,128)(2,1)S(1)} %collective-permute-done.21.refs_0_) | copy-start | bytes 442372
  105.8 0.8 copy-start.13
  106.6 0.7 copy-start.14
  109.3 7.6 %collective-permute-start.24 = (f32[72,512]{1,0:T(8,128)}, f32[72,512]{1,0:T(8,128)S(1)}, u32[]{:S(2)}, u32[]{:S(2)}) collective-permute-start(f32[72,512]{1,0:T(8,128)} %get-tuple-element.37), channel_id=1, source_target_pairs={{0,8},{8,0},{16,24},{24,16},{1,9},{9,1},{17,25},{25,17},{2,10},{10... | collective-permute-start | bytes 442376 | tf_op jit(solution)/shard_map/ppermute | solution.py:447
  109.3 7.6 %collective-permute-start.25 = (f32[72,512]{1,0:T(8,128)}, f32[72,512]{1,0:T(8,128)S(1)}, u32[]{:S(2)}, u32[]{:S(2)}) collective-permute-start(f32[72,512]{1,0:T(8,128)} %get-tuple-element.37), channel_id=1, source_target_pairs={{0,16},{8,24},{16,0},{24,8},{1,17},{9,25},{17,1},{25,9},{2,18},{10... | collective-permute-start | bytes 442376 | tf_op jit(solution)/shard_map/ppermute | solution.py:447
  110.8 7.8 %collective-permute-start.26 = (f32[72,512]{1,0:T(8,128)}, f32[72,512]{1,0:T(8,128)}, u32[]{:S(2)}, u32[]{:S(2)}) collective-permute-start(f32[72,512]{1,0:T(8,128)} %get-tuple-element.37), channel_id=1, source_target_pairs={{0,24},{8,16},{16,8},{24,0},{1,25},{9,17},{17,9},{25,1},{2,26},{10... | collective-permute-start | bytes 442376 | tf_op jit(solution)/shard_map/ppermute | solution.py:447
  113.3 2.7 %copy-start.10 = (f32[64,1024]{1,0:T(8,128)S(1)}, f32[64,1024]{1,0:T(8,128)}, u32[]{:S(2)}) copy-start(f32[64,1024]{1,0:T(8,128)} %get-tuple-element.36) | copy-start | bytes 786436
  113.3 5.3 %copy-start.12 = (f32[72,512]{1,0:T(8,128)S(1)}, f32[72,512]{1,0:T(8,128)}, u32[]{:S(2)}) copy-start(f32[72,512]{1,0:T(8,128)} %get-tuple-element.37) | copy-start | bytes 442372
where the time goes:
time: 126 us; the launch traced here: 125 us
  starting transfers between devices  45.4 us (36%)
  waiting for transfers between devices  32.3 us (26%)
  local copies, waits for them, and re-layouts  21.6 us (17%)
  Pallas kernels  18.3 us (15%)
  other arithmetic  6.4 us (5%)
  between operations  1.52 us (1%)
    ppermute x7, waiting for transfers between devices, gather_stages(): last = lax.ppermute(leaving, grid, pairs)  11.6 us
    ppermute x3, starting transfers between devices, compute(): lax.ppermute(rounded[step - 1], 'row', [(i, (i + step) % rows) for i in r...  9.51 us
    ppermute x2, starting transfers between devices, gather_stages(): cross_out = lax.ppermute(cross, 'row', outer)  9.3 us
    ppermute x1, waiting for transfers between devices, compute(): lax.ppermute(diag_send[step - 1], grid, everyone_pairs[step])  8.45 us
    unnamed x34, local copies, waits for them, and re-layouts  8.36 us
    ppermute x7, starting transfers between devices, gather_stages(): last = lax.ppermute(leaving, grid, pairs)  8.3 us
    pallas_call x1, Pallas kernels, compute(): pl.pallas_call(functools.partial(last_kernel, sources, rows, cols, col_bl...  7.63 us
    ppermute x2, starting transfers between devices, gather_stages(): near = lax.ppermute(own, 'row', outer)  7.57 us
  transfers between devices with their start and end apart: 27, of which 11 were waited for; matrix products, arithmetic and copies ran while one was open for 13% of the time, Pallas kernels for 8%

commit v1 on v0

v1 whole, which is shorter than its diff:
```python
import functools

import jax
import jax.numpy as jnp
from jax import lax
from jax.experimental import pallas as pl
from jax.experimental.pallas import tpu as pltpu
from jax.sharding import PartitionSpec as P


BS = 128
BR = 8
BC = 128
MIB = 1 << 20


def shift_pairs(rows, cols, step, valid):
    return [
        (r * cols + c, r * cols + (c + step) % cols)
        for r in range(rows)
        if valid(r)
        for c in range(cols)
    ]


def gather_stages(shard, rows, cols):
    grid = ("row", "col")
    if rows != 4:
        full = lax.all_gather(shard, grid, axis=0, tiled=True).reshape((rows, cols) + shard.shape)
        c = lax.axis_index("col")
        stages = []
        for row in range(rows):
            line = [lax.dynamic_index_in_dim(full[row], (c - step) % cols, 0, False) for step in range(cols)]
            stages.append([[piece] for piece in line])
        return stages, [[row] * rows for row in range(rows)]
    sources = [[0, 1, 2, 3], [1, 0, 3, 2], [2, 2, 1, 1], [3, 3, 0, 0]]
    outer = [(0, 1), (1, 0), (2, 3), (3, 2)]
    inner = [(1, 2), (2, 1)]
    r = lax.axis_index("row")
    middle = jnp.logical_or(r == 1, r == 2)
    height = shard.shape[0] // 2
    stages = [[[] for _ in range(cols)] for _ in range(rows)]
    for part in (0, 1):
        own = shard[part * height : (part + 1) * height]
        near = lax.ppermute(own, "row", outer)
        cross = lax.ppermute(own, "row", inner)
        cross_out = lax.ppermute(cross, "row", outer)
        far = lax.ppermute(near, "row", inner)
        far_out = lax.ppermute(far, "row", outer)
        line = [
            lambda: own,
            lambda: near,
            lambda: jnp.where(middle, cross, cross_out),
            lambda: jnp.where(middle, far, far_out),
        ]
        last = None
        opened = []
        for stage, make in enumerate(line):
            piece = make()
            stages[stage][0].append(piece)
            leaving = piece
            if last is not None:
                leaving, _ = lax.optimization_barrier((piece, last))
            for step in range(1, cols):
                if stage == 1 and part == 1:
                    relayed, _ = lax.optimization_barrier((opened[step - 1], far_out))
                    stages[stage][step].append(lax.ppermute(relayed, "row", outer))
                    continue
                pairs = shift_pairs(rows, cols, step, lambda r: True)
                last = lax.ppermute(leaving, grid, pairs)
                stages[stage][step].append(last)
                if stage == 0:
                    opened.append(last)
    return stages, sources


def counts_of(ancestors, inverse, rows, cols):
    row_blocks, col_blocks = inverse.shape[1] // BS, inverse.shape[2] // BS
    r = lax.axis_index("row")
    c = lax.axis_index("col")

    def below(limit):
        total = jnp.int32(0)
        for i in range(ancestors.shape[0]):
            total = total + (ancestors[i] < limit).astype(jnp.int32)
        return total

    row_first, row_last = below(r * row_blocks), below((r + 1) * row_blocks)
    col_first, col_last = below(c * col_blocks), below((c + 1) * col_blocks)
    count = row_last - row_first
    return rows, cols, row_blocks, col_blocks, row_first, count, col_first, col_last


def source_row(sources, stage):
    r = lax.axis_index("row")
    total = jnp.int32(0)
    for row, source in enumerate(sources[stage]):
        total = total + jnp.where(r == row, source, 0)
    return total


def fill(full, pieces, sources, stage, cols):
    c = lax.axis_index("col")
    source = source_row(sources, stage)
    chunks = len(pieces) // cols
    height = pieces[0].shape[0]
    for step in range(cols):
        shard = source * cols + lax.rem(c - step + cols, cols)
        for chunk in range(chunks):
            start = pl.multiple_of((shard * chunks + chunk) * height, height)
            full[pl.ds(start, height), :] = pieces[step * chunks + chunk][...]


def multiply(acc, inverse, full, ancestors, counts, i, source):
    rows, _, row_blocks, col_blocks = counts[:4]
    row_first, _, col_first, col_last = counts[4:]
    stage_blocks = ancestors.shape[0] // rows
    low = source * stage_blocks
    r = lax.axis_index("row")
    c = lax.axis_index("col")

    @pl.when(jnp.logical_and(low < col_last, low + stage_blocks > col_first))
    def _():
        row = pl.multiple_of((ancestors[row_first + i] - r * row_blocks) * BS, BS)
        left = []
        for n in range(stage_blocks):
            k = low + n
            inside = jnp.logical_and(k >= col_first, k < col_last)
            block = jnp.where(inside, ancestors[k] - c * col_blocks, 0)
            value = inverse[:, pl.ds(row, BS), pl.ds(pl.multiple_of(block * BS, BS), BS)]
            left.append(value.reshape(2 * BS, BS) * inside.astype(value.dtype))
        place = pl.ds(pl.multiple_of(low * BS, BS), stage_blocks * BS)
        acc[...] += jnp.dot(
            jnp.concatenate(left, axis=1), full[place, :], preferred_element_type=jnp.float32
        )


def combine(acc):
    half = acc.shape[1] // 2
    return acc[:BS, :half] - acc[BS:, half:], acc[:BS, half:] + acc[BS:, :half]


def early_kernel(sources, stages, rows, cols, ancestors, inverse, *refs):
    early, full, acc = refs[-3:]
    pieces = refs[:-3]
    each = len(pieces) // len(stages)
    half = acc.shape[1] // 2
    for n, stage in enumerate(stages):
        fill(full, pieces[n * each : (n + 1) * each], sources, stage, cols)
    counts = counts_of(ancestors, inverse, rows, cols)

    @pl.loop(0, counts[5])
    def _(i):
        acc[...] = jnp.zeros_like(acc)
        for stage in stages:
            multiply(acc, inverse, full, ancestors, counts, i, source_row(sources, stage))
        real, imag = combine(acc)
        early[i, :, :half] = real
        early[i, :, half:] = imag


def last_kernel(
    sources, stages, rows, cols, ancestors, table, slot, owner, inverse, early, *refs
):
    keep, send, diag_keep, diag_send, full, acc, diag, tiles, leaving = refs[-9:]
    pieces = refs[:-9]
    each = len(pieces) // rows
    wide = acc.shape[1]
    half = wide // 2
    row_blocks = early.shape[0]
    own_blocks = row_blocks // cols
    r = lax.axis_index("row")
    c = lax.axis_index("col")
    for stage in range(rows):
        fill(full, pieces[stage * each : (stage + 1) * each], sources, stage, cols)
    counts = counts_of(ancestors, inverse, rows, cols)
    row_first, row_count = counts[4:6]
    keep[...] = jnp.zeros_like(keep)
    leaving[...] = jnp.zeros_like(leaving)
    diag[...] = jnp.zeros_like(diag)
    tiles[...] = jnp.zeros_like(tiles)
    weight_real = table[0, slot[0]]
    weight_imag = table[1, slot[0]]

    @pl.loop(0, row_count)
    def _(i):
        acc[:BS, :] = early[i]
        acc[BS:, :] = jnp.zeros((BS, wide), jnp.float32)
        for stage in stages:
            multiply(acc, inverse, full, ancestors, counts, i, source_row(sources, stage))
        real, imag = combine(acc)
        block = ancestors[row_first + i] - r * row_blocks
        place = block // own_blocks
        across = half // BC
        within = lax.rem(block, own_blocks) * (BS * 2 * across)
        turn = lax.rem(place - c + cols, cols)

        def lay(target, start):
            for j in range(across):
                for n, value in enumerate((real, imag)):
                    rows_of = pl.ds(start + 2 * j + n, BS, stride=2 * across)
                    target[rows_of, :] = -value[:, j * BC : (j + 1) * BC]

        @pl.when(turn == 0)
        def _():
            lay(keep, within)

        @pl.when(turn > 0)
        def _():
            lay(leaving, (turn - 1) * keep.shape[0] + within)

        mixed = -(weight_real * imag + weight_imag * real)
        per_device = own_blocks * (BS // BR) * across
        first = lax.rem(c - place + cols, cols) * per_device + lax.rem(block, own_blocks) * (
            BS // BR
        ) * across
        for group in range(BS // BR):
            for j in range(across):
                tile = owner[first + group * across + j]
                tiles[j, tile] += mixed[group * BR : (group + 1) * BR, j * BC : (j + 1) * BC]

        rows_of = full[pl.ds(pl.multiple_of((row_first + i) * BS, BS), BS), :]
        real_high = real.astype(jnp.bfloat16)
        imag_high = imag.astype(jnp.bfloat16)
        real_low = (real - real_high.astype(jnp.float32)).astype(jnp.bfloat16)
        imag_low = (imag - imag_high.astype(jnp.float32)).astype(jnp.bfloat16)
        left = jnp.concatenate([rows_of[:, :half], rows_of[:, half:]], axis=0)
        left = jnp.concatenate([left, left], axis=0)
        right = jnp.concatenate(
            [
                jnp.concatenate([real_high, imag_high], axis=1),
                jnp.concatenate([-imag_high, real_high], axis=1),
                jnp.concatenate([real_low, imag_low], axis=1),
                jnp.concatenate([-imag_low, real_low], axis=1),
            ],
            axis=0,
        )
        diag[...] += lax.dot_general(
            left, right, (((0,), (0,)), ((), ())), preferred_element_type=jnp.float32
        )

    send[...] = leaving[...].astype(send.dtype)
    part = half // (rows * cols)
    poles = tiles.shape[1] // (rows * cols)
    for row in range(rows):
        for step in range(cols):
            place = row * cols + lax.rem(c + step, cols)
            value = diag[pl.ds(pl.multiple_of(place * part, part), part), :]
            if step == 0:
                diag_keep[row, :part] = value
                diag_keep[row, part:] = jnp.zeros((BR, wide), jnp.float32)
            else:
                diag_send[step - 1, row, :part] = value.astype(diag_send.dtype)
                diag_send[step - 1, row, part:] = jnp.zeros((BR, wide), diag_send.dtype)
            for pole in range(poles):
                total = tiles[0, pole * rows * cols + place]
                for j in range(1, half // BC):
                    total = total + tiles[j, pole * rows * cols + place]
                if step == 0:
                    diag_keep[row, part:, 2 * pole * BC : (2 * pole + 1) * BC] = total
                else:
                    diag_send[step - 1, row, part:, 2 * pole * BC : 2 * (pole + 1) * BC] = halves(total)


def halves(value):
    high = value.astype(jnp.bfloat16)
    low = (value - high.astype(jnp.float32)).astype(jnp.bfloat16)
    return jnp.concatenate([high, low], axis=1)


def regroup_kernel(poles, rows, kept, *refs):
    *rounded, own = refs[-rows:]
    arrived = refs[:-rows]
    part = own.shape[0] - BR
    r = lax.axis_index("row")

    def total(row):
        value = kept[row]
        for ref in arrived:
            value = value + ref[row].astype(jnp.float32)
        return value

    own[...] = total(r)
    for step in range(1, rows):
        value = total(lax.rem(r + step, rows))
        out = rounded[step - 1]
        out[:part] = value[:part].astype(out.dtype)
        for pole in range(poles):
            first = 2 * pole * BC
            band = value[part:, first : first + BC] + value[part:, first + BC : first + 2 * BC]
            out[part:, first : first + 2 * BC] = halves(band)


def finish_kernel(poles, table, slot, laid_dinv, own, *refs):
    diag_out, message = refs[-2:]
    arrived = refs[:-2]
    part, wide = own.shape[0] - BR, own.shape[1]
    across = wide // (2 * BC)
    total = own[...]
    for ref in arrived:
        total = total + ref[...].astype(jnp.float32)
    weight_real = table[0, slot[0]]
    weight_imag = table[1, slot[0]]
    for j in range(across):
        values = []
        for n in range(2):
            rows_of = pl.ds(2 * j + n, part, stride=2 * across)
            first = (n * across + j) * BC
            values.append(laid_dinv[rows_of, :] + total[:part, first : first + BC])
            diag_out[rows_of, :] = values[n]
        share = weight_real * values[1] + weight_imag * values[0]
        message[pl.ds(j, part, stride=across), :] = share
    for pole in range(poles):
        first = 2 * pole * BC
        band = total[part:, first : first + BC] + total[part:, first + BC : first + 2 * BC]
        start = part * across + pole * BR
        message[start : start + BR] = band


def compute(inverse, factor, dinv, ancestors, owner, weight_table, pole_slot):
    rows = lax.axis_size("row")
    cols = lax.axis_size("col")
    poles = lax.axis_size("pole")
    grid = ("row", "col")
    tile_count = poles * rows * cols
    here = inverse[0]
    wide = factor.shape[3]
    half = wide // 2
    rows_here = here.shape[1] // cols
    row_blocks = here.shape[1] // BS
    selected = ancestors.shape[1]
    part = half // (rows * cols)
    everyone = lambda r: True

    owners = [owner[:, 0]]
    for step in range(1, cols):
        pairs = shift_pairs(rows, cols, step, everyone)
        owners.append(lax.ppermute(owner[:, 0], grid, pairs))
    smem = pl.BlockSpec(memory_space=pltpu.SMEM)
    vmem = pl.BlockSpec(memory_space=pltpu.VMEM)
    whole = pl.BlockSpec(memory_space=pl.ANY)
    across = half // BC

    def laid(value):
        value = value.reshape(-1, 2, across, BC).transpose(0, 2, 1, 3)
        return value.reshape(-1, BC)

    def plain(value, shape):
        value = value.reshape(-1, across, 2, BC).transpose(0, 2, 1, 3)
        return value.reshape(shape)

    stages, sources = gather_stages(factor[0, 0], rows, cols)
    stages = [[chunk for step in stage for chunk in step] for stage in stages]
    late_owners, _ = lax.optimization_barrier((tuple(owners), stages[2][-1]))
    products = 2 * row_blocks * BS * 2 * wide * selected * BS // cols
    first = (0, rows - 2)
    last = tuple(stage for stage in range(rows) if stage not in first)
    early_pieces = [piece for stage in first for piece in stages[stage]]
    early = pl.pallas_call(
        functools.partial(early_kernel, sources, first, rows, cols),
        out_shape=jax.ShapeDtypeStruct((row_blocks, BS, wide), jnp.float32),
        in_specs=[smem, vmem] + [vmem] * len(early_pieces),
        out_specs=vmem,
        scratch_shapes=[
            pltpu.VMEM((selected * BS, wide), jnp.bfloat16),
            pltpu.VMEM((2 * BS, wide), jnp.float32),
        ],
        compiler_params=pltpu.CompilerParams(vmem_limit_bytes=24 * MIB),
        cost_estimate=pl.CostEstimate(
            flops=products * len(first) // rows, bytes_accessed=4 * MIB, transcendentals=0
        ),
        name="early_products",
    )(ancestors[0], here, *early_pieces)
    all_pieces = [piece for stage in stages for piece in stage]
    others = max(1, cols - 1)
    laid_rows = rows_here * wide // BC
    keep, send, diag_keep, diag_send = pl.pallas_call(
        functools.partial(last_kernel, sources, last, rows, cols),
        out_shape=(
            jax.ShapeDtypeStruct((laid_rows, BC), jnp.float32),
            jax.ShapeDtypeStruct((others * laid_rows, BC), jnp.bfloat16),
            jax.ShapeDtypeStruct((rows, part + BR, wide), jnp.float32),
            jax.ShapeDtypeStruct((others, rows, part + BR, wide), jnp.bfloat16),
        ),
        in_specs=[smem] * 4 + [vmem] * (2 + len(all_pieces)),
        out_specs=(vmem,) * 4,
        scratch_shapes=[
            pltpu.VMEM((selected * BS, wide), jnp.bfloat16),
            pltpu.VMEM((2 * BS, wide), jnp.float32),
            pltpu.VMEM((half, wide), jnp.float32),
            pltpu.VMEM((half // BC, tile_count, BR, BC), jnp.float32),
            pltpu.VMEM((others * laid_rows, BC), jnp.float32),
        ],
        compiler_params=pltpu.CompilerParams(vmem_limit_bytes=28 * MIB),
        cost_estimate=pl.CostEstimate(flops=products, bytes_accessed=8 * MIB, transcendentals=0),
        name="last_products",
    )(ancestors[0], weight_table, pole_slot, jnp.concatenate(late_owners), here, early, *all_pieces)

    everyone_pairs = [shift_pairs(rows, cols, step, everyone) for step in range(cols)]
    arrived = [
        lax.ppermute(diag_send[step - 1], grid, everyone_pairs[step]) for step in range(1, cols)
    ]
    *rounded, own = pl.pallas_call(
        functools.partial(regroup_kernel, poles, rows),
        out_shape=(jax.ShapeDtypeStruct((part + BR, wide), jnp.bfloat16),) * (rows - 1)
        + (jax.ShapeDtypeStruct((part + BR, wide), jnp.float32),),
        in_specs=[vmem] * (1 + len(arrived)),
        out_specs=(vmem,) * rows,
        compiler_params=pltpu.CompilerParams(vmem_limit_bytes=16 * MIB),
        name="regroup",
    )(diag_keep, *arrived)
    parts = [
        lax.ppermute(rounded[step - 1], "row", [(i, (i + step) % rows) for i in range(rows)])
        for step in range(1, rows)
    ]
    laid_diag, message = pl.pallas_call(
        functools.partial(finish_kernel, poles),
        out_shape=(
            jax.ShapeDtypeStruct((part * 2 * across, BC), jnp.float32),
            jax.ShapeDtypeStruct((part * across + poles * BR, BC), jnp.float32),
        ),
        in_specs=[smem] * 2 + [vmem] * (2 + len(parts)),
        out_specs=(vmem,) * 2,
        compiler_params=pltpu.CompilerParams(vmem_limit_bytes=8 * MIB),
        name="finish",
    )(weight_table, pole_slot, laid(dinv), own, *parts)
    diag_inverse = plain(laid_diag, dinv.shape)
    messages = [message]
    for step in range(1, poles):
        messages.append(lax.ppermute(message, "pole", [(i, i ^ step) for i in range(poles)]))

    def summed(values):
        while len(values) > 1:
            values = [a + b for a, b in zip(values[::2], values[1::2])]
        return values[0]

    split = part * across
    density_diag = summed([value[:split] for value in messages]).reshape(part, 1, half)
    start = split + lax.axis_index("pole") * BR
    tile_sum = summed([lax.dynamic_slice_in_dim(value, start, BR) for value in messages])[None]

    column = keep
    for step in range(1, cols):
        leaving = send[(step - 1) * laid_rows : step * laid_rows]
        column = column + lax.ppermute(leaving, grid, everyone_pairs[step])
    column_out = plain(column, (rows_here, 1, 1, 2, half))
    return (column_out, diag_inverse, density_diag, tile_sum)


def solution(mesh):
    in_specs = (
        P("pole", None, "row", "col"),
        P("pole", None, ("row", "col"), None),
        P(("row", "col"), "pole", None, None, None),
        P(),
        P(("row", "col"), None),
        P(),
        P("pole"),
    )
    out_specs = (
        P(("row", "col"), "pole", None, None, None),
        P(("row", "col"), "pole", None, None, None),
        P(("row", "col"), None, None),
        P(("pole", "row", "col"), None, None),
    )
    return jax.shard_map(compute, mesh=mesh, in_specs=in_specs, out_specs=out_specs, check_vma=False)
```

time: 126 us -> 109 us (0.87)
  local copies, waits for them, and re-layouts: 21.6 us -> 5.43 us
  starting transfers between devices: 45.4 us -> 53.5 us
  Pallas kernels: 18.3 us -> 11 us
  other arithmetic: 6.4 us -> 4.12 us
    ppermute x7, waiting for transfers between devices: 11.6 us -> 4.89 us  [gather_stages(): last = lax.ppermute(leaving, grid, pairs)]
    another operation x2 -> x0, local copies, waits for them, and re-layouts: 5.91 us -> none  [laid(): value = value.reshape(rows_here, 2, half // BC, BC).transpose(0, 2, 1, 3)]
    ppermute x3, waiting for transfers between devices: 1.69 us -> 7.45 us  [compute(): lax.ppermute(message, 'pole', [(i, i ^ step) for i in range(poles)])]
    ppermute x1, waiting for transfers between devices: 8.45 us -> 14.2 us  [compute(): lax.ppermute(diag_send[step - 1], grid, everyone_pairs[step])]
    reshape x4 -> x0, local copies, waits for them, and re-layouts: 5.63 us -> none  [the longest x2 4.7 us: laid(): value = value.reshape(rows_here, 2, half // BC, BC).transpose(0, 2, 1, 3)]
    ppermute x2, starting transfers between devices: 2.03 us -> 6.69 us  [gather_stages(): far_out = lax.ppermute(far, 'row', outer)]
    select_n x1 -> x0, other arithmetic: 4.45 us -> none  [compute(): column = jnp.where(listed, -column, 0.0)]
    pallas_call x4 -> x2, Pallas kernels: 13.9 us -> 9.47 us  [the longest x1 7.04 us: compute(): pl.pallas_call(functools.partial(last_kernel, sources, last, rows, cols),...]
  transfers between devices with their start and end apart: 27 -> 27, of which waited for: 11 -> 9; matrix products, arithmetic and copies ran while one was open for 13% -> 1% of each run, Pallas kernels for 8% -> 4%
where the time goes in v1:
time: 109 us
  starting transfers between devices  53.5 us (49%)
  waiting for transfers between devices  33 us (30%)
  Pallas kernels  11 us (10%)
  local copies, waits for them, and re-layouts  5.43 us (5%)
  other arithmetic  4.12 us (4%)
  between operations  1.49 us (1%)
    ppermute x1, waiting for transfers between devices, compute(): lax.ppermute(diag_send[step - 1], grid, everyone_pairs[step])  14.2 us
    ppermute x7, starting transfers between devices, gather_stages(): last = lax.ppermute(leaving, grid, pairs)  11.9 us
    ppermute x3, starting transfers between devices, compute(): lax.ppermute(rounded[step - 1], 'row', [(i, (i + step) % rows) for i in r...  8.52 us
    ppermute x2, starting transfers between devices, gather_stages(): cross_out = lax.ppermute(cross, 'row', outer)  8.05 us
    ppermute x2, starting transfers between devices, gather_stages(): near = lax.ppermute(own, 'row', outer)  7.5 us
    ppermute x3, waiting for transfers between devices, compute(): lax.ppermute(message, 'pole', [(i, i ^ step) for i in range(poles)])  7.45 us
    pallas_call x1, Pallas kernels, compute(): pl.pallas_call(functools.partial(last_kernel, sources, last, rows, cols),...  7.04 us
    ppermute x2, starting transfers between devices, gather_stages(): far_out = lax.ppermute(far, 'row', outer)  6.69 us
  transfers between devices with their start and end apart: 27, of which 9 were waited for; matrix products, arithmetic and copies ran while one was open for 1% of the time, Pallas kernels for 4%

profile of v1, /device:TPU:0, one launch (start us, length us, event | category | flops | bytes accessed | tf_op | source)
XLA Modules:
  0.0 108.6 jit_solution(15899337566082893273)
XLA Ops:
  0.6 0.0 copy-start.7
  0.7 1.1 slice_bitcast_fusion
  1.7 3.1 %collective-permute-start.8 = (bf16[128,1024]{1,0:T(8,128)(2,1)S(1)}, bf16[128,1024]{1,0:T(8,128)(2,1)S(1)}, u32[]{:S(2)}, u32[]{:S(2)}) collective-permute-start(bf16[128,1024]{1,0:T(8,128)(2,1)S(1)} %get-tuple-element.44.refs_0_), channel_id=1, source_target_pairs={{0,2},{2,0},{4,6},{6,4},{1,3},{3,1},{5,7},{7,5},{8,10},{10,8},{12,... | collective-permute-start | bytes 786440 | tf_op jit(solution)/shard_map/ppermute | solution.py:45
  4.8 0.7 collective-permute-start.6
  5.5 1.6 %collective-permute-start.5 = (bf16[128,1024]{1,0:T(8,128)(2,1)S(1)}, bf16[128,1024]{1,0:T(8,128)(2,1)S(1)}, u32[]{:S(2)}, u32[]{:S(2)}) collective-permute-start(bf16[128,1024]{1,0:T(8,128)(2,1)S(1)} %get-tuple-element.44.refs_0_), channel_id=1, source_target_pairs={{0,1},{1,0},{2,3},{3,2},{4,5},{5,4},{6,7},{7,6},{8,9},{9,8},{10,11... | collective-permute-start | bytes 786440 | tf_op jit(solution)/shard_map/ppermute | solution.py:70
  7.1 4.4 %collective-permute-start.11 = (bf16[128,1024]{1,0:T(8,128)(2,1)S(1)}, bf16[128,1024]{1,0:T(8,128)(2,1)S(1)}, u32[]{:S(2)}, u32[]{:S(2)}) collective-permute-start(bf16[128,1024]{1,0:T(8,128)(2,1)S(1)} %get-tuple-element.45.refs_1_), channel_id=1, source_target_pairs={{0,2},{2,0},{4,6},{6,4},{1,3},{3,1},{5,7},{7,5},{8,10},{10,8},{12,... | collective-permute-start | bytes 786440 | tf_op jit(solution)/shard_map/ppermute | solution.py:45
  11.5 0.7 collective-permute-start.1
  12.2 0.7 collective-permute-start.15
  12.9 4.7 %collective-permute-start.7 = (bf16[128,1024]{1,0:T(8,128)(2,1)S(1)}, bf16[128,1024]{1,0:T(8,128)(2,1)S(1)}, u32[]{:S(2)}, u32[]{:S(2)}) collective-permute-start(bf16[128,1024]{1,0:T(8,128)(2,1)S(1)} %collective-permute-done.6), channel_id=1, source_target_pairs={{0,2},{2,0},{4,6},{6,4},{1,3},{3,1},{5,7},{7,5},{8,10},{10,8},{12,... | collective-permute-start | bytes 786440 | tf_op jit(solution)/shard_map/ppermute | solution.py:47
  17.6 1.6 %collective-permute-start.9 = (bf16[128,1024]{1,0:T(8,128)(2,1)S(1)}, bf16[128,1024]{1,0:T(8,128)(2,1)S(1)}, u32[]{:S(2)}, u32[]{:S(2)}) collective-permute-start(bf16[128,1024]{1,0:T(8,128)(2,1)S(1)} %collective-permute-done.8.refs_4_), channel_id=1, source_target_pairs={{0,1},{1,0},{2,3},{3,2},{4,5},{5,4},{6,7},{7,6},{8,9},{9,8},{10,11... | collective-permute-start | bytes 786440 | tf_op jit(solution)/shard_map/ppermute | solution.py:70
  19.1 0.7 collective-permute-start.12
  19.8 3.4 %collective-permute-start.2 = (bf16[128,1024]{1,0:T(8,128)(2,1)S(1)}, bf16[128,1024]{1,0:T(8,128)(2,1)S(1)}, u32[]{:S(2)}, u32[]{:S(2)}) collective-permute-start(bf16[128,1024]{1,0:T(8,128)(2,1)S(1)} %collective-permute-done.1), channel_id=1, source_target_pairs={{0,2},{2,0},{4,6},{6,4},{1,3},{3,1},{5,7},{7,5},{8,10},{10,8},{12,... | collective-permute-start | bytes 786440 | tf_op jit(solution)/shard_map/ppermute | solution.py:47
  23.8 1.6 %collective-permute-start.3 = (bf16[128,1024]{1,0:T(8,128)(2,1)S(1)}, bf16[128,1024]{1,0:T(8,128)(2,1)S(1)}, u32[]{:S(2)}, u32[]{:S(2)}) collective-permute-start(bf16[128,1024]{1,0:T(8,128)(2,1)S(1)} %get-tuple-element.45.refs_1_), channel_id=1, source_target_pairs={{0,1},{1,0},{2,3},{3,2},{4,5},{5,4},{6,7},{7,6},{8,9},{9,8},{10,11... | collective-permute-start | bytes 786440 | tf_op jit(solution)/shard_map/ppermute | solution.py:70
  25.5 4.4 %collective-permute-start.16 = (bf16[128,1024]{1,0:T(8,128)(2,1)S(1)}, bf16[128,1024]{1,0:T(8,128)(2,1)S(1)}, u32[]{:S(2)}, u32[]{:S(2)}) collective-permute-start(bf16[128,1024]{1,0:T(8,128)(2,1)S(1)} %collective-permute-done.15), channel_id=1, source_target_pairs={{0,2},{2,0},{4,6},{6,4},{1,3},{3,1},{5,7},{7,5},{8,10},{10,8},{12,... | collective-permute-start | bytes 786440 | tf_op jit(solution)/shard_map/ppermute | solution.py:49
  29.8 0.0 copy-start.2
  29.9 0.5 collective-permute-start
  30.3 1.6 %collective-permute-start.10 = (bf16[128,1024]{1,0:T(8,128)(2,1)S(1)}, bf16[128,1024]{1,0:T(8,128)(2,1)S(1)}, u32[]{:S(2)}, u32[]{:S(2)}) collective-permute-start(bf16[128,1024]{1,0:T(8,128)(2,1)S(1)} %broadcast_select_fusion.2.refs_4_.refs_8_), channel_id=1, source_target_pairs={{0,1},{1,0},{2,3},{3,2},{4,5},{5,4},{6,7},{7,6},{8,9},{9,8},{10,11... | collective-permute-start | bytes 786440 | tf_op jit(solution)/shard_map/ppermute | solution.py:70
  32.0 2.3 %collective-permute-start.13 = (bf16[128,1024]{1,0:T(8,128)(2,1)S(1)}, bf16[128,1024]{1,0:T(8,128)(2,1)S(1)}, u32[]{:S(2)}, u32[]{:S(2)}) collective-permute-start(bf16[128,1024]{1,0:T(8,128)(2,1)S(1)} %collective-permute-done.12), channel_id=1, source_target_pairs={{0,2},{2,0},{4,6},{6,4},{1,3},{3,1},{5,7},{7,5},{8,10},{10,8},{12,... | collective-permute-start | bytes 786440 | tf_op jit(solution)/shard_map/ppermute | solution.py:49
  34.3 0.6 collective-permute-start.4
  34.9 3.2 %collective-permute-done.10.refs_6_.refs_10_ = bf16[128,1024]{1,0:T(8,128)(2,1)S(1)} collective-permute-done((bf16[128,1024]{1,0:T(8,128)(2,1)S(1)}, bf16[128,1024]{1,0:T(8,128)(2,1)S(1)}, u32[]{:S(2)}, u32[]{:S(2)}) %collective-permute-start.10) | collective-permute-done | bytes 262176 | tf_op jit(solution)/shard_map/ppermute | solution.py:70
  38.1 2.5 %collective-permute-start.17 = (bf16[128,1024]{1,0:T(8,128)(2,1)S(1)}, bf16[128,1024]{1,0:T(8,128)(2,1)S(1)}, u32[]{:S(2)}, u32[]{:S(2)}) collective-permute-start(bf16[128,1024]{1,0:T(8,128)(2,1)S(1)} %broadcast_select_fusion.1.refs_12_), channel_id=1, source_target_pairs={{0,1},{1,0},{2,3},{3,2},{4,5},{5,4},{6,7},{7,6},{8,9},{9,8},{10,11... | collective-permute-start | bytes 786440 | tf_op jit(solution)/shard_map/ppermute | solution.py:70
  40.6 2.8 %collective-permute-start.14 = (bf16[128,1024]{1,0:T(8,128)(2,1)S(1)}, bf16[128,1024]{1,0:T(8,128)(2,1)S(1)}, u32[]{:S(2)}, u32[]{:S(2)}) collective-permute-start(bf16[128,1024]{1,0:T(8,128)(2,1)S(1)} %collective-permute-done.3.refs_3_), channel_id=1, source_target_pairs={{0,2},{2,0},{4,6},{6,4},{1,3},{3,1},{5,7},{7,5},{8,10},{10,8},{12,... | collective-permute-start | bytes 786440 | tf_op jit(solution)/shard_map/ppermute | solution.py:67
  43.5 0.3 collective-permute-done.4.refs_7_.refs_11_
  43.8 2.5 %collective-permute-start.18 = (bf16[128,1024]{1,0:T(8,128)(2,1)S(1)}, bf16[128,1024]{1,0:T(8,128)(2,1)S(1)}, u32[]{:S(2)}, u32[]{:S(2)}) collective-permute-start(bf16[128,1024]{1,0:T(8,128)(2,1)S(1)} %broadcast_select_fusion.refs_13_), channel_id=1, source_target_pairs={{0,1},{1,0},{2,3},{3,2},{4,5},{5,4},{6,7},{7,6},{8,9},{9,8},{10,11... | collective-permute-start | bytes 786440 | tf_op jit(solution)/shard_map/ppermute | solution.py:70
  46.3 0.0 copy-start
  46.3 3.4 %copy-done = bf16[1,2,1024,2048]{3,2,1,0:T(8,128)(2,1)S(1)} copy-done((bf16[1,2,1024,2048]{3,2,1,0:T(8,128)(2,1)S(1)}, bf16[1,2,1024,2048]{3,2,1,0:T(8,128)(2,1)}, u32[]{:S(2)}) %copy-start) | copy-done | bytes 8388632
  49.7 2.4 %early_products.1.early = f32[8,128,1024]{2,1,0:T(8,128)S(1)} custom-call(s32[16]{0:T(128)S(1)} %bitcast.29, bf16[2,1024,2048]{2,1,0:T(8,128)(2,1)S(1)} %bitcast.26, bf16[128,1024]{1,0:T(8,128)(2,1)S(1)} %get-tuple-element.44.refs_0_, bf16[128,1024]{1,0:T(8,128)(2,1)S(1)} %get-tuple-element.45.refs_1_, bf16[128,1024]{1,0:T(8,128)(2,1)S(1)} %collective-permute-done.5.refs_2_, ...), custom_call_target="tpu_custom_call" | custom-call | flops 2147483648 | bytes 4194304 | tf_op jit(solution)/shard_map/early_products/pallas_call | solution.py:359
  52.1 1.4 %collective-permute-done.18.refs_15_ = bf16[128,1024]{1,0:T(8,128)(2,1)S(1)} collective-permute-done((bf16[128,1024]{1,0:T(8,128)(2,1)S(1)}, bf16[128,1024]{1,0:T(8,128)(2,1)S(1)}, u32[]{:S(2)}, u32[]{:S(2)}) %collective-permute-start.18) | collective-permute-done | bytes 262176 | tf_op jit(solution)/shard_map/ppermute | solution.py:70
  53.6 0.9 copy-done.3
  54.5 7.0 %last_products.1 = (f32[4096,128]{1,0:T(8,128)S(1)}, bf16[4096,128]{1,0:T(8,128)(2,1)}, f32[4,72,1024]{2,1,0:T(8,128)S(1)}, bf16[1,4,72,1024]{3,2,1,0:T(8,128)(2,1)S(1)}) custom-call(s32[16]{0:T(128)S(1)} %bitcast.30, f32[2,16]{1,0:T(2,128)S(1)} %copy-done.5, s32[1]{0:T(128)S(6)} %copy.15.slot, s32[512]{0:T(512)S(1)} %pad_add_fusion.owner, ...), custom_call_target="tpu_custom_call" | custom-call | flops 4294967296 | bytes 8388608 | tf_op jit(solution)/shard_map/last_products/pallas_call | solution.py:377
  61.5 3.0 %collective-permute-start.20 = (bf16[4,72,1024]{2,1,0:T(8,128)(2,1)S(1)}, bf16[4,72,1024]{2,1,0:T(8,128)(2,1)S(1)}, u32[]{:S(2)}, u32[]{:S(2)}) collective-permute-start(bf16[4,72,1024]{2,1,0:T(8,128)(2,1)S(1)} %bitcast.31), channel_id=1, source_target_pairs={{0,1},{1,0},{2,3},{3,2},{4,5},{5,4},{6,7},{7,6},{8,9},{9,8},{10,11... | collective-permute-start | bytes 1769480 | tf_op jit(solution)/shard_map/ppermute | solution.py:401
  64.5 0.0 collective-permute-start.19
  64.6 14.2 %collective-permute-done.20.refs_0_ = bf16[4,72,1024]{2,1,0:T(8,128)(2,1)S(1)} collective-permute-done((bf16[4,72,1024]{2,1,0:T(8,128)(2,1)S(1)}, bf16[4,72,1024]{2,1,0:T(8,128)(2,1)S(1)}, u32[]{:S(2)}, u32[]{:S(2)}) %collective-permute-start.20) | collective-permute-done | bytes 589856 | tf_op jit(solution)/shard_map/ppermute | solution.py:401
  78.7 0.1 regroup.1
  78.9 2.5 %collective-permute-start.21 = (bf16[72,1024]{1,0:T(8,128)(2,1)S(1)}, bf16[72,1024]{1,0:T(8,128)(2,1)S(1)}, u32[]{:S(2)}, u32[]{:S(2)}) collective-permute-start(bf16[72,1024]{1,0:T(8,128)(2,1)S(1)} %get-tuple-element.35), channel_id=1, source_target_pairs={{0,2},{2,4},{4,6},{6,0},{1,3},{3,5},{5,7},{7,1},{8,10},{10,12},{12... | collective-permute-start | bytes 442376 | tf_op jit(solution)/shard_map/ppermute | solution.py:413
  81.4 5.9 %collective-permute-start.22 = (bf16[72,1024]{1,0:T(8,128)(2,1)S(1)}, bf16[72,1024]{1,0:T(8,128)(2,1)S(1)}, u32[]{:S(2)}, u32[]{:S(2)}) collective-permute-start(bf16[72,1024]{1,0:T(8,128)(2,1)S(1)} %get-tuple-element.36), channel_id=1, source_target_pairs={{0,4},{2,6},{4,0},{6,2},{1,5},{3,7},{5,1},{7,3},{8,12},{10,14},{12... | collective-permute-start | bytes 442376 | tf_op jit(solution)/shard_map/ppermute | solution.py:413
  87.3 0.1 collective-permute-start.23
  87.4 2.6 %collective-permute-done.21.refs_0_ = bf16[72,1024]{1,0:T(8,128)(2,1)S(1)} collective-permute-done((bf16[72,1024]{1,0:T(8,128)(2,1)S(1)}, bf16[72,1024]{1,0:T(8,128)(2,1)S(1)}, u32[]{:S(2)}, u32[]{:S(2)}) %collective-permute-start.21) | collective-permute-done | bytes 147488 | tf_op jit(solution)/shard_map/ppermute | solution.py:413
  90.0 3.2 %collective-permute-done.22.refs_1_ = bf16[72,1024]{1,0:T(8,128)(2,1)S(1)} collective-permute-done((bf16[72,1024]{1,0:T(8,128)(2,1)S(1)}, bf16[72,1024]{1,0:T(8,128)(2,1)S(1)}, u32[]{:S(2)}, u32[]{:S(2)}) %collective-permute-start.22) | collective-permute-done | bytes 147488 | tf_op jit(solution)/shard_map/ppermute | solution.py:413
  93.1 0.8 collective-permute-done.23.refs_2_
  93.9 1.4 %finish.1 = (f32[512,128]{1,0:T(8,128)}, f32[288,128]{1,0:T(8,128)S(1)}) custom-call(f32[2,16]{1,0:T(2,128)S(1)} %copy-done.5, s32[1]{0:T(128)S(6)} %copy.15.slot, f32[512,128]{1,0:T(8,128)S(1)} %bitcast.28, f32[72,1024]{1,0:T(8,128)S(1)} %get-tuple-element.34.own, bf16[72,1024]{1,0:T(8,128)(2,1)S(1)} %collective-permute-done.21.refs_0_, ...), custom_call_target="tpu_custom_call" | custom-call | tf_op jit(solution)/shard_map/finish/pallas_call | solution.py:416
  95.3 1.5 %collective-permute-start.25 = (f32[288,128]{1,0:T(8,128)S(1)}, f32[288,128]{1,0:T(8,128)S(1)}, u32[]{:S(2)}, u32[]{:S(2)}) collective-permute-start(f32[288,128]{1,0:T(8,128)S(1)} %get-tuple-element.39), channel_id=1, source_target_pairs={{0,16},{8,24},{16,0},{24,8},{1,17},{9,25},{17,1},{25,9},{2,18},{10... | collective-permute-start | bytes 442376 | tf_op jit(solution)/shard_map/ppermute | solution.py:430
  96.8 0.4 collective-permute-start.24
  97.2 4.2 %collective-permute-done.26 = f32[288,128]{1,0:T(8,128)S(1)} collective-permute-done((f32[288,128]{1,0:T(8,128)S(1)}, f32[288,128]{1,0:T(8,128)S(1)}, u32[]{:S(2)}, u32[]{:S(2)}) %collective-permute-start.26) | collective-permute-done | bytes 147488 | tf_op jit(solution)/shard_map/ppermute | solution.py:430
  101.4 3.2 %collective-permute-done.25 = f32[288,128]{1,0:T(8,128)S(1)} collective-permute-done((f32[288,128]{1,0:T(8,128)S(1)}, f32[288,128]{1,0:T(8,128)S(1)}, u32[]{:S(2)}, u32[]{:S(2)}) %collective-permute-start.25) | collective-permute-done | bytes 147488 | tf_op jit(solution)/shard_map/ppermute | solution.py:430
  104.6 0.6 add_bitcast_fusion
  105.2 0.7 fusion
  105.9 2.7 %convert_add_fusion = f32[4096,128]{1,0:T(8,128)} fusion(f32[4096,128]{1,0:T(8,128)S(1)} %get-tuple-element.30, bf16[4096,128]{1,0:T(8,128)(2,1)} %collective-permute-done.19), kind=kLoop, calls=%fused_computation | loop fusion | flops 1048576 | bytes 5242880 | tf_op jit(solution)/shard_map/add | solution.py:445
  (35 shorter events, 0.2 us)
Async XLA Ops:
  0.6 45.6 %copy-start.7 = (s32[256,1]{0,1:T(1,128)S(1)}, s32[256,1]{0,1:T(1,128)}, u32[]{:S(2)}) copy-start(s32[256,1]{0,1:T(1,128)} %param.11) | copy-start | bytes 3076
  0.6 45.6 %copy-start.6 = (s32[1,16]{1,0:T(1,128)S(1)}, s32[1,16]{1,0:T(1,128)}, u32[]{:S(2)}) copy-start(s32[1,16]{1,0:T(1,128)} %param.10) | copy-start | bytes 196
  1.7 10.4 %collective-permute-start.8 = (bf16[128,1024]{1,0:T(8,128)(2,1)S(1)}, bf16[128,1024]{1,0:T(8,128)(2,1)S(1)}, u32[]{:S(2)}, u32[]{:S(2)}) collective-permute-start(bf16[128,1024]{1,0:T(8,128)(2,1)S(1)} %get-tuple-element.44.refs_0_), channel_id=1, source_target_pairs={{0,2},{2,0},{4,6},{6,4},{1,3},{3,1},{5,7},{7,5},{8,10},{10,8},{12,... | collective-permute-start | bytes 786440 | tf_op jit(solution)/shard_map/ppermute | solution.py:45
  4.8 8.0 %collective-permute-start.6 = (bf16[128,1024]{1,0:T(8,128)(2,1)S(1)}, bf16[128,1024]{1,0:T(8,128)(2,1)S(1)}, u32[]{:S(2)}, u32[]{:S(2)}) collective-permute-start(bf16[128,1024]{1,0:T(8,128)(2,1)S(1)} %get-tuple-element.44.refs_0_), channel_id=1, source_target_pairs={{2,4},{4,2},{3,5},{5,3},{10,12},{12,10},{11,13},{13,11},{18,20},{2... | collective-permute-start | bytes 786440 | tf_op jit(solution)/shard_map/ppermute | solution.py:46
  5.5 12.0 %collective-permute-start.5 = (bf16[128,1024]{1,0:T(8,128)(2,1)S(1)}, bf16[128,1024]{1,0:T(8,128)(2,1)S(1)}, u32[]{:S(2)}, u32[]{:S(2)}) collective-permute-start(bf16[128,1024]{1,0:T(8,128)(2,1)S(1)} %get-tuple-element.44.refs_0_), channel_id=1, source_target_pairs={{0,1},{1,0},{2,3},{3,2},{4,5},{5,4},{6,7},{7,6},{8,9},{9,8},{10,11... | collective-permute-start | bytes 786440 | tf_op jit(solution)/shard_map/ppermute | solution.py:70
  7.1 12.0 %collective-permute-start.11 = (bf16[128,1024]{1,0:T(8,128)(2,1)S(1)}, bf16[128,1024]{1,0:T(8,128)(2,1)S(1)}, u32[]{:S(2)}, u32[]{:S(2)}) collective-permute-start(bf16[128,1024]{1,0:T(8,128)(2,1)S(1)} %get-tuple-element.45.refs_1_), channel_id=1, source_target_pairs={{0,2},{2,0},{4,6},{6,4},{1,3},{3,1},{5,7},{7,5},{8,10},{10,8},{12,... | collective-permute-start | bytes 786440 | tf_op jit(solution)/shard_map/ppermute | solution.py:45
  11.5 8.3 %collective-permute-start.1 = (bf16[128,1024]{1,0:T(8,128)(2,1)S(1)}, bf16[128,1024]{1,0:T(8,128)(2,1)S(1)}, u32[]{:S(2)}, u32[]{:S(2)}) collective-permute-start(bf16[128,1024]{1,0:T(8,128)(2,1)S(1)} %get-tuple-element.45.refs_1_), channel_id=1, source_target_pairs={{2,4},{4,2},{3,5},{5,3},{10,12},{12,10},{11,13},{13,11},{18,20},{2... | collective-permute-start | bytes 786440 | tf_op jit(solution)/shard_map/ppermute | solution.py:46
  12.2 11.6 %collective-permute-start.15 = (bf16[128,1024]{1,0:T(8,128)(2,1)S(1)}, bf16[128,1024]{1,0:T(8,128)(2,1)S(1)}, u32[]{:S(2)}, u32[]{:S(2)}) collective-permute-start(bf16[128,1024]{1,0:T(8,128)(2,1)S(1)} %collective-permute-done.8.refs_4_), channel_id=1, source_target_pairs={{2,4},{4,2},{3,5},{5,3},{10,12},{12,10},{11,13},{13,11},{18,20},{2... | collective-permute-start | bytes 786440 | tf_op jit(solution)/shard_map/ppermute | solution.py:48
  12.9 12.6 %collective-permute-start.7 = (bf16[128,1024]{1,0:T(8,128)(2,1)S(1)}, bf16[128,1024]{1,0:T(8,128)(2,1)S(1)}, u32[]{:S(2)}, u32[]{:S(2)}) collective-permute-start(bf16[128,1024]{1,0:T(8,128)(2,1)S(1)} %collective-permute-done.6), channel_id=1, source_target_pairs={{0,2},{2,0},{4,6},{6,4},{1,3},{3,1},{5,7},{7,5},{8,10},{10,8},{12,... | collective-permute-start | bytes 786440 | tf_op jit(solution)/shard_map/ppermute | solution.py:47
  17.6 12.3 %collective-permute-start.9 = (bf16[128,1024]{1,0:T(8,128)(2,1)S(1)}, bf16[128,1024]{1,0:T(8,128)(2,1)S(1)}, u32[]{:S(2)}, u32[]{:S(2)}) collective-permute-start(bf16[128,1024]{1,0:T(8,128)(2,1)S(1)} %collective-permute-done.8.refs_4_), channel_id=1, source_target_pairs={{0,1},{1,0},{2,3},{3,2},{4,5},{5,4},{6,7},{7,6},{8,9},{9,8},{10,11... | collective-permute-start | bytes 786440 | tf_op jit(solution)/shard_map/ppermute | solution.py:70
  19.1 11.2 %collective-permute-start.12 = (bf16[128,1024]{1,0:T(8,128)(2,1)S(1)}, bf16[128,1024]{1,0:T(8,128)(2,1)S(1)}, u32[]{:S(2)}, u32[]{:S(2)}) collective-permute-start(bf16[128,1024]{1,0:T(8,128)(2,1)S(1)} %collective-permute-done.11.refs_5_), channel_id=1, source_target_pairs={{2,4},{4,2},{3,5},{5,3},{10,12},{12,10},{11,13},{13,11},{18,20},{2... | collective-permute-start | bytes 786440 | tf_op jit(solution)/shard_map/ppermute | solution.py:48
  19.8 12.2 %collective-permute-start.2 = (bf16[128,1024]{1,0:T(8,128)(2,1)S(1)}, bf16[128,1024]{1,0:T(8,128)(2,1)S(1)}, u32[]{:S(2)}, u32[]{:S(2)}) collective-permute-start(bf16[128,1024]{1,0:T(8,128)(2,1)S(1)} %collective-permute-done.1), channel_id=1, source_target_pairs={{0,2},{2,0},{4,6},{6,4},{1,3},{3,1},{5,7},{7,5},{8,10},{10,8},{12,... | collective-permute-start | bytes 786440 | tf_op jit(solution)/shard_map/ppermute | solution.py:47
  23.8 10.5 %collective-permute-start.3 = (bf16[128,1024]{1,0:T(8,128)(2,1)S(1)}, bf16[128,1024]{1,0:T(8,128)(2,1)S(1)}, u32[]{:S(2)}, u32[]{:S(2)}) collective-permute-start(bf16[128,1024]{1,0:T(8,128)(2,1)S(1)} %get-tuple-element.45.refs_1_), channel_id=1, source_target_pairs={{0,1},{1,0},{2,3},{3,2},{4,5},{5,4},{6,7},{7,6},{8,9},{9,8},{10,11... | collective-permute-start | bytes 786440 | tf_op jit(solution)/shard_map/ppermute | solution.py:70
  25.5 9.5 %collective-permute-start.16 = (bf16[128,1024]{1,0:T(8,128)(2,1)S(1)}, bf16[128,1024]{1,0:T(8,128)(2,1)S(1)}, u32[]{:S(2)}, u32[]{:S(2)}) collective-permute-start(bf16[128,1024]{1,0:T(8,128)(2,1)S(1)} %collective-permute-done.15), channel_id=1, source_target_pairs={{0,2},{2,0},{4,6},{6,4},{1,3},{3,1},{5,7},{7,5},{8,10},{10,8},{12,... | collective-permute-start | bytes 786440 | tf_op jit(solution)/shard_map/ppermute | solution.py:49
  29.8 22.2 %copy-start.2 = (bf16[128,1024]{1,0:T(8,128)(2,1)}, bf16[128,1024]{1,0:T(8,128)(2,1)S(1)}, u32[]{:S(2)}) copy-start(bf16[128,1024]{1,0:T(8,128)(2,1)S(1)} %collective-permute-done.9.refs_6_) | copy-start | bytes 786436
  29.9 13.9 %collective-permute-start = (s32[256]{0:T(256)}, s32[256]{0:T(256)S(1)}, u32[]{:S(2)}, u32[]{:S(2)}) collective-permute-start(s32[256]{0:T(256)} %bitcast.34), channel_id=1, source_target_pairs={{0,1},{1,0},{2,3},{3,2},{4,5},{5,4},{6,7},{7,6},{8,9},{9,8},{10,11... | collective-permute-start | bytes 3080 | tf_op jit(solution)/shard_map/ppermute | solution.py:338
  30.3 7.8 %collective-permute-start.10 = (bf16[128,1024]{1,0:T(8,128)(2,1)S(1)}, bf16[128,1024]{1,0:T(8,128)(2,1)S(1)}, u32[]{:S(2)}, u32[]{:S(2)}) collective-permute-start(bf16[128,1024]{1,0:T(8,128)(2,1)S(1)} %broadcast_select_fusion.2.refs_4_.refs_8_), channel_id=1, source_target_pairs={{0,1},{1,0},{2,3},{3,2},{4,5},{5,4},{6,7},{7,6},{8,9},{9,8},{10,11... | collective-permute-start | bytes 786440 | tf_op jit(solution)/shard_map/ppermute | solution.py:70
  32.0 8.7 %collective-permute-start.13 = (bf16[128,1024]{1,0:T(8,128)(2,1)S(1)}, bf16[128,1024]{1,0:T(8,128)(2,1)S(1)}, u32[]{:S(2)}, u32[]{:S(2)}) collective-permute-start(bf16[128,1024]{1,0:T(8,128)(2,1)S(1)} %collective-permute-done.12), channel_id=1, source_target_pairs={{0,2},{2,0},{4,6},{6,4},{1,3},{3,1},{5,7},{7,5},{8,10},{10,8},{12,... | collective-permute-start | bytes 786440 | tf_op jit(solution)/shard_map/ppermute | solution.py:49
  34.3 9.4 %collective-permute-start.4 = (bf16[128,1024]{1,0:T(8,128)(2,1)S(1)}, bf16[128,1024]{1,0:T(8,128)(2,1)S(1)}, u32[]{:S(2)}, u32[]{:S(2)}) collective-permute-start(bf16[128,1024]{1,0:T(8,128)(2,1)S(1)} %broadcast_select_fusion.3.refs_5_.refs_9_), channel_id=1, source_target_pairs={{0,1},{1,0},{2,3},{3,2},{4,5},{5,4},{6,7},{7,6},{8,9},{9,8},{10,11... | collective-permute-start | bytes 786440 | tf_op jit(solution)/shard_map/ppermute | solution.py:70
  38.1 14.0 %collective-permute-start.17 = (bf16[128,1024]{1,0:T(8,128)(2,1)S(1)}, bf16[128,1024]{1,0:T(8,128)(2,1)S(1)}, u32[]{:S(2)}, u32[]{:S(2)}) collective-permute-start(bf16[128,1024]{1,0:T(8,128)(2,1)S(1)} %broadcast_select_fusion.1.refs_12_), channel_id=1, source_target_pairs={{0,1},{1,0},{2,3},{3,2},{4,5},{5,4},{6,7},{7,6},{8,9},{9,8},{10,11... | collective-permute-start | bytes 786440 | tf_op jit(solution)/shard_map/ppermute | solution.py:70
  40.6 11.5 %collective-permute-start.14 = (bf16[128,1024]{1,0:T(8,128)(2,1)S(1)}, bf16[128,1024]{1,0:T(8,128)(2,1)S(1)}, u32[]{:S(2)}, u32[]{:S(2)}) collective-permute-start(bf16[128,1024]{1,0:T(8,128)(2,1)S(1)} %collective-permute-done.3.refs_3_), channel_id=1, source_target_pairs={{0,2},{2,0},{4,6},{6,4},{1,3},{3,1},{5,7},{7,5},{8,10},{10,8},{12,... | collective-permute-start | bytes 786440 | tf_op jit(solution)/shard_map/ppermute | solution.py:67
  43.8 9.8 %collective-permute-start.18 = (bf16[128,1024]{1,0:T(8,128)(2,1)S(1)}, bf16[128,1024]{1,0:T(8,128)(2,1)S(1)}, u32[]{:S(2)}, u32[]{:S(2)}) collective-permute-start(bf16[128,1024]{1,0:T(8,128)(2,1)S(1)} %broadcast_select_fusion.refs_13_), channel_id=1, source_target_pairs={{0,1},{1,0},{2,3},{3,2},{4,5},{5,4},{6,7},{7,6},{8,9},{9,8},{10,11... | collective-permute-start | bytes 786440 | tf_op jit(solution)/shard_map/ppermute | solution.py:70
  46.3 3.4 %copy-start = (bf16[1,2,1024,2048]{3,2,1,0:T(8,128)(2,1)S(1)}, bf16[1,2,1024,2048]{3,2,1,0:T(8,128)(2,1)}, u32[]{:S(2)}) copy-start(bf16[1,2,1024,2048]{3,2,1,0:T(8,128)(2,1)} %param.7) | copy-start | bytes 25165828
  49.7 3.9 %copy-start.1 = (bf16[1,2,1024,2048]{3,2,1,0:T(8,128)(2,1)S(1)}, bf16[1,2,1024,2048]{3,2,1,0:T(8,128)(2,1)}, u32[]{:S(2)}) copy-start(bf16[1,2,1024,2048]{3,2,1,0:T(8,128)(2,1)} %param.7) | copy-start | bytes 25165828
  49.7 3.9 %copy-start.5 = (f32[2,16]{1,0:T(2,128)S(1)}, f32[2,16]{1,0:T(2,128)}, u32[]{:S(2)}) copy-start(f32[2,16]{1,0:T(2,128)} %table.3) | copy-start | bytes 388
  49.7 44.3 %copy-start.4 = (f32[64,1,1,2,512]{4,3,2,1,0:T(2,128)S(1)}, f32[64,1,1,2,512]{4,3,2,1,0:T(2,128)}, u32[]{:S(2)}) copy-start(f32[64,1,1,2,512]{4,3,2,1,0:T(2,128)} %param.9) | copy-start | bytes 786436
  53.6 1.0 copy-start.3
  61.5 17.2 %collective-permute-start.20 = (bf16[4,72,1024]{2,1,0:T(8,128)(2,1)S(1)}, bf16[4,72,1024]{2,1,0:T(8,128)(2,1)S(1)}, u32[]{:S(2)}, u32[]{:S(2)}) collective-permute-start(bf16[4,72,1024]{2,1,0:T(8,128)(2,1)S(1)} %bitcast.31), channel_id=1, source_target_pairs={{0,1},{1,0},{2,3},{3,2},{4,5},{5,4},{6,7},{7,6},{8,9},{9,8},{10,11... | collective-permute-start | bytes 1769480 | tf_op jit(solution)/shard_map/ppermute | solution.py:401
  64.5 41.4 %collective-permute-start.19 = (bf16[4096,128]{1,0:T(8,128)(2,1)}, bf16[4096,128]{1,0:T(8,128)(2,1)}, u32[]{:S(2)}, u32[]{:S(2)}) collective-permute-start(bf16[4096,128]{1,0:T(8,128)(2,1)} %get-tuple-element.31), channel_id=1, source_target_pairs={{0,1},{1,0},{2,3},{3,2},{4,5},{5,4},{6,7},{7,6},{8,9},{9,8},{10,11... | collective-permute-start | bytes 3145736 | tf_op jit(solution)/shard_map/ppermute | solution.py:445
  78.9 11.1 %collective-permute-start.21 = (bf16[72,1024]{1,0:T(8,128)(2,1)S(1)}, bf16[72,1024]{1,0:T(8,128)(2,1)S(1)}, u32[]{:S(2)}, u32[]{:S(2)}) collective-permute-start(bf16[72,1024]{1,0:T(8,128)(2,1)S(1)} %get-tuple-element.35), channel_id=1, source_target_pairs={{0,2},{2,4},{4,6},{6,0},{1,3},{3,5},{5,7},{7,1},{8,10},{10,12},{12... | collective-permute-start | bytes 442376 | tf_op jit(solution)/shard_map/ppermute | solution.py:413
  81.4 11.7 %collective-permute-start.22 = (bf16[72,1024]{1,0:T(8,128)(2,1)S(1)}, bf16[72,1024]{1,0:T(8,128)(2,1)S(1)}, u32[]{:S(2)}, u32[]{:S(2)}) collective-permute-start(bf16[72,1024]{1,0:T(8,128)(2,1)S(1)} %get-tuple-element.36), channel_id=1, source_target_pairs={{0,4},{2,6},{4,0},{6,2},{1,5},{3,7},{5,1},{7,3},{8,12},{10,14},{12... | collective-permute-start | bytes 442376 | tf_op jit(solution)/shard_map/ppermute | solution.py:413
  87.3 6.6 %collective-permute-start.23 = (bf16[72,1024]{1,0:T(8,128)(2,1)S(1)}, bf16[72,1024]{1,0:T(8,128)(2,1)S(1)}, u32[]{:S(2)}, u32[]{:S(2)}) collective-permute-start(bf16[72,1024]{1,0:T(8,128)(2,1)S(1)} %get-tuple-element.37), channel_id=1, source_target_pairs={{0,6},{2,0},{4,2},{6,4},{1,7},{3,1},{5,3},{7,5},{8,14},{10,8},{12,... | collective-permute-start | bytes 442376 | tf_op jit(solution)/shard_map/ppermute | solution.py:413
  95.3 6.1 %collective-permute-start.26 = (f32[288,128]{1,0:T(8,128)S(1)}, f32[288,128]{1,0:T(8,128)S(1)}, u32[]{:S(2)}, u32[]{:S(2)}) collective-permute-start(f32[288,128]{1,0:T(8,128)S(1)} %get-tuple-element.39), channel_id=1, source_target_pairs={{0,24},{8,16},{16,8},{24,0},{1,25},{9,17},{17,9},{25,1},{2,26},{10... | collective-permute-start | bytes 442376 | tf_op jit(solution)/shard_map/ppermute | solution.py:430
  95.3 9.3 %collective-permute-start.25 = (f32[288,128]{1,0:T(8,128)S(1)}, f32[288,128]{1,0:T(8,128)S(1)}, u32[]{:S(2)}, u32[]{:S(2)}) collective-permute-start(f32[288,128]{1,0:T(8,128)S(1)} %get-tuple-element.39), channel_id=1, source_target_pairs={{0,16},{8,24},{16,0},{24,8},{1,17},{9,25},{17,1},{25,9},{2,18},{10... | collective-permute-start | bytes 442376 | tf_op jit(solution)/shard_map/ppermute | solution.py:430
  96.8 7.8 %collective-permute-start.24 = (f32[288,128]{1,0:T(8,128)S(1)}, f32[288,128]{1,0:T(8,128)S(1)}, u32[]{:S(2)}, u32[]{:S(2)}) collective-permute-start(f32[288,128]{1,0:T(8,128)S(1)} %get-tuple-element.39), channel_id=1, source_target_pairs={{0,8},{8,0},{16,24},{24,16},{1,9},{9,1},{17,25},{25,17},{2,10},{10... | collective-permute-start | bytes 442376 | tf_op jit(solution)/shard_map/ppermute | solution.py:430

commit v2 on v1

--- a/solution.py
+++ b/solution.py
@@ -12,6 +12,7 @@
 BR = 8
 BC = 128
 MIB = 1 << 20
+SPLIT = (1, 3)
 
 
 def shift_pairs(rows, cols, step, valid):
@@ -111,9 +112,9 @@
             full[pl.ds(start, height), :] = pieces[step * chunks + chunk][...]
 
 
-def multiply(acc, inverse, full, ancestors, counts, i, source):
+def multiply(acc, inverse, full, ancestors, counts, pair, source):
     rows, _, row_blocks, col_blocks = counts[:4]
-    row_first, _, col_first, col_last = counts[4:]
+    row_first, row_count, col_first, col_last = counts[4:]
     stage_blocks = ancestors.shape[0] // rows
     low = source * stage_blocks
     r = lax.axis_index("row")
@@ -121,52 +122,75 @@
 
     @pl.when(jnp.logical_and(low < col_last, low + stage_blocks > col_first))
     def _():
-        row = pl.multiple_of((ancestors[row_first + i] - r * row_blocks) * BS, BS)
         left = []
         for n in range(stage_blocks):
             k = low + n
             inside = jnp.logical_and(k >= col_first, k < col_last)
             block = jnp.where(inside, ancestors[k] - c * col_blocks, 0)
-            value = inverse[:, pl.ds(row, BS), pl.ds(pl.multiple_of(block * BS, BS), BS)]
-            left.append(value.reshape(2 * BS, BS) * inside.astype(value.dtype))
+            column = pl.ds(pl.multiple_of(block * BS, BS), BS)
+            both = []
+            for i in range(2):
+                listed = ancestors[row_first + jnp.minimum(2 * pair + i, row_count - 1)]
+                row = pl.multiple_of((listed - r * row_blocks) * BS, BS)
+                both.append(inverse[:, pl.ds(row, BS), column].reshape(2 * BS, BS))
+            value = jnp.concatenate(both, axis=0)
+            left.append(value * inside.astype(value.dtype))
         place = pl.ds(pl.multiple_of(low * BS, BS), stage_blocks * BS)
         acc[...] += jnp.dot(
             jnp.concatenate(left, axis=1), full[place, :], preferred_element_type=jnp.float32
         )
 
 
-def combine(acc):
+def combine(acc, n):
     half = acc.shape[1] // 2
-    return acc[:BS, :half] - acc[BS:, half:], acc[:BS, half:] + acc[BS:, :half]
-
-
-def early_kernel(sources, stages, rows, cols, ancestors, inverse, *refs):
+    upper, lower = acc.at[2 * n * BS : (2 * n + 1) * BS], acc.at[(2 * n + 1) * BS : (2 * n + 2) * BS]
+    return upper[:, :half] - lower[:, half:], upper[:, half:] + lower[:, :half]
+
+
+def add_products(sources, stages, ancestors, inverse, before, full, acc, counts, store):
+    row_count = counts[5]
+
+    @pl.loop(0, (row_count + 1) // 2)
+    def _(pair):
+        if before is None:
+            acc[...] = jnp.zeros_like(acc)
+        else:
+            for n in range(2):
+                i = jnp.minimum(2 * pair + n, row_count - 1)
+                acc[2 * n * BS : (2 * n + 1) * BS, :] = before[i]
+                acc[(2 * n + 1) * BS : (2 * n + 2) * BS, :] = jnp.zeros((BS, acc.shape[1]), acc.dtype)
+        for stage in stages:
+            multiply(acc, inverse, full, ancestors, counts, pair, source_row(sources, stage))
+        for n in range(2):
+
+            @pl.when(2 * pair + n < row_count)
+            def _():
+                store(2 * pair + n, *combine(acc, n))
+
+
+def early_kernel(sources, stages, added, rows, cols, ancestors, inverse, *refs):
     early, full, acc = refs[-3:]
-    pieces = refs[:-3]
+    before = refs[0] if added else None
+    pieces = refs[1 if added else 0 : -3]
     each = len(pieces) // len(stages)
     half = acc.shape[1] // 2
     for n, stage in enumerate(stages):
         fill(full, pieces[n * each : (n + 1) * each], sources, stage, cols)
     counts = counts_of(ancestors, inverse, rows, cols)
 
-    @pl.loop(0, counts[5])
-    def _(i):
-        acc[...] = jnp.zeros_like(acc)
-        for stage in stages:
-            multiply(acc, inverse, full, ancestors, counts, i, source_row(sources, stage))
-        real, imag = combine(acc)
+    def store(i, real, imag):
         early[i, :, :half] = real
         early[i, :, half:] = imag
 
-
-def last_kernel(
-    sources, stages, rows, cols, ancestors, table, slot, owner, inverse, early, *refs
-):
-    keep, send, diag_keep, diag_send, full, acc, diag, tiles, leaving = refs[-9:]
-    pieces = refs[:-9]
+    add_products(sources, stages, ancestors, inverse, before, full, acc, counts, store)
+
+
+def last_kernel(sources, stages, rows, cols, ancestors, inverse, early, *refs):
+    keep, *sends, total, turned, full, acc, leaving = refs[-(6 + len(SPLIT)) :]
+    pieces = refs[: -(6 + len(SPLIT))]
     each = len(pieces) // rows
-    wide = acc.shape[1]
-    half = wide // 2
+    half = acc.shape[1] // 2
+    across = half // BC
     row_blocks = early.shape[0]
     own_blocks = row_blocks // cols
     r = lax.axis_index("row")
@@ -174,26 +198,16 @@
     for stage in range(rows):
         fill(full, pieces[stage * each : (stage + 1) * each], sources, stage, cols)
     counts = counts_of(ancestors, inverse, rows, cols)
-    row_first, row_count = counts[4:6]
+    row_first = counts[4]
     keep[...] = jnp.zeros_like(keep)
     leaving[...] = jnp.zeros_like(leaving)
-    diag[...] = jnp.zeros_like(diag)
-    tiles[...] = jnp.zeros_like(tiles)
-    weight_real = table[0, slot[0]]
-    weight_imag = table[1, slot[0]]
-
-    @pl.loop(0, row_count)
-    def _(i):
-        acc[:BS, :] = early[i]
-        acc[BS:, :] = jnp.zeros((BS, wide), jnp.float32)
-        for stage in stages:
-            multiply(acc, inverse, full, ancestors, counts, i, source_row(sources, stage))
-        real, imag = combine(acc)
+
+    def store(i, real, imag):
+        total[i, :, :half] = real
+        total[i, :, half:] = imag
         block = ancestors[row_first + i] - r * row_blocks
-        place = block // own_blocks
-        across = half // BC
         within = lax.rem(block, own_blocks) * (BS * 2 * across)
-        turn = lax.rem(place - c + cols, cols)
+        turn = lax.rem(block // own_blocks - c + cols, cols)
 
         def lay(target, start):
             for j in range(across):
@@ -209,6 +223,64 @@
         def _():
             lay(leaving, (turn - 1) * keep.shape[0] + within)
 
+        rows_of = full[pl.ds(pl.multiple_of((row_first + i) * BS, BS), BS), :]
+        left = jnp.concatenate([rows_of[:, :half], rows_of[:, half:]], axis=0)
+        turned[i] = left.T
+
+    add_products(sources, stages, ancestors, inverse, early, full, acc, counts, store)
+    height = keep.shape[0]
+    for step in range(cols - 1):
+        first = 0
+        for send, share in zip(sends, SPLIT):
+            size = height * share // sum(SPLIT)
+            value = leaving[step * height + first : step * height + first + size, :]
+            send[step * size : (step + 1) * size, :] = value.astype(send.dtype)
+            first += size
+
+
+def diag_kernel(poles, rows, cols, row_blocks, ancestors, table, slot, owner, total, turned, *refs):
+    diag_keep, diag_send, diag, tiles = refs
+    half, wide = diag.shape
+    across = half // BC
+    own_blocks = row_blocks // cols
+    r = lax.axis_index("row")
+    c = lax.axis_index("col")
+
+    def below(limit):
+        count = jnp.int32(0)
+        for i in range(ancestors.shape[0]):
+            count = count + (ancestors[i] < limit).astype(jnp.int32)
+        return count
+
+    row_first = below(r * row_blocks)
+    diag[...] = jnp.zeros_like(diag)
+    tiles[...] = jnp.zeros_like(tiles)
+    weight_real = table[0, slot[0]]
+    weight_imag = table[1, slot[0]]
+
+    @pl.loop(0, below((r + 1) * row_blocks) - row_first)
+    def _(i):
+        real = total[i, :, :half]
+        imag = total[i, :, half:]
+        left = turned[i]
+        real_high = real.astype(jnp.bfloat16)
+        imag_high = imag.astype(jnp.bfloat16)
+        real_low = (real - real_high.astype(jnp.float32)).astype(jnp.bfloat16)
+        imag_low = (imag - imag_high.astype(jnp.float32)).astype(jnp.bfloat16)
+        right = jnp.concatenate(
+            [
+                jnp.concatenate([real_high, imag_high], axis=1),
+                jnp.concatenate([-imag_high, real_high], axis=1),
+                jnp.concatenate([real_low, imag_low], axis=1),
+                jnp.concatenate([-imag_low, real_low], axis=1),
+            ],
+            axis=0,
+        )
+        diag[...] += jnp.dot(
+            jnp.concatenate([left, left], axis=1), right, preferred_element_type=jnp.float32
+        )
+        block = ancestors[row_first + i] - r * row_blocks
+        place = block // own_blocks
         mixed = -(weight_real * imag + weight_imag * real)
         per_device = own_blocks * (BS // BR) * across
         first = lax.rem(c - place + cols, cols) * per_device + lax.rem(block, own_blocks) * (
@@ -219,29 +291,7 @@
                 tile = owner[first + group * across + j]
                 tiles[j, tile] += mixed[group * BR : (group + 1) * BR, j * BC : (j + 1) * BC]
 
-        rows_of = full[pl.ds(pl.multiple_of((row_first + i) * BS, BS), BS), :]
-        real_high = real.astype(jnp.bfloat16)
-        imag_high = imag.astype(jnp.bfloat16)
-        real_low = (real - real_high.astype(jnp.float32)).astype(jnp.bfloat16)
-        imag_low = (imag - imag_high.astype(jnp.float32)).astype(jnp.bfloat16)
-        left = jnp.concatenate([rows_of[:, :half], rows_of[:, half:]], axis=0)
-        left = jnp.concatenate([left, left], axis=0)
-        right = jnp.concatenate(
-            [
-                jnp.concatenate([real_high, imag_high], axis=1),
-                jnp.concatenate([-imag_high, real_high], axis=1),
-                jnp.concatenate([real_low, imag_low], axis=1),
-                jnp.concatenate([-imag_low, real_low], axis=1),
-            ],
-            axis=0,
-        )
-        diag[...] += lax.dot_general(
-            left, right, (((0,), (0,)), ((), ())), preferred_element_type=jnp.float32
-        )
-
-    send[...] = leaving[...].astype(send.dtype)
     part = half // (rows * cols)
-    poles = tiles.shape[1] // (rows * cols)
     for row in range(rows):
         for step in range(cols):
             place = row * cols + lax.rem(c + step, cols)
@@ -253,13 +303,30 @@
                 diag_send[step - 1, row, :part] = value.astype(diag_send.dtype)
                 diag_send[step - 1, row, part:] = jnp.zeros((BR, wide), diag_send.dtype)
             for pole in range(poles):
-                total = tiles[0, pole * rows * cols + place]
-                for j in range(1, half // BC):
-                    total = total + tiles[j, pole * rows * cols + place]
+                sum_of = tiles[0, pole * rows * cols + place]
+                for j in range(1, across):
+                    sum_of = sum_of + tiles[j, pole * rows * cols + place]
                 if step == 0:
-                    diag_keep[row, part:, 2 * pole * BC : (2 * pole + 1) * BC] = total
+                    diag_keep[row, part:, 2 * pole * BC : (2 * pole + 1) * BC] = sum_of
                 else:
-                    diag_send[step - 1, row, part:, 2 * pole * BC : 2 * (pole + 1) * BC] = halves(total)
+                    diag_send[step - 1, row, part:, 2 * pole * BC : 2 * (pole + 1) * BC] = halves(sum_of)
+
+
+def join_kernel(steps, keep, *refs):
+    out = refs[-1]
+    block = pl.program_id(0)
+    first = 0
+    for n, share in enumerate(SPLIT):
+        arrived = refs[n * steps : (n + 1) * steps]
+
+        @pl.when(jnp.logical_and(block >= first, block < first + share))
+        def _():
+            value = keep[...]
+            for ref in arrived:
+                value = value + ref[...].astype(jnp.float32)
+            out[...] = value
+
+        first += share
 
 
 def halves(value):
@@ -353,52 +420,74 @@
     stages = [[chunk for step in stage for chunk in step] for stage in stages]
     late_owners, _ = lax.optimization_barrier((tuple(owners), stages[2][-1]))
     products = 2 * row_blocks * BS * 2 * wide * selected * BS // cols
-    first = (0, rows - 2)
-    last = tuple(stage for stage in range(rows) if stage not in first)
-    early_pieces = [piece for stage in first for piece in stages[stage]]
-    early = pl.pallas_call(
-        functools.partial(early_kernel, sources, first, rows, cols),
-        out_shape=jax.ShapeDtypeStruct((row_blocks, BS, wide), jnp.float32),
-        in_specs=[smem, vmem] + [vmem] * len(early_pieces),
-        out_specs=vmem,
-        scratch_shapes=[
-            pltpu.VMEM((selected * BS, wide), jnp.bfloat16),
-            pltpu.VMEM((2 * BS, wide), jnp.float32),
-        ],
-        compiler_params=pltpu.CompilerParams(vmem_limit_bytes=24 * MIB),
-        cost_estimate=pl.CostEstimate(
-            flops=products * len(first) // rows, bytes_accessed=4 * MIB, transcendentals=0
-        ),
-        name="early_products",
-    )(ancestors[0], here, *early_pieces)
+    scratch = [
+        pltpu.VMEM((selected * BS, wide), jnp.bfloat16),
+        pltpu.VMEM((4 * BS, wide), jnp.float32),
+    ]
+    row_products = jax.ShapeDtypeStruct((row_blocks, BS, wide), jnp.float32)
+    groups = [(0,)] + ([(rows - 2,)] if rows > 2 else [])
+    last = tuple(stage for stage in range(rows) if (stage,) not in groups)
+    early = []
+    for group in groups:
+        group_pieces = [piece for stage in group for piece in stages[stage]]
+        early = [
+            pl.pallas_call(
+                functools.partial(early_kernel, sources, group, bool(early), rows, cols),
+                out_shape=row_products,
+                in_specs=[smem, vmem] + [vmem] * (len(early) + len(group_pieces)),
+                out_specs=vmem,
+                scratch_shapes=scratch,
+                input_output_aliases={2: 0} if early else {},
+                compiler_params=pltpu.CompilerParams(vmem_limit_bytes=24 * MIB),
+                cost_estimate=pl.CostEstimate(
+                    flops=products * len(group) // rows,
+                    bytes_accessed=4 * MIB,
+                    transcendentals=0,
+                ),
+                name="early_products",
+            )(ancestors[0], here, *early, *group_pieces)
+        ]
     all_pieces = [piece for stage in stages for piece in stage]
     others = max(1, cols - 1)
     laid_rows = rows_here * wide // BC
-    keep, send, diag_keep, diag_send = pl.pallas_call(
+    sizes = [laid_rows * share // sum(SPLIT) for share in SPLIT]
+    keep, *sends, total, turned = pl.pallas_call(
         functools.partial(last_kernel, sources, last, rows, cols),
+        out_shape=(jax.ShapeDtypeStruct((laid_rows, BC), jnp.float32),)
+        + tuple(jax.ShapeDtypeStruct((others * size, BC), jnp.bfloat16) for size in sizes)
+        + (row_products, jax.ShapeDtypeStruct((row_blocks, half, 2 * BS), jnp.bfloat16)),
+        in_specs=[smem] + [vmem] * (2 + len(all_pieces)),
+        out_specs=(vmem,) * (3 + len(SPLIT)),
+        scratch_shapes=scratch + [pltpu.VMEM((others * laid_rows, BC), jnp.float32)],
+        compiler_params=pltpu.CompilerParams(vmem_limit_bytes=28 * MIB),
+        cost_estimate=pl.CostEstimate(
+            flops=products // 2, bytes_accessed=8 * MIB, transcendentals=0
+        ),
+        name="last_products",
+    )(ancestors[0], here, *early, *all_pieces)
+    diag_keep, diag_send = pl.pallas_call(
+        functools.partial(diag_kernel, poles, rows, cols, row_blocks),
         out_shape=(
-            jax.ShapeDtypeStruct((laid_rows, BC), jnp.float32),
-            jax.ShapeDtypeStruct((others * laid_rows, BC), jnp.bfloat16),
             jax.ShapeDtypeStruct((rows, part + BR, wide), jnp.float32),
             jax.ShapeDtypeStruct((others, rows, part + BR, wide), jnp.bfloat16),
         ),
-        in_specs=[smem] * 4 + [vmem] * (2 + len(all_pieces)),
-        out_specs=(vmem,) * 4,
+        in_specs=[smem] * 4 + [vmem] * 2,
+        out_specs=(vmem,) * 2,
         scratch_shapes=[
-            pltpu.VMEM((selected * BS, wide), jnp.bfloat16),
-            pltpu.VMEM((2 * BS, wide), jnp.float32),
             pltpu.VMEM((half, wide), jnp.float32),
             pltpu.VMEM((half // BC, tile_count, BR, BC), jnp.float32),
-            pltpu.VMEM((others * laid_rows, BC), jnp.float32),
         ],
-        compiler_params=pltpu.CompilerParams(vmem_limit_bytes=28 * MIB),
-        cost_estimate=pl.CostEstimate(flops=products, bytes_accessed=8 * MIB, transcendentals=0),
-        name="last_products",
-    )(ancestors[0], weight_table, pole_slot, jnp.concatenate(late_owners), here, early, *all_pieces)
+        compiler_params=pltpu.CompilerParams(vmem_limit_bytes=20 * MIB),
+        cost_estimate=pl.CostEstimate(
+            flops=products // 2, bytes_accessed=8 * MIB, transcendentals=0
+        ),
+        name="diag_products",
+    )(ancestors[0], weight_table, pole_slot, jnp.concatenate(late_owners), total, turned)
 
     everyone_pairs = [shift_pairs(rows, cols, step, everyone) for step in range(cols)]
     arrived = [
-        lax.ppermute(diag_send[step - 1], grid, everyone_pairs[step]) for step in range(1, cols)
+        lax.ppermute(diag_send[step - 1], grid, everyone_pairs[step])
+        for step in range(1, cols)
     ]
     *rounded, own = pl.pallas_call(
         functools.partial(regroup_kernel, poles, rows),
@@ -439,10 +528,30 @@
     start = split + lax.axis_index("pole") * BR
     tile_sum = summed([lax.dynamic_slice_in_dim(value, start, BR) for value in messages])[None]
 
-    column = keep
-    for step in range(1, cols):
-        leaving = send[(step - 1) * laid_rows : step * laid_rows]
-        column = column + lax.ppermute(leaving, grid, everyone_pairs[step])
+    parts = []
+    for send, size in zip(sends, sizes):
+        parts += [
+            lax.ppermute(send[(step - 1) * size : step * size], grid, everyone_pairs[step])
+            for step in range(1, cols)
+        ]
+    block = laid_rows // sum(SPLIT)
+    specs = [pl.BlockSpec((block, BC), lambda i: (i, 0))]
+    first = 0
+    for share in SPLIT:
+        spec = pl.BlockSpec(
+            (block, BC), lambda i, f=first, n=share: (jnp.clip(i - f, 0, n - 1), 0)
+        )
+        specs += [spec] * (cols - 1)
+        first += share
+    column = pl.pallas_call(
+        functools.partial(join_kernel, cols - 1),
+        grid=(sum(SPLIT),),
+        out_shape=jax.ShapeDtypeStruct((laid_rows, BC), jnp.float32),
+        in_specs=specs,
+        out_specs=pl.BlockSpec((block, BC), lambda i: (i, 0)),
+        compiler_params=pltpu.CompilerParams(vmem_limit_bytes=16 * MIB),
+        name="join_columns",
+    )(keep, *parts)
     column_out = plain(column, (rows_here, 1, 1, 2, half))
     return (column_out, diag_inverse, density_diag, tile_sum)
 

time: 109 us -> 110 us (level)
  starting transfers between devices: 53.5 us -> 46.2 us
  waiting for transfers between devices: 33 us -> 38.6 us
  Pallas kernels: 11 us -> 15 us
    pallas_call x1 -> x4, Pallas kernels: 2.43 us -> 8.67 us  [the longest x2 3.65 us: compute(): pl.pallas_call(functools.partial(early_kernel, sources, group, bool(early...]
    ppermute x2, waiting for transfers between devices: 0.01 us -> 5.37 us  [gather_stages(): cross_out = lax.ppermute(cross, 'row', outer)]
    ppermute x1 -> x2, starting transfers between devices: 0.02 us -> 3.12 us  [compute(): lax.ppermute(send[(step - 1) * size:step * size], grid, everyone_pairs[st...]
    add x1 -> x0, other arithmetic: 2.71 us -> none  [compute(): column = column + lax.ppermute(leaving, grid, everyone_pairs[step])]
    ppermute x7, waiting for transfers between devices: 4.89 us -> 7.6 us  [gather_stages(): last = lax.ppermute(leaving, grid, pairs)]
    ppermute x2, starting transfers between devices: 6.69 us -> 4.04 us  [gather_stages(): far_out = lax.ppermute(far, 'row', outer)]
    pallas_call x1, Pallas kernels: 7.04 us -> 4.82 us  [compute(): pl.pallas_call(functools.partial(last_kernel, sources, last, rows, cols),...]
    ppermute x3, waiting for transfers between devices: 7.45 us -> 5.26 us  [compute(): lax.ppermute(message, 'pole', [(i, i ^ step) for i in range(poles)])]
  transfers between devices with their start and end apart: 27 -> 28, of which waited for: 9 -> 12; matrix products, arithmetic and copies ran while one was open for 1% -> 0% of each run, Pallas kernels for 4% -> 6%
where the time goes in v2:
time: 110 us
  starting transfers between devices  46.2 us (42%)
  waiting for transfers between devices  38.6 us (35%)
  Pallas kernels  15 us (14%)
  local copies, waits for them, and re-layouts  5.63 us (5%)
  other arithmetic  3.05 us (3%)
  between operations  1.56 us (1%)
    ppermute x1, waiting for transfers between devices, compute(): lax.ppermute(diag_send[step - 1], grid, everyone_pairs[step])  14.2 us
    ppermute x7, starting transfers between devices, gather_stages(): last = lax.ppermute(leaving, grid, pairs)  9.85 us
    ppermute x2, starting transfers between devices, gather_stages(): near = lax.ppermute(own, 'row', outer)  7.75 us
    ppermute x7, waiting for transfers between devices, gather_stages(): last = lax.ppermute(leaving, grid, pairs)  7.6 us
    ppermute x2, starting transfers between devices, gather_stages(): cross_out = lax.ppermute(cross, 'row', outer)  6.73 us
    ppermute x3, starting transfers between devices, compute(): lax.ppermute(rounded[step - 1], 'row', [(i, (i + step) % rows) for i in r...  6.61 us
    ppermute x2, waiting for transfers between devices, gather_stages(): cross_out = lax.ppermute(cross, 'row', outer)  5.37 us
    ppermute x3, waiting for transfers between devices, compute(): lax.ppermute(message, 'pole', [(i, i ^ step) for i in range(poles)])  5.26 us
  transfers between devices with their start and end apart: 28, of which 12 were waited for; matrix products, arithmetic and copies ran while one was open for 0% of the time, Pallas kernels for 6%

profile of v2, /device:TPU:0, one launch (start us, length us, event | category | flops | bytes accessed | tf_op | source)
XLA Modules:
  0.0 110.0 jit_solution(2210239616436458200)
XLA Ops:
  0.6 1.1 slice_bitcast_fusion
  1.7 0.7 collective-permute-start.2
  2.4 5.9 %collective-permute-start.6 = (bf16[128,1024]{1,0:T(8,128)(2,1)S(1)}, bf16[128,1024]{1,0:T(8,128)(2,1)S(1)}, u32[]{:S(2)}, u32[]{:S(2)}) collective-permute-start(bf16[128,1024]{1,0:T(8,128)(2,1)S(1)} %get-tuple-element.51.refs_0_), channel_id=1, source_target_pairs={{0,2},{2,0},{4,6},{6,4},{1,3},{3,1},{5,7},{7,5},{8,10},{10,8},{12,... | collective-permute-start | bytes 786440 | tf_op jit(solution)/shard_map/ppermute | solution.py:46
  8.3 1.5 %collective-permute-start = (bf16[128,1024]{1,0:T(8,128)(2,1)S(1)}, bf16[128,1024]{1,0:T(8,128)(2,1)S(1)}, u32[]{:S(2)}, u32[]{:S(2)}) collective-permute-start(bf16[128,1024]{1,0:T(8,128)(2,1)S(1)} %get-tuple-element.51.refs_0_), channel_id=1, source_target_pairs={{0,1},{1,0},{2,3},{3,2},{4,5},{5,4},{6,7},{7,6},{8,9},{9,8},{10,11... | collective-permute-start | bytes 786440 | tf_op jit(solution)/shard_map/ppermute | solution.py:71
  9.8 0.7 collective-permute-start.4
  10.5 1.8 %collective-permute-start.10 = (bf16[128,1024]{1,0:T(8,128)(2,1)S(1)}, bf16[128,1024]{1,0:T(8,128)(2,1)S(1)}, u32[]{:S(2)}, u32[]{:S(2)}) collective-permute-start(bf16[128,1024]{1,0:T(8,128)(2,1)S(1)} %get-tuple-element.50.refs_1_), channel_id=1, source_target_pairs={{0,2},{2,0},{4,6},{6,4},{1,3},{3,1},{5,7},{7,5},{8,10},{10,8},{12,... | collective-permute-start | bytes 786440 | tf_op jit(solution)/shard_map/ppermute | solution.py:46
  12.3 3.4 %collective-permute-start.3 = (bf16[128,1024]{1,0:T(8,128)(2,1)S(1)}, bf16[128,1024]{1,0:T(8,128)(2,1)S(1)}, u32[]{:S(2)}, u32[]{:S(2)}) collective-permute-start(bf16[128,1024]{1,0:T(8,128)(2,1)S(1)} %collective-permute-done.2), channel_id=1, source_target_pairs={{0,2},{2,0},{4,6},{6,4},{1,3},{3,1},{5,7},{7,5},{8,10},{10,8},{12,... | collective-permute-start | bytes 786440 | tf_op jit(solution)/shard_map/ppermute | solution.py:48
  15.7 0.7 collective-permute-start.14
  16.4 1.7 %collective-permute-start.7 = (bf16[128,1024]{1,0:T(8,128)(2,1)S(1)}, bf16[128,1024]{1,0:T(8,128)(2,1)S(1)}, u32[]{:S(2)}, u32[]{:S(2)}) collective-permute-start(bf16[128,1024]{1,0:T(8,128)(2,1)S(1)} %collective-permute-done.6.refs_4_), channel_id=1, source_target_pairs={{0,1},{1,0},{2,3},{3,2},{4,5},{5,4},{6,7},{7,6},{8,9},{9,8},{10,11... | collective-permute-start | bytes 786440 | tf_op jit(solution)/shard_map/ppermute | solution.py:71
  18.1 3.3 %collective-permute-start.5 = (bf16[128,1024]{1,0:T(8,128)(2,1)S(1)}, bf16[128,1024]{1,0:T(8,128)(2,1)S(1)}, u32[]{:S(2)}, u32[]{:S(2)}) collective-permute-start(bf16[128,1024]{1,0:T(8,128)(2,1)S(1)} %collective-permute-done.4), channel_id=1, source_target_pairs={{0,2},{2,0},{4,6},{6,4},{1,3},{3,1},{5,7},{7,5},{8,10},{10,8},{12,... | collective-permute-start | bytes 786440 | tf_op jit(solution)/shard_map/ppermute | solution.py:48
  21.5 0.7 collective-permute-start.11
  22.8 3.9 %collective-permute-done.3 = bf16[128,1024]{1,0:T(8,128)(2,1)S(1)} collective-permute-done((bf16[128,1024]{1,0:T(8,128)(2,1)S(1)}, bf16[128,1024]{1,0:T(8,128)(2,1)S(1)}, u32[]{:S(2)}, u32[]{:S(2)}) %collective-permute-start.3) | collective-permute-done | bytes 262176 | tf_op jit(solution)/shard_map/ppermute | solution.py:48
  26.7 1.5 %collective-permute-start.1 = (bf16[128,1024]{1,0:T(8,128)(2,1)S(1)}, bf16[128,1024]{1,0:T(8,128)(2,1)S(1)}, u32[]{:S(2)}, u32[]{:S(2)}) collective-permute-start(bf16[128,1024]{1,0:T(8,128)(2,1)S(1)} %get-tuple-element.50.refs_1_), channel_id=1, source_target_pairs={{0,1},{1,0},{2,3},{3,2},{4,5},{5,4},{6,7},{7,6},{8,9},{9,8},{10,11... | collective-permute-start | bytes 786440 | tf_op jit(solution)/shard_map/ppermute | solution.py:71
  28.2 2.0 %collective-permute-start.15 = (bf16[128,1024]{1,0:T(8,128)(2,1)S(1)}, bf16[128,1024]{1,0:T(8,128)(2,1)S(1)}, u32[]{:S(2)}, u32[]{:S(2)}) collective-permute-start(bf16[128,1024]{1,0:T(8,128)(2,1)S(1)} %collective-permute-done.14), channel_id=1, source_target_pairs={{0,2},{2,0},{4,6},{6,4},{1,3},{3,1},{5,7},{7,5},{8,10},{10,8},{12,... | collective-permute-start | bytes 786440 | tf_op jit(solution)/shard_map/ppermute | solution.py:50
  30.3 0.6 collective-permute-start.20
  30.9 1.4 %collective-permute-done.5 = bf16[128,1024]{1,0:T(8,128)(2,1)S(1)} collective-permute-done((bf16[128,1024]{1,0:T(8,128)(2,1)S(1)}, bf16[128,1024]{1,0:T(8,128)(2,1)S(1)}, u32[]{:S(2)}, u32[]{:S(2)}) %collective-permute-start.5) | collective-permute-done | bytes 262176 | tf_op jit(solution)/shard_map/ppermute | solution.py:48
  32.3 1.5 %collective-permute-start.8 = (bf16[128,1024]{1,0:T(8,128)(2,1)S(1)}, bf16[128,1024]{1,0:T(8,128)(2,1)S(1)}, u32[]{:S(2)}, u32[]{:S(2)}) collective-permute-start(bf16[128,1024]{1,0:T(8,128)(2,1)S(1)} %broadcast_select_fusion.3.refs_1_.refs_8_), channel_id=1, source_target_pairs={{0,1},{1,0},{2,3},{3,2},{4,5},{5,4},{6,7},{7,6},{8,9},{9,8},{10,11... | collective-permute-start | bytes 786440 | tf_op jit(solution)/shard_map/ppermute | solution.py:71
  33.9 2.0 %collective-permute-start.12 = (bf16[128,1024]{1,0:T(8,128)(2,1)S(1)}, bf16[128,1024]{1,0:T(8,128)(2,1)S(1)}, u32[]{:S(2)}, u32[]{:S(2)}) collective-permute-start(bf16[128,1024]{1,0:T(8,128)(2,1)S(1)} %collective-permute-done.11), channel_id=1, source_target_pairs={{0,2},{2,0},{4,6},{6,4},{1,3},{3,1},{5,7},{7,5},{8,10},{10,8},{12,... | collective-permute-start | bytes 786440 | tf_op jit(solution)/shard_map/ppermute | solution.py:50
  35.9 0.6 collective-permute-start.9
  36.5 1.5 %collective-permute-done.15 = bf16[128,1024]{1,0:T(8,128)(2,1)S(1)} collective-permute-done((bf16[128,1024]{1,0:T(8,128)(2,1)S(1)}, bf16[128,1024]{1,0:T(8,128)(2,1)S(1)}, u32[]{:S(2)}, u32[]{:S(2)}) %collective-permute-start.15) | collective-permute-done | bytes 262176 | tf_op jit(solution)/shard_map/ppermute | solution.py:50
  38.0 3.5 %collective-permute-done.8.refs_3_.refs_10_ = bf16[128,1024]{1,0:T(8,128)(2,1)S(1)} collective-permute-done((bf16[128,1024]{1,0:T(8,128)(2,1)S(1)}, bf16[128,1024]{1,0:T(8,128)(2,1)S(1)}, u32[]{:S(2)}, u32[]{:S(2)}) %collective-permute-start.8) | collective-permute-done | bytes 262176 | tf_op jit(solution)/shard_map/ppermute | solution.py:71
  41.5 1.5 %collective-permute-start.16 = (bf16[128,1024]{1,0:T(8,128)(2,1)S(1)}, bf16[128,1024]{1,0:T(8,128)(2,1)S(1)}, u32[]{:S(2)}, u32[]{:S(2)}) collective-permute-start(bf16[128,1024]{1,0:T(8,128)(2,1)S(1)} %broadcast_select_fusion.1.refs_12_), channel_id=1, source_target_pairs={{0,1},{1,0},{2,3},{3,2},{4,5},{5,4},{6,7},{7,6},{8,9},{9,8},{10,11... | collective-permute-start | bytes 786440 | tf_op jit(solution)/shard_map/ppermute | solution.py:71
  43.1 4.1 %collective-permute-done.9.refs_4_.refs_11_ = bf16[128,1024]{1,0:T(8,128)(2,1)S(1)} collective-permute-done((bf16[128,1024]{1,0:T(8,128)(2,1)S(1)}, bf16[128,1024]{1,0:T(8,128)(2,1)S(1)}, u32[]{:S(2)}, u32[]{:S(2)}) %collective-permute-start.9) | collective-permute-done | bytes 262176 | tf_op jit(solution)/shard_map/ppermute | solution.py:71
  47.1 1.5 %collective-permute-start.17 = (bf16[128,1024]{1,0:T(8,128)(2,1)S(1)}, bf16[128,1024]{1,0:T(8,128)(2,1)S(1)}, u32[]{:S(2)}, u32[]{:S(2)}) collective-permute-start(bf16[128,1024]{1,0:T(8,128)(2,1)S(1)} %broadcast_select_fusion.refs_13_), channel_id=1, source_target_pairs={{0,1},{1,0},{2,3},{3,2},{4,5},{5,4},{6,7},{7,6},{8,9},{9,8},{10,11... | collective-permute-start | bytes 786440 | tf_op jit(solution)/shard_map/ppermute | solution.py:71
  48.6 2.0 %collective-permute-start.13 = (bf16[128,1024]{1,0:T(8,128)(2,1)S(1)}, bf16[128,1024]{1,0:T(8,128)(2,1)S(1)}, u32[]{:S(2)}, u32[]{:S(2)}) collective-permute-start(bf16[128,1024]{1,0:T(8,128)(2,1)S(1)} %collective-permute-done.1.refs_3_), channel_id=1, source_target_pairs={{0,2},{2,0},{4,6},{6,4},{1,3},{3,1},{5,7},{7,5},{8,10},{10,8},{12,... | collective-permute-start | bytes 786440 | tf_op jit(solution)/shard_map/ppermute | solution.py:68
  50.7 3.4 %copy-done = bf16[1,2,1024,2048]{3,2,1,0:T(8,128)(2,1)S(1)} copy-done((bf16[1,2,1024,2048]{3,2,1,0:T(8,128)(2,1)S(1)}, bf16[1,2,1024,2048]{3,2,1,0:T(8,128)(2,1)}, u32[]{:S(2)}) %copy-start) | copy-done | bytes 8388632
  54.1 2.5 %early_products.2.refs_0_ = f32[8,128,1024]{2,1,0:T(8,128)S(1)} custom-call(s32[16]{0:T(128)S(1)} %bitcast.32, bf16[2,1024,2048]{2,1,0:T(8,128)(2,1)S(1)} %bitcast.26, bf16[128,1024]{1,0:T(8,128)(2,1)S(1)} %get-tuple-element.51.refs_0_, bf16[128,1024]{1,0:T(8,128)(2,1)S(1)} %get-tuple-element.50.refs_1_, bf16[128,1024]{1,0:T(8,128)(2,1)S(1)} %collective-permute-done.refs_2_, ...), custom_call_target="tpu_custom_call" | custom-call | flops 1073741824 | bytes 4194304 | tf_op jit(solution)/shard_map/early_products/pallas_call | solution.py:434
  56.7 1.1 %early_products.3.early = f32[8,128,1024]{2,1,0:T(8,128)S(1)} custom-call(s32[16]{0:T(128)S(1)} %bitcast.33, bf16[2,1024,2048]{2,1,0:T(8,128)(2,1)S(1)} %bitcast.27, f32[8,128,1024]{2,1,0:T(8,128)S(1)} %early_products.2.refs_0_, bf16[128,1024]{1,0:T(8,128)(2,1)S(1)} %broadcast_select_fusion.3.refs_1_.refs_8_, ...), custom_call_target="tpu_custom_call", output_to_operand_aliasing={{}: (2, {})} | custom-call | flops 1073741824 | bytes 4194304 | tf_op jit(solution)/shard_map/early_products/pallas_call | solution.py:434
  57.9 0.9 slice-done.1
  59.0 4.8 %last_products.1 = (f32[4096,128]{1,0:T(8,128)S(1)}, bf16[1024,128]{1,0:T(8,128)(2,1)}, bf16[3072,128]{1,0:T(8,128)(2,1)}, f32[8,128,1024]{2,1,0:T(8,128)S(1)}, bf16[8,512,256]{2,1,0:T(8,128)(2,1)S(1)}) custom-call(s32[16]{0:T(128)S(1)} %bitcast.34, bf16[2,1024,2048]{2,1,0:T(8,128)(2,1)S(1)} %bitcast.30, f32[8,128,1024]{2,1,0:T(8,128)S(1)} %early_products.3.early, ...), custom_call_target="tpu_custom_call" | custom-call | flops 2147483648 | bytes 8388608 | tf_op jit(solution)/shard_map/last_products/pallas_call | solution.py:454
  63.9 3.1 %diag_products.1 = (f32[4,72,1024]{2,1,0:T(8,128)S(1)}, bf16[1,4,72,1024]{3,2,1,0:T(8,128)(2,1)S(1)}) custom-call(s32[16]{0:T(128)S(1)} %bitcast.35, f32[2,16]{1,0:T(2,128)S(1)} %copy-done.9, s32[1]{0:T(128)S(6)} %copy.17.slot, s32[512]{0:T(512)S(1)} %pad_add_fusion.owner, f32[8,128,1024]{2,1,0:T(8,128)S(1)} %get-tuple-element.36.total, ...), custom_call_target="tpu_custom_call" | custom-call | flops 2147483648 | bytes 8388608 | tf_op jit(solution)/shard_map/diag_products/pallas_call | solution.py:468
  67.0 1.0 collective-permute-start.21
  68.0 1.1 %collective-permute-start.19 = (bf16[3072,128]{1,0:T(8,128)(2,1)}, bf16[3072,128]{1,0:T(8,128)(2,1)S(1)}, u32[]{:S(2)}, u32[]{:S(2)}) collective-permute-start(bf16[3072,128]{1,0:T(8,128)(2,1)} %get-tuple-element.33), channel_id=1, source_target_pairs={{0,1},{1,0},{2,3},{3,2},{4,5},{5,4},{6,7},{7,6},{8,9},{9,8},{10,11... | collective-permute-start | bytes 2359304 | tf_op jit(solution)/shard_map/ppermute | solution.py:534
  69.1 14.2 %collective-permute-done.21.refs_0_ = bf16[4,72,1024]{2,1,0:T(8,128)(2,1)S(1)} collective-permute-done((bf16[4,72,1024]{2,1,0:T(8,128)(2,1)S(1)}, bf16[4,72,1024]{2,1,0:T(8,128)(2,1)S(1)}, u32[]{:S(2)}, u32[]{:S(2)}) %collective-permute-start.21) | collective-permute-done | bytes 589856 | tf_op jit(solution)/shard_map/ppermute | solution.py:489
  83.3 0.1 regroup.1
  83.5 6.6 %collective-permute-start.23 = (bf16[72,1024]{1,0:T(8,128)(2,1)S(1)}, bf16[72,1024]{1,0:T(8,128)(2,1)S(1)}, u32[]{:S(2)}, u32[]{:S(2)}) collective-permute-start(bf16[72,1024]{1,0:T(8,128)(2,1)S(1)} %get-tuple-element.42), channel_id=1, source_target_pairs={{0,4},{2,6},{4,0},{6,2},{1,5},{3,7},{5,1},{7,3},{8,12},{10,14},{12... | collective-permute-start | bytes 442376 | tf_op jit(solution)/shard_map/ppermute | solution.py:502
  90.0 2.0 %collective-permute-start.18 = (bf16[1024,128]{1,0:T(8,128)(2,1)}, bf16[1024,128]{1,0:T(8,128)(2,1)S(1)}, u32[]{:S(2)}, u32[]{:S(2)}) collective-permute-start(bf16[1024,128]{1,0:T(8,128)(2,1)} %get-tuple-element.32), channel_id=1, source_target_pairs={{0,1},{1,0},{2,3},{3,2},{4,5},{5,4},{6,7},{7,6},{8,9},{9,8},{10,11... | collective-permute-start | bytes 786440 | tf_op jit(solution)/shard_map/ppermute | solution.py:534
  92.1 0.6 collective-permute-done.22.refs_0_
  92.7 3.2 %collective-permute-done.23.refs_1_ = bf16[72,1024]{1,0:T(8,128)(2,1)S(1)} collective-permute-done((bf16[72,1024]{1,0:T(8,128)(2,1)S(1)}, bf16[72,1024]{1,0:T(8,128)(2,1)S(1)}, u32[]{:S(2)}, u32[]{:S(2)}) %collective-permute-start.23) | collective-permute-done | bytes 147488 | tf_op jit(solution)/shard_map/ppermute | solution.py:502
  95.9 0.8 collective-permute-done.24.refs_2_
  96.7 1.4 %finish.1 = (f32[512,128]{1,0:T(8,128)}, f32[288,128]{1,0:T(8,128)S(1)}) custom-call(f32[2,16]{1,0:T(2,128)S(1)} %copy-done.9, s32[1]{0:T(128)S(6)} %copy.17.slot, f32[512,128]{1,0:T(8,128)S(1)} %bitcast.31, f32[72,1024]{1,0:T(8,128)S(1)} %get-tuple-element.40.own, bf16[72,1024]{1,0:T(8,128)(2,1)S(1)} %collective-permute-done.22.refs_0_, ...), custom_call_target="tpu_custom_call" | custom-call | tf_op jit(solution)/shard_map/finish/pallas_call | solution.py:505
  98.0 1.5 %collective-permute-start.26 = (f32[288,128]{1,0:T(8,128)S(1)}, f32[288,128]{1,0:T(8,128)}, u32[]{:S(2)}, u32[]{:S(2)}) collective-permute-start(f32[288,128]{1,0:T(8,128)S(1)} %get-tuple-element.45), channel_id=1, source_target_pairs={{0,16},{8,24},{16,0},{24,8},{1,17},{9,25},{17,1},{25,9},{2,18},{10... | collective-permute-start | bytes 442376 | tf_op jit(solution)/shard_map/ppermute | solution.py:519
  99.5 0.4 collective-permute-start.27
  100.0 1.9 %join_columns.1 = f32[4096,128]{1,0:T(8,128)} custom-call(f32[4096,128]{1,0:T(8,128)S(1)} %get-tuple-element.31.keep, bf16[1024,128]{1,0:T(8,128)(2,1)S(1)} %collective-permute-done.18.refs_0_, bf16[3072,128]{1,0:T(8,128)(2,1)S(1)} %collective-permute-done.19.refs_1_), custom_call_target="tpu_custom_call" | custom-call | tf_op jit(solution)/shard_map/join_columns/pallas_call | solution.py:546
  101.8 3.0 %collective-permute-done.26 = f32[288,128]{1,0:T(8,128)} collective-permute-done((f32[288,128]{1,0:T(8,128)S(1)}, f32[288,128]{1,0:T(8,128)}, u32[]{:S(2)}, u32[]{:S(2)}) %collective-permute-start.26) | collective-permute-done | bytes 147488 | tf_op jit(solution)/shard_map/ppermute | solution.py:519
  104.9 2.2 %collective-permute-done.27 = f32[288,128]{1,0:T(8,128)} collective-permute-done((f32[288,128]{1,0:T(8,128)S(1)}, f32[288,128]{1,0:T(8,128)}, u32[]{:S(2)}, u32[]{:S(2)}) %collective-permute-start.27) | collective-permute-done | bytes 147488 | tf_op jit(solution)/shard_map/ppermute | solution.py:519
  107.1 1.6 %fusion = f32[256,128]{1,0:T(8,128)} fusion(f32[288,128]{1,0:T(8,128)} %collective-permute-done.27, f32[288,128]{1,0:T(8,128)} %collective-permute-done.26, f32[288,128]{1,0:T(8,128)S(1)} %collective-permute-done.25, f32[288,128]{1,0:T(8,128)S(1)} %get-tuple-element.45), kind=kLoop, calls=%fused_computation.7 | loop fusion | flops 98304 | bytes 655360 | tf_op jit(solution)/shard_map/add | solution.py:523
  108.8 1.3 %add_bitcast_fusion = f32[1,8,128]{2,1,0:T(8,128)} fusion(f32[288,128]{1,0:T(8,128)} %collective-permute-done.27, s32[]{:T(128)S(6)} %select_n.31, f32[288,128]{1,0:T(8,128)} %collective-permute-done.26, f32[288,128]{1,0:T(8,128)S(1)} %collective-permute-done.25, f32[288,128]{1,0:T(8,128)S(1)} %get-tuple-element.45), kind=kLoop, calls=%fused_computation.9 | loop fusion | flops 3072 | bytes 20484 | tf_op jit(solution)/shard_map/broadcast_in_dim | solution.py:529
  (50 shorter events, 0.5 us)
Async XLA Ops:
  0.6 50.0 %copy-start.8 = (s32[1,16]{1,0:T(1,128)S(1)}, s32[1,16]{1,0:T(1,128)}, u32[]{:S(2)}) copy-start(s32[1,16]{1,0:T(1,128)} %param.10) | copy-start | bytes 196
  1.7 10.6 %collective-permute-start.2 = (bf16[128,1024]{1,0:T(8,128)(2,1)S(1)}, bf16[128,1024]{1,0:T(8,128)(2,1)S(1)}, u32[]{:S(2)}, u32[]{:S(2)}) collective-permute-start(bf16[128,1024]{1,0:T(8,128)(2,1)S(1)} %get-tuple-element.51.refs_0_), channel_id=1, source_target_pairs={{2,4},{4,2},{3,5},{5,3},{10,12},{12,10},{11,13},{13,11},{18,20},{2... | collective-permute-start | bytes 786440 | tf_op jit(solution)/shard_map/ppermute | solution.py:47
  2.4 13.3 %collective-permute-start.6 = (bf16[128,1024]{1,0:T(8,128)(2,1)S(1)}, bf16[128,1024]{1,0:T(8,128)(2,1)S(1)}, u32[]{:S(2)}, u32[]{:S(2)}) collective-permute-start(bf16[128,1024]{1,0:T(8,128)(2,1)S(1)} %get-tuple-element.51.refs_0_), channel_id=1, source_target_pairs={{0,2},{2,0},{4,6},{6,4},{1,3},{3,1},{5,7},{7,5},{8,10},{10,8},{12,... | collective-permute-start | bytes 786440 | tf_op jit(solution)/shard_map/ppermute | solution.py:46
  8.3 8.1 %collective-permute-start = (bf16[128,1024]{1,0:T(8,128)(2,1)S(1)}, bf16[128,1024]{1,0:T(8,128)(2,1)S(1)}, u32[]{:S(2)}, u32[]{:S(2)}) collective-permute-start(bf16[128,1024]{1,0:T(8,128)(2,1)S(1)} %get-tuple-element.51.refs_0_), channel_id=1, source_target_pairs={{0,1},{1,0},{2,3},{3,2},{4,5},{5,4},{6,7},{7,6},{8,9},{9,8},{10,11... | collective-permute-start | bytes 786440 | tf_op jit(solution)/shard_map/ppermute | solution.py:71
  9.8 8.3 %collective-permute-start.4 = (bf16[128,1024]{1,0:T(8,128)(2,1)S(1)}, bf16[128,1024]{1,0:T(8,128)(2,1)S(1)}, u32[]{:S(2)}, u32[]{:S(2)}) collective-permute-start(bf16[128,1024]{1,0:T(8,128)(2,1)S(1)} %get-tuple-element.50.refs_1_), channel_id=1, source_target_pairs={{2,4},{4,2},{3,5},{5,3},{10,12},{12,10},{11,13},{13,11},{18,20},{2... | collective-permute-start | bytes 786440 | tf_op jit(solution)/shard_map/ppermute | solution.py:47
  10.5 10.9 %collective-permute-start.10 = (bf16[128,1024]{1,0:T(8,128)(2,1)S(1)}, bf16[128,1024]{1,0:T(8,128)(2,1)S(1)}, u32[]{:S(2)}, u32[]{:S(2)}) collective-permute-start(bf16[128,1024]{1,0:T(8,128)(2,1)S(1)} %get-tuple-element.50.refs_1_), channel_id=1, source_target_pairs={{0,2},{2,0},{4,6},{6,4},{1,3},{3,1},{5,7},{7,5},{8,10},{10,8},{12,... | collective-permute-start | bytes 786440 | tf_op jit(solution)/shard_map/ppermute | solution.py:46
  12.3 14.4 %collective-permute-start.3 = (bf16[128,1024]{1,0:T(8,128)(2,1)S(1)}, bf16[128,1024]{1,0:T(8,128)(2,1)S(1)}, u32[]{:S(2)}, u32[]{:S(2)}) collective-permute-start(bf16[128,1024]{1,0:T(8,128)(2,1)S(1)} %collective-permute-done.2), channel_id=1, source_target_pairs={{0,2},{2,0},{4,6},{6,4},{1,3},{3,1},{5,7},{7,5},{8,10},{10,8},{12,... | collective-permute-start | bytes 786440 | tf_op jit(solution)/shard_map/ppermute | solution.py:48
  15.7 34.9 %copy-start.1 = (bf16[128,1024]{1,0:T(8,128)(2,1)}, bf16[128,1024]{1,0:T(8,128)(2,1)S(1)}, u32[]{:S(2)}) copy-start(bf16[128,1024]{1,0:T(8,128)(2,1)S(1)} %collective-permute-done.6.refs_4_) | copy-start | bytes 786436
  15.7 12.5 %collective-permute-start.14 = (bf16[128,1024]{1,0:T(8,128)(2,1)S(1)}, bf16[128,1024]{1,0:T(8,128)(2,1)S(1)}, u32[]{:S(2)}, u32[]{:S(2)}) collective-permute-start(bf16[128,1024]{1,0:T(8,128)(2,1)S(1)} %collective-permute-done.6.refs_4_), channel_id=1, source_target_pairs={{2,4},{4,2},{3,5},{5,3},{10,12},{12,10},{11,13},{13,11},{18,20},{2... | collective-permute-start | bytes 786440 | tf_op jit(solution)/shard_map/ppermute | solution.py:49
  16.4 13.9 %collective-permute-start.7 = (bf16[128,1024]{1,0:T(8,128)(2,1)S(1)}, bf16[128,1024]{1,0:T(8,128)(2,1)S(1)}, u32[]{:S(2)}, u32[]{:S(2)}) collective-permute-start(bf16[128,1024]{1,0:T(8,128)(2,1)S(1)} %collective-permute-done.6.refs_4_), channel_id=1, source_target_pairs={{0,1},{1,0},{2,3},{3,2},{4,5},{5,4},{6,7},{7,6},{8,9},{9,8},{10,11... | collective-permute-start | bytes 786440 | tf_op jit(solution)/shard_map/ppermute | solution.py:71
  18.1 14.2 %collective-permute-start.5 = (bf16[128,1024]{1,0:T(8,128)(2,1)S(1)}, bf16[128,1024]{1,0:T(8,128)(2,1)S(1)}, u32[]{:S(2)}, u32[]{:S(2)}) collective-permute-start(bf16[128,1024]{1,0:T(8,128)(2,1)S(1)} %collective-permute-done.4), channel_id=1, source_target_pairs={{0,2},{2,0},{4,6},{6,4},{1,3},{3,1},{5,7},{7,5},{8,10},{10,8},{12,... | collective-permute-start | bytes 786440 | tf_op jit(solution)/shard_map/ppermute | solution.py:48
  21.5 35.2 %copy-start.3 = (bf16[128,1024]{1,0:T(8,128)(2,1)}, bf16[128,1024]{1,0:T(8,128)(2,1)S(1)}, u32[]{:S(2)}) copy-start(bf16[128,1024]{1,0:T(8,128)(2,1)S(1)} %collective-permute-done.10.refs_5_) | copy-start | bytes 786436
  21.5 12.4 %collective-permute-start.11 = (bf16[128,1024]{1,0:T(8,128)(2,1)S(1)}, bf16[128,1024]{1,0:T(8,128)(2,1)S(1)}, u32[]{:S(2)}, u32[]{:S(2)}) collective-permute-start(bf16[128,1024]{1,0:T(8,128)(2,1)S(1)} %collective-permute-done.10.refs_5_), channel_id=1, source_target_pairs={{2,4},{4,2},{3,5},{5,3},{10,12},{12,10},{11,13},{13,11},{18,20},{2... | collective-permute-start | bytes 786440 | tf_op jit(solution)/shard_map/ppermute | solution.py:49
  26.7 9.2 %collective-permute-start.1 = (bf16[128,1024]{1,0:T(8,128)(2,1)S(1)}, bf16[128,1024]{1,0:T(8,128)(2,1)S(1)}, u32[]{:S(2)}, u32[]{:S(2)}) collective-permute-start(bf16[128,1024]{1,0:T(8,128)(2,1)S(1)} %get-tuple-element.50.refs_1_), channel_id=1, source_target_pairs={{0,1},{1,0},{2,3},{3,2},{4,5},{5,4},{6,7},{7,6},{8,9},{9,8},{10,11... | collective-permute-start | bytes 786440 | tf_op jit(solution)/shard_map/ppermute | solution.py:71
  28.2 9.7 %collective-permute-start.15 = (bf16[128,1024]{1,0:T(8,128)(2,1)S(1)}, bf16[128,1024]{1,0:T(8,128)(2,1)S(1)}, u32[]{:S(2)}, u32[]{:S(2)}) collective-permute-start(bf16[128,1024]{1,0:T(8,128)(2,1)S(1)} %collective-permute-done.14), channel_id=1, source_target_pairs={{0,2},{2,0},{4,6},{6,4},{1,3},{3,1},{5,7},{7,5},{8,10},{10,8},{12,... | collective-permute-start | bytes 786440 | tf_op jit(solution)/shard_map/ppermute | solution.py:50
  30.3 26.3 %copy-start.5 = (bf16[128,1024]{1,0:T(8,128)(2,1)}, bf16[128,1024]{1,0:T(8,128)(2,1)S(1)}, u32[]{:S(2)}) copy-start(bf16[128,1024]{1,0:T(8,128)(2,1)S(1)} %collective-permute-done.7.refs_6_) | copy-start | bytes 786436
  30.3 26.4 %collective-permute-start.20 = (s32[256]{0:T(256)}, s32[256]{0:T(256)S(1)}, u32[]{:S(2)}, u32[]{:S(2)}) collective-permute-start(s32[256]{0:T(256)} %bitcast.39), channel_id=1, source_target_pairs={{0,1},{1,0},{2,3},{3,2},{4,5},{5,4},{6,7},{7,6},{8,9},{9,8},{10,11... | collective-permute-start | bytes 3080 | tf_op jit(solution)/shard_map/ppermute | solution.py:405
  32.3 9.2 %collective-permute-start.8 = (bf16[128,1024]{1,0:T(8,128)(2,1)S(1)}, bf16[128,1024]{1,0:T(8,128)(2,1)S(1)}, u32[]{:S(2)}, u32[]{:S(2)}) collective-permute-start(bf16[128,1024]{1,0:T(8,128)(2,1)S(1)} %broadcast_select_fusion.3.refs_1_.refs_8_), channel_id=1, source_target_pairs={{0,1},{1,0},{2,3},{3,2},{4,5},{5,4},{6,7},{7,6},{8,9},{9,8},{10,11... | collective-permute-start | bytes 786440 | tf_op jit(solution)/shard_map/ppermute | solution.py:71
  33.9 9.2 %collective-permute-start.12 = (bf16[128,1024]{1,0:T(8,128)(2,1)S(1)}, bf16[128,1024]{1,0:T(8,128)(2,1)S(1)}, u32[]{:S(2)}, u32[]{:S(2)}) collective-permute-start(bf16[128,1024]{1,0:T(8,128)(2,1)S(1)} %collective-permute-done.11), channel_id=1, source_target_pairs={{0,2},{2,0},{4,6},{6,4},{1,3},{3,1},{5,7},{7,5},{8,10},{10,8},{12,... | collective-permute-start | bytes 786440 | tf_op jit(solution)/shard_map/ppermute | solution.py:50
  35.9 11.2 %collective-permute-start.9 = (bf16[128,1024]{1,0:T(8,128)(2,1)S(1)}, bf16[128,1024]{1,0:T(8,128)(2,1)S(1)}, u32[]{:S(2)}, u32[]{:S(2)}) collective-permute-start(bf16[128,1024]{1,0:T(8,128)(2,1)S(1)} %broadcast_select_fusion.2.refs_2_.refs_9_), channel_id=1, source_target_pairs={{0,1},{1,0},{2,3},{3,2},{4,5},{5,4},{6,7},{7,6},{8,9},{9,8},{10,11... | collective-permute-start | bytes 786440 | tf_op jit(solution)/shard_map/ppermute | solution.py:71
  41.5 16.4 %collective-permute-start.16 = (bf16[128,1024]{1,0:T(8,128)(2,1)S(1)}, bf16[128,1024]{1,0:T(8,128)(2,1)S(1)}, u32[]{:S(2)}, u32[]{:S(2)}) collective-permute-start(bf16[128,1024]{1,0:T(8,128)(2,1)S(1)} %broadcast_select_fusion.1.refs_12_), channel_id=1, source_target_pairs={{0,1},{1,0},{2,3},{3,2},{4,5},{5,4},{6,7},{7,6},{8,9},{9,8},{10,11... | collective-permute-start | bytes 786440 | tf_op jit(solution)/shard_map/ppermute | solution.py:71
  47.1 10.7 %collective-permute-start.17 = (bf16[128,1024]{1,0:T(8,128)(2,1)S(1)}, bf16[128,1024]{1,0:T(8,128)(2,1)S(1)}, u32[]{:S(2)}, u32[]{:S(2)}) collective-permute-start(bf16[128,1024]{1,0:T(8,128)(2,1)S(1)} %broadcast_select_fusion.refs_13_), channel_id=1, source_target_pairs={{0,1},{1,0},{2,3},{3,2},{4,5},{5,4},{6,7},{7,6},{8,9},{9,8},{10,11... | collective-permute-start | bytes 786440 | tf_op jit(solution)/shard_map/ppermute | solution.py:71
  48.6 9.2 %collective-permute-start.13 = (bf16[128,1024]{1,0:T(8,128)(2,1)S(1)}, bf16[128,1024]{1,0:T(8,128)(2,1)S(1)}, u32[]{:S(2)}, u32[]{:S(2)}) collective-permute-start(bf16[128,1024]{1,0:T(8,128)(2,1)S(1)} %collective-permute-done.1.refs_3_), channel_id=1, source_target_pairs={{0,2},{2,0},{4,6},{6,4},{1,3},{3,1},{5,7},{7,5},{8,10},{10,8},{12,... | collective-permute-start | bytes 786440 | tf_op jit(solution)/shard_map/ppermute | solution.py:68
  50.7 3.4 %copy-start = (bf16[1,2,1024,2048]{3,2,1,0:T(8,128)(2,1)S(1)}, bf16[1,2,1024,2048]{3,2,1,0:T(8,128)(2,1)}, u32[]{:S(2)}) copy-start(bf16[1,2,1024,2048]{3,2,1,0:T(8,128)(2,1)} %param.7) | copy-start | bytes 25165828
  54.1 3.8 %slice-start = ((s8[8388608]{0:T(1024)(128)(4,1)}), s8[4194304]{0:T(1024)(128)(4,1)S(1)}, s32[]{:S(2)}) async-start(s8[8388608]{0:T(1024)(128)(4,1)} %bitcast.28), calls=%async_computation | async-start | bytes 8388608
  56.6 1.2 %copy-start.10 = (s32[256,1]{0,1:T(1,128)S(1)}, s32[256,1]{0,1:T(1,128)}, u32[]{:S(2)}) copy-start(s32[256,1]{0,1:T(1,128)} %param.11) | copy-start | bytes 3076
  56.7 2.2 %slice-start.1 = ((s8[8388608]{0:T(1024)(128)(4,1)}), s8[4194304]{0:T(1024)(128)(4,1)S(1)}, s32[]{:S(2)}) async-start(s8[8388608]{0:T(1024)(128)(4,1)} %bitcast.28), calls=%async_computation.1 | async-start | bytes 8388608
  56.7 2.2 %copy-start.2 = (bf16[128,1024]{1,0:T(8,128)(2,1)S(1)}, bf16[128,1024]{1,0:T(8,128)(2,1)}, u32[]{:S(2)}) copy-start(bf16[128,1024]{1,0:T(8,128)(2,1)} %copy-done.1) | copy-start | bytes 786436
  56.7 2.3 %copy-start.4 = (bf16[128,1024]{1,0:T(8,128)(2,1)S(1)}, bf16[128,1024]{1,0:T(8,128)(2,1)}, u32[]{:S(2)}) copy-start(bf16[128,1024]{1,0:T(8,128)(2,1)} %copy-done.3) | copy-start | bytes 786436
  56.7 2.3 %copy-start.6 = (bf16[128,1024]{1,0:T(8,128)(2,1)S(1)}, bf16[128,1024]{1,0:T(8,128)(2,1)}, u32[]{:S(2)}) copy-start(bf16[128,1024]{1,0:T(8,128)(2,1)} %copy-done.5) | copy-start | bytes 786436
  57.8 6.0 %copy-start.9 = (f32[2,16]{1,0:T(2,128)S(1)}, f32[2,16]{1,0:T(2,128)}, u32[]{:S(2)}) copy-start(f32[2,16]{1,0:T(2,128)} %table.3) | copy-start | bytes 388
  63.9 32.8 %copy-start.7 = (f32[64,1,1,2,512]{4,3,2,1,0:T(2,128)S(1)}, f32[64,1,1,2,512]{4,3,2,1,0:T(2,128)}, u32[]{:S(2)}) copy-start(f32[64,1,1,2,512]{4,3,2,1,0:T(2,128)} %param.9) | copy-start | bytes 786436
  67.0 16.3 %collective-permute-start.21 = (bf16[4,72,1024]{2,1,0:T(8,128)(2,1)S(1)}, bf16[4,72,1024]{2,1,0:T(8,128)(2,1)S(1)}, u32[]{:S(2)}, u32[]{:S(2)}) collective-permute-start(bf16[4,72,1024]{2,1,0:T(8,128)(2,1)S(1)} %bitcast.36), channel_id=1, source_target_pairs={{0,1},{1,0},{2,3},{3,2},{4,5},{5,4},{6,7},{7,6},{8,9},{9,8},{10,11... | collective-permute-start | bytes 1769480 | tf_op jit(solution)/shard_map/ppermute | solution.py:489
  68.0 32.0 %collective-permute-start.19 = (bf16[3072,128]{1,0:T(8,128)(2,1)}, bf16[3072,128]{1,0:T(8,128)(2,1)S(1)}, u32[]{:S(2)}, u32[]{:S(2)}) collective-permute-start(bf16[3072,128]{1,0:T(8,128)(2,1)} %get-tuple-element.33), channel_id=1, source_target_pairs={{0,1},{1,0},{2,3},{3,2},{4,5},{5,4},{6,7},{7,6},{8,9},{9,8},{10,11... | collective-permute-start | bytes 2359304 | tf_op jit(solution)/shard_map/ppermute | solution.py:534
  83.4 9.3 %collective-permute-start.22 = (bf16[72,1024]{1,0:T(8,128)(2,1)S(1)}, bf16[72,1024]{1,0:T(8,128)(2,1)S(1)}, u32[]{:S(2)}, u32[]{:S(2)}) collective-permute-start(bf16[72,1024]{1,0:T(8,128)(2,1)S(1)} %get-tuple-element.41), channel_id=1, source_target_pairs={{0,2},{2,4},{4,6},{6,0},{1,3},{3,5},{5,7},{7,1},{8,10},{10,12},{12... | collective-permute-start | bytes 442376 | tf_op jit(solution)/shard_map/ppermute | solution.py:502
  83.5 12.4 %collective-permute-start.23 = (bf16[72,1024]{1,0:T(8,128)(2,1)S(1)}, bf16[72,1024]{1,0:T(8,128)(2,1)S(1)}, u32[]{:S(2)}, u32[]{:S(2)}) collective-permute-start(bf16[72,1024]{1,0:T(8,128)(2,1)S(1)} %get-tuple-element.42), channel_id=1, source_target_pairs={{0,4},{2,6},{4,0},{6,2},{1,5},{3,7},{5,1},{7,3},{8,12},{10,14},{12... | collective-permute-start | bytes 442376 | tf_op jit(solution)/shard_map/ppermute | solution.py:502
  90.0 6.6 %collective-permute-start.24 = (bf16[72,1024]{1,0:T(8,128)(2,1)S(1)}, bf16[72,1024]{1,0:T(8,128)(2,1)S(1)}, u32[]{:S(2)}, u32[]{:S(2)}) collective-permute-start(bf16[72,1024]{1,0:T(8,128)(2,1)S(1)} %get-tuple-element.43), channel_id=1, source_target_pairs={{0,6},{2,0},{4,2},{6,4},{1,7},{3,1},{5,3},{7,5},{8,14},{10,8},{12,... | collective-permute-start | bytes 442376 | tf_op jit(solution)/shard_map/ppermute | solution.py:502
  90.0 9.9 %collective-permute-start.18 = (bf16[1024,128]{1,0:T(8,128)(2,1)}, bf16[1024,128]{1,0:T(8,128)(2,1)S(1)}, u32[]{:S(2)}, u32[]{:S(2)}) collective-permute-start(bf16[1024,128]{1,0:T(8,128)(2,1)} %get-tuple-element.32), channel_id=1, source_target_pairs={{0,1},{1,0},{2,3},{3,2},{4,5},{5,4},{6,7},{7,6},{8,9},{9,8},{10,11... | collective-permute-start | bytes 786440 | tf_op jit(solution)/shard_map/ppermute | solution.py:534
  98.0 3.8 %collective-permute-start.25 = (f32[288,128]{1,0:T(8,128)S(1)}, f32[288,128]{1,0:T(8,128)S(1)}, u32[]{:S(2)}, u32[]{:S(2)}) collective-permute-start(f32[288,128]{1,0:T(8,128)S(1)} %get-tuple-element.45), channel_id=1, source_target_pairs={{0,8},{8,0},{16,24},{24,16},{1,9},{9,1},{17,25},{25,17},{2,10},{10... | collective-permute-start | bytes 442376 | tf_op jit(solution)/shard_map/ppermute | solution.py:519
  98.0 6.8 %collective-permute-start.26 = (f32[288,128]{1,0:T(8,128)S(1)}, f32[288,128]{1,0:T(8,128)}, u32[]{:S(2)}, u32[]{:S(2)}) collective-permute-start(f32[288,128]{1,0:T(8,128)S(1)} %get-tuple-element.45), channel_id=1, source_target_pairs={{0,16},{8,24},{16,0},{24,8},{1,17},{9,25},{17,1},{25,9},{2,18},{10... | collective-permute-start | bytes 442376 | tf_op jit(solution)/shard_map/ppermute | solution.py:519
  99.5 7.6 %collective-permute-start.27 = (f32[288,128]{1,0:T(8,128)S(1)}, f32[288,128]{1,0:T(8,128)}, u32[]{:S(2)}, u32[]{:S(2)}) collective-permute-start(f32[288,128]{1,0:T(8,128)S(1)} %get-tuple-element.45), channel_id=1, source_target_pairs={{0,24},{8,16},{16,8},{24,0},{1,25},{9,17},{17,9},{25,1},{2,26},{10... | collective-permute-start | bytes 442376 | tf_op jit(solution)/shard_map/ppermute | solution.py:519

commit v3 on v2

--- a/solution.py
+++ b/solution.py
@@ -12,7 +12,7 @@
 BR = 8
 BC = 128
 MIB = 1 << 20
-SPLIT = (1, 3)
+SPLIT = (1, 7)
 
 
 def shift_pairs(rows, cols, step, valid):
@@ -312,6 +312,16 @@
                     diag_send[step - 1, row, part:, 2 * pole * BC : 2 * (pole + 1) * BC] = halves(sum_of)
 
 
+def density_kernel(split, *refs):
+    *messages, density, tile = refs
+    start = pl.multiple_of(split + lax.axis_index("pole") * BR, BR)
+    for place, out in ((pl.ds(0, split), density.at[...]), (pl.ds(start, BR), tile.at[0])):
+        values = [message[place, :] for message in messages]
+        while len(values) > 1:
+            values = [a + b for a, b in zip(values[::2], values[1::2])]
+        out[...] = values[0]
+
+
 def join_kernel(steps, keep, *refs):
     out = refs[-1]
     block = pl.program_id(0)
@@ -425,8 +435,8 @@
         pltpu.VMEM((4 * BS, wide), jnp.float32),
     ]
     row_products = jax.ShapeDtypeStruct((row_blocks, BS, wide), jnp.float32)
-    groups = [(0,)] + ([(rows - 2,)] if rows > 2 else [])
-    last = tuple(stage for stage in range(rows) if (stage,) not in groups)
+    groups = [(0, rows - 2)] if rows > 2 else [(0,)]
+    last = tuple(stage for stage in range(rows) if stage not in groups[0])
     early = []
     for group in groups:
         group_pieces = [piece for stage in group for piece in stages[stage]]
@@ -518,15 +528,19 @@
     for step in range(1, poles):
         messages.append(lax.ppermute(message, "pole", [(i, i ^ step) for i in range(poles)]))
 
-    def summed(values):
-        while len(values) > 1:
-            values = [a + b for a, b in zip(values[::2], values[1::2])]
-        return values[0]
-
     split = part * across
-    density_diag = summed([value[:split] for value in messages]).reshape(part, 1, half)
-    start = split + lax.axis_index("pole") * BR
-    tile_sum = summed([lax.dynamic_slice_in_dim(value, start, BR) for value in messages])[None]
+    laid_density, tile_sum = pl.pallas_call(
+        functools.partial(density_kernel, split),
+        out_shape=(
+            jax.ShapeDtypeStruct((split, BC), jnp.float32),
+            jax.ShapeDtypeStruct((1, BR, BC), jnp.float32),
+        ),
+        in_specs=[vmem] * poles,
+        out_specs=(vmem,) * 2,
+        compiler_params=pltpu.CompilerParams(vmem_limit_bytes=8 * MIB),
+        name="density",
+    )(*messages)
+    density_diag = laid_density.reshape(part, 1, half)
 
     parts = []
     for send, size in zip(sends, sizes):

time: 110 us -> 119 us (1.082)
  waiting for transfers between devices: 38.6 us -> 53.8 us
  starting transfers between devices: 46.2 us -> 43.1 us
  other arithmetic: 3.05 us -> 0.13 us
    ppermute x1, waiting for transfers between devices: 14.2 us -> 26.3 us  [compute(): lax.ppermute(diag_send[step - 1], grid, everyone_pairs[step])]
    ppermute x3, waiting for transfers between devices: 4.6 us -> 7.44 us  [compute(): lax.ppermute(rounded[step - 1], 'row', [(i, (i + step) % rows) for i in r...]
    ppermute x3, starting transfers between devices: 6.61 us -> 3.88 us  [compute(): lax.ppermute(rounded[step - 1], 'row', [(i, (i + step) % rows) for i in r...]
    add x1 -> x0, other arithmetic: 1.65 us -> none  [summed(): values = [a + b for a, b in zip(values[::2], values[1::2])]]
    broadcast_in_dim x1 -> x0, other arithmetic: 1.27 us -> none  [compute(): summed([lax.dynamic_slice_in_dim(value, start, BR) for value in messages])]
    pallas_call x2 -> x1, Pallas kernels: 3.65 us -> 2.63 us  [compute(): pl.pallas_call(functools.partial(early_kernel, sources, group, bool(early...]
    unnamed x26 -> x12, local copies, waits for them, and re-layouts: 4.56 us -> 4.1 us
  transfers between devices with their start and end apart: 28 -> 28, of which waited for: 12 -> 10; matrix products, arithmetic and copies ran while one was open for 0% -> 0% of each run, Pallas kernels for 6% -> 7%
where the time goes in v3:
time: 119 us
  waiting for transfers between devices  53.8 us (45%)
  starting transfers between devices  43.1 us (36%)
  Pallas kernels  14.9 us (13%)
  local copies, waits for them, and re-layouts  5.17 us (4%)
  between operations  1.48 us (1%)
    ppermute x1, waiting for transfers between devices, compute(): lax.ppermute(diag_send[step - 1], grid, everyone_pairs[step])  26.3 us
    ppermute x7, starting transfers between devices, gather_stages(): last = lax.ppermute(leaving, grid, pairs)  9.85 us
    ppermute x2, starting transfers between devices, gather_stages(): near = lax.ppermute(own, 'row', outer)  7.75 us
    ppermute x7, waiting for transfers between devices, gather_stages(): last = lax.ppermute(leaving, grid, pairs)  7.6 us
    ppermute x3, waiting for transfers between devices, compute(): lax.ppermute(rounded[step - 1], 'row', [(i, (i + step) % rows) for i in r...  7.44 us
    ppermute x2, starting transfers between devices, gather_stages(): cross_out = lax.ppermute(cross, 'row', outer)  6.73 us
    ppermute x3, waiting for transfers between devices, compute(): lax.ppermute(message, 'pole', [(i, i ^ step) for i in range(poles)])  5.59 us
    ppermute x2, waiting for transfers between devices, gather_stages(): cross_out = lax.ppermute(cross, 'row', outer)  5.39 us
  transfers between devices with their start and end apart: 28, of which 10 were waited for; matrix products, arithmetic and copies ran while one was open for 0% of the time, Pallas kernels for 7%

profile of v3, /device:TPU:0, one launch (start us, length us, event | category | flops | bytes accessed | tf_op | source)
XLA Modules:
  0.0 118.6 jit_solution(1715261813139505906)
XLA Ops:
  0.6 0.0 copy-start.5
  0.7 1.1 slice_bitcast_fusion
  1.7 0.7 collective-permute-start.2
  2.4 5.9 %collective-permute-start.6 = (bf16[128,1024]{1,0:T(8,128)(2,1)S(1)}, bf16[128,1024]{1,0:T(8,128)(2,1)S(1)}, u32[]{:S(2)}, u32[]{:S(2)}) collective-permute-start(bf16[128,1024]{1,0:T(8,128)(2,1)S(1)} %get-tuple-element.55.refs_0_), channel_id=1, source_target_pairs={{0,2},{2,0},{4,6},{6,4},{1,3},{3,1},{5,7},{7,5},{8,10},{10,8},{12,... | collective-permute-start | bytes 786440 | tf_op jit(solution)/shard_map/ppermute | solution.py:46
  8.3 1.5 %collective-permute-start = (bf16[128,1024]{1,0:T(8,128)(2,1)S(1)}, bf16[128,1024]{1,0:T(8,128)(2,1)S(1)}, u32[]{:S(2)}, u32[]{:S(2)}) collective-permute-start(bf16[128,1024]{1,0:T(8,128)(2,1)S(1)} %get-tuple-element.55.refs_0_), channel_id=1, source_target_pairs={{0,1},{1,0},{2,3},{3,2},{4,5},{5,4},{6,7},{7,6},{8,9},{9,8},{10,11... | collective-permute-start | bytes 786440 | tf_op jit(solution)/shard_map/ppermute | solution.py:71
  9.9 0.7 collective-permute-start.4
  10.5 1.8 %collective-permute-start.10 = (bf16[128,1024]{1,0:T(8,128)(2,1)S(1)}, bf16[128,1024]{1,0:T(8,128)(2,1)S(1)}, u32[]{:S(2)}, u32[]{:S(2)}) collective-permute-start(bf16[128,1024]{1,0:T(8,128)(2,1)S(1)} %get-tuple-element.54.refs_1_), channel_id=1, source_target_pairs={{0,2},{2,0},{4,6},{6,4},{1,3},{3,1},{5,7},{7,5},{8,10},{10,8},{12,... | collective-permute-start | bytes 786440 | tf_op jit(solution)/shard_map/ppermute | solution.py:46
  12.4 3.4 %collective-permute-start.3 = (bf16[128,1024]{1,0:T(8,128)(2,1)S(1)}, bf16[128,1024]{1,0:T(8,128)(2,1)S(1)}, u32[]{:S(2)}, u32[]{:S(2)}) collective-permute-start(bf16[128,1024]{1,0:T(8,128)(2,1)S(1)} %collective-permute-done.2), channel_id=1, source_target_pairs={{0,2},{2,0},{4,6},{6,4},{1,3},{3,1},{5,7},{7,5},{8,10},{10,8},{12,... | collective-permute-start | bytes 786440 | tf_op jit(solution)/shard_map/ppermute | solution.py:48
  15.8 0.7 collective-permute-start.14
  16.4 1.7 %collective-permute-start.7 = (bf16[128,1024]{1,0:T(8,128)(2,1)S(1)}, bf16[128,1024]{1,0:T(8,128)(2,1)S(1)}, u32[]{:S(2)}, u32[]{:S(2)}) collective-permute-start(bf16[128,1024]{1,0:T(8,128)(2,1)S(1)} %collective-permute-done.6.refs_4_), channel_id=1, source_target_pairs={{0,1},{1,0},{2,3},{3,2},{4,5},{5,4},{6,7},{7,6},{8,9},{9,8},{10,11... | collective-permute-start | bytes 786440 | tf_op jit(solution)/shard_map/ppermute | solution.py:71
  18.1 3.3 %collective-permute-start.5 = (bf16[128,1024]{1,0:T(8,128)(2,1)S(1)}, bf16[128,1024]{1,0:T(8,128)(2,1)S(1)}, u32[]{:S(2)}, u32[]{:S(2)}) collective-permute-start(bf16[128,1024]{1,0:T(8,128)(2,1)S(1)} %collective-permute-done.4), channel_id=1, source_target_pairs={{0,2},{2,0},{4,6},{6,4},{1,3},{3,1},{5,7},{7,5},{8,10},{10,8},{12,... | collective-permute-start | bytes 786440 | tf_op jit(solution)/shard_map/ppermute | solution.py:48
  21.5 0.7 collective-permute-start.11
  22.8 3.9 %collective-permute-done.3 = bf16[128,1024]{1,0:T(8,128)(2,1)S(1)} collective-permute-done((bf16[128,1024]{1,0:T(8,128)(2,1)S(1)}, bf16[128,1024]{1,0:T(8,128)(2,1)S(1)}, u32[]{:S(2)}, u32[]{:S(2)}) %collective-permute-start.3) | collective-permute-done | bytes 262176 | tf_op jit(solution)/shard_map/ppermute | solution.py:48
  26.7 1.5 %collective-permute-start.1 = (bf16[128,1024]{1,0:T(8,128)(2,1)S(1)}, bf16[128,1024]{1,0:T(8,128)(2,1)S(1)}, u32[]{:S(2)}, u32[]{:S(2)}) collective-permute-start(bf16[128,1024]{1,0:T(8,128)(2,1)S(1)} %get-tuple-element.54.refs_1_), channel_id=1, source_target_pairs={{0,1},{1,0},{2,3},{3,2},{4,5},{5,4},{6,7},{7,6},{8,9},{9,8},{10,11... | collective-permute-start | bytes 786440 | tf_op jit(solution)/shard_map/ppermute | solution.py:71
  28.3 2.0 %collective-permute-start.15 = (bf16[128,1024]{1,0:T(8,128)(2,1)S(1)}, bf16[128,1024]{1,0:T(8,128)(2,1)S(1)}, u32[]{:S(2)}, u32[]{:S(2)}) collective-permute-start(bf16[128,1024]{1,0:T(8,128)(2,1)S(1)} %collective-permute-done.14), channel_id=1, source_target_pairs={{0,2},{2,0},{4,6},{6,4},{1,3},{3,1},{5,7},{7,5},{8,10},{10,8},{12,... | collective-permute-start | bytes 786440 | tf_op jit(solution)/shard_map/ppermute | solution.py:50
  30.3 0.6 collective-permute-start.20
  30.9 1.5 %collective-permute-done.5 = bf16[128,1024]{1,0:T(8,128)(2,1)S(1)} collective-permute-done((bf16[128,1024]{1,0:T(8,128)(2,1)S(1)}, bf16[128,1024]{1,0:T(8,128)(2,1)S(1)}, u32[]{:S(2)}, u32[]{:S(2)}) %collective-permute-start.5) | collective-permute-done | bytes 262176 | tf_op jit(solution)/shard_map/ppermute | solution.py:48
  32.4 1.5 %collective-permute-start.8 = (bf16[128,1024]{1,0:T(8,128)(2,1)S(1)}, bf16[128,1024]{1,0:T(8,128)(2,1)S(1)}, u32[]{:S(2)}, u32[]{:S(2)}) collective-permute-start(bf16[128,1024]{1,0:T(8,128)(2,1)S(1)} %broadcast_select_fusion.3.refs_4_.refs_8_), channel_id=1, source_target_pairs={{0,1},{1,0},{2,3},{3,2},{4,5},{5,4},{6,7},{7,6},{8,9},{9,8},{10,11... | collective-permute-start | bytes 786440 | tf_op jit(solution)/shard_map/ppermute | solution.py:71
  33.9 2.0 %collective-permute-start.12 = (bf16[128,1024]{1,0:T(8,128)(2,1)S(1)}, bf16[128,1024]{1,0:T(8,128)(2,1)S(1)}, u32[]{:S(2)}, u32[]{:S(2)}) collective-permute-start(bf16[128,1024]{1,0:T(8,128)(2,1)S(1)} %collective-permute-done.11), channel_id=1, source_target_pairs={{0,2},{2,0},{4,6},{6,4},{1,3},{3,1},{5,7},{7,5},{8,10},{10,8},{12,... | collective-permute-start | bytes 786440 | tf_op jit(solution)/shard_map/ppermute | solution.py:50
  35.9 0.6 collective-permute-start.9
  36.5 1.5 %collective-permute-done.15 = bf16[128,1024]{1,0:T(8,128)(2,1)S(1)} collective-permute-done((bf16[128,1024]{1,0:T(8,128)(2,1)S(1)}, bf16[128,1024]{1,0:T(8,128)(2,1)S(1)}, u32[]{:S(2)}, u32[]{:S(2)}) %collective-permute-start.15) | collective-permute-done | bytes 262176 | tf_op jit(solution)/shard_map/ppermute | solution.py:50
  38.0 3.5 %collective-permute-done.8.refs_6_.refs_10_ = bf16[128,1024]{1,0:T(8,128)(2,1)S(1)} collective-permute-done((bf16[128,1024]{1,0:T(8,128)(2,1)S(1)}, bf16[128,1024]{1,0:T(8,128)(2,1)S(1)}, u32[]{:S(2)}, u32[]{:S(2)}) %collective-permute-start.8) | collective-permute-done | bytes 262176 | tf_op jit(solution)/shard_map/ppermute | solution.py:71
  41.5 1.5 %collective-permute-start.16 = (bf16[128,1024]{1,0:T(8,128)(2,1)S(1)}, bf16[128,1024]{1,0:T(8,128)(2,1)S(1)}, u32[]{:S(2)}, u32[]{:S(2)}) collective-permute-start(bf16[128,1024]{1,0:T(8,128)(2,1)S(1)} %broadcast_select_fusion.1.refs_12_), channel_id=1, source_target_pairs={{0,1},{1,0},{2,3},{3,2},{4,5},{5,4},{6,7},{7,6},{8,9},{9,8},{10,11... | collective-permute-start | bytes 786440 | tf_op jit(solution)/shard_map/ppermute | solution.py:71
  43.1 4.1 %collective-permute-done.9.refs_7_.refs_11_ = bf16[128,1024]{1,0:T(8,128)(2,1)S(1)} collective-permute-done((bf16[128,1024]{1,0:T(8,128)(2,1)S(1)}, bf16[128,1024]{1,0:T(8,128)(2,1)S(1)}, u32[]{:S(2)}, u32[]{:S(2)}) %collective-permute-start.9) | collective-permute-done | bytes 262176 | tf_op jit(solution)/shard_map/ppermute | solution.py:71
  47.1 1.5 %collective-permute-start.17 = (bf16[128,1024]{1,0:T(8,128)(2,1)S(1)}, bf16[128,1024]{1,0:T(8,128)(2,1)S(1)}, u32[]{:S(2)}, u32[]{:S(2)}) collective-permute-start(bf16[128,1024]{1,0:T(8,128)(2,1)S(1)} %broadcast_select_fusion.refs_13_), channel_id=1, source_target_pairs={{0,1},{1,0},{2,3},{3,2},{4,5},{5,4},{6,7},{7,6},{8,9},{9,8},{10,11... | collective-permute-start | bytes 786440 | tf_op jit(solution)/shard_map/ppermute | solution.py:71
  48.7 2.0 %collective-permute-start.13 = (bf16[128,1024]{1,0:T(8,128)(2,1)S(1)}, bf16[128,1024]{1,0:T(8,128)(2,1)S(1)}, u32[]{:S(2)}, u32[]{:S(2)}) collective-permute-start(bf16[128,1024]{1,0:T(8,128)(2,1)S(1)} %collective-permute-done.1.refs_3_), channel_id=1, source_target_pairs={{0,2},{2,0},{4,6},{6,4},{1,3},{3,1},{5,7},{7,5},{8,10},{10,8},{12,... | collective-permute-start | bytes 786440 | tf_op jit(solution)/shard_map/ppermute | solution.py:68
  50.7 3.4 %copy-done = bf16[1,2,1024,2048]{3,2,1,0:T(8,128)(2,1)S(1)} copy-done((bf16[1,2,1024,2048]{3,2,1,0:T(8,128)(2,1)S(1)}, bf16[1,2,1024,2048]{3,2,1,0:T(8,128)(2,1)}, u32[]{:S(2)}) %copy-start) | copy-done | bytes 8388632
  54.1 2.6 %early_products.1.early = f32[8,128,1024]{2,1,0:T(8,128)S(1)} custom-call(s32[16]{0:T(128)S(1)} %bitcast.27, bf16[2,1024,2048]{2,1,0:T(8,128)(2,1)S(1)} %bitcast.24, bf16[128,1024]{1,0:T(8,128)(2,1)S(1)} %get-tuple-element.55.refs_0_, bf16[128,1024]{1,0:T(8,128)(2,1)S(1)} %get-tuple-element.54.refs_1_, bf16[128,1024]{1,0:T(8,128)(2,1)S(1)} %collective-permute-done.refs_2_, ...), custom_call_target="tpu_custom_call" | custom-call | flops 2147483648 | bytes 4194304 | tf_op jit(solution)/shard_map/early_products/pallas_call | solution.py:444
  56.8 0.7 copy-done.1
  57.5 3.9 %last_products.1 = (f32[4096,128]{1,0:T(8,128)S(1)}, bf16[512,128]{1,0:T(8,128)(2,1)S(1)}, bf16[3584,128]{1,0:T(8,128)(2,1)S(1)}, f32[8,128,1024]{2,1,0:T(8,128)S(1)}, bf16[8,512,256]{2,1,0:T(8,128)(2,1)S(1)}) custom-call(s32[16]{0:T(128)S(1)} %bitcast.28, bf16[2,1024,2048]{2,1,0:T(8,128)(2,1)S(1)} %bitcast.25, f32[8,128,1024]{2,1,0:T(8,128)S(1)} %early_products.1.early, ...), custom_call_target="tpu_custom_call" | custom-call | flops 2147483648 | bytes 8388608 | tf_op jit(solution)/shard_map/last_products/pallas_call | solution.py:464
  61.4 2.0 %collective-permute-start.19 = (bf16[3584,128]{1,0:T(8,128)(2,1)S(1)}, bf16[3584,128]{1,0:T(8,128)(2,1)S(1)}, u32[]{:S(2)}, u32[]{:S(2)}) collective-permute-start(bf16[3584,128]{1,0:T(8,128)(2,1)S(1)} %get-tuple-element.35), channel_id=1, source_target_pairs={{0,1},{1,0},{2,3},{3,2},{4,5},{5,4},{6,7},{7,6},{8,9},{9,8},{10,11... | collective-permute-start | bytes 2752520 | tf_op jit(solution)/shard_map/ppermute | solution.py:548
  63.5 3.1 %diag_products.1 = (f32[4,72,1024]{2,1,0:T(8,128)S(1)}, bf16[1,4,72,1024]{3,2,1,0:T(8,128)(2,1)S(1)}) custom-call(s32[16]{0:T(128)S(1)} %bitcast.29, f32[2,16]{1,0:T(2,128)S(1)} %copy-done.4, s32[1]{0:T(128)S(6)} %copy.15.slot, s32[512]{0:T(512)S(1)} %pad_add_fusion.owner, f32[8,128,1024]{2,1,0:T(8,128)S(1)} %get-tuple-element.38.total, ...), custom_call_target="tpu_custom_call" | custom-call | flops 2147483648 | bytes 8388608 | tf_op jit(solution)/shard_map/diag_products/pallas_call | solution.py:478
  66.6 0.1 collective-permute-start.21
  66.8 26.3 %collective-permute-done.21.refs_0_ = bf16[4,72,1024]{2,1,0:T(8,128)(2,1)S(1)} collective-permute-done((bf16[4,72,1024]{2,1,0:T(8,128)(2,1)S(1)}, bf16[4,72,1024]{2,1,0:T(8,128)(2,1)S(1)}, u32[]{:S(2)}, u32[]{:S(2)}) %collective-permute-start.21) | collective-permute-done | bytes 589856 | tf_op jit(solution)/shard_map/ppermute | solution.py:499
  93.1 0.1 regroup.1
  93.2 0.8 collective-permute-start.22
  94.0 1.6 %collective-permute-start.23 = (bf16[72,1024]{1,0:T(8,128)(2,1)S(1)}, bf16[72,1024]{1,0:T(8,128)(2,1)S(1)}, u32[]{:S(2)}, u32[]{:S(2)}) collective-permute-start(bf16[72,1024]{1,0:T(8,128)(2,1)S(1)} %get-tuple-element.44), channel_id=1, source_target_pairs={{0,4},{2,6},{4,0},{6,2},{1,5},{3,7},{5,1},{7,3},{8,12},{10,14},{12... | collective-permute-start | bytes 442376 | tf_op jit(solution)/shard_map/ppermute | solution.py:512
  95.6 1.4 %collective-permute-start.24 = (bf16[72,1024]{1,0:T(8,128)(2,1)S(1)}, bf16[72,1024]{1,0:T(8,128)(2,1)S(1)}, u32[]{:S(2)}, u32[]{:S(2)}) collective-permute-start(bf16[72,1024]{1,0:T(8,128)(2,1)S(1)} %get-tuple-element.45), channel_id=1, source_target_pairs={{0,6},{2,0},{4,2},{6,4},{1,7},{3,1},{5,3},{7,5},{8,14},{10,8},{12,... | collective-permute-start | bytes 442376 | tf_op jit(solution)/shard_map/ppermute | solution.py:512
  97.1 3.3 %collective-permute-done.22.refs_0_ = bf16[72,1024]{1,0:T(8,128)(2,1)S(1)} collective-permute-done((bf16[72,1024]{1,0:T(8,128)(2,1)S(1)}, bf16[72,1024]{1,0:T(8,128)(2,1)S(1)}, u32[]{:S(2)}, u32[]{:S(2)}) %collective-permute-start.22) | collective-permute-done | bytes 147488 | tf_op jit(solution)/shard_map/ppermute | solution.py:512
  100.4 4.1 %collective-permute-done.23.refs_1_ = bf16[72,1024]{1,0:T(8,128)(2,1)S(1)} collective-permute-done((bf16[72,1024]{1,0:T(8,128)(2,1)S(1)}, bf16[72,1024]{1,0:T(8,128)(2,1)S(1)}, u32[]{:S(2)}, u32[]{:S(2)}) %collective-permute-start.23) | collective-permute-done | bytes 147488 | tf_op jit(solution)/shard_map/ppermute | solution.py:512
  104.5 1.4 %finish.1 = (f32[512,128]{1,0:T(8,128)}, f32[288,128]{1,0:T(8,128)S(1)}) custom-call(f32[2,16]{1,0:T(2,128)S(1)} %copy-done.4, s32[1]{0:T(128)S(6)} %copy.15.slot, f32[512,128]{1,0:T(8,128)S(1)} %bitcast.26, f32[72,1024]{1,0:T(8,128)S(1)} %get-tuple-element.42.own, bf16[72,1024]{1,0:T(8,128)(2,1)S(1)} %collective-permute-done.22.refs_0_, ...), custom_call_target="tpu_custom_call" | custom-call | tf_op jit(solution)/shard_map/finish/pallas_call | solution.py:515
  105.9 1.5 %collective-permute-start.26 = (f32[288,128]{1,0:T(8,128)S(1)}, f32[288,128]{1,0:T(8,128)S(1)}, u32[]{:S(2)}, u32[]{:S(2)}) collective-permute-start(f32[288,128]{1,0:T(8,128)S(1)} %get-tuple-element.47.refs_0_), channel_id=1, source_target_pairs={{0,16},{8,24},{16,0},{24,8},{1,17},{9,25},{17,1},{25,9},{2,18},{10... | collective-permute-start | bytes 442376 | tf_op jit(solution)/shard_map/ppermute | solution.py:529
  107.4 0.4 collective-permute-start.27
  107.7 1.5 %collective-permute-start.18 = (bf16[512,128]{1,0:T(8,128)(2,1)S(1)}, bf16[512,128]{1,0:T(8,128)(2,1)S(1)}, u32[]{:S(2)}, u32[]{:S(2)}) collective-permute-start(bf16[512,128]{1,0:T(8,128)(2,1)S(1)} %get-tuple-element.34), channel_id=1, source_target_pairs={{0,1},{1,0},{2,3},{3,2},{4,5},{5,4},{6,7},{7,6},{8,9},{9,8},{10,11... | collective-permute-start | bytes 393224 | tf_op jit(solution)/shard_map/ppermute | solution.py:548
  109.3 3.4 %collective-permute-done.26.refs_2_ = f32[288,128]{1,0:T(8,128)S(1)} collective-permute-done((f32[288,128]{1,0:T(8,128)S(1)}, f32[288,128]{1,0:T(8,128)S(1)}, u32[]{:S(2)}, u32[]{:S(2)}) %collective-permute-start.26) | collective-permute-done | bytes 147488 | tf_op jit(solution)/shard_map/ppermute | solution.py:529
  112.6 2.2 %collective-permute-done.27.refs_3_ = f32[288,128]{1,0:T(8,128)S(1)} collective-permute-done((f32[288,128]{1,0:T(8,128)S(1)}, f32[288,128]{1,0:T(8,128)S(1)}, u32[]{:S(2)}, u32[]{:S(2)}) %collective-permute-start.27) | collective-permute-done | bytes 147488 | tf_op jit(solution)/shard_map/ppermute | solution.py:529
  114.8 0.7 density.1
  115.5 3.0 %join_columns.1 = f32[4096,128]{1,0:T(8,128)} custom-call(f32[4096,128]{1,0:T(8,128)S(1)} %get-tuple-element.33.keep, bf16[512,128]{1,0:T(8,128)(2,1)S(1)} %collective-permute-done.18.refs_0_, bf16[3584,128]{1,0:T(8,128)(2,1)S(1)} %collective-permute-done.19.refs_1_), custom_call_target="tpu_custom_call" | custom-call | tf_op jit(solution)/shard_map/join_columns/pallas_call | solution.py:560
  (33 shorter events, 0.2 us)
Async XLA Ops:
  0.6 50.1 %copy-start.5 = (s32[256,1]{0,1:T(1,128)S(1)}, s32[256,1]{0,1:T(1,128)}, u32[]{:S(2)}) copy-start(s32[256,1]{0,1:T(1,128)} %param.11) | copy-start | bytes 3076
  0.6 50.1 %copy-start.3 = (s32[1,16]{1,0:T(1,128)S(1)}, s32[1,16]{1,0:T(1,128)}, u32[]{:S(2)}) copy-start(s32[1,16]{1,0:T(1,128)} %param.10) | copy-start | bytes 196
  1.7 10.6 %collective-permute-start.2 = (bf16[128,1024]{1,0:T(8,128)(2,1)S(1)}, bf16[128,1024]{1,0:T(8,128)(2,1)S(1)}, u32[]{:S(2)}, u32[]{:S(2)}) collective-permute-start(bf16[128,1024]{1,0:T(8,128)(2,1)S(1)} %get-tuple-element.55.refs_0_), channel_id=1, source_target_pairs={{2,4},{4,2},{3,5},{5,3},{10,12},{12,10},{11,13},{13,11},{18,20},{2... | collective-permute-start | bytes 786440 | tf_op jit(solution)/shard_map/ppermute | solution.py:47
  2.4 13.3 %collective-permute-start.6 = (bf16[128,1024]{1,0:T(8,128)(2,1)S(1)}, bf16[128,1024]{1,0:T(8,128)(2,1)S(1)}, u32[]{:S(2)}, u32[]{:S(2)}) collective-permute-start(bf16[128,1024]{1,0:T(8,128)(2,1)S(1)} %get-tuple-element.55.refs_0_), channel_id=1, source_target_pairs={{0,2},{2,0},{4,6},{6,4},{1,3},{3,1},{5,7},{7,5},{8,10},{10,8},{12,... | collective-permute-start | bytes 786440 | tf_op jit(solution)/shard_map/ppermute | solution.py:46
  8.3 8.1 %collective-permute-start = (bf16[128,1024]{1,0:T(8,128)(2,1)S(1)}, bf16[128,1024]{1,0:T(8,128)(2,1)S(1)}, u32[]{:S(2)}, u32[]{:S(2)}) collective-permute-start(bf16[128,1024]{1,0:T(8,128)(2,1)S(1)} %get-tuple-element.55.refs_0_), channel_id=1, source_target_pairs={{0,1},{1,0},{2,3},{3,2},{4,5},{5,4},{6,7},{7,6},{8,9},{9,8},{10,11... | collective-permute-start | bytes 786440 | tf_op jit(solution)/shard_map/ppermute | solution.py:71
  9.9 8.3 %collective-permute-start.4 = (bf16[128,1024]{1,0:T(8,128)(2,1)S(1)}, bf16[128,1024]{1,0:T(8,128)(2,1)S(1)}, u32[]{:S(2)}, u32[]{:S(2)}) collective-permute-start(bf16[128,1024]{1,0:T(8,128)(2,1)S(1)} %get-tuple-element.54.refs_1_), channel_id=1, source_target_pairs={{2,4},{4,2},{3,5},{5,3},{10,12},{12,10},{11,13},{13,11},{18,20},{2... | collective-permute-start | bytes 786440 | tf_op jit(solution)/shard_map/ppermute | solution.py:47
  10.5 10.9 %collective-permute-start.10 = (bf16[128,1024]{1,0:T(8,128)(2,1)S(1)}, bf16[128,1024]{1,0:T(8,128)(2,1)S(1)}, u32[]{:S(2)}, u32[]{:S(2)}) collective-permute-start(bf16[128,1024]{1,0:T(8,128)(2,1)S(1)} %get-tuple-element.54.refs_1_), channel_id=1, source_target_pairs={{0,2},{2,0},{4,6},{6,4},{1,3},{3,1},{5,7},{7,5},{8,10},{10,8},{12,... | collective-permute-start | bytes 786440 | tf_op jit(solution)/shard_map/ppermute | solution.py:46
  12.4 14.4 %collective-permute-start.3 = (bf16[128,1024]{1,0:T(8,128)(2,1)S(1)}, bf16[128,1024]{1,0:T(8,128)(2,1)S(1)}, u32[]{:S(2)}, u32[]{:S(2)}) collective-permute-start(bf16[128,1024]{1,0:T(8,128)(2,1)S(1)} %collective-permute-done.2), channel_id=1, source_target_pairs={{0,2},{2,0},{4,6},{6,4},{1,3},{3,1},{5,7},{7,5},{8,10},{10,8},{12,... | collective-permute-start | bytes 786440 | tf_op jit(solution)/shard_map/ppermute | solution.py:48
  15.8 12.5 %collective-permute-start.14 = (bf16[128,1024]{1,0:T(8,128)(2,1)S(1)}, bf16[128,1024]{1,0:T(8,128)(2,1)S(1)}, u32[]{:S(2)}, u32[]{:S(2)}) collective-permute-start(bf16[128,1024]{1,0:T(8,128)(2,1)S(1)} %collective-permute-done.6.refs_4_), channel_id=1, source_target_pairs={{2,4},{4,2},{3,5},{5,3},{10,12},{12,10},{11,13},{13,11},{18,20},{2... | collective-permute-start | bytes 786440 | tf_op jit(solution)/shard_map/ppermute | solution.py:49
  16.4 13.9 %collective-permute-start.7 = (bf16[128,1024]{1,0:T(8,128)(2,1)S(1)}, bf16[128,1024]{1,0:T(8,128)(2,1)S(1)}, u32[]{:S(2)}, u32[]{:S(2)}) collective-permute-start(bf16[128,1024]{1,0:T(8,128)(2,1)S(1)} %collective-permute-done.6.refs_4_), channel_id=1, source_target_pairs={{0,1},{1,0},{2,3},{3,2},{4,5},{5,4},{6,7},{7,6},{8,9},{9,8},{10,11... | collective-permute-start | bytes 786440 | tf_op jit(solution)/shard_map/ppermute | solution.py:71
  18.1 14.2 %collective-permute-start.5 = (bf16[128,1024]{1,0:T(8,128)(2,1)S(1)}, bf16[128,1024]{1,0:T(8,128)(2,1)S(1)}, u32[]{:S(2)}, u32[]{:S(2)}) collective-permute-start(bf16[128,1024]{1,0:T(8,128)(2,1)S(1)} %collective-permute-done.4), channel_id=1, source_target_pairs={{0,2},{2,0},{4,6},{6,4},{1,3},{3,1},{5,7},{7,5},{8,10},{10,8},{12,... | collective-permute-start | bytes 786440 | tf_op jit(solution)/shard_map/ppermute | solution.py:48
  21.5 12.4 %collective-permute-start.11 = (bf16[128,1024]{1,0:T(8,128)(2,1)S(1)}, bf16[128,1024]{1,0:T(8,128)(2,1)S(1)}, u32[]{:S(2)}, u32[]{:S(2)}) collective-permute-start(bf16[128,1024]{1,0:T(8,128)(2,1)S(1)} %collective-permute-done.10.refs_5_), channel_id=1, source_target_pairs={{2,4},{4,2},{3,5},{5,3},{10,12},{12,10},{11,13},{13,11},{18,20},{2... | collective-permute-start | bytes 786440 | tf_op jit(solution)/shard_map/ppermute | solution.py:49
  26.7 9.2 %collective-permute-start.1 = (bf16[128,1024]{1,0:T(8,128)(2,1)S(1)}, bf16[128,1024]{1,0:T(8,128)(2,1)S(1)}, u32[]{:S(2)}, u32[]{:S(2)}) collective-permute-start(bf16[128,1024]{1,0:T(8,128)(2,1)S(1)} %get-tuple-element.54.refs_1_), channel_id=1, source_target_pairs={{0,1},{1,0},{2,3},{3,2},{4,5},{5,4},{6,7},{7,6},{8,9},{9,8},{10,11... | collective-permute-start | bytes 786440 | tf_op jit(solution)/shard_map/ppermute | solution.py:71
  28.3 9.7 %collective-permute-start.15 = (bf16[128,1024]{1,0:T(8,128)(2,1)S(1)}, bf16[128,1024]{1,0:T(8,128)(2,1)S(1)}, u32[]{:S(2)}, u32[]{:S(2)}) collective-permute-start(bf16[128,1024]{1,0:T(8,128)(2,1)S(1)} %collective-permute-done.14), channel_id=1, source_target_pairs={{0,2},{2,0},{4,6},{6,4},{1,3},{3,1},{5,7},{7,5},{8,10},{10,8},{12,... | collective-permute-start | bytes 786440 | tf_op jit(solution)/shard_map/ppermute | solution.py:50
  30.3 20.4 %collective-permute-start.20 = (s32[256]{0:T(256)}, s32[256]{0:T(256)S(1)}, u32[]{:S(2)}, u32[]{:S(2)}) collective-permute-start(s32[256]{0:T(256)} %bitcast.32), channel_id=1, source_target_pairs={{0,1},{1,0},{2,3},{3,2},{4,5},{5,4},{6,7},{7,6},{8,9},{9,8},{10,11... | collective-permute-start | bytes 3080 | tf_op jit(solution)/shard_map/ppermute | solution.py:415
  32.4 9.2 %collective-permute-start.8 = (bf16[128,1024]{1,0:T(8,128)(2,1)S(1)}, bf16[128,1024]{1,0:T(8,128)(2,1)S(1)}, u32[]{:S(2)}, u32[]{:S(2)}) collective-permute-start(bf16[128,1024]{1,0:T(8,128)(2,1)S(1)} %broadcast_select_fusion.3.refs_4_.refs_8_), channel_id=1, source_target_pairs={{0,1},{1,0},{2,3},{3,2},{4,5},{5,4},{6,7},{7,6},{8,9},{9,8},{10,11... | collective-permute-start | bytes 786440 | tf_op jit(solution)/shard_map/ppermute | solution.py:71
  33.9 9.2 %collective-permute-start.12 = (bf16[128,1024]{1,0:T(8,128)(2,1)S(1)}, bf16[128,1024]{1,0:T(8,128)(2,1)S(1)}, u32[]{:S(2)}, u32[]{:S(2)}) collective-permute-start(bf16[128,1024]{1,0:T(8,128)(2,1)S(1)} %collective-permute-done.11), channel_id=1, source_target_pairs={{0,2},{2,0},{4,6},{6,4},{1,3},{3,1},{5,7},{7,5},{8,10},{10,8},{12,... | collective-permute-start | bytes 786440 | tf_op jit(solution)/shard_map/ppermute | solution.py:50
  35.9 11.2 %collective-permute-start.9 = (bf16[128,1024]{1,0:T(8,128)(2,1)S(1)}, bf16[128,1024]{1,0:T(8,128)(2,1)S(1)}, u32[]{:S(2)}, u32[]{:S(2)}) collective-permute-start(bf16[128,1024]{1,0:T(8,128)(2,1)S(1)} %broadcast_select_fusion.2.refs_5_.refs_9_), channel_id=1, source_target_pairs={{0,1},{1,0},{2,3},{3,2},{4,5},{5,4},{6,7},{7,6},{8,9},{9,8},{10,11... | collective-permute-start | bytes 786440 | tf_op jit(solution)/shard_map/ppermute | solution.py:71
  41.5 15.2 %collective-permute-start.16 = (bf16[128,1024]{1,0:T(8,128)(2,1)S(1)}, bf16[128,1024]{1,0:T(8,128)(2,1)S(1)}, u32[]{:S(2)}, u32[]{:S(2)}) collective-permute-start(bf16[128,1024]{1,0:T(8,128)(2,1)S(1)} %broadcast_select_fusion.1.refs_12_), channel_id=1, source_target_pairs={{0,1},{1,0},{2,3},{3,2},{4,5},{5,4},{6,7},{7,6},{8,9},{9,8},{10,11... | collective-permute-start | bytes 786440 | tf_op jit(solution)/shard_map/ppermute | solution.py:71
  47.1 9.6 %collective-permute-start.17 = (bf16[128,1024]{1,0:T(8,128)(2,1)S(1)}, bf16[128,1024]{1,0:T(8,128)(2,1)S(1)}, u32[]{:S(2)}, u32[]{:S(2)}) collective-permute-start(bf16[128,1024]{1,0:T(8,128)(2,1)S(1)} %broadcast_select_fusion.refs_13_), channel_id=1, source_target_pairs={{0,1},{1,0},{2,3},{3,2},{4,5},{5,4},{6,7},{7,6},{8,9},{9,8},{10,11... | collective-permute-start | bytes 786440 | tf_op jit(solution)/shard_map/ppermute | solution.py:71
  48.7 8.1 %collective-permute-start.13 = (bf16[128,1024]{1,0:T(8,128)(2,1)S(1)}, bf16[128,1024]{1,0:T(8,128)(2,1)S(1)}, u32[]{:S(2)}, u32[]{:S(2)}) collective-permute-start(bf16[128,1024]{1,0:T(8,128)(2,1)S(1)} %collective-permute-done.1.refs_3_), channel_id=1, source_target_pairs={{0,2},{2,0},{4,6},{6,4},{1,3},{3,1},{5,7},{7,5},{8,10},{10,8},{12,... | collective-permute-start | bytes 786440 | tf_op jit(solution)/shard_map/ppermute | solution.py:68
  50.7 3.4 %copy-start = (bf16[1,2,1024,2048]{3,2,1,0:T(8,128)(2,1)S(1)}, bf16[1,2,1024,2048]{3,2,1,0:T(8,128)(2,1)}, u32[]{:S(2)}) copy-start(bf16[1,2,1024,2048]{3,2,1,0:T(8,128)(2,1)} %param.7) | copy-start | bytes 25165828
  54.1 3.4 %copy-start.1 = (bf16[1,2,1024,2048]{3,2,1,0:T(8,128)(2,1)S(1)}, bf16[1,2,1024,2048]{3,2,1,0:T(8,128)(2,1)}, u32[]{:S(2)}) copy-start(bf16[1,2,1024,2048]{3,2,1,0:T(8,128)(2,1)} %param.7) | copy-start | bytes 25165828
  56.7 6.7 %copy-start.4 = (f32[2,16]{1,0:T(2,128)S(1)}, f32[2,16]{1,0:T(2,128)}, u32[]{:S(2)}) copy-start(f32[2,16]{1,0:T(2,128)} %table.3) | copy-start | bytes 388
  61.4 54.1 %collective-permute-start.19 = (bf16[3584,128]{1,0:T(8,128)(2,1)S(1)}, bf16[3584,128]{1,0:T(8,128)(2,1)S(1)}, u32[]{:S(2)}, u32[]{:S(2)}) collective-permute-start(bf16[3584,128]{1,0:T(8,128)(2,1)S(1)} %get-tuple-element.35), channel_id=1, source_target_pairs={{0,1},{1,0},{2,3},{3,2},{4,5},{5,4},{6,7},{7,6},{8,9},{9,8},{10,11... | collective-permute-start | bytes 2752520 | tf_op jit(solution)/shard_map/ppermute | solution.py:548
  63.5 41.0 %copy-start.2 = (f32[64,1,1,2,512]{4,3,2,1,0:T(2,128)S(1)}, f32[64,1,1,2,512]{4,3,2,1,0:T(2,128)}, u32[]{:S(2)}) copy-start(f32[64,1,1,2,512]{4,3,2,1,0:T(2,128)} %param.9) | copy-start | bytes 786436
  66.6 26.4 %collective-permute-start.21 = (bf16[4,72,1024]{2,1,0:T(8,128)(2,1)S(1)}, bf16[4,72,1024]{2,1,0:T(8,128)(2,1)S(1)}, u32[]{:S(2)}, u32[]{:S(2)}) collective-permute-start(bf16[4,72,1024]{2,1,0:T(8,128)(2,1)S(1)} %bitcast.30), channel_id=1, source_target_pairs={{0,1},{1,0},{2,3},{3,2},{4,5},{5,4},{6,7},{7,6},{8,9},{9,8},{10,11... | collective-permute-start | bytes 1769480 | tf_op jit(solution)/shard_map/ppermute | solution.py:499
  93.2 7.2 %collective-permute-start.22 = (bf16[72,1024]{1,0:T(8,128)(2,1)S(1)}, bf16[72,1024]{1,0:T(8,128)(2,1)S(1)}, u32[]{:S(2)}, u32[]{:S(2)}) collective-permute-start(bf16[72,1024]{1,0:T(8,128)(2,1)S(1)} %get-tuple-element.43), channel_id=1, source_target_pairs={{0,2},{2,4},{4,6},{6,0},{1,3},{3,5},{5,7},{7,1},{8,10},{10,12},{12... | collective-permute-start | bytes 442376 | tf_op jit(solution)/shard_map/ppermute | solution.py:512
  94.0 10.5 %collective-permute-start.23 = (bf16[72,1024]{1,0:T(8,128)(2,1)S(1)}, bf16[72,1024]{1,0:T(8,128)(2,1)S(1)}, u32[]{:S(2)}, u32[]{:S(2)}) collective-permute-start(bf16[72,1024]{1,0:T(8,128)(2,1)S(1)} %get-tuple-element.44), channel_id=1, source_target_pairs={{0,4},{2,6},{4,0},{6,2},{1,5},{3,7},{5,1},{7,3},{8,12},{10,14},{12... | collective-permute-start | bytes 442376 | tf_op jit(solution)/shard_map/ppermute | solution.py:512
  95.6 8.9 %collective-permute-start.24 = (bf16[72,1024]{1,0:T(8,128)(2,1)S(1)}, bf16[72,1024]{1,0:T(8,128)(2,1)S(1)}, u32[]{:S(2)}, u32[]{:S(2)}) collective-permute-start(bf16[72,1024]{1,0:T(8,128)(2,1)S(1)} %get-tuple-element.45), channel_id=1, source_target_pairs={{0,6},{2,0},{4,2},{6,4},{1,7},{3,1},{5,3},{7,5},{8,14},{10,8},{12,... | collective-permute-start | bytes 442376 | tf_op jit(solution)/shard_map/ppermute | solution.py:512
  105.9 3.4 %collective-permute-start.25 = (f32[288,128]{1,0:T(8,128)S(1)}, f32[288,128]{1,0:T(8,128)S(1)}, u32[]{:S(2)}, u32[]{:S(2)}) collective-permute-start(f32[288,128]{1,0:T(8,128)S(1)} %get-tuple-element.47.refs_0_), channel_id=1, source_target_pairs={{0,8},{8,0},{16,24},{24,16},{1,9},{9,1},{17,25},{25,17},{2,10},{10... | collective-permute-start | bytes 442376 | tf_op jit(solution)/shard_map/ppermute | solution.py:529
  105.9 6.7 %collective-permute-start.26 = (f32[288,128]{1,0:T(8,128)S(1)}, f32[288,128]{1,0:T(8,128)S(1)}, u32[]{:S(2)}, u32[]{:S(2)}) collective-permute-start(f32[288,128]{1,0:T(8,128)S(1)} %get-tuple-element.47.refs_0_), channel_id=1, source_target_pairs={{0,16},{8,24},{16,0},{24,8},{1,17},{9,25},{17,1},{25,9},{2,18},{10... | collective-permute-start | bytes 442376 | tf_op jit(solution)/shard_map/ppermute | solution.py:529
  107.4 7.5 %collective-permute-start.27 = (f32[288,128]{1,0:T(8,128)S(1)}, f32[288,128]{1,0:T(8,128)S(1)}, u32[]{:S(2)}, u32[]{:S(2)}) collective-permute-start(f32[288,128]{1,0:T(8,128)S(1)} %get-tuple-element.47.refs_0_), channel_id=1, source_target_pairs={{0,24},{8,16},{16,8},{24,0},{1,25},{9,17},{17,9},{25,1},{2,26},{10... | collective-permute-start | bytes 442376 | tf_op jit(solution)/shard_map/ppermute | solution.py:529
  107.7 7.8 %collective-permute-start.18 = (bf16[512,128]{1,0:T(8,128)(2,1)S(1)}, bf16[512,128]{1,0:T(8,128)(2,1)S(1)}, u32[]{:S(2)}, u32[]{:S(2)}) collective-permute-start(bf16[512,128]{1,0:T(8,128)(2,1)S(1)} %get-tuple-element.34), channel_id=1, source_target_pairs={{0,1},{1,0},{2,3},{3,2},{4,5},{5,4},{6,7},{7,6},{8,9},{9,8},{10,11... | collective-permute-start | bytes 393224 | tf_op jit(solution)/shard_map/ppermute | solution.py:548

commit v4 on v3

--- a/solution.py
+++ b/solution.py
@@ -12,7 +12,7 @@
 BR = 8
 BC = 128
 MIB = 1 << 20
-SPLIT = (1, 7)
+SPLIT = (4,)
 
 
 def shift_pairs(rows, cols, step, valid):
@@ -60,7 +60,7 @@
             piece = make()
             stages[stage][0].append(piece)
             leaving = piece
-            if last is not None:
+            if last is not None and stage < rows - 1:
                 leaving, _ = lax.optimization_barrier((piece, last))
             for step in range(1, cols):
                 if stage == 1 and part == 1:
@@ -428,7 +428,6 @@
 
     stages, sources = gather_stages(factor[0, 0], rows, cols)
     stages = [[chunk for step in stage for chunk in step] for stage in stages]
-    late_owners, _ = lax.optimization_barrier((tuple(owners), stages[2][-1]))
     products = 2 * row_blocks * BS * 2 * wide * selected * BS // cols
     scratch = [
         pltpu.VMEM((selected * BS, wide), jnp.bfloat16),
@@ -457,6 +456,7 @@
                 name="early_products",
             )(ancestors[0], here, *early, *group_pieces)
         ]
+    late_owners, _ = lax.optimization_barrier((tuple(owners), early))
     all_pieces = [piece for stage in stages for piece in stage]
     others = max(1, cols - 1)
     laid_rows = rows_here * wide // BC

time: 119 us -> 121 us (1.017)
  waiting for transfers between devices: 53.8 us -> 58.2 us
    ppermute x7, waiting for transfers between devices: 7.6 us -> 3.7 us  [gather_stages(): last = lax.ppermute(leaving, grid, pairs)]
    ppermute x1, waiting for transfers between devices: 26.3 us -> 30 us  [compute(): lax.ppermute(diag_send[step - 1], grid, everyone_pairs[step])]
    ppermute x2, waiting for transfers between devices: 1.46 us -> 4.32 us  [gather_stages(): far_out = lax.ppermute(far, 'row', outer)]
    ppermute x3, waiting for transfers between devices: 5.59 us -> 7.09 us  [compute(): lax.ppermute(message, 'pole', [(i, i ^ step) for i in range(poles)])]
    ppermute x2 -> x1, starting transfers between devices: 3.54 us -> 3.05 us  [compute(): lax.ppermute(send[(step - 1) * size:step * size], grid, everyone_pairs[st...]
  transfers between devices with their start and end apart: 28 -> 27, of which waited for: 10 -> 11; matrix products, arithmetic and copies ran while one was open for 0% -> 0% of each run, Pallas kernels for 7% -> 7%
where the time goes in v4:
time: 121 us; the launch traced here: 120 us
  waiting for transfers between devices  58.2 us (48%)
  starting transfers between devices  42.4 us (35%)
  Pallas kernels  13.8 us (11%)
  local copies, waits for them, and re-layouts  4.47 us (4%)
  between operations  1.46 us (1%)
    ppermute x1, waiting for transfers between devices, compute(): lax.ppermute(diag_send[step - 1], grid, everyone_pairs[step])  30 us
    ppermute x7, starting transfers between devices, gather_stages(): last = lax.ppermute(leaving, grid, pairs)  9.98 us
    ppermute x2, starting transfers between devices, gather_stages(): near = lax.ppermute(own, 'row', outer)  7.75 us
    ppermute x3, waiting for transfers between devices, compute(): lax.ppermute(rounded[step - 1], 'row', [(i, (i + step) % rows) for i in r...  7.66 us
    ppermute x3, waiting for transfers between devices, compute(): lax.ppermute(message, 'pole', [(i, i ^ step) for i in range(poles)])  7.09 us
    ppermute x2, starting transfers between devices, gather_stages(): cross_out = lax.ppermute(cross, 'row', outer)  6.73 us
    ppermute x2, waiting for transfers between devices, gather_stages(): cross_out = lax.ppermute(cross, 'row', outer)  5.39 us
    ppermute x2, waiting for transfers between devices, gather_stages(): far_out = lax.ppermute(far, 'row', outer)  4.32 us
  transfers between devices with their start and end apart: 27, of which 11 were waited for; matrix products, arithmetic and copies ran while one was open for 0% of the time, Pallas kernels for 7%

profile of v4, /device:TPU:0, one launch (start us, length us, event | category | flops | bytes accessed | tf_op | source)
XLA Modules:
  0.0 120.4 jit_solution(2312521623909397784)
XLA Ops:
  0.6 1.1 slice_bitcast_fusion
  1.7 0.7 collective-permute-start.2
  2.4 5.9 %collective-permute-start.6 = (bf16[128,1024]{1,0:T(8,128)(2,1)S(1)}, bf16[128,1024]{1,0:T(8,128)(2,1)S(1)}, u32[]{:S(2)}, u32[]{:S(2)}) collective-permute-start(bf16[128,1024]{1,0:T(8,128)(2,1)S(1)} %get-tuple-element.49.refs_0_), channel_id=1, source_target_pairs={{0,2},{2,0},{4,6},{6,4},{1,3},{3,1},{5,7},{7,5},{8,10},{10,8},{12,... | collective-permute-start | bytes 786440 | tf_op jit(solution)/shard_map/ppermute | solution.py:46
  8.3 1.5 %collective-permute-start = (bf16[128,1024]{1,0:T(8,128)(2,1)S(1)}, bf16[128,1024]{1,0:T(8,128)(2,1)S(1)}, u32[]{:S(2)}, u32[]{:S(2)}) collective-permute-start(bf16[128,1024]{1,0:T(8,128)(2,1)S(1)} %get-tuple-element.49.refs_0_), channel_id=1, source_target_pairs={{0,1},{1,0},{2,3},{3,2},{4,5},{5,4},{6,7},{7,6},{8,9},{9,8},{10,11... | collective-permute-start | bytes 786440 | tf_op jit(solution)/shard_map/ppermute | solution.py:71
  9.8 0.7 collective-permute-start.4
  10.5 1.8 %collective-permute-start.10 = (bf16[128,1024]{1,0:T(8,128)(2,1)S(1)}, bf16[128,1024]{1,0:T(8,128)(2,1)S(1)}, u32[]{:S(2)}, u32[]{:S(2)}) collective-permute-start(bf16[128,1024]{1,0:T(8,128)(2,1)S(1)} %get-tuple-element.48.refs_1_), channel_id=1, source_target_pairs={{0,2},{2,0},{4,6},{6,4},{1,3},{3,1},{5,7},{7,5},{8,10},{10,8},{12,... | collective-permute-start | bytes 786440 | tf_op jit(solution)/shard_map/ppermute | solution.py:46
  12.3 0.0 collective-permute-done.2
  12.3 3.4 %collective-permute-start.3 = (bf16[128,1024]{1,0:T(8,128)(2,1)S(1)}, bf16[128,1024]{1,0:T(8,128)(2,1)S(1)}, u32[]{:S(2)}, u32[]{:S(2)}) collective-permute-start(bf16[128,1024]{1,0:T(8,128)(2,1)S(1)} %collective-permute-done.2), channel_id=1, source_target_pairs={{0,2},{2,0},{4,6},{6,4},{1,3},{3,1},{5,7},{7,5},{8,10},{10,8},{12,... | collective-permute-start | bytes 786440 | tf_op jit(solution)/shard_map/ppermute | solution.py:48
  15.7 0.7 collective-permute-start.14
  16.4 1.7 %collective-permute-start.7 = (bf16[128,1024]{1,0:T(8,128)(2,1)S(1)}, bf16[128,1024]{1,0:T(8,128)(2,1)S(1)}, u32[]{:S(2)}, u32[]{:S(2)}) collective-permute-start(bf16[128,1024]{1,0:T(8,128)(2,1)S(1)} %collective-permute-done.6.refs_4_), channel_id=1, source_target_pairs={{0,1},{1,0},{2,3},{3,2},{4,5},{5,4},{6,7},{7,6},{8,9},{9,8},{10,11... | collective-permute-start | bytes 786440 | tf_op jit(solution)/shard_map/ppermute | solution.py:71
  18.1 3.3 %collective-permute-start.5 = (bf16[128,1024]{1,0:T(8,128)(2,1)S(1)}, bf16[128,1024]{1,0:T(8,128)(2,1)S(1)}, u32[]{:S(2)}, u32[]{:S(2)}) collective-permute-start(bf16[128,1024]{1,0:T(8,128)(2,1)S(1)} %collective-permute-done.4), channel_id=1, source_target_pairs={{0,2},{2,0},{4,6},{6,4},{1,3},{3,1},{5,7},{7,5},{8,10},{10,8},{12,... | collective-permute-start | bytes 786440 | tf_op jit(solution)/shard_map/ppermute | solution.py:48
  21.5 0.7 collective-permute-start.11
  22.8 3.9 %collective-permute-done.3 = bf16[128,1024]{1,0:T(8,128)(2,1)S(1)} collective-permute-done((bf16[128,1024]{1,0:T(8,128)(2,1)S(1)}, bf16[128,1024]{1,0:T(8,128)(2,1)S(1)}, u32[]{:S(2)}, u32[]{:S(2)}) %collective-permute-start.3) | collective-permute-done | bytes 262176 | tf_op jit(solution)/shard_map/ppermute | solution.py:48
  26.7 1.5 %collective-permute-start.1 = (bf16[128,1024]{1,0:T(8,128)(2,1)S(1)}, bf16[128,1024]{1,0:T(8,128)(2,1)S(1)}, u32[]{:S(2)}, u32[]{:S(2)}) collective-permute-start(bf16[128,1024]{1,0:T(8,128)(2,1)S(1)} %get-tuple-element.48.refs_1_), channel_id=1, source_target_pairs={{0,1},{1,0},{2,3},{3,2},{4,5},{5,4},{6,7},{7,6},{8,9},{9,8},{10,11... | collective-permute-start | bytes 786440 | tf_op jit(solution)/shard_map/ppermute | solution.py:71
  28.2 2.0 %collective-permute-start.15 = (bf16[128,1024]{1,0:T(8,128)(2,1)S(1)}, bf16[128,1024]{1,0:T(8,128)(2,1)S(1)}, u32[]{:S(2)}, u32[]{:S(2)}) collective-permute-start(bf16[128,1024]{1,0:T(8,128)(2,1)S(1)} %collective-permute-done.14), channel_id=1, source_target_pairs={{0,2},{2,0},{4,6},{6,4},{1,3},{3,1},{5,7},{7,5},{8,10},{10,8},{12,... | collective-permute-start | bytes 786440 | tf_op jit(solution)/shard_map/ppermute | solution.py:50
  30.3 0.6 collective-permute-start.19
  30.9 1.5 %collective-permute-done.5 = bf16[128,1024]{1,0:T(8,128)(2,1)S(1)} collective-permute-done((bf16[128,1024]{1,0:T(8,128)(2,1)S(1)}, bf16[128,1024]{1,0:T(8,128)(2,1)S(1)}, u32[]{:S(2)}, u32[]{:S(2)}) %collective-permute-start.5) | collective-permute-done | bytes 262176 | tf_op jit(solution)/shard_map/ppermute | solution.py:48
  32.3 1.5 %collective-permute-start.8 = (bf16[128,1024]{1,0:T(8,128)(2,1)S(1)}, bf16[128,1024]{1,0:T(8,128)(2,1)S(1)}, u32[]{:S(2)}, u32[]{:S(2)}) collective-permute-start(bf16[128,1024]{1,0:T(8,128)(2,1)S(1)} %broadcast_select_fusion.3.refs_4_.refs_8_), channel_id=1, source_target_pairs={{0,1},{1,0},{2,3},{3,2},{4,5},{5,4},{6,7},{7,6},{8,9},{9,8},{10,11... | collective-permute-start | bytes 786440 | tf_op jit(solution)/shard_map/ppermute | solution.py:71
  33.9 2.0 %collective-permute-start.12 = (bf16[128,1024]{1,0:T(8,128)(2,1)S(1)}, bf16[128,1024]{1,0:T(8,128)(2,1)S(1)}, u32[]{:S(2)}, u32[]{:S(2)}) collective-permute-start(bf16[128,1024]{1,0:T(8,128)(2,1)S(1)} %collective-permute-done.11), channel_id=1, source_target_pairs={{0,2},{2,0},{4,6},{6,4},{1,3},{3,1},{5,7},{7,5},{8,10},{10,8},{12,... | collective-permute-start | bytes 786440 | tf_op jit(solution)/shard_map/ppermute | solution.py:50
  35.9 0.6 collective-permute-start.9
  36.5 1.5 %collective-permute-done.15 = bf16[128,1024]{1,0:T(8,128)(2,1)S(1)} collective-permute-done((bf16[128,1024]{1,0:T(8,128)(2,1)S(1)}, bf16[128,1024]{1,0:T(8,128)(2,1)S(1)}, u32[]{:S(2)}, u32[]{:S(2)}) %collective-permute-start.15) | collective-permute-done | bytes 262176 | tf_op jit(solution)/shard_map/ppermute | solution.py:50
  38.0 1.6 %collective-permute-start.16 = (bf16[128,1024]{1,0:T(8,128)(2,1)S(1)}, bf16[128,1024]{1,0:T(8,128)(2,1)S(1)}, u32[]{:S(2)}, u32[]{:S(2)}) collective-permute-start(bf16[128,1024]{1,0:T(8,128)(2,1)S(1)} %broadcast_select_fusion.1.refs_12_), channel_id=1, source_target_pairs={{0,1},{1,0},{2,3},{3,2},{4,5},{5,4},{6,7},{7,6},{8,9},{9,8},{10,11... | collective-permute-start | bytes 786440 | tf_op jit(solution)/shard_map/ppermute | solution.py:71
  39.6 2.9 %collective-permute-done.12 = bf16[128,1024]{1,0:T(8,128)(2,1)S(1)} collective-permute-done((bf16[128,1024]{1,0:T(8,128)(2,1)S(1)}, bf16[128,1024]{1,0:T(8,128)(2,1)S(1)}, u32[]{:S(2)}, u32[]{:S(2)}) %collective-permute-start.12) | collective-permute-done | bytes 262176 | tf_op jit(solution)/shard_map/ppermute | solution.py:50
  42.5 1.6 %collective-permute-start.17 = (bf16[128,1024]{1,0:T(8,128)(2,1)S(1)}, bf16[128,1024]{1,0:T(8,128)(2,1)S(1)}, u32[]{:S(2)}, u32[]{:S(2)}) collective-permute-start(bf16[128,1024]{1,0:T(8,128)(2,1)S(1)} %broadcast_select_fusion.refs_13_), channel_id=1, source_target_pairs={{0,1},{1,0},{2,3},{3,2},{4,5},{5,4},{6,7},{7,6},{8,9},{9,8},{10,11... | collective-permute-start | bytes 786440 | tf_op jit(solution)/shard_map/ppermute | solution.py:71
  44.1 1.7 %collective-permute-start.13 = (bf16[128,1024]{1,0:T(8,128)(2,1)S(1)}, bf16[128,1024]{1,0:T(8,128)(2,1)S(1)}, u32[]{:S(2)}, u32[]{:S(2)}) collective-permute-start(bf16[128,1024]{1,0:T(8,128)(2,1)S(1)} %collective-permute-done.1.refs_3_), channel_id=1, source_target_pairs={{0,2},{2,0},{4,6},{6,4},{1,3},{3,1},{5,7},{7,5},{8,10},{10,8},{12,... | collective-permute-start | bytes 786440 | tf_op jit(solution)/shard_map/ppermute | solution.py:68
  45.8 1.3 %collective-permute-done.9.refs_7_.refs_11_ = bf16[128,1024]{1,0:T(8,128)(2,1)S(1)} collective-permute-done((bf16[128,1024]{1,0:T(8,128)(2,1)S(1)}, bf16[128,1024]{1,0:T(8,128)(2,1)S(1)}, u32[]{:S(2)}, u32[]{:S(2)}) %collective-permute-start.9) | collective-permute-done | bytes 262176 | tf_op jit(solution)/shard_map/ppermute | solution.py:71
  47.1 3.4 %copy-done = bf16[1,2,1024,2048]{3,2,1,0:T(8,128)(2,1)S(1)} copy-done((bf16[1,2,1024,2048]{3,2,1,0:T(8,128)(2,1)S(1)}, bf16[1,2,1024,2048]{3,2,1,0:T(8,128)(2,1)}, u32[]{:S(2)}) %copy-start) | copy-done | bytes 8388632
  50.5 2.6 %early_products.1.early = f32[8,128,1024]{2,1,0:T(8,128)S(1)} custom-call(s32[16]{0:T(128)S(1)} %bitcast.27, bf16[2,1024,2048]{2,1,0:T(8,128)(2,1)S(1)} %bitcast.24, bf16[128,1024]{1,0:T(8,128)(2,1)S(1)} %get-tuple-element.49.refs_0_, bf16[128,1024]{1,0:T(8,128)(2,1)S(1)} %get-tuple-element.48.refs_1_, bf16[128,1024]{1,0:T(8,128)(2,1)S(1)} %collective-permute-done.refs_2_, ...), custom_call_target="tpu_custom_call" | custom-call | flops 2147483648 | bytes 4194304 | tf_op jit(solution)/shard_map/early_products/pallas_call | solution.py:443
  53.2 0.0 copy-start.4
  53.2 2.4 %collective-permute-done.17.refs_15_ = bf16[128,1024]{1,0:T(8,128)(2,1)S(1)} collective-permute-done((bf16[128,1024]{1,0:T(8,128)(2,1)S(1)}, bf16[128,1024]{1,0:T(8,128)(2,1)S(1)}, u32[]{:S(2)}, u32[]{:S(2)}) %collective-permute-start.17) | collective-permute-done | bytes 262176 | tf_op jit(solution)/shard_map/ppermute | solution.py:71
  55.6 3.9 %last_products.1 = (f32[4096,128]{1,0:T(8,128)S(1)}, bf16[4096,128]{1,0:T(8,128)(2,1)S(1)}, f32[8,128,1024]{2,1,0:T(8,128)S(1)}, bf16[8,512,256]{2,1,0:T(8,128)(2,1)S(1)}) custom-call(s32[16]{0:T(128)S(1)} %bitcast.28, bf16[2,1024,2048]{2,1,0:T(8,128)(2,1)S(1)} %bitcast.25, f32[8,128,1024]{2,1,0:T(8,128)S(1)} %early_products.1.early, ...), custom_call_target="tpu_custom_call" | custom-call | flops 2147483648 | bytes 8388608 | tf_op jit(solution)/shard_map/last_products/pallas_call | solution.py:464
  59.5 3.1 %collective-permute-start.18 = (bf16[4096,128]{1,0:T(8,128)(2,1)S(1)}, bf16[4096,128]{1,0:T(8,128)(2,1)S(1)}, u32[]{:S(2)}, u32[]{:S(2)}) collective-permute-start(bf16[4096,128]{1,0:T(8,128)(2,1)S(1)} %get-tuple-element.29), channel_id=1, source_target_pairs={{0,1},{1,0},{2,3},{3,2},{4,5},{5,4},{6,7},{7,6},{8,9},{9,8},{10,11... | collective-permute-start | bytes 3145736 | tf_op jit(solution)/shard_map/ppermute | solution.py:548
  62.6 3.1 %diag_products.1 = (f32[4,72,1024]{2,1,0:T(8,128)S(1)}, bf16[1,4,72,1024]{3,2,1,0:T(8,128)(2,1)S(1)}) custom-call(s32[16]{0:T(128)S(1)} %bitcast.29, f32[2,16]{1,0:T(2,128)S(1)} %copy-done.4, s32[1]{0:T(128)S(6)} %copy.15.slot, s32[512]{0:T(512)S(1)} %pad_add_fusion.owner, f32[8,128,1024]{2,1,0:T(8,128)S(1)} %get-tuple-element.32.total, ...), custom_call_target="tpu_custom_call" | custom-call | flops 2147483648 | bytes 8388608 | tf_op jit(solution)/shard_map/diag_products/pallas_call | solution.py:478
  65.7 0.1 collective-permute-start.20
  65.8 30.0 %collective-permute-done.20.refs_0_ = bf16[4,72,1024]{2,1,0:T(8,128)(2,1)S(1)} collective-permute-done((bf16[4,72,1024]{2,1,0:T(8,128)(2,1)S(1)}, bf16[4,72,1024]{2,1,0:T(8,128)(2,1)S(1)}, u32[]{:S(2)}, u32[]{:S(2)}) %collective-permute-start.20) | collective-permute-done | bytes 589856 | tf_op jit(solution)/shard_map/ppermute | solution.py:499
  95.9 0.1 regroup.1
  96.0 0.8 collective-permute-start.21
  96.8 1.6 %collective-permute-start.22 = (bf16[72,1024]{1,0:T(8,128)(2,1)S(1)}, bf16[72,1024]{1,0:T(8,128)(2,1)S(1)}, u32[]{:S(2)}, u32[]{:S(2)}) collective-permute-start(bf16[72,1024]{1,0:T(8,128)(2,1)S(1)} %get-tuple-element.38), channel_id=1, source_target_pairs={{0,4},{2,6},{4,0},{6,2},{1,5},{3,7},{5,1},{7,3},{8,12},{10,14},{12... | collective-permute-start | bytes 442376 | tf_op jit(solution)/shard_map/ppermute | solution.py:512
  98.4 1.4 %collective-permute-start.23 = (bf16[72,1024]{1,0:T(8,128)(2,1)S(1)}, bf16[72,1024]{1,0:T(8,128)(2,1)S(1)}, u32[]{:S(2)}, u32[]{:S(2)}) collective-permute-start(bf16[72,1024]{1,0:T(8,128)(2,1)S(1)} %get-tuple-element.39), channel_id=1, source_target_pairs={{0,6},{2,0},{4,2},{6,4},{1,7},{3,1},{5,3},{7,5},{8,14},{10,8},{12,... | collective-permute-start | bytes 442376 | tf_op jit(solution)/shard_map/ppermute | solution.py:512
  99.8 3.8 %collective-permute-done.21.refs_0_ = bf16[72,1024]{1,0:T(8,128)(2,1)S(1)} collective-permute-done((bf16[72,1024]{1,0:T(8,128)(2,1)S(1)}, bf16[72,1024]{1,0:T(8,128)(2,1)S(1)}, u32[]{:S(2)}, u32[]{:S(2)}) %collective-permute-start.21) | collective-permute-done | bytes 147488 | tf_op jit(solution)/shard_map/ppermute | solution.py:512
  103.6 3.9 %collective-permute-done.22.refs_1_ = bf16[72,1024]{1,0:T(8,128)(2,1)S(1)} collective-permute-done((bf16[72,1024]{1,0:T(8,128)(2,1)S(1)}, bf16[72,1024]{1,0:T(8,128)(2,1)S(1)}, u32[]{:S(2)}, u32[]{:S(2)}) %collective-permute-start.22) | collective-permute-done | bytes 147488 | tf_op jit(solution)/shard_map/ppermute | solution.py:512
  107.5 1.4 %finish.1 = (f32[512,128]{1,0:T(8,128)}, f32[288,128]{1,0:T(8,128)S(1)}) custom-call(f32[2,16]{1,0:T(2,128)S(1)} %copy-done.4, s32[1]{0:T(128)S(6)} %copy.15.slot, f32[512,128]{1,0:T(8,128)S(1)} %bitcast.26, f32[72,1024]{1,0:T(8,128)S(1)} %get-tuple-element.36.own, bf16[72,1024]{1,0:T(8,128)(2,1)S(1)} %collective-permute-done.21.refs_0_, ...), custom_call_target="tpu_custom_call" | custom-call | tf_op jit(solution)/shard_map/finish/pallas_call | solution.py:515
  108.9 1.5 %collective-permute-start.25 = (f32[288,128]{1,0:T(8,128)S(1)}, f32[288,128]{1,0:T(8,128)S(1)}, u32[]{:S(2)}, u32[]{:S(2)}) collective-permute-start(f32[288,128]{1,0:T(8,128)S(1)} %get-tuple-element.41.refs_0_), channel_id=1, source_target_pairs={{0,16},{8,24},{16,0},{24,8},{1,17},{9,25},{17,1},{25,9},{2,18},{10... | collective-permute-start | bytes 442376 | tf_op jit(solution)/shard_map/ppermute | solution.py:529
  110.4 0.4 collective-permute-start.26
  110.8 4.9 %collective-permute-done.25.refs_2_ = f32[288,128]{1,0:T(8,128)S(1)} collective-permute-done((f32[288,128]{1,0:T(8,128)S(1)}, f32[288,128]{1,0:T(8,128)S(1)}, u32[]{:S(2)}, u32[]{:S(2)}) %collective-permute-start.25) | collective-permute-done | bytes 147488 | tf_op jit(solution)/shard_map/ppermute | solution.py:529
  115.6 2.2 %collective-permute-done.26.refs_3_ = f32[288,128]{1,0:T(8,128)S(1)} collective-permute-done((f32[288,128]{1,0:T(8,128)S(1)}, f32[288,128]{1,0:T(8,128)S(1)}, u32[]{:S(2)}, u32[]{:S(2)}) %collective-permute-start.26) | collective-permute-done | bytes 147488 | tf_op jit(solution)/shard_map/ppermute | solution.py:529
  117.8 0.7 density.1
  118.5 1.9 %join_columns.1 = f32[4096,128]{1,0:T(8,128)} custom-call(f32[4096,128]{1,0:T(8,128)S(1)} %get-tuple-element.28.keep, bf16[4096,128]{1,0:T(8,128)(2,1)S(1)} %collective-permute-done.18.refs_0_), custom_call_target="tpu_custom_call" | custom-call | tf_op jit(solution)/shard_map/join_columns/pallas_call | solution.py:560
  (31 shorter events, 0.2 us)
Async XLA Ops:
  0.6 46.5 %copy-start.3 = (s32[1,16]{1,0:T(1,128)S(1)}, s32[1,16]{1,0:T(1,128)}, u32[]{:S(2)}) copy-start(s32[1,16]{1,0:T(1,128)} %param.10) | copy-start | bytes 196
  1.7 10.6 %collective-permute-start.2 = (bf16[128,1024]{1,0:T(8,128)(2,1)S(1)}, bf16[128,1024]{1,0:T(8,128)(2,1)S(1)}, u32[]{:S(2)}, u32[]{:S(2)}) collective-permute-start(bf16[128,1024]{1,0:T(8,128)(2,1)S(1)} %get-tuple-element.49.refs_0_), channel_id=1, source_target_pairs={{2,4},{4,2},{3,5},{5,3},{10,12},{12,10},{11,13},{13,11},{18,20},{2... | collective-permute-start | bytes 786440 | tf_op jit(solution)/shard_map/ppermute | solution.py:47
  2.4 13.3 %collective-permute-start.6 = (bf16[128,1024]{1,0:T(8,128)(2,1)S(1)}, bf16[128,1024]{1,0:T(8,128)(2,1)S(1)}, u32[]{:S(2)}, u32[]{:S(2)}) collective-permute-start(bf16[128,1024]{1,0:T(8,128)(2,1)S(1)} %get-tuple-element.49.refs_0_), channel_id=1, source_target_pairs={{0,2},{2,0},{4,6},{6,4},{1,3},{3,1},{5,7},{7,5},{8,10},{10,8},{12,... | collective-permute-start | bytes 786440 | tf_op jit(solution)/shard_map/ppermute | solution.py:46
  8.3 8.1 %collective-permute-start = (bf16[128,1024]{1,0:T(8,128)(2,1)S(1)}, bf16[128,1024]{1,0:T(8,128)(2,1)S(1)}, u32[]{:S(2)}, u32[]{:S(2)}) collective-permute-start(bf16[128,1024]{1,0:T(8,128)(2,1)S(1)} %get-tuple-element.49.refs_0_), channel_id=1, source_target_pairs={{0,1},{1,0},{2,3},{3,2},{4,5},{5,4},{6,7},{7,6},{8,9},{9,8},{10,11... | collective-permute-start | bytes 786440 | tf_op jit(solution)/shard_map/ppermute | solution.py:71
  9.8 8.3 %collective-permute-start.4 = (bf16[128,1024]{1,0:T(8,128)(2,1)S(1)}, bf16[128,1024]{1,0:T(8,128)(2,1)S(1)}, u32[]{:S(2)}, u32[]{:S(2)}) collective-permute-start(bf16[128,1024]{1,0:T(8,128)(2,1)S(1)} %get-tuple-element.48.refs_1_), channel_id=1, source_target_pairs={{2,4},{4,2},{3,5},{5,3},{10,12},{12,10},{11,13},{13,11},{18,20},{2... | collective-permute-start | bytes 786440 | tf_op jit(solution)/shard_map/ppermute | solution.py:47
  10.5 10.9 %collective-permute-start.10 = (bf16[128,1024]{1,0:T(8,128)(2,1)S(1)}, bf16[128,1024]{1,0:T(8,128)(2,1)S(1)}, u32[]{:S(2)}, u32[]{:S(2)}) collective-permute-start(bf16[128,1024]{1,0:T(8,128)(2,1)S(1)} %get-tuple-element.48.refs_1_), channel_id=1, source_target_pairs={{0,2},{2,0},{4,6},{6,4},{1,3},{3,1},{5,7},{7,5},{8,10},{10,8},{12,... | collective-permute-start | bytes 786440 | tf_op jit(solution)/shard_map/ppermute | solution.py:46
  12.3 14.4 %collective-permute-start.3 = (bf16[128,1024]{1,0:T(8,128)(2,1)S(1)}, bf16[128,1024]{1,0:T(8,128)(2,1)S(1)}, u32[]{:S(2)}, u32[]{:S(2)}) collective-permute-start(bf16[128,1024]{1,0:T(8,128)(2,1)S(1)} %collective-permute-done.2), channel_id=1, source_target_pairs={{0,2},{2,0},{4,6},{6,4},{1,3},{3,1},{5,7},{7,5},{8,10},{10,8},{12,... | collective-permute-start | bytes 786440 | tf_op jit(solution)/shard_map/ppermute | solution.py:48
  15.7 12.5 %collective-permute-start.14 = (bf16[128,1024]{1,0:T(8,128)(2,1)S(1)}, bf16[128,1024]{1,0:T(8,128)(2,1)S(1)}, u32[]{:S(2)}, u32[]{:S(2)}) collective-permute-start(bf16[128,1024]{1,0:T(8,128)(2,1)S(1)} %collective-permute-done.6.refs_4_), channel_id=1, source_target_pairs={{2,4},{4,2},{3,5},{5,3},{10,12},{12,10},{11,13},{13,11},{18,20},{2... | collective-permute-start | bytes 786440 | tf_op jit(solution)/shard_map/ppermute | solution.py:49
  16.4 13.9 %collective-permute-start.7 = (bf16[128,1024]{1,0:T(8,128)(2,1)S(1)}, bf16[128,1024]{1,0:T(8,128)(2,1)S(1)}, u32[]{:S(2)}, u32[]{:S(2)}) collective-permute-start(bf16[128,1024]{1,0:T(8,128)(2,1)S(1)} %collective-permute-done.6.refs_4_), channel_id=1, source_target_pairs={{0,1},{1,0},{2,3},{3,2},{4,5},{5,4},{6,7},{7,6},{8,9},{9,8},{10,11... | collective-permute-start | bytes 786440 | tf_op jit(solution)/shard_map/ppermute | solution.py:71
  18.1 14.2 %collective-permute-start.5 = (bf16[128,1024]{1,0:T(8,128)(2,1)S(1)}, bf16[128,1024]{1,0:T(8,128)(2,1)S(1)}, u32[]{:S(2)}, u32[]{:S(2)}) collective-permute-start(bf16[128,1024]{1,0:T(8,128)(2,1)S(1)} %collective-permute-done.4), channel_id=1, source_target_pairs={{0,2},{2,0},{4,6},{6,4},{1,3},{3,1},{5,7},{7,5},{8,10},{10,8},{12,... | collective-permute-start | bytes 786440 | tf_op jit(solution)/shard_map/ppermute | solution.py:48
  21.5 12.4 %collective-permute-start.11 = (bf16[128,1024]{1,0:T(8,128)(2,1)S(1)}, bf16[128,1024]{1,0:T(8,128)(2,1)S(1)}, u32[]{:S(2)}, u32[]{:S(2)}) collective-permute-start(bf16[128,1024]{1,0:T(8,128)(2,1)S(1)} %collective-permute-done.10.refs_5_), channel_id=1, source_target_pairs={{2,4},{4,2},{3,5},{5,3},{10,12},{12,10},{11,13},{13,11},{18,20},{2... | collective-permute-start | bytes 786440 | tf_op jit(solution)/shard_map/ppermute | solution.py:49
  26.7 9.2 %collective-permute-start.1 = (bf16[128,1024]{1,0:T(8,128)(2,1)S(1)}, bf16[128,1024]{1,0:T(8,128)(2,1)S(1)}, u32[]{:S(2)}, u32[]{:S(2)}) collective-permute-start(bf16[128,1024]{1,0:T(8,128)(2,1)S(1)} %get-tuple-element.48.refs_1_), channel_id=1, source_target_pairs={{0,1},{1,0},{2,3},{3,2},{4,5},{5,4},{6,7},{7,6},{8,9},{9,8},{10,11... | collective-permute-start | bytes 786440 | tf_op jit(solution)/shard_map/ppermute | solution.py:71
  28.2 9.7 %collective-permute-start.15 = (bf16[128,1024]{1,0:T(8,128)(2,1)S(1)}, bf16[128,1024]{1,0:T(8,128)(2,1)S(1)}, u32[]{:S(2)}, u32[]{:S(2)}) collective-permute-start(bf16[128,1024]{1,0:T(8,128)(2,1)S(1)} %collective-permute-done.14), channel_id=1, source_target_pairs={{0,2},{2,0},{4,6},{6,4},{1,3},{3,1},{5,7},{7,5},{8,10},{10,8},{12,... | collective-permute-start | bytes 786440 | tf_op jit(solution)/shard_map/ppermute | solution.py:50
  30.3 22.9 %collective-permute-start.19 = (s32[256]{0:T(256)}, s32[256]{0:T(256)S(1)}, u32[]{:S(2)}, u32[]{:S(2)}) collective-permute-start(s32[256]{0:T(256)} %bitcast.32), channel_id=1, source_target_pairs={{0,1},{1,0},{2,3},{3,2},{4,5},{5,4},{6,7},{7,6},{8,9},{9,8},{10,11... | collective-permute-start | bytes 3080 | tf_op jit(solution)/shard_map/ppermute | solution.py:415
  32.3 11.7 %collective-permute-start.8 = (bf16[128,1024]{1,0:T(8,128)(2,1)S(1)}, bf16[128,1024]{1,0:T(8,128)(2,1)S(1)}, u32[]{:S(2)}, u32[]{:S(2)}) collective-permute-start(bf16[128,1024]{1,0:T(8,128)(2,1)S(1)} %broadcast_select_fusion.3.refs_4_.refs_8_), channel_id=1, source_target_pairs={{0,1},{1,0},{2,3},{3,2},{4,5},{5,4},{6,7},{7,6},{8,9},{9,8},{10,11... | collective-permute-start | bytes 786440 | tf_op jit(solution)/shard_map/ppermute | solution.py:71
  33.9 8.6 %collective-permute-start.12 = (bf16[128,1024]{1,0:T(8,128)(2,1)S(1)}, bf16[128,1024]{1,0:T(8,128)(2,1)S(1)}, u32[]{:S(2)}, u32[]{:S(2)}) collective-permute-start(bf16[128,1024]{1,0:T(8,128)(2,1)S(1)} %collective-permute-done.11), channel_id=1, source_target_pairs={{0,2},{2,0},{4,6},{6,4},{1,3},{3,1},{5,7},{7,5},{8,10},{10,8},{12,... | collective-permute-start | bytes 786440 | tf_op jit(solution)/shard_map/ppermute | solution.py:50
  35.9 11.2 %collective-permute-start.9 = (bf16[128,1024]{1,0:T(8,128)(2,1)S(1)}, bf16[128,1024]{1,0:T(8,128)(2,1)S(1)}, u32[]{:S(2)}, u32[]{:S(2)}) collective-permute-start(bf16[128,1024]{1,0:T(8,128)(2,1)S(1)} %broadcast_select_fusion.2.refs_5_.refs_9_), channel_id=1, source_target_pairs={{0,1},{1,0},{2,3},{3,2},{4,5},{5,4},{6,7},{7,6},{8,9},{9,8},{10,11... | collective-permute-start | bytes 786440 | tf_op jit(solution)/shard_map/ppermute | solution.py:71
  38.0 15.2 %collective-permute-start.16 = (bf16[128,1024]{1,0:T(8,128)(2,1)S(1)}, bf16[128,1024]{1,0:T(8,128)(2,1)S(1)}, u32[]{:S(2)}, u32[]{:S(2)}) collective-permute-start(bf16[128,1024]{1,0:T(8,128)(2,1)S(1)} %broadcast_select_fusion.1.refs_12_), channel_id=1, source_target_pairs={{0,1},{1,0},{2,3},{3,2},{4,5},{5,4},{6,7},{7,6},{8,9},{9,8},{10,11... | collective-permute-start | bytes 786440 | tf_op jit(solution)/shard_map/ppermute | solution.py:71
  42.5 13.1 %collective-permute-start.17 = (bf16[128,1024]{1,0:T(8,128)(2,1)S(1)}, bf16[128,1024]{1,0:T(8,128)(2,1)S(1)}, u32[]{:S(2)}, u32[]{:S(2)}) collective-permute-start(bf16[128,1024]{1,0:T(8,128)(2,1)S(1)} %broadcast_select_fusion.refs_13_), channel_id=1, source_target_pairs={{0,1},{1,0},{2,3},{3,2},{4,5},{5,4},{6,7},{7,6},{8,9},{9,8},{10,11... | collective-permute-start | bytes 786440 | tf_op jit(solution)/shard_map/ppermute | solution.py:71
  44.1 11.5 %collective-permute-start.13 = (bf16[128,1024]{1,0:T(8,128)(2,1)S(1)}, bf16[128,1024]{1,0:T(8,128)(2,1)S(1)}, u32[]{:S(2)}, u32[]{:S(2)}) collective-permute-start(bf16[128,1024]{1,0:T(8,128)(2,1)S(1)} %collective-permute-done.1.refs_3_), channel_id=1, source_target_pairs={{0,2},{2,0},{4,6},{6,4},{1,3},{3,1},{5,7},{7,5},{8,10},{10,8},{12,... | collective-permute-start | bytes 786440 | tf_op jit(solution)/shard_map/ppermute | solution.py:68
  47.1 3.4 %copy-start = (bf16[1,2,1024,2048]{3,2,1,0:T(8,128)(2,1)S(1)}, bf16[1,2,1024,2048]{3,2,1,0:T(8,128)(2,1)}, u32[]{:S(2)}) copy-start(bf16[1,2,1024,2048]{3,2,1,0:T(8,128)(2,1)} %param.7) | copy-start | bytes 25165828
  50.5 2.7 %copy-start.5 = (s32[256,1]{0,1:T(1,128)S(1)}, s32[256,1]{0,1:T(1,128)}, u32[]{:S(2)}) copy-start(s32[256,1]{0,1:T(1,128)} %param.11) | copy-start | bytes 3076
  50.5 5.1 %copy-start.1 = (bf16[1,2,1024,2048]{3,2,1,0:T(8,128)(2,1)S(1)}, bf16[1,2,1024,2048]{3,2,1,0:T(8,128)(2,1)}, u32[]{:S(2)}) copy-start(bf16[1,2,1024,2048]{3,2,1,0:T(8,128)(2,1)} %param.7) | copy-start | bytes 25165828
  53.2 9.4 %copy-start.4 = (f32[2,16]{1,0:T(2,128)S(1)}, f32[2,16]{1,0:T(2,128)}, u32[]{:S(2)}) copy-start(f32[2,16]{1,0:T(2,128)} %table.3) | copy-start | bytes 388
  59.5 59.0 %collective-permute-start.18 = (bf16[4096,128]{1,0:T(8,128)(2,1)S(1)}, bf16[4096,128]{1,0:T(8,128)(2,1)S(1)}, u32[]{:S(2)}, u32[]{:S(2)}) collective-permute-start(bf16[4096,128]{1,0:T(8,128)(2,1)S(1)} %get-tuple-element.29), channel_id=1, source_target_pairs={{0,1},{1,0},{2,3},{3,2},{4,5},{5,4},{6,7},{7,6},{8,9},{9,8},{10,11... | collective-permute-start | bytes 3145736 | tf_op jit(solution)/shard_map/ppermute | solution.py:548
  62.6 44.9 %copy-start.2 = (f32[64,1,1,2,512]{4,3,2,1,0:T(2,128)S(1)}, f32[64,1,1,2,512]{4,3,2,1,0:T(2,128)}, u32[]{:S(2)}) copy-start(f32[64,1,1,2,512]{4,3,2,1,0:T(2,128)} %param.9) | copy-start | bytes 786436
  65.7 30.1 %collective-permute-start.20 = (bf16[4,72,1024]{2,1,0:T(8,128)(2,1)S(1)}, bf16[4,72,1024]{2,1,0:T(8,128)(2,1)S(1)}, u32[]{:S(2)}, u32[]{:S(2)}) collective-permute-start(bf16[4,72,1024]{2,1,0:T(8,128)(2,1)S(1)} %bitcast.30), channel_id=1, source_target_pairs={{0,1},{1,0},{2,3},{3,2},{4,5},{5,4},{6,7},{7,6},{8,9},{9,8},{10,11... | collective-permute-start | bytes 1769480 | tf_op jit(solution)/shard_map/ppermute | solution.py:499
  96.0 7.7 %collective-permute-start.21 = (bf16[72,1024]{1,0:T(8,128)(2,1)S(1)}, bf16[72,1024]{1,0:T(8,128)(2,1)S(1)}, u32[]{:S(2)}, u32[]{:S(2)}) collective-permute-start(bf16[72,1024]{1,0:T(8,128)(2,1)S(1)} %get-tuple-element.37), channel_id=1, source_target_pairs={{0,2},{2,4},{4,6},{6,0},{1,3},{3,5},{5,7},{7,1},{8,10},{10,12},{12... | collective-permute-start | bytes 442376 | tf_op jit(solution)/shard_map/ppermute | solution.py:512
  96.8 10.7 %collective-permute-start.22 = (bf16[72,1024]{1,0:T(8,128)(2,1)S(1)}, bf16[72,1024]{1,0:T(8,128)(2,1)S(1)}, u32[]{:S(2)}, u32[]{:S(2)}) collective-permute-start(bf16[72,1024]{1,0:T(8,128)(2,1)S(1)} %get-tuple-element.38), channel_id=1, source_target_pairs={{0,4},{2,6},{4,0},{6,2},{1,5},{3,7},{5,1},{7,3},{8,12},{10,14},{12... | collective-permute-start | bytes 442376 | tf_op jit(solution)/shard_map/ppermute | solution.py:512
  98.4 9.1 %collective-permute-start.23 = (bf16[72,1024]{1,0:T(8,128)(2,1)S(1)}, bf16[72,1024]{1,0:T(8,128)(2,1)S(1)}, u32[]{:S(2)}, u32[]{:S(2)}) collective-permute-start(bf16[72,1024]{1,0:T(8,128)(2,1)S(1)} %get-tuple-element.39), channel_id=1, source_target_pairs={{0,6},{2,0},{4,2},{6,4},{1,7},{3,1},{5,3},{7,5},{8,14},{10,8},{12,... | collective-permute-start | bytes 442376 | tf_op jit(solution)/shard_map/ppermute | solution.py:512
  108.9 1.9 %collective-permute-start.24 = (f32[288,128]{1,0:T(8,128)S(1)}, f32[288,128]{1,0:T(8,128)S(1)}, u32[]{:S(2)}, u32[]{:S(2)}) collective-permute-start(f32[288,128]{1,0:T(8,128)S(1)} %get-tuple-element.41.refs_0_), channel_id=1, source_target_pairs={{0,8},{8,0},{16,24},{24,16},{1,9},{9,1},{17,25},{25,17},{2,10},{10... | collective-permute-start | bytes 442376 | tf_op jit(solution)/shard_map/ppermute | solution.py:529
  108.9 6.7 %collective-permute-start.25 = (f32[288,128]{1,0:T(8,128)S(1)}, f32[288,128]{1,0:T(8,128)S(1)}, u32[]{:S(2)}, u32[]{:S(2)}) collective-permute-start(f32[288,128]{1,0:T(8,128)S(1)} %get-tuple-element.41.refs_0_), channel_id=1, source_target_pairs={{0,16},{8,24},{16,0},{24,8},{1,17},{9,25},{17,1},{25,9},{2,18},{10... | collective-permute-start | bytes 442376 | tf_op jit(solution)/shard_map/ppermute | solution.py:529
  110.4 7.5 %collective-permute-start.26 = (f32[288,128]{1,0:T(8,128)S(1)}, f32[288,128]{1,0:T(8,128)S(1)}, u32[]{:S(2)}, u32[]{:S(2)}) collective-permute-start(f32[288,128]{1,0:T(8,128)S(1)} %get-tuple-element.41.refs_0_), channel_id=1, source_target_pairs={{0,24},{8,16},{16,8},{24,0},{1,25},{9,17},{17,9},{25,1},{2,26},{10... | collective-permute-start | bytes 442376 | tf_op jit(solution)/shard_map/ppermute | solution.py:529

commit v5 on v4

--- a/solution.py
+++ b/solution.py
@@ -120,11 +120,13 @@
     r = lax.axis_index("row")
     c = lax.axis_index("col")
 
-    @pl.when(jnp.logical_and(low < col_last, low + stage_blocks > col_first))
-    def _():
+    start = jnp.maximum(low, col_first)
+    width = jnp.minimum(low + stage_blocks, col_last) - start
+
+    def add(first, blocks):
         left = []
-        for n in range(stage_blocks):
-            k = low + n
+        for n in range(blocks):
+            k = first + n
             inside = jnp.logical_and(k >= col_first, k < col_last)
             block = jnp.where(inside, ancestors[k] - c * col_blocks, 0)
             column = pl.ds(pl.multiple_of(block * BS, BS), BS)
@@ -135,10 +137,20 @@
                 both.append(inverse[:, pl.ds(row, BS), column].reshape(2 * BS, BS))
             value = jnp.concatenate(both, axis=0)
             left.append(value * inside.astype(value.dtype))
-        place = pl.ds(pl.multiple_of(low * BS, BS), stage_blocks * BS)
+        place = pl.ds(pl.multiple_of(first * BS, BS), blocks * BS)
         acc[...] += jnp.dot(
             jnp.concatenate(left, axis=1), full[place, :], preferred_element_type=jnp.float32
         )
+
+    few = stage_blocks // 2
+
+    @pl.when(width > few)
+    def _():
+        add(low, stage_blocks)
+
+    @pl.when(jnp.logical_and(width > 0, width <= few))
+    def _():
+        add(jnp.minimum(start, low + stage_blocks - few), few)
 
 
 def combine(acc, n):
@@ -166,6 +178,11 @@
             @pl.when(2 * pair + n < row_count)
             def _():
                 store(2 * pair + n, *combine(acc, n))
+
+
+def list_kernel(ancestors, out):
+    for i in range(ancestors.shape[0]):
+        out[i] = ancestors[i]
 
 
 def early_kernel(sources, stages, added, rows, cols, ancestors, inverse, *refs):
@@ -436,6 +453,15 @@
     row_products = jax.ShapeDtypeStruct((row_blocks, BS, wide), jnp.float32)
     groups = [(0, rows - 2)] if rows > 2 else [(0,)]
     last = tuple(stage for stage in range(rows) if stage not in groups[0])
+    listing = pl.pallas_call(
+        list_kernel,
+        out_shape=jax.ShapeDtypeStruct((selected,), jnp.int32),
+        in_specs=[smem],
+        out_specs=smem,
+        compiler_params=pltpu.CompilerParams(vmem_limit_bytes=MIB),
+        cost_estimate=pl.CostEstimate(flops=products, bytes_accessed=8 * MIB, transcendentals=0),
+        name="list_blocks",
+    )(ancestors[0])
     early = []
     for group in groups:
         group_pieces = [piece for stage in group for piece in stages[stage]]
@@ -454,7 +480,7 @@
                     transcendentals=0,
                 ),
                 name="early_products",
-            )(ancestors[0], here, *early, *group_pieces)
+            )(listing, here, *early, *group_pieces)
         ]
     late_owners, _ = lax.optimization_barrier((tuple(owners), early))
     all_pieces = [piece for stage in stages for piece in stage]

time: 121 us -> 122 us (level)
  waiting for transfers between devices: 58.2 us -> 54 us
  starting transfers between devices: 42.4 us -> 46.2 us
    ppermute x2, waiting for transfers between devices: 5.39 us -> 0.01 us  [gather_stages(): cross_out = lax.ppermute(cross, 'row', outer)]
    ppermute x7, waiting for transfers between devices: 3.7 us -> 7.02 us  [gather_stages(): last = lax.ppermute(leaving, grid, pairs)]
    ppermute x2, starting transfers between devices: 6.73 us -> 9.56 us  [gather_stages(): cross_out = lax.ppermute(cross, 'row', outer)]
    ppermute x3, starting transfers between devices: 3.88 us -> 5.93 us  [compute(): lax.ppermute(rounded[step - 1], 'row', [(i, (i + step) % rows) for i in r...]
    ppermute x2, waiting for transfers between devices: 4.32 us -> 2.43 us  [gather_stages(): far_out = lax.ppermute(far, 'row', outer)]
    ppermute x7, starting transfers between devices: 9.98 us -> 8.37 us  [gather_stages(): last = lax.ppermute(leaving, grid, pairs)]
    unnamed x12 -> x14, local copies, waits for them, and re-layouts: 3.4 us -> 4.05 us
  transfers between devices with their start and end apart: 27 -> 27, of which waited for: 11 -> 10; matrix products, arithmetic and copies ran while one was open for 0% -> 0% of each run, Pallas kernels for 7% -> 8%
where the time goes in v5:
time: 122 us; the launch traced here: 121 us
  waiting for transfers between devices  54 us (44%)
  starting transfers between devices  46.2 us (38%)
  Pallas kernels  14.4 us (12%)
  local copies, waits for them, and re-layouts  5.12 us (4%)
  between operations  1.47 us (1%)
    ppermute x1, waiting for transfers between devices, compute(): lax.ppermute(diag_send[step - 1], grid, everyone_pairs[step])  30 us
    ppermute x2, starting transfers between devices, gather_stages(): cross_out = lax.ppermute(cross, 'row', outer)  9.56 us
    ppermute x7, starting transfers between devices, gather_stages(): last = lax.ppermute(leaving, grid, pairs)  8.37 us
    ppermute x3, waiting for transfers between devices, compute(): lax.ppermute(rounded[step - 1], 'row', [(i, (i + step) % rows) for i in r...  7.46 us
    ppermute x2, starting transfers between devices, gather_stages(): near = lax.ppermute(own, 'row', outer)  7.27 us
    ppermute x3, waiting for transfers between devices, compute(): lax.ppermute(message, 'pole', [(i, i ^ step) for i in range(poles)])  7.09 us
    ppermute x7, waiting for transfers between devices, gather_stages(): last = lax.ppermute(leaving, grid, pairs)  7.02 us
    ppermute x3, starting transfers between devices, compute(): lax.ppermute(rounded[step - 1], 'row', [(i, (i + step) % rows) for i in r...  5.93 us
  transfers between devices with their start and end apart: 27, of which 10 were waited for; matrix products, arithmetic and copies ran while one was open for 0% of the time, Pallas kernels for 8%

profile of v5, /device:TPU:0, one launch (start us, length us, event | category | flops | bytes accessed | tf_op | source)
XLA Modules:
  0.0 121.4 jit_solution(7969333094551488311)
XLA Ops:
  0.6 1.1 slice_bitcast_fusion
  1.7 3.1 %collective-permute-start = (bf16[128,1024]{1,0:T(8,128)(2,1)S(1)}, bf16[128,1024]{1,0:T(8,128)(2,1)S(1)}, u32[]{:S(2)}, u32[]{:S(2)}) collective-permute-start(bf16[128,1024]{1,0:T(8,128)(2,1)S(1)} %get-tuple-element.49.refs_0_), channel_id=1, source_target_pairs={{0,1},{1,0},{2,3},{3,2},{4,5},{5,4},{6,7},{7,6},{8,9},{9,8},{10,11... | collective-permute-start | bytes 786440 | tf_op jit(solution)/shard_map/ppermute | solution.py:71
  4.8 1.6 %collective-permute-start.6 = (bf16[128,1024]{1,0:T(8,128)(2,1)S(1)}, bf16[128,1024]{1,0:T(8,128)(2,1)S(1)}, u32[]{:S(2)}, u32[]{:S(2)}) collective-permute-start(bf16[128,1024]{1,0:T(8,128)(2,1)S(1)} %get-tuple-element.49.refs_0_), channel_id=1, source_target_pairs={{0,2},{2,0},{4,6},{6,4},{1,3},{3,1},{5,7},{7,5},{8,10},{10,8},{12,... | collective-permute-start | bytes 786440 | tf_op jit(solution)/shard_map/ppermute | solution.py:46
  6.3 0.7 collective-permute-start.2
  7.0 0.7 collective-permute-start.4
  7.7 5.7 %collective-permute-start.10 = (bf16[128,1024]{1,0:T(8,128)(2,1)S(1)}, bf16[128,1024]{1,0:T(8,128)(2,1)S(1)}, u32[]{:S(2)}, u32[]{:S(2)}) collective-permute-start(bf16[128,1024]{1,0:T(8,128)(2,1)S(1)} %get-tuple-element.48.refs_1_), channel_id=1, source_target_pairs={{0,2},{2,0},{4,6},{6,4},{1,3},{3,1},{5,7},{7,5},{8,10},{10,8},{12,... | collective-permute-start | bytes 786440 | tf_op jit(solution)/shard_map/ppermute | solution.py:46
  13.4 0.5 collective-permute-start.7
  13.9 0.7 collective-permute-start.14
  14.6 3.9 %collective-permute-start.3 = (bf16[128,1024]{1,0:T(8,128)(2,1)S(1)}, bf16[128,1024]{1,0:T(8,128)(2,1)S(1)}, u32[]{:S(2)}, u32[]{:S(2)}) collective-permute-start(bf16[128,1024]{1,0:T(8,128)(2,1)S(1)} %collective-permute-done.2), channel_id=1, source_target_pairs={{0,2},{2,0},{4,6},{6,4},{1,3},{3,1},{5,7},{7,5},{8,10},{10,8},{12,... | collective-permute-start | bytes 786440 | tf_op jit(solution)/shard_map/ppermute | solution.py:48
  18.5 5.6 %collective-permute-start.5 = (bf16[128,1024]{1,0:T(8,128)(2,1)S(1)}, bf16[128,1024]{1,0:T(8,128)(2,1)S(1)}, u32[]{:S(2)}, u32[]{:S(2)}) collective-permute-start(bf16[128,1024]{1,0:T(8,128)(2,1)S(1)} %collective-permute-done.4), channel_id=1, source_target_pairs={{0,2},{2,0},{4,6},{6,4},{1,3},{3,1},{5,7},{7,5},{8,10},{10,8},{12,... | collective-permute-start | bytes 786440 | tf_op jit(solution)/shard_map/ppermute | solution.py:48
  24.2 0.7 collective-permute-start.11
  24.8 0.0 copy-start.4
  24.8 0.6 copy-done.4
  25.5 1.1 list_blocks.1.ancestors
  27.3 0.6 collective-permute-start.1
  27.9 3.3 %collective-permute-start.15 = (bf16[128,1024]{1,0:T(8,128)(2,1)S(1)}, bf16[128,1024]{1,0:T(8,128)(2,1)S(1)}, u32[]{:S(2)}, u32[]{:S(2)}) collective-permute-start(bf16[128,1024]{1,0:T(8,128)(2,1)S(1)} %collective-permute-done.14), channel_id=1, source_target_pairs={{0,2},{2,0},{4,6},{6,4},{1,3},{3,1},{5,7},{7,5},{8,10},{10,8},{12,... | collective-permute-start | bytes 786440 | tf_op jit(solution)/shard_map/ppermute | solution.py:50
  31.2 1.6 %collective-permute-start.19 = (s32[256]{0:T(256)S(1)}, s32[256]{0:T(256)S(1)}, u32[]{:S(2)}, u32[]{:S(2)}) collective-permute-start(s32[256]{0:T(256)S(1)} %bitcast.32), channel_id=1, source_target_pairs={{0,1},{1,0},{2,3},{3,2},{4,5},{5,4},{6,7},{7,6},{8,9},{9,8},{10,11... | collective-permute-start | bytes 3080 | tf_op jit(solution)/shard_map/ppermute | solution.py:432
  32.8 0.5 collective-permute-start.8
  33.3 0.7 collective-permute-start.12
  34.0 2.3 %collective-permute-done.1.refs_3_ = bf16[128,1024]{1,0:T(8,128)(2,1)S(1)} collective-permute-done((bf16[128,1024]{1,0:T(8,128)(2,1)S(1)}, bf16[128,1024]{1,0:T(8,128)(2,1)S(1)}, u32[]{:S(2)}, u32[]{:S(2)}) %collective-permute-start.1) | collective-permute-done | bytes 262176 | tf_op jit(solution)/shard_map/ppermute | solution.py:71
  36.3 0.7 collective-permute-start.9
  37.0 0.9 collective-permute-done.15
  37.9 1.8 %collective-permute-start.16 = (bf16[128,1024]{1,0:T(8,128)(2,1)S(1)}, bf16[128,1024]{1,0:T(8,128)(2,1)S(1)}, u32[]{:S(2)}, u32[]{:S(2)}) collective-permute-start(bf16[128,1024]{1,0:T(8,128)(2,1)S(1)} %broadcast_select_fusion.1.refs_12_), channel_id=1, source_target_pairs={{0,1},{1,0},{2,3},{3,2},{4,5},{5,4},{6,7},{7,6},{8,9},{9,8},{10,11... | collective-permute-start | bytes 786440 | tf_op jit(solution)/shard_map/ppermute | solution.py:71
  39.8 1.6 %collective-permute-done.12 = bf16[128,1024]{1,0:T(8,128)(2,1)S(1)} collective-permute-done((bf16[128,1024]{1,0:T(8,128)(2,1)S(1)}, bf16[128,1024]{1,0:T(8,128)(2,1)S(1)}, u32[]{:S(2)}, u32[]{:S(2)}) %collective-permute-start.12) | collective-permute-done | bytes 262176 | tf_op jit(solution)/shard_map/ppermute | solution.py:50
  41.4 1.2 collective-permute-start.17
  42.6 2.9 %collective-permute-start.13 = (bf16[128,1024]{1,0:T(8,128)(2,1)S(1)}, bf16[128,1024]{1,0:T(8,128)(2,1)S(1)}, u32[]{:S(2)}, u32[]{:S(2)}) collective-permute-start(bf16[128,1024]{1,0:T(8,128)(2,1)S(1)} %collective-permute-done.1.refs_3_), channel_id=1, source_target_pairs={{0,2},{2,0},{4,6},{6,4},{1,3},{3,1},{5,7},{7,5},{8,10},{10,8},{12,... | collective-permute-start | bytes 786440 | tf_op jit(solution)/shard_map/ppermute | solution.py:68
  45.4 2.1 %collective-permute-done.9.refs_7_.refs_11_ = bf16[128,1024]{1,0:T(8,128)(2,1)S(1)} collective-permute-done((bf16[128,1024]{1,0:T(8,128)(2,1)S(1)}, bf16[128,1024]{1,0:T(8,128)(2,1)S(1)}, u32[]{:S(2)}, u32[]{:S(2)}) %collective-permute-start.9) | collective-permute-done | bytes 262176 | tf_op jit(solution)/shard_map/ppermute | solution.py:71
  47.6 3.4 %copy-done = bf16[1,2,1024,2048]{3,2,1,0:T(8,128)(2,1)S(1)} copy-done((bf16[1,2,1024,2048]{3,2,1,0:T(8,128)(2,1)S(1)}, bf16[1,2,1024,2048]{3,2,1,0:T(8,128)(2,1)}, u32[]{:S(2)}) %copy-start) | copy-done | bytes 8388632
  51.0 2.7 %early_products.1.early = f32[8,128,1024]{2,1,0:T(8,128)S(1)} custom-call(s32[16]{0:T(128)S(1)} %list_blocks.1.ancestors, bf16[2,1024,2048]{2,1,0:T(8,128)(2,1)S(1)} %bitcast.24, bf16[128,1024]{1,0:T(8,128)(2,1)S(1)} %get-tuple-element.49.refs_0_, bf16[128,1024]{1,0:T(8,128)(2,1)S(1)} %get-tuple-element.48.refs_1_, ...), custom_call_target="tpu_custom_call" | custom-call | flops 2147483648 | bytes 4194304 | tf_op jit(solution)/shard_map/early_products/pallas_call | solution.py:469
  53.7 2.5 %collective-permute-done.17.refs_15_ = bf16[128,1024]{1,0:T(8,128)(2,1)S(1)} collective-permute-done((bf16[128,1024]{1,0:T(8,128)(2,1)S(1)}, bf16[128,1024]{1,0:T(8,128)(2,1)S(1)}, u32[]{:S(2)}, u32[]{:S(2)}) %collective-permute-start.17) | collective-permute-done | bytes 262176 | tf_op jit(solution)/shard_map/ppermute | solution.py:71
  56.2 3.4 %last_products.1 = (f32[4096,128]{1,0:T(8,128)S(1)}, bf16[4096,128]{1,0:T(8,128)(2,1)S(1)}, f32[8,128,1024]{2,1,0:T(8,128)S(1)}, bf16[8,512,256]{2,1,0:T(8,128)(2,1)S(1)}) custom-call(s32[16]{0:T(128)S(1)} %bitcast.28, bf16[2,1024,2048]{2,1,0:T(8,128)(2,1)S(1)} %bitcast.25, f32[8,128,1024]{2,1,0:T(8,128)S(1)} %early_products.1.early, ...), custom_call_target="tpu_custom_call" | custom-call | flops 2147483648 | bytes 8388608 | tf_op jit(solution)/shard_map/last_products/pallas_call | solution.py:490
  59.7 2.0 %collective-permute-start.18 = (bf16[4096,128]{1,0:T(8,128)(2,1)S(1)}, bf16[4096,128]{1,0:T(8,128)(2,1)S(1)}, u32[]{:S(2)}, u32[]{:S(2)}) collective-permute-start(bf16[4096,128]{1,0:T(8,128)(2,1)S(1)} %get-tuple-element.29), channel_id=1, source_target_pairs={{0,1},{1,0},{2,3},{3,2},{4,5},{5,4},{6,7},{7,6},{8,9},{9,8},{10,11... | collective-permute-start | bytes 3145736 | tf_op jit(solution)/shard_map/ppermute | solution.py:574
  61.7 3.1 %diag_products.1 = (f32[4,72,1024]{2,1,0:T(8,128)S(1)}, bf16[1,4,72,1024]{3,2,1,0:T(8,128)(2,1)S(1)}) custom-call(s32[16]{0:T(128)S(1)} %bitcast.29, f32[2,16]{1,0:T(2,128)S(1)} %copy-done.3, s32[1]{0:T(128)S(6)} %copy.15.slot, s32[512]{0:T(512)S(1)} %pad_add_fusion.owner, f32[8,128,1024]{2,1,0:T(8,128)S(1)} %get-tuple-element.32.total, ...), custom_call_target="tpu_custom_call" | custom-call | flops 2147483648 | bytes 8388608 | tf_op jit(solution)/shard_map/diag_products/pallas_call | solution.py:504
  64.8 0.2 collective-permute-start.20
  65.0 30.0 %collective-permute-done.20.refs_0_ = bf16[4,72,1024]{2,1,0:T(8,128)(2,1)S(1)} collective-permute-done((bf16[4,72,1024]{2,1,0:T(8,128)(2,1)S(1)}, bf16[4,72,1024]{2,1,0:T(8,128)(2,1)S(1)}, u32[]{:S(2)}, u32[]{:S(2)}) %collective-permute-start.20) | collective-permute-done | bytes 589856 | tf_op jit(solution)/shard_map/ppermute | solution.py:525
  94.9 0.1 regroup.1
  95.1 1.0 collective-permute-start.21
  96.1 4.8 %collective-permute-start.22 = (bf16[72,1024]{1,0:T(8,128)(2,1)S(1)}, bf16[72,1024]{1,0:T(8,128)(2,1)S(1)}, u32[]{:S(2)}, u32[]{:S(2)}) collective-permute-start(bf16[72,1024]{1,0:T(8,128)(2,1)S(1)} %get-tuple-element.38), channel_id=1, source_target_pairs={{0,4},{2,6},{4,0},{6,2},{1,5},{3,7},{5,1},{7,3},{8,12},{10,14},{12... | collective-permute-start | bytes 442376 | tf_op jit(solution)/shard_map/ppermute | solution.py:538
  100.9 0.1 collective-permute-start.23
  101.0 3.1 %collective-permute-done.21.refs_0_ = bf16[72,1024]{1,0:T(8,128)(2,1)S(1)} collective-permute-done((bf16[72,1024]{1,0:T(8,128)(2,1)S(1)}, bf16[72,1024]{1,0:T(8,128)(2,1)S(1)}, u32[]{:S(2)}, u32[]{:S(2)}) %collective-permute-start.21) | collective-permute-done | bytes 147488 | tf_op jit(solution)/shard_map/ppermute | solution.py:538
  104.1 4.3 %collective-permute-done.22.refs_1_ = bf16[72,1024]{1,0:T(8,128)(2,1)S(1)} collective-permute-done((bf16[72,1024]{1,0:T(8,128)(2,1)S(1)}, bf16[72,1024]{1,0:T(8,128)(2,1)S(1)}, u32[]{:S(2)}, u32[]{:S(2)}) %collective-permute-start.22) | collective-permute-done | bytes 147488 | tf_op jit(solution)/shard_map/ppermute | solution.py:538
  108.5 1.4 %finish.1 = (f32[512,128]{1,0:T(8,128)}, f32[288,128]{1,0:T(8,128)S(1)}) custom-call(f32[2,16]{1,0:T(2,128)S(1)} %copy-done.3, s32[1]{0:T(128)S(6)} %copy.15.slot, f32[512,128]{1,0:T(8,128)S(1)} %bitcast.26, f32[72,1024]{1,0:T(8,128)S(1)} %get-tuple-element.36.own, bf16[72,1024]{1,0:T(8,128)(2,1)S(1)} %collective-permute-done.21.refs_0_, ...), custom_call_target="tpu_custom_call" | custom-call | tf_op jit(solution)/shard_map/finish/pallas_call | solution.py:541
  109.8 1.5 %collective-permute-start.25 = (f32[288,128]{1,0:T(8,128)S(1)}, f32[288,128]{1,0:T(8,128)S(1)}, u32[]{:S(2)}, u32[]{:S(2)}) collective-permute-start(f32[288,128]{1,0:T(8,128)S(1)} %get-tuple-element.41.refs_0_), channel_id=1, source_target_pairs={{0,16},{8,24},{16,0},{24,8},{1,17},{9,25},{17,1},{25,9},{2,18},{10... | collective-permute-start | bytes 442376 | tf_op jit(solution)/shard_map/ppermute | solution.py:555
  111.3 0.4 collective-permute-start.26
  111.7 4.9 %collective-permute-done.25.refs_2_ = f32[288,128]{1,0:T(8,128)S(1)} collective-permute-done((f32[288,128]{1,0:T(8,128)S(1)}, f32[288,128]{1,0:T(8,128)S(1)}, u32[]{:S(2)}, u32[]{:S(2)}) %collective-permute-start.25) | collective-permute-done | bytes 147488 | tf_op jit(solution)/shard_map/ppermute | solution.py:555
  116.6 2.2 %collective-permute-done.26.refs_3_ = f32[288,128]{1,0:T(8,128)S(1)} collective-permute-done((f32[288,128]{1,0:T(8,128)S(1)}, f32[288,128]{1,0:T(8,128)S(1)}, u32[]{:S(2)}, u32[]{:S(2)}) %collective-permute-start.26) | collective-permute-done | bytes 147488 | tf_op jit(solution)/shard_map/ppermute | solution.py:555
  118.8 0.7 density.1
  119.5 1.9 %join_columns.1 = f32[4096,128]{1,0:T(8,128)} custom-call(f32[4096,128]{1,0:T(8,128)S(1)} %get-tuple-element.28.keep, bf16[4096,128]{1,0:T(8,128)(2,1)S(1)} %collective-permute-done.18.refs_0_), custom_call_target="tpu_custom_call" | custom-call | tf_op jit(solution)/shard_map/join_columns/pallas_call | solution.py:586
  (34 shorter events, 0.2 us)
Async XLA Ops:
  1.7 11.7 %collective-permute-start = (bf16[128,1024]{1,0:T(8,128)(2,1)S(1)}, bf16[128,1024]{1,0:T(8,128)(2,1)S(1)}, u32[]{:S(2)}, u32[]{:S(2)}) collective-permute-start(bf16[128,1024]{1,0:T(8,128)(2,1)S(1)} %get-tuple-element.49.refs_0_), channel_id=1, source_target_pairs={{0,1},{1,0},{2,3},{3,2},{4,5},{5,4},{6,7},{7,6},{8,9},{9,8},{10,11... | collective-permute-start | bytes 786440 | tf_op jit(solution)/shard_map/ppermute | solution.py:71
  4.8 8.6 %collective-permute-start.6 = (bf16[128,1024]{1,0:T(8,128)(2,1)S(1)}, bf16[128,1024]{1,0:T(8,128)(2,1)S(1)}, u32[]{:S(2)}, u32[]{:S(2)}) collective-permute-start(bf16[128,1024]{1,0:T(8,128)(2,1)S(1)} %get-tuple-element.49.refs_0_), channel_id=1, source_target_pairs={{0,2},{2,0},{4,6},{6,4},{1,3},{3,1},{5,7},{7,5},{8,10},{10,8},{12,... | collective-permute-start | bytes 786440 | tf_op jit(solution)/shard_map/ppermute | solution.py:46
  6.3 8.2 %collective-permute-start.2 = (bf16[128,1024]{1,0:T(8,128)(2,1)S(1)}, bf16[128,1024]{1,0:T(8,128)(2,1)S(1)}, u32[]{:S(2)}, u32[]{:S(2)}) collective-permute-start(bf16[128,1024]{1,0:T(8,128)(2,1)S(1)} %get-tuple-element.49.refs_0_), channel_id=1, source_target_pairs={{2,4},{4,2},{3,5},{5,3},{10,12},{12,10},{11,13},{13,11},{18,20},{2... | collective-permute-start | bytes 786440 | tf_op jit(solution)/shard_map/ppermute | solution.py:47
  7.0 11.5 %collective-permute-start.4 = (bf16[128,1024]{1,0:T(8,128)(2,1)S(1)}, bf16[128,1024]{1,0:T(8,128)(2,1)S(1)}, u32[]{:S(2)}, u32[]{:S(2)}) collective-permute-start(bf16[128,1024]{1,0:T(8,128)(2,1)S(1)} %get-tuple-element.48.refs_1_), channel_id=1, source_target_pairs={{2,4},{4,2},{3,5},{5,3},{10,12},{12,10},{11,13},{13,11},{18,20},{2... | collective-permute-start | bytes 786440 | tf_op jit(solution)/shard_map/ppermute | solution.py:47
  7.7 16.5 %collective-permute-start.10 = (bf16[128,1024]{1,0:T(8,128)(2,1)S(1)}, bf16[128,1024]{1,0:T(8,128)(2,1)S(1)}, u32[]{:S(2)}, u32[]{:S(2)}) collective-permute-start(bf16[128,1024]{1,0:T(8,128)(2,1)S(1)} %get-tuple-element.48.refs_1_), channel_id=1, source_target_pairs={{0,2},{2,0},{4,6},{6,4},{1,3},{3,1},{5,7},{7,5},{8,10},{10,8},{12,... | collective-permute-start | bytes 786440 | tf_op jit(solution)/shard_map/ppermute | solution.py:46
  13.4 17.8 %collective-permute-start.7 = (bf16[128,1024]{1,0:T(8,128)(2,1)S(1)}, bf16[128,1024]{1,0:T(8,128)(2,1)S(1)}, u32[]{:S(2)}, u32[]{:S(2)}) collective-permute-start(bf16[128,1024]{1,0:T(8,128)(2,1)S(1)} %collective-permute-done.6.refs_4_), channel_id=1, source_target_pairs={{0,1},{1,0},{2,3},{3,2},{4,5},{5,4},{6,7},{7,6},{8,9},{9,8},{10,11... | collective-permute-start | bytes 786440 | tf_op jit(solution)/shard_map/ppermute | solution.py:71
  13.9 14.0 %collective-permute-start.14 = (bf16[128,1024]{1,0:T(8,128)(2,1)S(1)}, bf16[128,1024]{1,0:T(8,128)(2,1)S(1)}, u32[]{:S(2)}, u32[]{:S(2)}) collective-permute-start(bf16[128,1024]{1,0:T(8,128)(2,1)S(1)} %collective-permute-done.6.refs_4_), channel_id=1, source_target_pairs={{2,4},{4,2},{3,5},{5,3},{10,12},{12,10},{11,13},{13,11},{18,20},{2... | collective-permute-start | bytes 786440 | tf_op jit(solution)/shard_map/ppermute | solution.py:49
  14.6 12.7 %collective-permute-start.3 = (bf16[128,1024]{1,0:T(8,128)(2,1)S(1)}, bf16[128,1024]{1,0:T(8,128)(2,1)S(1)}, u32[]{:S(2)}, u32[]{:S(2)}) collective-permute-start(bf16[128,1024]{1,0:T(8,128)(2,1)S(1)} %collective-permute-done.2), channel_id=1, source_target_pairs={{0,2},{2,0},{4,6},{6,4},{1,3},{3,1},{5,7},{7,5},{8,10},{10,8},{12,... | collective-permute-start | bytes 786440 | tf_op jit(solution)/shard_map/ppermute | solution.py:48
  18.5 14.2 %collective-permute-start.5 = (bf16[128,1024]{1,0:T(8,128)(2,1)S(1)}, bf16[128,1024]{1,0:T(8,128)(2,1)S(1)}, u32[]{:S(2)}, u32[]{:S(2)}) collective-permute-start(bf16[128,1024]{1,0:T(8,128)(2,1)S(1)} %collective-permute-done.4), channel_id=1, source_target_pairs={{0,2},{2,0},{4,6},{6,4},{1,3},{3,1},{5,7},{7,5},{8,10},{10,8},{12,... | collective-permute-start | bytes 786440 | tf_op jit(solution)/shard_map/ppermute | solution.py:48
  24.2 9.1 %collective-permute-start.11 = (bf16[128,1024]{1,0:T(8,128)(2,1)S(1)}, bf16[128,1024]{1,0:T(8,128)(2,1)S(1)}, u32[]{:S(2)}, u32[]{:S(2)}) collective-permute-start(bf16[128,1024]{1,0:T(8,128)(2,1)S(1)} %collective-permute-done.10.refs_5_), channel_id=1, source_target_pairs={{2,4},{4,2},{3,5},{5,3},{10,12},{12,10},{11,13},{13,11},{18,20},{2... | collective-permute-start | bytes 786440 | tf_op jit(solution)/shard_map/ppermute | solution.py:49
  24.8 0.7 copy-start.4
  25.5 5.7 %copy-start.6 = (s32[256,1]{0,1:T(1,128)S(1)}, s32[256,1]{0,1:T(1,128)}, u32[]{:S(2)}) copy-start(s32[256,1]{0,1:T(1,128)} %param.11) | copy-start | bytes 3076
  27.3 9.0 %collective-permute-start.1 = (bf16[128,1024]{1,0:T(8,128)(2,1)S(1)}, bf16[128,1024]{1,0:T(8,128)(2,1)S(1)}, u32[]{:S(2)}, u32[]{:S(2)}) collective-permute-start(bf16[128,1024]{1,0:T(8,128)(2,1)S(1)} %get-tuple-element.48.refs_1_), channel_id=1, source_target_pairs={{0,1},{1,0},{2,3},{3,2},{4,5},{5,4},{6,7},{7,6},{8,9},{9,8},{10,11... | collective-permute-start | bytes 786440 | tf_op jit(solution)/shard_map/ppermute | solution.py:71
  27.9 10.0 %collective-permute-start.15 = (bf16[128,1024]{1,0:T(8,128)(2,1)S(1)}, bf16[128,1024]{1,0:T(8,128)(2,1)S(1)}, u32[]{:S(2)}, u32[]{:S(2)}) collective-permute-start(bf16[128,1024]{1,0:T(8,128)(2,1)S(1)} %collective-permute-done.14), channel_id=1, source_target_pairs={{0,2},{2,0},{4,6},{6,4},{1,3},{3,1},{5,7},{7,5},{8,10},{10,8},{12,... | collective-permute-start | bytes 786440 | tf_op jit(solution)/shard_map/ppermute | solution.py:50
  31.2 22.4 %collective-permute-start.19 = (s32[256]{0:T(256)S(1)}, s32[256]{0:T(256)S(1)}, u32[]{:S(2)}, u32[]{:S(2)}) collective-permute-start(s32[256]{0:T(256)S(1)} %bitcast.32), channel_id=1, source_target_pairs={{0,1},{1,0},{2,3},{3,2},{4,5},{5,4},{6,7},{7,6},{8,9},{9,8},{10,11... | collective-permute-start | bytes 3080 | tf_op jit(solution)/shard_map/ppermute | solution.py:432
  32.8 9.8 %collective-permute-start.8 = (bf16[128,1024]{1,0:T(8,128)(2,1)S(1)}, bf16[128,1024]{1,0:T(8,128)(2,1)S(1)}, u32[]{:S(2)}, u32[]{:S(2)}) collective-permute-start(bf16[128,1024]{1,0:T(8,128)(2,1)S(1)} %broadcast_select_fusion.3.refs_4_.refs_8_), channel_id=1, source_target_pairs={{0,1},{1,0},{2,3},{3,2},{4,5},{5,4},{6,7},{7,6},{8,9},{9,8},{10,11... | collective-permute-start | bytes 786440 | tf_op jit(solution)/shard_map/ppermute | solution.py:71
  33.3 8.0 %collective-permute-start.12 = (bf16[128,1024]{1,0:T(8,128)(2,1)S(1)}, bf16[128,1024]{1,0:T(8,128)(2,1)S(1)}, u32[]{:S(2)}, u32[]{:S(2)}) collective-permute-start(bf16[128,1024]{1,0:T(8,128)(2,1)S(1)} %collective-permute-done.11), channel_id=1, source_target_pairs={{0,2},{2,0},{4,6},{6,4},{1,3},{3,1},{5,7},{7,5},{8,10},{10,8},{12,... | collective-permute-start | bytes 786440 | tf_op jit(solution)/shard_map/ppermute | solution.py:50
  36.3 11.3 %collective-permute-start.9 = (bf16[128,1024]{1,0:T(8,128)(2,1)S(1)}, bf16[128,1024]{1,0:T(8,128)(2,1)S(1)}, u32[]{:S(2)}, u32[]{:S(2)}) collective-permute-start(bf16[128,1024]{1,0:T(8,128)(2,1)S(1)} %broadcast_select_fusion.2.refs_5_.refs_9_), channel_id=1, source_target_pairs={{0,1},{1,0},{2,3},{3,2},{4,5},{5,4},{6,7},{7,6},{8,9},{9,8},{10,11... | collective-permute-start | bytes 786440 | tf_op jit(solution)/shard_map/ppermute | solution.py:71
  37.9 15.8 %collective-permute-start.16 = (bf16[128,1024]{1,0:T(8,128)(2,1)S(1)}, bf16[128,1024]{1,0:T(8,128)(2,1)S(1)}, u32[]{:S(2)}, u32[]{:S(2)}) collective-permute-start(bf16[128,1024]{1,0:T(8,128)(2,1)S(1)} %broadcast_select_fusion.1.refs_12_), channel_id=1, source_target_pairs={{0,1},{1,0},{2,3},{3,2},{4,5},{5,4},{6,7},{7,6},{8,9},{9,8},{10,11... | collective-permute-start | bytes 786440 | tf_op jit(solution)/shard_map/ppermute | solution.py:71
  41.4 14.9 %collective-permute-start.17 = (bf16[128,1024]{1,0:T(8,128)(2,1)S(1)}, bf16[128,1024]{1,0:T(8,128)(2,1)S(1)}, u32[]{:S(2)}, u32[]{:S(2)}) collective-permute-start(bf16[128,1024]{1,0:T(8,128)(2,1)S(1)} %broadcast_select_fusion.refs_13_), channel_id=1, source_target_pairs={{0,1},{1,0},{2,3},{3,2},{4,5},{5,4},{6,7},{7,6},{8,9},{9,8},{10,11... | collective-permute-start | bytes 786440 | tf_op jit(solution)/shard_map/ppermute | solution.py:71
  42.6 13.7 %collective-permute-start.13 = (bf16[128,1024]{1,0:T(8,128)(2,1)S(1)}, bf16[128,1024]{1,0:T(8,128)(2,1)S(1)}, u32[]{:S(2)}, u32[]{:S(2)}) collective-permute-start(bf16[128,1024]{1,0:T(8,128)(2,1)S(1)} %collective-permute-done.1.refs_3_), channel_id=1, source_target_pairs={{0,2},{2,0},{4,6},{6,4},{1,3},{3,1},{5,7},{7,5},{8,10},{10,8},{12,... | collective-permute-start | bytes 786440 | tf_op jit(solution)/shard_map/ppermute | solution.py:68
  47.6 3.4 %copy-start = (bf16[1,2,1024,2048]{3,2,1,0:T(8,128)(2,1)S(1)}, bf16[1,2,1024,2048]{3,2,1,0:T(8,128)(2,1)}, u32[]{:S(2)}) copy-start(bf16[1,2,1024,2048]{3,2,1,0:T(8,128)(2,1)} %param.7) | copy-start | bytes 25165828
  51.0 5.3 %copy-start.1 = (bf16[1,2,1024,2048]{3,2,1,0:T(8,128)(2,1)S(1)}, bf16[1,2,1024,2048]{3,2,1,0:T(8,128)(2,1)}, u32[]{:S(2)}) copy-start(bf16[1,2,1024,2048]{3,2,1,0:T(8,128)(2,1)} %param.7) | copy-start | bytes 25165828
  51.0 5.3 %copy-start.5 = (s32[1,16]{1,0:T(1,128)S(1)}, s32[1,16]{1,0:T(1,128)}, u32[]{:S(2)}) copy-start(s32[1,16]{1,0:T(1,128)} %param.10) | copy-start | bytes 196
  53.7 8.0 %copy-start.3 = (f32[2,16]{1,0:T(2,128)S(1)}, f32[2,16]{1,0:T(2,128)}, u32[]{:S(2)}) copy-start(f32[2,16]{1,0:T(2,128)} %table.3) | copy-start | bytes 388
  59.7 59.8 %collective-permute-start.18 = (bf16[4096,128]{1,0:T(8,128)(2,1)S(1)}, bf16[4096,128]{1,0:T(8,128)(2,1)S(1)}, u32[]{:S(2)}, u32[]{:S(2)}) collective-permute-start(bf16[4096,128]{1,0:T(8,128)(2,1)S(1)} %get-tuple-element.29), channel_id=1, source_target_pairs={{0,1},{1,0},{2,3},{3,2},{4,5},{5,4},{6,7},{7,6},{8,9},{9,8},{10,11... | collective-permute-start | bytes 3145736 | tf_op jit(solution)/shard_map/ppermute | solution.py:574
  61.7 46.8 %copy-start.2 = (f32[64,1,1,2,512]{4,3,2,1,0:T(2,128)S(1)}, f32[64,1,1,2,512]{4,3,2,1,0:T(2,128)}, u32[]{:S(2)}) copy-start(f32[64,1,1,2,512]{4,3,2,1,0:T(2,128)} %param.9) | copy-start | bytes 786436
  64.8 30.1 %collective-permute-start.20 = (bf16[4,72,1024]{2,1,0:T(8,128)(2,1)S(1)}, bf16[4,72,1024]{2,1,0:T(8,128)(2,1)S(1)}, u32[]{:S(2)}, u32[]{:S(2)}) collective-permute-start(bf16[4,72,1024]{2,1,0:T(8,128)(2,1)S(1)} %bitcast.30), channel_id=1, source_target_pairs={{0,1},{1,0},{2,3},{3,2},{4,5},{5,4},{6,7},{7,6},{8,9},{9,8},{10,11... | collective-permute-start | bytes 1769480 | tf_op jit(solution)/shard_map/ppermute | solution.py:525
  95.1 9.1 %collective-permute-start.21 = (bf16[72,1024]{1,0:T(8,128)(2,1)S(1)}, bf16[72,1024]{1,0:T(8,128)(2,1)S(1)}, u32[]{:S(2)}, u32[]{:S(2)}) collective-permute-start(bf16[72,1024]{1,0:T(8,128)(2,1)S(1)} %get-tuple-element.37), channel_id=1, source_target_pairs={{0,2},{2,4},{4,6},{6,0},{1,3},{3,5},{5,7},{7,1},{8,10},{10,12},{12... | collective-permute-start | bytes 442376 | tf_op jit(solution)/shard_map/ppermute | solution.py:538
  96.1 12.3 %collective-permute-start.22 = (bf16[72,1024]{1,0:T(8,128)(2,1)S(1)}, bf16[72,1024]{1,0:T(8,128)(2,1)S(1)}, u32[]{:S(2)}, u32[]{:S(2)}) collective-permute-start(bf16[72,1024]{1,0:T(8,128)(2,1)S(1)} %get-tuple-element.38), channel_id=1, source_target_pairs={{0,4},{2,6},{4,0},{6,2},{1,5},{3,7},{5,1},{7,3},{8,12},{10,14},{12... | collective-permute-start | bytes 442376 | tf_op jit(solution)/shard_map/ppermute | solution.py:538
  100.9 7.6 %collective-permute-start.23 = (bf16[72,1024]{1,0:T(8,128)(2,1)S(1)}, bf16[72,1024]{1,0:T(8,128)(2,1)S(1)}, u32[]{:S(2)}, u32[]{:S(2)}) collective-permute-start(bf16[72,1024]{1,0:T(8,128)(2,1)S(1)} %get-tuple-element.39), channel_id=1, source_target_pairs={{0,6},{2,0},{4,2},{6,4},{1,7},{3,1},{5,3},{7,5},{8,14},{10,8},{12,... | collective-permute-start | bytes 442376 | tf_op jit(solution)/shard_map/ppermute | solution.py:538
  109.8 1.9 %collective-permute-start.24 = (f32[288,128]{1,0:T(8,128)S(1)}, f32[288,128]{1,0:T(8,128)S(1)}, u32[]{:S(2)}, u32[]{:S(2)}) collective-permute-start(f32[288,128]{1,0:T(8,128)S(1)} %get-tuple-element.41.refs_0_), channel_id=1, source_target_pairs={{0,8},{8,0},{16,24},{24,16},{1,9},{9,1},{17,25},{25,17},{2,10},{10... | collective-permute-start | bytes 442376 | tf_op jit(solution)/shard_map/ppermute | solution.py:555
  109.8 6.7 %collective-permute-start.25 = (f32[288,128]{1,0:T(8,128)S(1)}, f32[288,128]{1,0:T(8,128)S(1)}, u32[]{:S(2)}, u32[]{:S(2)}) collective-permute-start(f32[288,128]{1,0:T(8,128)S(1)} %get-tuple-element.41.refs_0_), channel_id=1, source_target_pairs={{0,16},{8,24},{16,0},{24,8},{1,17},{9,25},{17,1},{25,9},{2,18},{10... | collective-permute-start | bytes 442376 | tf_op jit(solution)/shard_map/ppermute | solution.py:555
  111.3 7.5 %collective-permute-start.26 = (f32[288,128]{1,0:T(8,128)S(1)}, f32[288,128]{1,0:T(8,128)S(1)}, u32[]{:S(2)}, u32[]{:S(2)}) collective-permute-start(f32[288,128]{1,0:T(8,128)S(1)} %get-tuple-element.41.refs_0_), channel_id=1, source_target_pairs={{0,24},{8,16},{16,8},{24,0},{1,25},{9,17},{17,9},{25,1},{2,26},{10... | collective-permute-start | bytes 442376 | tf_op jit(solution)/shard_map/ppermute | solution.py:555

commit v6 on v5

--- a/solution.py
+++ b/solution.py
@@ -43,11 +43,15 @@
     stages = [[[] for _ in range(cols)] for _ in range(rows)]
     for part in (0, 1):
         own = shard[part * height : (part + 1) * height]
-        near = lax.ppermute(own, "row", outer)
-        cross = lax.ppermute(own, "row", inner)
-        cross_out = lax.ppermute(cross, "row", outer)
-        far = lax.ppermute(near, "row", inner)
-        far_out = lax.ppermute(far, "row", outer)
+
+        def hop(value, pairs):
+            return lax.ppermute(value, "row", pairs)
+
+        near = hop(own, outer)
+        cross = hop(own, inner)
+        cross_out = hop(cross, outer)
+        far = hop(near, inner)
+        far_out = hop(far, outer)
         line = [
             lambda: own,
             lambda: near,
@@ -186,9 +190,9 @@
 
 
 def early_kernel(sources, stages, added, rows, cols, ancestors, inverse, *refs):
-    early, full, acc = refs[-3:]
+    early, turned, full, acc = refs[-4:]
     before = refs[0] if added else None
-    pieces = refs[1 if added else 0 : -3]
+    pieces = refs[1 if added else 0 : -4]
     each = len(pieces) // len(stages)
     half = acc.shape[1] // 2
     for n, stage in enumerate(stages):
@@ -200,24 +204,65 @@
         early[i, :, half:] = imag
 
     add_products(sources, stages, ancestors, inverse, before, full, acc, counts, store)
+    turn_blocks(sources, stages, ancestors, full, counts, turned)
+
+
+def brought(sources, stages, rows, selected, block):
+    stage_blocks = selected // rows
+    found = False
+    for stage in stages:
+        low = source_row(sources, stage) * stage_blocks
+        found = jnp.logical_or(found, jnp.logical_and(block >= low, block < low + stage_blocks))
+    return found
+
+
+def turn_blocks(sources, stages, ancestors, full, counts, turned):
+    half = full.shape[1] // 2
+    rows, row_first, row_count = counts[0], counts[4], counts[5]
+
+    @pl.loop(0, row_count)
+    def _(i):
+        block = row_first + i
+
+        @pl.when(brought(sources, stages, rows, ancestors.shape[0], block))
+        def _():
+            rows_of = full[pl.ds(pl.multiple_of(block * BS, BS), BS), :]
+            left = jnp.concatenate([rows_of[:, :half], rows_of[:, half:]], axis=0)
+            turned[i] = left.T
 
 
 def last_kernel(sources, stages, rows, cols, ancestors, inverse, early, *refs):
     keep, *sends, total, turned, full, acc, leaving = refs[-(6 + len(SPLIT)) :]
     pieces = refs[: -(6 + len(SPLIT))]
-    each = len(pieces) // rows
+    each = len(pieces) // len(stages)
     half = acc.shape[1] // 2
     across = half // BC
     row_blocks = early.shape[0]
     own_blocks = row_blocks // cols
     r = lax.axis_index("row")
     c = lax.axis_index("col")
-    for stage in range(rows):
-        fill(full, pieces[stage * each : (stage + 1) * each], sources, stage, cols)
+    for n, stage in enumerate(stages):
+        fill(full, pieces[n * each : (n + 1) * each], sources, stage, cols)
     counts = counts_of(ancestors, inverse, rows, cols)
     row_first = counts[4]
-    keep[...] = jnp.zeros_like(keep)
-    leaving[...] = jnp.zeros_like(leaving)
+    size = BS * 2 * across
+
+    for n in range(row_blocks):
+        listed = False
+        for k in range(ancestors.shape[0]):
+            listed = jnp.logical_or(listed, ancestors[k] == r * row_blocks + n)
+        turn = lax.rem(n // own_blocks - c + cols, cols)
+        within = n % own_blocks * size
+
+        @pl.when(jnp.logical_and(jnp.logical_not(listed), turn == 0))
+        def _():
+            keep[within : within + size, :] = jnp.zeros((size, BC), jnp.float32)
+
+        @pl.when(jnp.logical_and(jnp.logical_not(listed), turn > 0))
+        def _():
+            start = pl.multiple_of((turn - 1) * keep.shape[0] + within, size)
+            leaving[pl.ds(start, size), :] = jnp.zeros((size, BC), jnp.float32)
+
 
     def store(i, real, imag):
         total[i, :, :half] = real
@@ -240,11 +285,8 @@
         def _():
             lay(leaving, (turn - 1) * keep.shape[0] + within)
 
-        rows_of = full[pl.ds(pl.multiple_of((row_first + i) * BS, BS), BS), :]
-        left = jnp.concatenate([rows_of[:, :half], rows_of[:, half:]], axis=0)
-        turned[i] = left.T
-
     add_products(sources, stages, ancestors, inverse, early, full, acc, counts, store)
+    turn_blocks(sources, stages, ancestors, full, counts, turned)
     height = keep.shape[0]
     for step in range(cols - 1):
         first = 0
@@ -255,8 +297,10 @@
             first += size
 
 
-def diag_kernel(poles, rows, cols, row_blocks, ancestors, table, slot, owner, total, turned, *refs):
-    diag_keep, diag_send, diag, tiles = refs
+def diag_kernel(
+    sources, first_stages, poles, rows, cols, row_blocks, ancestors, table, slot, owner, *refs
+):
+    total, first_turned, turned, diag_keep, diag_send, diag, tiles = refs
     half, wide = diag.shape
     across = half // BC
     own_blocks = row_blocks // cols
@@ -275,38 +319,60 @@
     weight_real = table[0, slot[0]]
     weight_imag = table[1, slot[0]]
 
-    @pl.loop(0, below((r + 1) * row_blocks) - row_first)
-    def _(i):
+    row_count = below((r + 1) * row_blocks) - row_first
+
+    def operands(i):
         real = total[i, :, :half]
         imag = total[i, :, half:]
+        first = brought(sources, first_stages, rows, ancestors.shape[0], row_first + i)
+
+        @pl.when(first)
+        def _():
+            turned[i] = first_turned[i]
+
         left = turned[i]
         real_high = real.astype(jnp.bfloat16)
         imag_high = imag.astype(jnp.bfloat16)
         real_low = (real - real_high.astype(jnp.float32)).astype(jnp.bfloat16)
         imag_low = (imag - imag_high.astype(jnp.float32)).astype(jnp.bfloat16)
-        right = jnp.concatenate(
-            [
-                jnp.concatenate([real_high, imag_high], axis=1),
-                jnp.concatenate([-imag_high, real_high], axis=1),
-                jnp.concatenate([real_low, imag_low], axis=1),
-                jnp.concatenate([-imag_low, real_low], axis=1),
-            ],
-            axis=0,
-        )
-        diag[...] += jnp.dot(
-            jnp.concatenate([left, left], axis=1), right, preferred_element_type=jnp.float32
-        )
+        right = [
+            jnp.concatenate([real_high, imag_high], axis=1),
+            jnp.concatenate([-imag_high, real_high], axis=1),
+            jnp.concatenate([real_low, imag_low], axis=1),
+            jnp.concatenate([-imag_low, real_low], axis=1),
+        ]
         block = ancestors[row_first + i] - r * row_blocks
         place = block // own_blocks
         mixed = -(weight_real * imag + weight_imag * real)
         per_device = own_blocks * (BS // BR) * across
-        first = lax.rem(c - place + cols, cols) * per_device + lax.rem(block, own_blocks) * (
+        start = lax.rem(c - place + cols, cols) * per_device + lax.rem(block, own_blocks) * (
             BS // BR
         ) * across
         for group in range(BS // BR):
             for j in range(across):
-                tile = owner[first + group * across + j]
+                tile = owner[start + group * across + j]
                 tiles[j, tile] += mixed[group * BR : (group + 1) * BR, j * BC : (j + 1) * BC]
+        return [left, left], right
+
+    def add(blocks):
+        left, right = [], []
+        for i in blocks:
+            more_left, more_right = operands(i)
+            left += more_left
+            right += more_right
+        diag[...] += jnp.dot(
+            jnp.concatenate(left, axis=1),
+            jnp.concatenate(right, axis=0),
+            preferred_element_type=jnp.float32,
+        )
+
+    @pl.loop(0, row_count // 2)
+    def _(pair):
+        add([2 * pair, 2 * pair + 1])
+
+    @pl.when(lax.rem(row_count, 2) == 1)
+    def _():
+        add([row_count - 1])
 
     part = half // (rows * cols)
     for row in range(rows):
@@ -459,31 +525,27 @@
         in_specs=[smem],
         out_specs=smem,
         compiler_params=pltpu.CompilerParams(vmem_limit_bytes=MIB),
-        cost_estimate=pl.CostEstimate(flops=products, bytes_accessed=8 * MIB, transcendentals=0),
+        cost_estimate=pl.CostEstimate(
+            flops=products // 3, bytes_accessed=0, transcendentals=0
+        ),
         name="list_blocks",
     )(ancestors[0])
-    early = []
-    for group in groups:
-        group_pieces = [piece for stage in group for piece in stages[stage]]
-        early = [
-            pl.pallas_call(
-                functools.partial(early_kernel, sources, group, bool(early), rows, cols),
-                out_shape=row_products,
-                in_specs=[smem, vmem] + [vmem] * (len(early) + len(group_pieces)),
-                out_specs=vmem,
-                scratch_shapes=scratch,
-                input_output_aliases={2: 0} if early else {},
-                compiler_params=pltpu.CompilerParams(vmem_limit_bytes=24 * MIB),
-                cost_estimate=pl.CostEstimate(
-                    flops=products * len(group) // rows,
-                    bytes_accessed=4 * MIB,
-                    transcendentals=0,
-                ),
-                name="early_products",
-            )(listing, here, *early, *group_pieces)
-        ]
+    turned_blocks = jax.ShapeDtypeStruct((row_blocks, half, 2 * BS), jnp.bfloat16)
+    early_pieces = [piece for stage in groups[0] for piece in stages[stage]]
+    early, first_turned = pl.pallas_call(
+        functools.partial(early_kernel, sources, groups[0], False, rows, cols),
+        out_shape=(row_products, turned_blocks),
+        in_specs=[smem, vmem] + [vmem] * len(early_pieces),
+        out_specs=(vmem,) * 2,
+        scratch_shapes=scratch,
+        compiler_params=pltpu.CompilerParams(vmem_limit_bytes=24 * MIB),
+        cost_estimate=pl.CostEstimate(
+            flops=products // 2, bytes_accessed=4 * MIB, transcendentals=0
+        ),
+        name="early_products",
+    )(listing, here, *early_pieces)
     late_owners, _ = lax.optimization_barrier((tuple(owners), early))
-    all_pieces = [piece for stage in stages for piece in stage]
+    all_pieces = [piece for stage in last for piece in stages[stage]]
     others = max(1, cols - 1)
     laid_rows = rows_here * wide // BC
     sizes = [laid_rows * share // sum(SPLIT) for share in SPLIT]
@@ -491,7 +553,7 @@
         functools.partial(last_kernel, sources, last, rows, cols),
         out_shape=(jax.ShapeDtypeStruct((laid_rows, BC), jnp.float32),)
         + tuple(jax.ShapeDtypeStruct((others * size, BC), jnp.bfloat16) for size in sizes)
-        + (row_products, jax.ShapeDtypeStruct((row_blocks, half, 2 * BS), jnp.bfloat16)),
+        + (row_products, turned_blocks),
         in_specs=[smem] + [vmem] * (2 + len(all_pieces)),
         out_specs=(vmem,) * (3 + len(SPLIT)),
         scratch_shapes=scratch + [pltpu.VMEM((others * laid_rows, BC), jnp.float32)],
@@ -500,14 +562,14 @@
             flops=products // 2, bytes_accessed=8 * MIB, transcendentals=0
         ),
         name="last_products",
-    )(ancestors[0], here, *early, *all_pieces)
+    )(ancestors[0], here, early, *all_pieces)
     diag_keep, diag_send = pl.pallas_call(
-        functools.partial(diag_kernel, poles, rows, cols, row_blocks),
+        functools.partial(diag_kernel, sources, groups[0], poles, rows, cols, row_blocks),
         out_shape=(
             jax.ShapeDtypeStruct((rows, part + BR, wide), jnp.float32),
             jax.ShapeDtypeStruct((others, rows, part + BR, wide), jnp.bfloat16),
         ),
-        in_specs=[smem] * 4 + [vmem] * 2,
+        in_specs=[smem] * 4 + [vmem] * 3,
         out_specs=(vmem,) * 2,
         scratch_shapes=[
             pltpu.VMEM((half, wide), jnp.float32),
@@ -518,7 +580,7 @@
             flops=products // 2, bytes_accessed=8 * MIB, transcendentals=0
         ),
         name="diag_products",
-    )(ancestors[0], weight_table, pole_slot, jnp.concatenate(late_owners), total, turned)
+    )(ancestors[0], weight_table, pole_slot, jnp.concatenate(late_owners), total, first_turned, turned)
 
     everyone_pairs = [shift_pairs(rows, cols, step, everyone) for step in range(cols)]
     arrived = [

time: 122 us -> 124 us (1.016)
  local copies, waits for them, and re-layouts: 5.12 us -> 8.5 us
  starting transfers between devices: 46.2 us -> 44.1 us
    ppermute x10, waiting for transfers between devices: 2.45 us -> 7.91 us  [hop(): return lax.ppermute(value, 'row', pairs)]
    ppermute x7, waiting for transfers between devices: 7.02 us -> 3.29 us  [gather_stages(): last = lax.ppermute(leaving, grid, pairs)]
    unnamed x14, local copies, waits for them, and re-layouts: 4.05 us -> 7.43 us
    ppermute x10, starting transfers between devices: 23.4 us -> 21.2 us  [hop(): return lax.ppermute(value, 'row', pairs)]
    ppermute x7, starting transfers between devices: 8.37 us -> 9.98 us  [gather_stages(): last = lax.ppermute(leaving, grid, pairs)]
  transfers between devices with their start and end apart: 27 -> 27, of which waited for: 10 -> 11; matrix products, arithmetic and copies ran while one was open for 0% -> 0% of each run, Pallas kernels for 8% -> 8%
where the time goes in v6:
time: 124 us; the launch traced here: 123 us
  waiting for transfers between devices  54.4 us (44%)
  starting transfers between devices  44.1 us (36%)
  Pallas kernels  14.8 us (12%)
  local copies, waits for them, and re-layouts  8.5 us (7%)
  between operations  1.47 us (1%)
    ppermute x1, waiting for transfers between devices, compute(): lax.ppermute(diag_send[step - 1], grid, everyone_pairs[step])  29.7 us
    ppermute x10, starting transfers between devices, hop(): return lax.ppermute(value, 'row', pairs)  21.2 us
    ppermute x7, starting transfers between devices, gather_stages(): last = lax.ppermute(leaving, grid, pairs)  9.98 us
    ppermute x10, waiting for transfers between devices, hop(): return lax.ppermute(value, 'row', pairs)  7.91 us
    unnamed x14, local copies, waits for them, and re-layouts  7.43 us
    ppermute x3, waiting for transfers between devices, compute(): lax.ppermute(message, 'pole', [(i, i ^ step) for i in range(poles)])  7.09 us
    ppermute x3, waiting for transfers between devices, compute(): lax.ppermute(rounded[step - 1], 'row', [(i, (i + step) % rows) for i in r...  6.42 us
    ppermute x3, starting transfers between devices, compute(): lax.ppermute(rounded[step - 1], 'row', [(i, (i + step) % rows) for i in r...  5.6 us
  transfers between devices with their start and end apart: 27, of which 11 were waited for; matrix products, arithmetic and copies ran while one was open for 0% of the time, Pallas kernels for 8%

profile of v6, /device:TPU:0, one launch (start us, length us, event | category | flops | bytes accessed | tf_op | source)
XLA Modules:
  0.0 123.3 jit_solution(17163758822940476177)
XLA Ops:
  0.6 1.1 slice_bitcast_fusion
  1.7 0.7 collective-permute-start.2
  2.4 5.9 %collective-permute-start.6 = (bf16[128,1024]{1,0:T(8,128)(2,1)S(1)}, bf16[128,1024]{1,0:T(8,128)(2,1)S(1)}, u32[]{:S(2)}, u32[]{:S(2)}) collective-permute-start(bf16[128,1024]{1,0:T(8,128)(2,1)S(1)} %get-tuple-element.53.refs_0_), channel_id=1, source_target_pairs={{0,2},{2,0},{4,6},{6,4},{1,3},{3,1},{5,7},{7,5},{8,10},{10,8},{12,... | collective-permute-start | bytes 786440 | tf_op jit(solution)/shard_map/ppermute | solution.py:48
  8.3 1.5 %collective-permute-start = (bf16[128,1024]{1,0:T(8,128)(2,1)S(1)}, bf16[128,1024]{1,0:T(8,128)(2,1)S(1)}, u32[]{:S(2)}, u32[]{:S(2)}) collective-permute-start(bf16[128,1024]{1,0:T(8,128)(2,1)S(1)} %get-tuple-element.53.refs_0_), channel_id=1, source_target_pairs={{0,1},{1,0},{2,3},{3,2},{4,5},{5,4},{6,7},{7,6},{8,9},{9,8},{10,11... | collective-permute-start | bytes 786440 | tf_op jit(solution)/shard_map/ppermute | solution.py:75
  9.8 0.7 collective-permute-start.4
  10.5 1.8 %collective-permute-start.10 = (bf16[128,1024]{1,0:T(8,128)(2,1)S(1)}, bf16[128,1024]{1,0:T(8,128)(2,1)S(1)}, u32[]{:S(2)}, u32[]{:S(2)}) collective-permute-start(bf16[128,1024]{1,0:T(8,128)(2,1)S(1)} %get-tuple-element.52.refs_1_), channel_id=1, source_target_pairs={{0,2},{2,0},{4,6},{6,4},{1,3},{3,1},{5,7},{7,5},{8,10},{10,8},{12,... | collective-permute-start | bytes 786440 | tf_op jit(solution)/shard_map/ppermute | solution.py:48
  12.3 3.4 %collective-permute-start.3 = (bf16[128,1024]{1,0:T(8,128)(2,1)S(1)}, bf16[128,1024]{1,0:T(8,128)(2,1)S(1)}, u32[]{:S(2)}, u32[]{:S(2)}) collective-permute-start(bf16[128,1024]{1,0:T(8,128)(2,1)S(1)} %collective-permute-done.2), channel_id=1, source_target_pairs={{0,2},{2,0},{4,6},{6,4},{1,3},{3,1},{5,7},{7,5},{8,10},{10,8},{12,... | collective-permute-start | bytes 786440 | tf_op jit(solution)/shard_map/ppermute | solution.py:48
  15.7 0.7 collective-permute-start.14
  16.4 1.7 %collective-permute-start.7 = (bf16[128,1024]{1,0:T(8,128)(2,1)S(1)}, bf16[128,1024]{1,0:T(8,128)(2,1)S(1)}, u32[]{:S(2)}, u32[]{:S(2)}) collective-permute-start(bf16[128,1024]{1,0:T(8,128)(2,1)S(1)} %collective-permute-done.6.refs_0_), channel_id=1, source_target_pairs={{0,1},{1,0},{2,3},{3,2},{4,5},{5,4},{6,7},{7,6},{8,9},{9,8},{10,11... | collective-permute-start | bytes 786440 | tf_op jit(solution)/shard_map/ppermute | solution.py:75
  18.1 3.3 %collective-permute-start.5 = (bf16[128,1024]{1,0:T(8,128)(2,1)S(1)}, bf16[128,1024]{1,0:T(8,128)(2,1)S(1)}, u32[]{:S(2)}, u32[]{:S(2)}) collective-permute-start(bf16[128,1024]{1,0:T(8,128)(2,1)S(1)} %collective-permute-done.4), channel_id=1, source_target_pairs={{0,2},{2,0},{4,6},{6,4},{1,3},{3,1},{5,7},{7,5},{8,10},{10,8},{12,... | collective-permute-start | bytes 786440 | tf_op jit(solution)/shard_map/ppermute | solution.py:48
  21.4 0.7 collective-permute-start.11
  22.1 0.6 copy-done.4
  22.8 1.1 list_blocks.1.ancestors
  24.6 2.1 %collective-permute-done.3 = bf16[128,1024]{1,0:T(8,128)(2,1)S(1)} collective-permute-done((bf16[128,1024]{1,0:T(8,128)(2,1)S(1)}, bf16[128,1024]{1,0:T(8,128)(2,1)S(1)}, u32[]{:S(2)}, u32[]{:S(2)}) %collective-permute-start.3) | collective-permute-done | bytes 262176 | tf_op jit(solution)/shard_map/ppermute | solution.py:48
  26.7 1.5 %collective-permute-start.1 = (bf16[128,1024]{1,0:T(8,128)(2,1)S(1)}, bf16[128,1024]{1,0:T(8,128)(2,1)S(1)}, u32[]{:S(2)}, u32[]{:S(2)}) collective-permute-start(bf16[128,1024]{1,0:T(8,128)(2,1)S(1)} %get-tuple-element.52.refs_1_), channel_id=1, source_target_pairs={{0,1},{1,0},{2,3},{3,2},{4,5},{5,4},{6,7},{7,6},{8,9},{9,8},{10,11... | collective-permute-start | bytes 786440 | tf_op jit(solution)/shard_map/ppermute | solution.py:75
  28.2 2.0 %collective-permute-start.15 = (bf16[128,1024]{1,0:T(8,128)(2,1)S(1)}, bf16[128,1024]{1,0:T(8,128)(2,1)S(1)}, u32[]{:S(2)}, u32[]{:S(2)}) collective-permute-start(bf16[128,1024]{1,0:T(8,128)(2,1)S(1)} %collective-permute-done.14), channel_id=1, source_target_pairs={{0,2},{2,0},{4,6},{6,4},{1,3},{3,1},{5,7},{7,5},{8,10},{10,8},{12,... | collective-permute-start | bytes 786440 | tf_op jit(solution)/shard_map/ppermute | solution.py:48
  30.3 0.6 collective-permute-start.19
  30.9 1.4 %collective-permute-done.5 = bf16[128,1024]{1,0:T(8,128)(2,1)S(1)} collective-permute-done((bf16[128,1024]{1,0:T(8,128)(2,1)S(1)}, bf16[128,1024]{1,0:T(8,128)(2,1)S(1)}, u32[]{:S(2)}, u32[]{:S(2)}) %collective-permute-start.5) | collective-permute-done | bytes 262176 | tf_op jit(solution)/shard_map/ppermute | solution.py:48
  32.3 1.5 %collective-permute-start.8 = (bf16[128,1024]{1,0:T(8,128)(2,1)S(1)}, bf16[128,1024]{1,0:T(8,128)(2,1)S(1)}, u32[]{:S(2)}, u32[]{:S(2)}) collective-permute-start(bf16[128,1024]{1,0:T(8,128)(2,1)S(1)} %broadcast_select_fusion.3.refs_4_), channel_id=1, source_target_pairs={{0,1},{1,0},{2,3},{3,2},{4,5},{5,4},{6,7},{7,6},{8,9},{9,8},{10,11... | collective-permute-start | bytes 786440 | tf_op jit(solution)/shard_map/ppermute | solution.py:75
  33.8 2.0 %collective-permute-start.12 = (bf16[128,1024]{1,0:T(8,128)(2,1)S(1)}, bf16[128,1024]{1,0:T(8,128)(2,1)S(1)}, u32[]{:S(2)}, u32[]{:S(2)}) collective-permute-start(bf16[128,1024]{1,0:T(8,128)(2,1)S(1)} %collective-permute-done.11), channel_id=1, source_target_pairs={{0,2},{2,0},{4,6},{6,4},{1,3},{3,1},{5,7},{7,5},{8,10},{10,8},{12,... | collective-permute-start | bytes 786440 | tf_op jit(solution)/shard_map/ppermute | solution.py:48
  35.9 0.6 collective-permute-start.9
  36.5 1.5 %collective-permute-done.15 = bf16[128,1024]{1,0:T(8,128)(2,1)S(1)} collective-permute-done((bf16[128,1024]{1,0:T(8,128)(2,1)S(1)}, bf16[128,1024]{1,0:T(8,128)(2,1)S(1)}, u32[]{:S(2)}, u32[]{:S(2)}) %collective-permute-start.15) | collective-permute-done | bytes 262176 | tf_op jit(solution)/shard_map/ppermute | solution.py:48
  38.0 1.6 %collective-permute-start.16 = (bf16[128,1024]{1,0:T(8,128)(2,1)S(1)}, bf16[128,1024]{1,0:T(8,128)(2,1)S(1)}, u32[]{:S(2)}, u32[]{:S(2)}) collective-permute-start(bf16[128,1024]{1,0:T(8,128)(2,1)S(1)} %broadcast_select_fusion.1.refs_4_), channel_id=1, source_target_pairs={{0,1},{1,0},{2,3},{3,2},{4,5},{5,4},{6,7},{7,6},{8,9},{9,8},{10,11... | collective-permute-start | bytes 786440 | tf_op jit(solution)/shard_map/ppermute | solution.py:75
  39.6 2.9 %collective-permute-done.12 = bf16[128,1024]{1,0:T(8,128)(2,1)S(1)} collective-permute-done((bf16[128,1024]{1,0:T(8,128)(2,1)S(1)}, bf16[128,1024]{1,0:T(8,128)(2,1)S(1)}, u32[]{:S(2)}, u32[]{:S(2)}) %collective-permute-start.12) | collective-permute-done | bytes 262176 | tf_op jit(solution)/shard_map/ppermute | solution.py:48
  42.5 1.6 %collective-permute-start.17 = (bf16[128,1024]{1,0:T(8,128)(2,1)S(1)}, bf16[128,1024]{1,0:T(8,128)(2,1)S(1)}, u32[]{:S(2)}, u32[]{:S(2)}) collective-permute-start(bf16[128,1024]{1,0:T(8,128)(2,1)S(1)} %broadcast_select_fusion.refs_5_), channel_id=1, source_target_pairs={{0,1},{1,0},{2,3},{3,2},{4,5},{5,4},{6,7},{7,6},{8,9},{9,8},{10,11... | collective-permute-start | bytes 786440 | tf_op jit(solution)/shard_map/ppermute | solution.py:75
  44.0 1.7 %collective-permute-start.13 = (bf16[128,1024]{1,0:T(8,128)(2,1)S(1)}, bf16[128,1024]{1,0:T(8,128)(2,1)S(1)}, u32[]{:S(2)}, u32[]{:S(2)}) collective-permute-start(bf16[128,1024]{1,0:T(8,128)(2,1)S(1)} %collective-permute-done.1.refs_3_), channel_id=1, source_target_pairs={{0,2},{2,0},{4,6},{6,4},{1,3},{3,1},{5,7},{7,5},{8,10},{10,8},{12,... | collective-permute-start | bytes 786440 | tf_op jit(solution)/shard_map/ppermute | solution.py:72
  45.8 1.3 %collective-permute-done.9.refs_7_ = bf16[128,1024]{1,0:T(8,128)(2,1)S(1)} collective-permute-done((bf16[128,1024]{1,0:T(8,128)(2,1)S(1)}, bf16[128,1024]{1,0:T(8,128)(2,1)S(1)}, u32[]{:S(2)}, u32[]{:S(2)}) %collective-permute-start.9) | collective-permute-done | bytes 262176 | tf_op jit(solution)/shard_map/ppermute | solution.py:75
  47.1 3.4 %copy-done = bf16[1,2,1024,2048]{3,2,1,0:T(8,128)(2,1)S(1)} copy-done((bf16[1,2,1024,2048]{3,2,1,0:T(8,128)(2,1)S(1)}, bf16[1,2,1024,2048]{3,2,1,0:T(8,128)(2,1)}, u32[]{:S(2)}) %copy-start) | copy-done | bytes 8388632
  50.5 3.0 %early_products.1 = (f32[8,128,1024]{2,1,0:T(8,128)S(1)}, bf16[8,512,256]{2,1,0:T(8,128)(2,1)S(1)}) custom-call(s32[16]{0:T(128)S(1)} %list_blocks.1.ancestors, bf16[2,1024,2048]{2,1,0:T(8,128)(2,1)S(1)} %bitcast.24, bf16[128,1024]{1,0:T(8,128)(2,1)S(1)} %get-tuple-element.53.refs_0_, bf16[128,1024]{1,0:T(8,128)(2,1)S(1)} %get-tuple-element.52.refs_1_, ...), custom_call_target="tpu_custom_call" | custom-call | flops 2147483648 | bytes 4194304 | tf_op jit(solution)/shard_map/early_products/pallas_call | solution.py:535
  53.6 2.0 %collective-permute-done.17.refs_7_ = bf16[128,1024]{1,0:T(8,128)(2,1)S(1)} collective-permute-done((bf16[128,1024]{1,0:T(8,128)(2,1)S(1)}, bf16[128,1024]{1,0:T(8,128)(2,1)S(1)}, u32[]{:S(2)}, u32[]{:S(2)}) %collective-permute-start.17) | collective-permute-done | bytes 262176 | tf_op jit(solution)/shard_map/ppermute | solution.py:75
  55.6 3.4 %copy-done.1 = bf16[1,2,1024,2048]{3,2,1,0:T(8,128)(2,1)S(1)} copy-done((bf16[1,2,1024,2048]{3,2,1,0:T(8,128)(2,1)S(1)}, bf16[1,2,1024,2048]{3,2,1,0:T(8,128)(2,1)}, u32[]{:S(2)}) %copy-start.1) | copy-done | bytes 8388632
  58.9 3.0 %last_products.1 = (f32[4096,128]{1,0:T(8,128)S(1)}, bf16[4096,128]{1,0:T(8,128)(2,1)S(1)}, f32[8,128,1024]{2,1,0:T(8,128)S(1)}, bf16[8,512,256]{2,1,0:T(8,128)(2,1)S(1)}) custom-call(s32[16]{0:T(128)S(1)} %bitcast.28, bf16[2,1024,2048]{2,1,0:T(8,128)(2,1)S(1)} %bitcast.25, f32[8,128,1024]{2,1,0:T(8,128)S(1)} %get-tuple-element.29.early, ...), custom_call_target="tpu_custom_call" | custom-call | flops 2147483648 | bytes 8388608 | tf_op jit(solution)/shard_map/last_products/pallas_call | solution.py:552
  62.0 3.0 %collective-permute-start.18 = (bf16[4096,128]{1,0:T(8,128)(2,1)S(1)}, bf16[4096,128]{1,0:T(8,128)(2,1)S(1)}, u32[]{:S(2)}, u32[]{:S(2)}) collective-permute-start(bf16[4096,128]{1,0:T(8,128)(2,1)S(1)} %get-tuple-element.32), channel_id=1, source_target_pairs={{0,1},{1,0},{2,3},{3,2},{4,5},{5,4},{6,7},{7,6},{8,9},{9,8},{10,11... | collective-permute-start | bytes 3145736 | tf_op jit(solution)/shard_map/ppermute | solution.py:636
  65.0 3.5 %diag_products.1 = (f32[4,72,1024]{2,1,0:T(8,128)S(1)}, bf16[1,4,72,1024]{3,2,1,0:T(8,128)(2,1)S(1)}) custom-call(s32[16]{0:T(128)S(1)} %bitcast.29, f32[2,16]{1,0:T(2,128)S(1)} %copy-done.3, s32[1]{0:T(128)S(6)} %copy.15.slot, s32[512]{0:T(512)S(1)} %pad_add_fusion.owner, f32[8,128,1024]{2,1,0:T(8,128)S(1)} %get-tuple-element.35.refs_0_, ...), custom_call_target="tpu_custom_call" | custom-call | flops 2147483648 | bytes 8388608 | tf_op jit(solution)/shard_map/diag_products/pallas_call | solution.py:566
  68.6 29.7 %collective-permute-done.20.refs_0_ = bf16[4,72,1024]{2,1,0:T(8,128)(2,1)S(1)} collective-permute-done((bf16[4,72,1024]{2,1,0:T(8,128)(2,1)S(1)}, bf16[4,72,1024]{2,1,0:T(8,128)(2,1)S(1)}, u32[]{:S(2)}, u32[]{:S(2)}) %collective-permute-start.20) | collective-permute-done | bytes 589856 | tf_op jit(solution)/shard_map/ppermute | solution.py:587
  98.3 0.1 regroup.1
  98.4 1.5 %collective-permute-start.21 = (bf16[72,1024]{1,0:T(8,128)(2,1)S(1)}, bf16[72,1024]{1,0:T(8,128)(2,1)S(1)}, u32[]{:S(2)}, u32[]{:S(2)}) collective-permute-start(bf16[72,1024]{1,0:T(8,128)(2,1)S(1)} %get-tuple-element.41), channel_id=1, source_target_pairs={{0,2},{2,4},{4,6},{6,0},{1,3},{3,5},{5,7},{7,1},{8,10},{10,12},{12... | collective-permute-start | bytes 442376 | tf_op jit(solution)/shard_map/ppermute | solution.py:600
  100.0 1.3 %collective-permute-start.22 = (bf16[72,1024]{1,0:T(8,128)(2,1)S(1)}, bf16[72,1024]{1,0:T(8,128)(2,1)S(1)}, u32[]{:S(2)}, u32[]{:S(2)}) collective-permute-start(bf16[72,1024]{1,0:T(8,128)(2,1)S(1)} %get-tuple-element.42), channel_id=1, source_target_pairs={{0,4},{2,6},{4,0},{6,2},{1,5},{3,7},{5,1},{7,3},{8,12},{10,14},{12... | collective-permute-start | bytes 442376 | tf_op jit(solution)/shard_map/ppermute | solution.py:600
  101.3 2.7 %collective-permute-start.23 = (bf16[72,1024]{1,0:T(8,128)(2,1)S(1)}, bf16[72,1024]{1,0:T(8,128)(2,1)S(1)}, u32[]{:S(2)}, u32[]{:S(2)}) collective-permute-start(bf16[72,1024]{1,0:T(8,128)(2,1)S(1)} %get-tuple-element.43), channel_id=1, source_target_pairs={{0,6},{2,0},{4,2},{6,4},{1,7},{3,1},{5,3},{7,5},{8,14},{10,8},{12,... | collective-permute-start | bytes 442376 | tf_op jit(solution)/shard_map/ppermute | solution.py:600
  104.0 2.4 %collective-permute-done.21.refs_0_ = bf16[72,1024]{1,0:T(8,128)(2,1)S(1)} collective-permute-done((bf16[72,1024]{1,0:T(8,128)(2,1)S(1)}, bf16[72,1024]{1,0:T(8,128)(2,1)S(1)}, u32[]{:S(2)}, u32[]{:S(2)}) %collective-permute-start.21) | collective-permute-done | bytes 147488 | tf_op jit(solution)/shard_map/ppermute | solution.py:600
  106.4 4.0 %collective-permute-done.22.refs_1_ = bf16[72,1024]{1,0:T(8,128)(2,1)S(1)} collective-permute-done((bf16[72,1024]{1,0:T(8,128)(2,1)S(1)}, bf16[72,1024]{1,0:T(8,128)(2,1)S(1)}, u32[]{:S(2)}, u32[]{:S(2)}) %collective-permute-start.22) | collective-permute-done | bytes 147488 | tf_op jit(solution)/shard_map/ppermute | solution.py:600
  110.5 1.4 %finish.1 = (f32[512,128]{1,0:T(8,128)}, f32[288,128]{1,0:T(8,128)S(1)}) custom-call(f32[2,16]{1,0:T(2,128)S(1)} %copy-done.3, s32[1]{0:T(128)S(6)} %copy.15.slot, f32[512,128]{1,0:T(8,128)S(1)} %bitcast.26, f32[72,1024]{1,0:T(8,128)S(1)} %get-tuple-element.40.own, bf16[72,1024]{1,0:T(8,128)(2,1)S(1)} %collective-permute-done.21.refs_0_, ...), custom_call_target="tpu_custom_call" | custom-call | tf_op jit(solution)/shard_map/finish/pallas_call | solution.py:603
  111.8 1.5 %collective-permute-start.25 = (f32[288,128]{1,0:T(8,128)S(1)}, f32[288,128]{1,0:T(8,128)S(1)}, u32[]{:S(2)}, u32[]{:S(2)}) collective-permute-start(f32[288,128]{1,0:T(8,128)S(1)} %get-tuple-element.45.refs_0_), channel_id=1, source_target_pairs={{0,16},{8,24},{16,0},{24,8},{1,17},{9,25},{17,1},{25,9},{2,18},{10... | collective-permute-start | bytes 442376 | tf_op jit(solution)/shard_map/ppermute | solution.py:617
  113.3 0.4 collective-permute-start.26
  113.7 4.9 %collective-permute-done.25.refs_2_ = f32[288,128]{1,0:T(8,128)S(1)} collective-permute-done((f32[288,128]{1,0:T(8,128)S(1)}, f32[288,128]{1,0:T(8,128)S(1)}, u32[]{:S(2)}, u32[]{:S(2)}) %collective-permute-start.25) | collective-permute-done | bytes 147488 | tf_op jit(solution)/shard_map/ppermute | solution.py:617
  118.6 2.2 %collective-permute-done.26.refs_3_ = f32[288,128]{1,0:T(8,128)S(1)} collective-permute-done((f32[288,128]{1,0:T(8,128)S(1)}, f32[288,128]{1,0:T(8,128)S(1)}, u32[]{:S(2)}, u32[]{:S(2)}) %collective-permute-start.26) | collective-permute-done | bytes 147488 | tf_op jit(solution)/shard_map/ppermute | solution.py:617
  120.8 0.7 density.1
  121.5 1.8 %join_columns.1 = f32[4096,128]{1,0:T(8,128)} custom-call(f32[4096,128]{1,0:T(8,128)S(1)} %get-tuple-element.31.keep, bf16[4096,128]{1,0:T(8,128)(2,1)S(1)} %collective-permute-done.18.refs_0_), custom_call_target="tpu_custom_call" | custom-call | tf_op jit(solution)/shard_map/join_columns/pallas_call | solution.py:648
  (34 shorter events, 0.3 us)
Async XLA Ops:
  1.7 10.6 %collective-permute-start.2 = (bf16[128,1024]{1,0:T(8,128)(2,1)S(1)}, bf16[128,1024]{1,0:T(8,128)(2,1)S(1)}, u32[]{:S(2)}, u32[]{:S(2)}) collective-permute-start(bf16[128,1024]{1,0:T(8,128)(2,1)S(1)} %get-tuple-element.53.refs_0_), channel_id=1, source_target_pairs={{2,4},{4,2},{3,5},{5,3},{10,12},{12,10},{11,13},{13,11},{18,20},{2... | collective-permute-start | bytes 786440 | tf_op jit(solution)/shard_map/ppermute | solution.py:48
  2.4 13.3 %collective-permute-start.6 = (bf16[128,1024]{1,0:T(8,128)(2,1)S(1)}, bf16[128,1024]{1,0:T(8,128)(2,1)S(1)}, u32[]{:S(2)}, u32[]{:S(2)}) collective-permute-start(bf16[128,1024]{1,0:T(8,128)(2,1)S(1)} %get-tuple-element.53.refs_0_), channel_id=1, source_target_pairs={{0,2},{2,0},{4,6},{6,4},{1,3},{3,1},{5,7},{7,5},{8,10},{10,8},{12,... | collective-permute-start | bytes 786440 | tf_op jit(solution)/shard_map/ppermute | solution.py:48
  8.3 8.1 %collective-permute-start = (bf16[128,1024]{1,0:T(8,128)(2,1)S(1)}, bf16[128,1024]{1,0:T(8,128)(2,1)S(1)}, u32[]{:S(2)}, u32[]{:S(2)}) collective-permute-start(bf16[128,1024]{1,0:T(8,128)(2,1)S(1)} %get-tuple-element.53.refs_0_), channel_id=1, source_target_pairs={{0,1},{1,0},{2,3},{3,2},{4,5},{5,4},{6,7},{7,6},{8,9},{9,8},{10,11... | collective-permute-start | bytes 786440 | tf_op jit(solution)/shard_map/ppermute | solution.py:75
  9.8 8.3 %collective-permute-start.4 = (bf16[128,1024]{1,0:T(8,128)(2,1)S(1)}, bf16[128,1024]{1,0:T(8,128)(2,1)S(1)}, u32[]{:S(2)}, u32[]{:S(2)}) collective-permute-start(bf16[128,1024]{1,0:T(8,128)(2,1)S(1)} %get-tuple-element.52.refs_1_), channel_id=1, source_target_pairs={{2,4},{4,2},{3,5},{5,3},{10,12},{12,10},{11,13},{13,11},{18,20},{2... | collective-permute-start | bytes 786440 | tf_op jit(solution)/shard_map/ppermute | solution.py:48
  10.5 10.9 %collective-permute-start.10 = (bf16[128,1024]{1,0:T(8,128)(2,1)S(1)}, bf16[128,1024]{1,0:T(8,128)(2,1)S(1)}, u32[]{:S(2)}, u32[]{:S(2)}) collective-permute-start(bf16[128,1024]{1,0:T(8,128)(2,1)S(1)} %get-tuple-element.52.refs_1_), channel_id=1, source_target_pairs={{0,2},{2,0},{4,6},{6,4},{1,3},{3,1},{5,7},{7,5},{8,10},{10,8},{12,... | collective-permute-start | bytes 786440 | tf_op jit(solution)/shard_map/ppermute | solution.py:48
  12.3 14.4 %collective-permute-start.3 = (bf16[128,1024]{1,0:T(8,128)(2,1)S(1)}, bf16[128,1024]{1,0:T(8,128)(2,1)S(1)}, u32[]{:S(2)}, u32[]{:S(2)}) collective-permute-start(bf16[128,1024]{1,0:T(8,128)(2,1)S(1)} %collective-permute-done.2), channel_id=1, source_target_pairs={{0,2},{2,0},{4,6},{6,4},{1,3},{3,1},{5,7},{7,5},{8,10},{10,8},{12,... | collective-permute-start | bytes 786440 | tf_op jit(solution)/shard_map/ppermute | solution.py:48
  15.7 12.5 %collective-permute-start.14 = (bf16[128,1024]{1,0:T(8,128)(2,1)S(1)}, bf16[128,1024]{1,0:T(8,128)(2,1)S(1)}, u32[]{:S(2)}, u32[]{:S(2)}) collective-permute-start(bf16[128,1024]{1,0:T(8,128)(2,1)S(1)} %collective-permute-done.6.refs_0_), channel_id=1, source_target_pairs={{2,4},{4,2},{3,5},{5,3},{10,12},{12,10},{11,13},{13,11},{18,20},{2... | collective-permute-start | bytes 786440 | tf_op jit(solution)/shard_map/ppermute | solution.py:48
  16.4 13.9 %collective-permute-start.7 = (bf16[128,1024]{1,0:T(8,128)(2,1)S(1)}, bf16[128,1024]{1,0:T(8,128)(2,1)S(1)}, u32[]{:S(2)}, u32[]{:S(2)}) collective-permute-start(bf16[128,1024]{1,0:T(8,128)(2,1)S(1)} %collective-permute-done.6.refs_0_), channel_id=1, source_target_pairs={{0,1},{1,0},{2,3},{3,2},{4,5},{5,4},{6,7},{7,6},{8,9},{9,8},{10,11... | collective-permute-start | bytes 786440 | tf_op jit(solution)/shard_map/ppermute | solution.py:75
  18.1 14.2 %collective-permute-start.5 = (bf16[128,1024]{1,0:T(8,128)(2,1)S(1)}, bf16[128,1024]{1,0:T(8,128)(2,1)S(1)}, u32[]{:S(2)}, u32[]{:S(2)}) collective-permute-start(bf16[128,1024]{1,0:T(8,128)(2,1)S(1)} %collective-permute-done.4), channel_id=1, source_target_pairs={{0,2},{2,0},{4,6},{6,4},{1,3},{3,1},{5,7},{7,5},{8,10},{10,8},{12,... | collective-permute-start | bytes 786440 | tf_op jit(solution)/shard_map/ppermute | solution.py:48
  21.4 12.4 %collective-permute-start.11 = (bf16[128,1024]{1,0:T(8,128)(2,1)S(1)}, bf16[128,1024]{1,0:T(8,128)(2,1)S(1)}, u32[]{:S(2)}, u32[]{:S(2)}) collective-permute-start(bf16[128,1024]{1,0:T(8,128)(2,1)S(1)} %collective-permute-done.10.refs_1_), channel_id=1, source_target_pairs={{2,4},{4,2},{3,5},{5,3},{10,12},{12,10},{11,13},{13,11},{18,20},{2... | collective-permute-start | bytes 786440 | tf_op jit(solution)/shard_map/ppermute | solution.py:48
  22.1 0.7 copy-start.4
  22.8 7.5 %copy-start.6 = (s32[256,1]{0,1:T(1,128)S(1)}, s32[256,1]{0,1:T(1,128)}, u32[]{:S(2)}) copy-start(s32[256,1]{0,1:T(1,128)} %param.11) | copy-start | bytes 3076
  26.7 9.2 %collective-permute-start.1 = (bf16[128,1024]{1,0:T(8,128)(2,1)S(1)}, bf16[128,1024]{1,0:T(8,128)(2,1)S(1)}, u32[]{:S(2)}, u32[]{:S(2)}) collective-permute-start(bf16[128,1024]{1,0:T(8,128)(2,1)S(1)} %get-tuple-element.52.refs_1_), channel_id=1, source_target_pairs={{0,1},{1,0},{2,3},{3,2},{4,5},{5,4},{6,7},{7,6},{8,9},{9,8},{10,11... | collective-permute-start | bytes 786440 | tf_op jit(solution)/shard_map/ppermute | solution.py:75
  28.2 9.7 %collective-permute-start.15 = (bf16[128,1024]{1,0:T(8,128)(2,1)S(1)}, bf16[128,1024]{1,0:T(8,128)(2,1)S(1)}, u32[]{:S(2)}, u32[]{:S(2)}) collective-permute-start(bf16[128,1024]{1,0:T(8,128)(2,1)S(1)} %collective-permute-done.14), channel_id=1, source_target_pairs={{0,2},{2,0},{4,6},{6,4},{1,3},{3,1},{5,7},{7,5},{8,10},{10,8},{12,... | collective-permute-start | bytes 786440 | tf_op jit(solution)/shard_map/ppermute | solution.py:48
  30.3 23.3 %collective-permute-start.19 = (s32[256]{0:T(256)S(1)}, s32[256]{0:T(256)S(1)}, u32[]{:S(2)}, u32[]{:S(2)}) collective-permute-start(s32[256]{0:T(256)S(1)} %bitcast.32), channel_id=1, source_target_pairs={{0,1},{1,0},{2,3},{3,2},{4,5},{5,4},{6,7},{7,6},{8,9},{9,8},{10,11... | collective-permute-start | bytes 3080 | tf_op jit(solution)/shard_map/ppermute | solution.py:498
  32.3 11.7 %collective-permute-start.8 = (bf16[128,1024]{1,0:T(8,128)(2,1)S(1)}, bf16[128,1024]{1,0:T(8,128)(2,1)S(1)}, u32[]{:S(2)}, u32[]{:S(2)}) collective-permute-start(bf16[128,1024]{1,0:T(8,128)(2,1)S(1)} %broadcast_select_fusion.3.refs_4_), channel_id=1, source_target_pairs={{0,1},{1,0},{2,3},{3,2},{4,5},{5,4},{6,7},{7,6},{8,9},{9,8},{10,11... | collective-permute-start | bytes 786440 | tf_op jit(solution)/shard_map/ppermute | solution.py:75
  33.8 8.6 %collective-permute-start.12 = (bf16[128,1024]{1,0:T(8,128)(2,1)S(1)}, bf16[128,1024]{1,0:T(8,128)(2,1)S(1)}, u32[]{:S(2)}, u32[]{:S(2)}) collective-permute-start(bf16[128,1024]{1,0:T(8,128)(2,1)S(1)} %collective-permute-done.11), channel_id=1, source_target_pairs={{0,2},{2,0},{4,6},{6,4},{1,3},{3,1},{5,7},{7,5},{8,10},{10,8},{12,... | collective-permute-start | bytes 786440 | tf_op jit(solution)/shard_map/ppermute | solution.py:48
  35.9 11.2 %collective-permute-start.9 = (bf16[128,1024]{1,0:T(8,128)(2,1)S(1)}, bf16[128,1024]{1,0:T(8,128)(2,1)S(1)}, u32[]{:S(2)}, u32[]{:S(2)}) collective-permute-start(bf16[128,1024]{1,0:T(8,128)(2,1)S(1)} %broadcast_select_fusion.2.refs_5_), channel_id=1, source_target_pairs={{0,1},{1,0},{2,3},{3,2},{4,5},{5,4},{6,7},{7,6},{8,9},{9,8},{10,11... | collective-permute-start | bytes 786440 | tf_op jit(solution)/shard_map/ppermute | solution.py:75
  38.0 15.6 %collective-permute-start.16 = (bf16[128,1024]{1,0:T(8,128)(2,1)S(1)}, bf16[128,1024]{1,0:T(8,128)(2,1)S(1)}, u32[]{:S(2)}, u32[]{:S(2)}) collective-permute-start(bf16[128,1024]{1,0:T(8,128)(2,1)S(1)} %broadcast_select_fusion.1.refs_4_), channel_id=1, source_target_pairs={{0,1},{1,0},{2,3},{3,2},{4,5},{5,4},{6,7},{7,6},{8,9},{9,8},{10,11... | collective-permute-start | bytes 786440 | tf_op jit(solution)/shard_map/ppermute | solution.py:75
  42.5 13.1 %collective-permute-start.17 = (bf16[128,1024]{1,0:T(8,128)(2,1)S(1)}, bf16[128,1024]{1,0:T(8,128)(2,1)S(1)}, u32[]{:S(2)}, u32[]{:S(2)}) collective-permute-start(bf16[128,1024]{1,0:T(8,128)(2,1)S(1)} %broadcast_select_fusion.refs_5_), channel_id=1, source_target_pairs={{0,1},{1,0},{2,3},{3,2},{4,5},{5,4},{6,7},{7,6},{8,9},{9,8},{10,11... | collective-permute-start | bytes 786440 | tf_op jit(solution)/shard_map/ppermute | solution.py:75
  44.0 11.5 %collective-permute-start.13 = (bf16[128,1024]{1,0:T(8,128)(2,1)S(1)}, bf16[128,1024]{1,0:T(8,128)(2,1)S(1)}, u32[]{:S(2)}, u32[]{:S(2)}) collective-permute-start(bf16[128,1024]{1,0:T(8,128)(2,1)S(1)} %collective-permute-done.1.refs_3_), channel_id=1, source_target_pairs={{0,2},{2,0},{4,6},{6,4},{1,3},{3,1},{5,7},{7,5},{8,10},{10,8},{12,... | collective-permute-start | bytes 786440 | tf_op jit(solution)/shard_map/ppermute | solution.py:72
  47.1 3.4 %copy-start = (bf16[1,2,1024,2048]{3,2,1,0:T(8,128)(2,1)S(1)}, bf16[1,2,1024,2048]{3,2,1,0:T(8,128)(2,1)}, u32[]{:S(2)}) copy-start(bf16[1,2,1024,2048]{3,2,1,0:T(8,128)(2,1)} %param.7) | copy-start | bytes 25165828
  50.5 5.1 %copy-start.5 = (s32[1,16]{1,0:T(1,128)S(1)}, s32[1,16]{1,0:T(1,128)}, u32[]{:S(2)}) copy-start(s32[1,16]{1,0:T(1,128)} %param.10) | copy-start | bytes 196
  53.6 11.4 %copy-start.3 = (f32[2,16]{1,0:T(2,128)S(1)}, f32[2,16]{1,0:T(2,128)}, u32[]{:S(2)}) copy-start(f32[2,16]{1,0:T(2,128)} %table.3) | copy-start | bytes 388
  55.6 3.4 %copy-start.1 = (bf16[1,2,1024,2048]{3,2,1,0:T(8,128)(2,1)S(1)}, bf16[1,2,1024,2048]{3,2,1,0:T(8,128)(2,1)}, u32[]{:S(2)}) copy-start(bf16[1,2,1024,2048]{3,2,1,0:T(8,128)(2,1)} %param.7) | copy-start | bytes 25165828
  62.0 59.5 %collective-permute-start.18 = (bf16[4096,128]{1,0:T(8,128)(2,1)S(1)}, bf16[4096,128]{1,0:T(8,128)(2,1)S(1)}, u32[]{:S(2)}, u32[]{:S(2)}) collective-permute-start(bf16[4096,128]{1,0:T(8,128)(2,1)S(1)} %get-tuple-element.32), channel_id=1, source_target_pairs={{0,1},{1,0},{2,3},{3,2},{4,5},{5,4},{6,7},{7,6},{8,9},{9,8},{10,11... | collective-permute-start | bytes 3145736 | tf_op jit(solution)/shard_map/ppermute | solution.py:636
  65.0 45.4 %copy-start.2 = (f32[64,1,1,2,512]{4,3,2,1,0:T(2,128)S(1)}, f32[64,1,1,2,512]{4,3,2,1,0:T(2,128)}, u32[]{:S(2)}) copy-start(f32[64,1,1,2,512]{4,3,2,1,0:T(2,128)} %param.9) | copy-start | bytes 786436
  68.5 29.8 %collective-permute-start.20 = (bf16[4,72,1024]{2,1,0:T(8,128)(2,1)S(1)}, bf16[4,72,1024]{2,1,0:T(8,128)(2,1)S(1)}, u32[]{:S(2)}, u32[]{:S(2)}) collective-permute-start(bf16[4,72,1024]{2,1,0:T(8,128)(2,1)S(1)} %bitcast.30), channel_id=1, source_target_pairs={{0,1},{1,0},{2,3},{3,2},{4,5},{5,4},{6,7},{7,6},{8,9},{9,8},{10,11... | collective-permute-start | bytes 1769480 | tf_op jit(solution)/shard_map/ppermute | solution.py:587
  98.4 8.0 %collective-permute-start.21 = (bf16[72,1024]{1,0:T(8,128)(2,1)S(1)}, bf16[72,1024]{1,0:T(8,128)(2,1)S(1)}, u32[]{:S(2)}, u32[]{:S(2)}) collective-permute-start(bf16[72,1024]{1,0:T(8,128)(2,1)S(1)} %get-tuple-element.41), channel_id=1, source_target_pairs={{0,2},{2,4},{4,6},{6,0},{1,3},{3,5},{5,7},{7,1},{8,10},{10,12},{12... | collective-permute-start | bytes 442376 | tf_op jit(solution)/shard_map/ppermute | solution.py:600
  100.0 10.5 %collective-permute-start.22 = (bf16[72,1024]{1,0:T(8,128)(2,1)S(1)}, bf16[72,1024]{1,0:T(8,128)(2,1)S(1)}, u32[]{:S(2)}, u32[]{:S(2)}) collective-permute-start(bf16[72,1024]{1,0:T(8,128)(2,1)S(1)} %get-tuple-element.42), channel_id=1, source_target_pairs={{0,4},{2,6},{4,0},{6,2},{1,5},{3,7},{5,1},{7,3},{8,12},{10,14},{12... | collective-permute-start | bytes 442376 | tf_op jit(solution)/shard_map/ppermute | solution.py:600
  101.3 9.2 %collective-permute-start.23 = (bf16[72,1024]{1,0:T(8,128)(2,1)S(1)}, bf16[72,1024]{1,0:T(8,128)(2,1)S(1)}, u32[]{:S(2)}, u32[]{:S(2)}) collective-permute-start(bf16[72,1024]{1,0:T(8,128)(2,1)S(1)} %get-tuple-element.43), channel_id=1, source_target_pairs={{0,6},{2,0},{4,2},{6,4},{1,7},{3,1},{5,3},{7,5},{8,14},{10,8},{12,... | collective-permute-start | bytes 442376 | tf_op jit(solution)/shard_map/ppermute | solution.py:600
  111.8 1.9 %collective-permute-start.24 = (f32[288,128]{1,0:T(8,128)S(1)}, f32[288,128]{1,0:T(8,128)S(1)}, u32[]{:S(2)}, u32[]{:S(2)}) collective-permute-start(f32[288,128]{1,0:T(8,128)S(1)} %get-tuple-element.45.refs_0_), channel_id=1, source_target_pairs={{0,8},{8,0},{16,24},{24,16},{1,9},{9,1},{17,25},{25,17},{2,10},{10... | collective-permute-start | bytes 442376 | tf_op jit(solution)/shard_map/ppermute | solution.py:617
  111.8 6.7 %collective-permute-start.25 = (f32[288,128]{1,0:T(8,128)S(1)}, f32[288,128]{1,0:T(8,128)S(1)}, u32[]{:S(2)}, u32[]{:S(2)}) collective-permute-start(f32[288,128]{1,0:T(8,128)S(1)} %get-tuple-element.45.refs_0_), channel_id=1, source_target_pairs={{0,16},{8,24},{16,0},{24,8},{1,17},{9,25},{17,1},{25,9},{2,18},{10... | collective-permute-start | bytes 442376 | tf_op jit(solution)/shard_map/ppermute | solution.py:617
  113.3 7.5 %collective-permute-start.26 = (f32[288,128]{1,0:T(8,128)S(1)}, f32[288,128]{1,0:T(8,128)S(1)}, u32[]{:S(2)}, u32[]{:S(2)}) collective-permute-start(f32[288,128]{1,0:T(8,128)S(1)} %get-tuple-element.45.refs_0_), channel_id=1, source_target_pairs={{0,24},{8,16},{16,8},{24,0},{1,25},{9,17},{17,9},{25,1},{2,26},{10... | collective-permute-start | bytes 442376 | tf_op jit(solution)/shard_map/ppermute | solution.py:617

commit v7 on v6

--- a/solution.py
+++ b/solution.py
@@ -319,9 +319,8 @@
     weight_real = table[0, slot[0]]
     weight_imag = table[1, slot[0]]
 
-    row_count = below((r + 1) * row_blocks) - row_first
-
-    def operands(i):
+    @pl.loop(0, below((r + 1) * row_blocks) - row_first)
+    def _(i):
         real = total[i, :, :half]
         imag = total[i, :, half:]
         first = brought(sources, first_stages, rows, ancestors.shape[0], row_first + i)
@@ -335,44 +334,29 @@
         imag_high = imag.astype(jnp.bfloat16)
         real_low = (real - real_high.astype(jnp.float32)).astype(jnp.bfloat16)
         imag_low = (imag - imag_high.astype(jnp.float32)).astype(jnp.bfloat16)
-        right = [
-            jnp.concatenate([real_high, imag_high], axis=1),
-            jnp.concatenate([-imag_high, real_high], axis=1),
-            jnp.concatenate([real_low, imag_low], axis=1),
-            jnp.concatenate([-imag_low, real_low], axis=1),
-        ]
+        right = jnp.concatenate(
+            [
+                jnp.concatenate([real_high, imag_high], axis=1),
+                jnp.concatenate([-imag_high, real_high], axis=1),
+                jnp.concatenate([real_low, imag_low], axis=1),
+                jnp.concatenate([-imag_low, real_low], axis=1),
+            ],
+            axis=0,
+        )
+        diag[...] += jnp.dot(
+            jnp.concatenate([left, left], axis=1), right, preferred_element_type=jnp.float32
+        )
         block = ancestors[row_first + i] - r * row_blocks
         place = block // own_blocks
         mixed = -(weight_real * imag + weight_imag * real)
         per_device = own_blocks * (BS // BR) * across
-        start = lax.rem(c - place + cols, cols) * per_device + lax.rem(block, own_blocks) * (
+        first = lax.rem(c - place + cols, cols) * per_device + lax.rem(block, own_blocks) * (
             BS // BR
         ) * across
         for group in range(BS // BR):
             for j in range(across):
-                tile = owner[start + group * across + j]
+                tile = owner[first + group * across + j]
                 tiles[j, tile] += mixed[group * BR : (group + 1) * BR, j * BC : (j + 1) * BC]
-        return [left, left], right
-
-    def add(blocks):
-        left, right = [], []
-        for i in blocks:
-            more_left, more_right = operands(i)
-            left += more_left
-            right += more_right
-        diag[...] += jnp.dot(
-            jnp.concatenate(left, axis=1),
-            jnp.concatenate(right, axis=0),
-            preferred_element_type=jnp.float32,
-        )
-
-    @pl.loop(0, row_count // 2)
-    def _(pair):
-        add([2 * pair, 2 * pair + 1])
-
-    @pl.when(lax.rem(row_count, 2) == 1)
-    def _():
-        add([row_count - 1])
 
     part = half // (rows * cols)
     for row in range(rows):

time: 124 us -> 124 us (level)
  no operation moved by 1% of the time
where the time goes in v7:
time: 124 us; the launch traced here: 123 us
  waiting for transfers between devices  54.6 us (44%)
  starting transfers between devices  44.1 us (36%)
  Pallas kernels  14.6 us (12%)
  local copies, waits for them, and re-layouts  8.5 us (7%)
  between operations  1.47 us (1%)
    ppermute x1, waiting for transfers between devices, compute(): lax.ppermute(diag_send[step - 1], grid, everyone_pairs[step])  29.9 us
    ppermute x10, starting transfers between devices, hop(): return lax.ppermute(value, 'row', pairs)  21.2 us
    ppermute x7, starting transfers between devices, gather_stages(): last = lax.ppermute(leaving, grid, pairs)  9.98 us
    ppermute x10, waiting for transfers between devices, hop(): return lax.ppermute(value, 'row', pairs)  7.91 us
    unnamed x14, local copies, waits for them, and re-layouts  7.43 us
    ppermute x3, waiting for transfers between devices, compute(): lax.ppermute(message, 'pole', [(i, i ^ step) for i in range(poles)])  7.09 us
    ppermute x3, waiting for transfers between devices, compute(): lax.ppermute(rounded[step - 1], 'row', [(i, (i + step) % rows) for i in r...  6.42 us
    ppermute x3, starting transfers between devices, compute(): lax.ppermute(rounded[step - 1], 'row', [(i, (i + step) % rows) for i in r...  5.6 us
  transfers between devices with their start and end apart: 27, of which 11 were waited for; matrix products, arithmetic and copies ran while one was open for 0% of the time, Pallas kernels for 8%

profile of v7, /device:TPU:0, one launch (start us, length us, event | category | flops | bytes accessed | tf_op | source)
XLA Modules:
  0.0 123.3 jit_solution(2425228696496336962)
XLA Ops:
  0.6 1.1 slice_bitcast_fusion
  1.7 0.7 collective-permute-start.2
  2.4 5.9 %collective-permute-start.6 = (bf16[128,1024]{1,0:T(8,128)(2,1)S(1)}, bf16[128,1024]{1,0:T(8,128)(2,1)S(1)}, u32[]{:S(2)}, u32[]{:S(2)}) collective-permute-start(bf16[128,1024]{1,0:T(8,128)(2,1)S(1)} %get-tuple-element.53.refs_0_), channel_id=1, source_target_pairs={{0,2},{2,0},{4,6},{6,4},{1,3},{3,1},{5,7},{7,5},{8,10},{10,8},{12,... | collective-permute-start | bytes 786440 | tf_op jit(solution)/shard_map/ppermute | solution.py:48
  8.3 1.5 %collective-permute-start = (bf16[128,1024]{1,0:T(8,128)(2,1)S(1)}, bf16[128,1024]{1,0:T(8,128)(2,1)S(1)}, u32[]{:S(2)}, u32[]{:S(2)}) collective-permute-start(bf16[128,1024]{1,0:T(8,128)(2,1)S(1)} %get-tuple-element.53.refs_0_), channel_id=1, source_target_pairs={{0,1},{1,0},{2,3},{3,2},{4,5},{5,4},{6,7},{7,6},{8,9},{9,8},{10,11... | collective-permute-start | bytes 786440 | tf_op jit(solution)/shard_map/ppermute | solution.py:75
  9.8 0.7 collective-permute-start.4
  10.5 1.8 %collective-permute-start.10 = (bf16[128,1024]{1,0:T(8,128)(2,1)S(1)}, bf16[128,1024]{1,0:T(8,128)(2,1)S(1)}, u32[]{:S(2)}, u32[]{:S(2)}) collective-permute-start(bf16[128,1024]{1,0:T(8,128)(2,1)S(1)} %get-tuple-element.52.refs_1_), channel_id=1, source_target_pairs={{0,2},{2,0},{4,6},{6,4},{1,3},{3,1},{5,7},{7,5},{8,10},{10,8},{12,... | collective-permute-start | bytes 786440 | tf_op jit(solution)/shard_map/ppermute | solution.py:48
  12.3 3.4 %collective-permute-start.3 = (bf16[128,1024]{1,0:T(8,128)(2,1)S(1)}, bf16[128,1024]{1,0:T(8,128)(2,1)S(1)}, u32[]{:S(2)}, u32[]{:S(2)}) collective-permute-start(bf16[128,1024]{1,0:T(8,128)(2,1)S(1)} %collective-permute-done.2), channel_id=1, source_target_pairs={{0,2},{2,0},{4,6},{6,4},{1,3},{3,1},{5,7},{7,5},{8,10},{10,8},{12,... | collective-permute-start | bytes 786440 | tf_op jit(solution)/shard_map/ppermute | solution.py:48
  15.7 0.7 collective-permute-start.14
  16.4 1.7 %collective-permute-start.7 = (bf16[128,1024]{1,0:T(8,128)(2,1)S(1)}, bf16[128,1024]{1,0:T(8,128)(2,1)S(1)}, u32[]{:S(2)}, u32[]{:S(2)}) collective-permute-start(bf16[128,1024]{1,0:T(8,128)(2,1)S(1)} %collective-permute-done.6.refs_0_), channel_id=1, source_target_pairs={{0,1},{1,0},{2,3},{3,2},{4,5},{5,4},{6,7},{7,6},{8,9},{9,8},{10,11... | collective-permute-start | bytes 786440 | tf_op jit(solution)/shard_map/ppermute | solution.py:75
  18.1 3.3 %collective-permute-start.5 = (bf16[128,1024]{1,0:T(8,128)(2,1)S(1)}, bf16[128,1024]{1,0:T(8,128)(2,1)S(1)}, u32[]{:S(2)}, u32[]{:S(2)}) collective-permute-start(bf16[128,1024]{1,0:T(8,128)(2,1)S(1)} %collective-permute-done.4), channel_id=1, source_target_pairs={{0,2},{2,0},{4,6},{6,4},{1,3},{3,1},{5,7},{7,5},{8,10},{10,8},{12,... | collective-permute-start | bytes 786440 | tf_op jit(solution)/shard_map/ppermute | solution.py:48
  21.4 0.7 collective-permute-start.11
  22.1 0.6 copy-done.4
  22.8 1.1 list_blocks.1.ancestors
  24.6 2.1 %collective-permute-done.3 = bf16[128,1024]{1,0:T(8,128)(2,1)S(1)} collective-permute-done((bf16[128,1024]{1,0:T(8,128)(2,1)S(1)}, bf16[128,1024]{1,0:T(8,128)(2,1)S(1)}, u32[]{:S(2)}, u32[]{:S(2)}) %collective-permute-start.3) | collective-permute-done | bytes 262176 | tf_op jit(solution)/shard_map/ppermute | solution.py:48
  26.7 1.5 %collective-permute-start.1 = (bf16[128,1024]{1,0:T(8,128)(2,1)S(1)}, bf16[128,1024]{1,0:T(8,128)(2,1)S(1)}, u32[]{:S(2)}, u32[]{:S(2)}) collective-permute-start(bf16[128,1024]{1,0:T(8,128)(2,1)S(1)} %get-tuple-element.52.refs_1_), channel_id=1, source_target_pairs={{0,1},{1,0},{2,3},{3,2},{4,5},{5,4},{6,7},{7,6},{8,9},{9,8},{10,11... | collective-permute-start | bytes 786440 | tf_op jit(solution)/shard_map/ppermute | solution.py:75
  28.2 2.0 %collective-permute-start.15 = (bf16[128,1024]{1,0:T(8,128)(2,1)S(1)}, bf16[128,1024]{1,0:T(8,128)(2,1)S(1)}, u32[]{:S(2)}, u32[]{:S(2)}) collective-permute-start(bf16[128,1024]{1,0:T(8,128)(2,1)S(1)} %collective-permute-done.14), channel_id=1, source_target_pairs={{0,2},{2,0},{4,6},{6,4},{1,3},{3,1},{5,7},{7,5},{8,10},{10,8},{12,... | collective-permute-start | bytes 786440 | tf_op jit(solution)/shard_map/ppermute | solution.py:48
  30.3 0.6 collective-permute-start.19
  30.9 1.4 %collective-permute-done.5 = bf16[128,1024]{1,0:T(8,128)(2,1)S(1)} collective-permute-done((bf16[128,1024]{1,0:T(8,128)(2,1)S(1)}, bf16[128,1024]{1,0:T(8,128)(2,1)S(1)}, u32[]{:S(2)}, u32[]{:S(2)}) %collective-permute-start.5) | collective-permute-done | bytes 262176 | tf_op jit(solution)/shard_map/ppermute | solution.py:48
  32.3 1.5 %collective-permute-start.8 = (bf16[128,1024]{1,0:T(8,128)(2,1)S(1)}, bf16[128,1024]{1,0:T(8,128)(2,1)S(1)}, u32[]{:S(2)}, u32[]{:S(2)}) collective-permute-start(bf16[128,1024]{1,0:T(8,128)(2,1)S(1)} %broadcast_select_fusion.3.refs_4_), channel_id=1, source_target_pairs={{0,1},{1,0},{2,3},{3,2},{4,5},{5,4},{6,7},{7,6},{8,9},{9,8},{10,11... | collective-permute-start | bytes 786440 | tf_op jit(solution)/shard_map/ppermute | solution.py:75
  33.8 2.0 %collective-permute-start.12 = (bf16[128,1024]{1,0:T(8,128)(2,1)S(1)}, bf16[128,1024]{1,0:T(8,128)(2,1)S(1)}, u32[]{:S(2)}, u32[]{:S(2)}) collective-permute-start(bf16[128,1024]{1,0:T(8,128)(2,1)S(1)} %collective-permute-done.11), channel_id=1, source_target_pairs={{0,2},{2,0},{4,6},{6,4},{1,3},{3,1},{5,7},{7,5},{8,10},{10,8},{12,... | collective-permute-start | bytes 786440 | tf_op jit(solution)/shard_map/ppermute | solution.py:48
  35.9 0.6 collective-permute-start.9
  36.5 1.5 %collective-permute-done.15 = bf16[128,1024]{1,0:T(8,128)(2,1)S(1)} collective-permute-done((bf16[128,1024]{1,0:T(8,128)(2,1)S(1)}, bf16[128,1024]{1,0:T(8,128)(2,1)S(1)}, u32[]{:S(2)}, u32[]{:S(2)}) %collective-permute-start.15) | collective-permute-done | bytes 262176 | tf_op jit(solution)/shard_map/ppermute | solution.py:48
  38.0 1.6 %collective-permute-start.16 = (bf16[128,1024]{1,0:T(8,128)(2,1)S(1)}, bf16[128,1024]{1,0:T(8,128)(2,1)S(1)}, u32[]{:S(2)}, u32[]{:S(2)}) collective-permute-start(bf16[128,1024]{1,0:T(8,128)(2,1)S(1)} %broadcast_select_fusion.1.refs_4_), channel_id=1, source_target_pairs={{0,1},{1,0},{2,3},{3,2},{4,5},{5,4},{6,7},{7,6},{8,9},{9,8},{10,11... | collective-permute-start | bytes 786440 | tf_op jit(solution)/shard_map/ppermute | solution.py:75
  39.6 2.9 %collective-permute-done.12 = bf16[128,1024]{1,0:T(8,128)(2,1)S(1)} collective-permute-done((bf16[128,1024]{1,0:T(8,128)(2,1)S(1)}, bf16[128,1024]{1,0:T(8,128)(2,1)S(1)}, u32[]{:S(2)}, u32[]{:S(2)}) %collective-permute-start.12) | collective-permute-done | bytes 262176 | tf_op jit(solution)/shard_map/ppermute | solution.py:48
  42.5 1.6 %collective-permute-start.17 = (bf16[128,1024]{1,0:T(8,128)(2,1)S(1)}, bf16[128,1024]{1,0:T(8,128)(2,1)S(1)}, u32[]{:S(2)}, u32[]{:S(2)}) collective-permute-start(bf16[128,1024]{1,0:T(8,128)(2,1)S(1)} %broadcast_select_fusion.refs_5_), channel_id=1, source_target_pairs={{0,1},{1,0},{2,3},{3,2},{4,5},{5,4},{6,7},{7,6},{8,9},{9,8},{10,11... | collective-permute-start | bytes 786440 | tf_op jit(solution)/shard_map/ppermute | solution.py:75
  44.0 1.7 %collective-permute-start.13 = (bf16[128,1024]{1,0:T(8,128)(2,1)S(1)}, bf16[128,1024]{1,0:T(8,128)(2,1)S(1)}, u32[]{:S(2)}, u32[]{:S(2)}) collective-permute-start(bf16[128,1024]{1,0:T(8,128)(2,1)S(1)} %collective-permute-done.1.refs_3_), channel_id=1, source_target_pairs={{0,2},{2,0},{4,6},{6,4},{1,3},{3,1},{5,7},{7,5},{8,10},{10,8},{12,... | collective-permute-start | bytes 786440 | tf_op jit(solution)/shard_map/ppermute | solution.py:72
  45.8 1.3 %collective-permute-done.9.refs_7_ = bf16[128,1024]{1,0:T(8,128)(2,1)S(1)} collective-permute-done((bf16[128,1024]{1,0:T(8,128)(2,1)S(1)}, bf16[128,1024]{1,0:T(8,128)(2,1)S(1)}, u32[]{:S(2)}, u32[]{:S(2)}) %collective-permute-start.9) | collective-permute-done | bytes 262176 | tf_op jit(solution)/shard_map/ppermute | solution.py:75
  47.1 3.4 %copy-done = bf16[1,2,1024,2048]{3,2,1,0:T(8,128)(2,1)S(1)} copy-done((bf16[1,2,1024,2048]{3,2,1,0:T(8,128)(2,1)S(1)}, bf16[1,2,1024,2048]{3,2,1,0:T(8,128)(2,1)}, u32[]{:S(2)}) %copy-start) | copy-done | bytes 8388632
  50.5 3.0 %early_products.1 = (f32[8,128,1024]{2,1,0:T(8,128)S(1)}, bf16[8,512,256]{2,1,0:T(8,128)(2,1)S(1)}) custom-call(s32[16]{0:T(128)S(1)} %list_blocks.1.ancestors, bf16[2,1024,2048]{2,1,0:T(8,128)(2,1)S(1)} %bitcast.24, bf16[128,1024]{1,0:T(8,128)(2,1)S(1)} %get-tuple-element.53.refs_0_, bf16[128,1024]{1,0:T(8,128)(2,1)S(1)} %get-tuple-element.52.refs_1_, ...), custom_call_target="tpu_custom_call" | custom-call | flops 2147483648 | bytes 4194304 | tf_op jit(solution)/shard_map/early_products/pallas_call | solution.py:519
  53.6 2.0 %collective-permute-done.17.refs_7_ = bf16[128,1024]{1,0:T(8,128)(2,1)S(1)} collective-permute-done((bf16[128,1024]{1,0:T(8,128)(2,1)S(1)}, bf16[128,1024]{1,0:T(8,128)(2,1)S(1)}, u32[]{:S(2)}, u32[]{:S(2)}) %collective-permute-start.17) | collective-permute-done | bytes 262176 | tf_op jit(solution)/shard_map/ppermute | solution.py:75
  55.6 3.4 %copy-done.1 = bf16[1,2,1024,2048]{3,2,1,0:T(8,128)(2,1)S(1)} copy-done((bf16[1,2,1024,2048]{3,2,1,0:T(8,128)(2,1)S(1)}, bf16[1,2,1024,2048]{3,2,1,0:T(8,128)(2,1)}, u32[]{:S(2)}) %copy-start.1) | copy-done | bytes 8388632
  58.9 3.0 %last_products.1 = (f32[4096,128]{1,0:T(8,128)S(1)}, bf16[4096,128]{1,0:T(8,128)(2,1)S(1)}, f32[8,128,1024]{2,1,0:T(8,128)S(1)}, bf16[8,512,256]{2,1,0:T(8,128)(2,1)S(1)}) custom-call(s32[16]{0:T(128)S(1)} %bitcast.28, bf16[2,1024,2048]{2,1,0:T(8,128)(2,1)S(1)} %bitcast.25, f32[8,128,1024]{2,1,0:T(8,128)S(1)} %get-tuple-element.29.early, ...), custom_call_target="tpu_custom_call" | custom-call | flops 2147483648 | bytes 8388608 | tf_op jit(solution)/shard_map/last_products/pallas_call | solution.py:536
  62.0 3.0 %collective-permute-start.18 = (bf16[4096,128]{1,0:T(8,128)(2,1)S(1)}, bf16[4096,128]{1,0:T(8,128)(2,1)S(1)}, u32[]{:S(2)}, u32[]{:S(2)}) collective-permute-start(bf16[4096,128]{1,0:T(8,128)(2,1)S(1)} %get-tuple-element.32), channel_id=1, source_target_pairs={{0,1},{1,0},{2,3},{3,2},{4,5},{5,4},{6,7},{7,6},{8,9},{9,8},{10,11... | collective-permute-start | bytes 3145736 | tf_op jit(solution)/shard_map/ppermute | solution.py:620
  65.0 3.3 %diag_products.1 = (f32[4,72,1024]{2,1,0:T(8,128)S(1)}, bf16[1,4,72,1024]{3,2,1,0:T(8,128)(2,1)S(1)}) custom-call(s32[16]{0:T(128)S(1)} %bitcast.29, f32[2,16]{1,0:T(2,128)S(1)} %copy-done.3, s32[1]{0:T(128)S(6)} %copy.15.slot, s32[512]{0:T(512)S(1)} %pad_add_fusion.owner, f32[8,128,1024]{2,1,0:T(8,128)S(1)} %get-tuple-element.35.refs_0_, ...), custom_call_target="tpu_custom_call" | custom-call | flops 2147483648 | bytes 8388608 | tf_op jit(solution)/shard_map/diag_products/pallas_call | solution.py:550
  68.4 29.9 %collective-permute-done.20.refs_0_ = bf16[4,72,1024]{2,1,0:T(8,128)(2,1)S(1)} collective-permute-done((bf16[4,72,1024]{2,1,0:T(8,128)(2,1)S(1)}, bf16[4,72,1024]{2,1,0:T(8,128)(2,1)S(1)}, u32[]{:S(2)}, u32[]{:S(2)}) %collective-permute-start.20) | collective-permute-done | bytes 589856 | tf_op jit(solution)/shard_map/ppermute | solution.py:571
  98.3 0.1 regroup.1
  98.4 1.5 %collective-permute-start.21 = (bf16[72,1024]{1,0:T(8,128)(2,1)S(1)}, bf16[72,1024]{1,0:T(8,128)(2,1)S(1)}, u32[]{:S(2)}, u32[]{:S(2)}) collective-permute-start(bf16[72,1024]{1,0:T(8,128)(2,1)S(1)} %get-tuple-element.41), channel_id=1, source_target_pairs={{0,2},{2,4},{4,6},{6,0},{1,3},{3,5},{5,7},{7,1},{8,10},{10,12},{12... | collective-permute-start | bytes 442376 | tf_op jit(solution)/shard_map/ppermute | solution.py:584
  100.0 1.3 %collective-permute-start.22 = (bf16[72,1024]{1,0:T(8,128)(2,1)S(1)}, bf16[72,1024]{1,0:T(8,128)(2,1)S(1)}, u32[]{:S(2)}, u32[]{:S(2)}) collective-permute-start(bf16[72,1024]{1,0:T(8,128)(2,1)S(1)} %get-tuple-element.42), channel_id=1, source_target_pairs={{0,4},{2,6},{4,0},{6,2},{1,5},{3,7},{5,1},{7,3},{8,12},{10,14},{12... | collective-permute-start | bytes 442376 | tf_op jit(solution)/shard_map/ppermute | solution.py:584
  101.3 2.7 %collective-permute-start.23 = (bf16[72,1024]{1,0:T(8,128)(2,1)S(1)}, bf16[72,1024]{1,0:T(8,128)(2,1)S(1)}, u32[]{:S(2)}, u32[]{:S(2)}) collective-permute-start(bf16[72,1024]{1,0:T(8,128)(2,1)S(1)} %get-tuple-element.43), channel_id=1, source_target_pairs={{0,6},{2,0},{4,2},{6,4},{1,7},{3,1},{5,3},{7,5},{8,14},{10,8},{12,... | collective-permute-start | bytes 442376 | tf_op jit(solution)/shard_map/ppermute | solution.py:584
  104.0 2.4 %collective-permute-done.21.refs_0_ = bf16[72,1024]{1,0:T(8,128)(2,1)S(1)} collective-permute-done((bf16[72,1024]{1,0:T(8,128)(2,1)S(1)}, bf16[72,1024]{1,0:T(8,128)(2,1)S(1)}, u32[]{:S(2)}, u32[]{:S(2)}) %collective-permute-start.21) | collective-permute-done | bytes 147488 | tf_op jit(solution)/shard_map/ppermute | solution.py:584
  106.4 4.0 %collective-permute-done.22.refs_1_ = bf16[72,1024]{1,0:T(8,128)(2,1)S(1)} collective-permute-done((bf16[72,1024]{1,0:T(8,128)(2,1)S(1)}, bf16[72,1024]{1,0:T(8,128)(2,1)S(1)}, u32[]{:S(2)}, u32[]{:S(2)}) %collective-permute-start.22) | collective-permute-done | bytes 147488 | tf_op jit(solution)/shard_map/ppermute | solution.py:584
  110.5 1.4 %finish.1 = (f32[512,128]{1,0:T(8,128)}, f32[288,128]{1,0:T(8,128)S(1)}) custom-call(f32[2,16]{1,0:T(2,128)S(1)} %copy-done.3, s32[1]{0:T(128)S(6)} %copy.15.slot, f32[512,128]{1,0:T(8,128)S(1)} %bitcast.26, f32[72,1024]{1,0:T(8,128)S(1)} %get-tuple-element.40.own, bf16[72,1024]{1,0:T(8,128)(2,1)S(1)} %collective-permute-done.21.refs_0_, ...), custom_call_target="tpu_custom_call" | custom-call | tf_op jit(solution)/shard_map/finish/pallas_call | solution.py:587
  111.8 1.5 %collective-permute-start.25 = (f32[288,128]{1,0:T(8,128)S(1)}, f32[288,128]{1,0:T(8,128)S(1)}, u32[]{:S(2)}, u32[]{:S(2)}) collective-permute-start(f32[288,128]{1,0:T(8,128)S(1)} %get-tuple-element.45.refs_0_), channel_id=1, source_target_pairs={{0,16},{8,24},{16,0},{24,8},{1,17},{9,25},{17,1},{25,9},{2,18},{10... | collective-permute-start | bytes 442376 | tf_op jit(solution)/shard_map/ppermute | solution.py:601
  113.3 0.4 collective-permute-start.26
  113.7 4.9 %collective-permute-done.25.refs_2_ = f32[288,128]{1,0:T(8,128)S(1)} collective-permute-done((f32[288,128]{1,0:T(8,128)S(1)}, f32[288,128]{1,0:T(8,128)S(1)}, u32[]{:S(2)}, u32[]{:S(2)}) %collective-permute-start.25) | collective-permute-done | bytes 147488 | tf_op jit(solution)/shard_map/ppermute | solution.py:601
  118.6 2.2 %collective-permute-done.26.refs_3_ = f32[288,128]{1,0:T(8,128)S(1)} collective-permute-done((f32[288,128]{1,0:T(8,128)S(1)}, f32[288,128]{1,0:T(8,128)S(1)}, u32[]{:S(2)}, u32[]{:S(2)}) %collective-permute-start.26) | collective-permute-done | bytes 147488 | tf_op jit(solution)/shard_map/ppermute | solution.py:601
  120.8 0.7 density.1
  121.5 1.8 %join_columns.1 = f32[4096,128]{1,0:T(8,128)} custom-call(f32[4096,128]{1,0:T(8,128)S(1)} %get-tuple-element.31.keep, bf16[4096,128]{1,0:T(8,128)(2,1)S(1)} %collective-permute-done.18.refs_0_), custom_call_target="tpu_custom_call" | custom-call | tf_op jit(solution)/shard_map/join_columns/pallas_call | solution.py:632
  (34 shorter events, 0.3 us)
Async XLA Ops:
  1.7 10.6 %collective-permute-start.2 = (bf16[128,1024]{1,0:T(8,128)(2,1)S(1)}, bf16[128,1024]{1,0:T(8,128)(2,1)S(1)}, u32[]{:S(2)}, u32[]{:S(2)}) collective-permute-start(bf16[128,1024]{1,0:T(8,128)(2,1)S(1)} %get-tuple-element.53.refs_0_), channel_id=1, source_target_pairs={{2,4},{4,2},{3,5},{5,3},{10,12},{12,10},{11,13},{13,11},{18,20},{2... | collective-permute-start | bytes 786440 | tf_op jit(solution)/shard_map/ppermute | solution.py:48
  2.4 13.3 %collective-permute-start.6 = (bf16[128,1024]{1,0:T(8,128)(2,1)S(1)}, bf16[128,1024]{1,0:T(8,128)(2,1)S(1)}, u32[]{:S(2)}, u32[]{:S(2)}) collective-permute-start(bf16[128,1024]{1,0:T(8,128)(2,1)S(1)} %get-tuple-element.53.refs_0_), channel_id=1, source_target_pairs={{0,2},{2,0},{4,6},{6,4},{1,3},{3,1},{5,7},{7,5},{8,10},{10,8},{12,... | collective-permute-start | bytes 786440 | tf_op jit(solution)/shard_map/ppermute | solution.py:48
  8.3 8.1 %collective-permute-start = (bf16[128,1024]{1,0:T(8,128)(2,1)S(1)}, bf16[128,1024]{1,0:T(8,128)(2,1)S(1)}, u32[]{:S(2)}, u32[]{:S(2)}) collective-permute-start(bf16[128,1024]{1,0:T(8,128)(2,1)S(1)} %get-tuple-element.53.refs_0_), channel_id=1, source_target_pairs={{0,1},{1,0},{2,3},{3,2},{4,5},{5,4},{6,7},{7,6},{8,9},{9,8},{10,11... | collective-permute-start | bytes 786440 | tf_op jit(solution)/shard_map/ppermute | solution.py:75
  9.8 8.3 %collective-permute-start.4 = (bf16[128,1024]{1,0:T(8,128)(2,1)S(1)}, bf16[128,1024]{1,0:T(8,128)(2,1)S(1)}, u32[]{:S(2)}, u32[]{:S(2)}) collective-permute-start(bf16[128,1024]{1,0:T(8,128)(2,1)S(1)} %get-tuple-element.52.refs_1_), channel_id=1, source_target_pairs={{2,4},{4,2},{3,5},{5,3},{10,12},{12,10},{11,13},{13,11},{18,20},{2... | collective-permute-start | bytes 786440 | tf_op jit(solution)/shard_map/ppermute | solution.py:48
  10.5 10.9 %collective-permute-start.10 = (bf16[128,1024]{1,0:T(8,128)(2,1)S(1)}, bf16[128,1024]{1,0:T(8,128)(2,1)S(1)}, u32[]{:S(2)}, u32[]{:S(2)}) collective-permute-start(bf16[128,1024]{1,0:T(8,128)(2,1)S(1)} %get-tuple-element.52.refs_1_), channel_id=1, source_target_pairs={{0,2},{2,0},{4,6},{6,4},{1,3},{3,1},{5,7},{7,5},{8,10},{10,8},{12,... | collective-permute-start | bytes 786440 | tf_op jit(solution)/shard_map/ppermute | solution.py:48
  12.3 14.4 %collective-permute-start.3 = (bf16[128,1024]{1,0:T(8,128)(2,1)S(1)}, bf16[128,1024]{1,0:T(8,128)(2,1)S(1)}, u32[]{:S(2)}, u32[]{:S(2)}) collective-permute-start(bf16[128,1024]{1,0:T(8,128)(2,1)S(1)} %collective-permute-done.2), channel_id=1, source_target_pairs={{0,2},{2,0},{4,6},{6,4},{1,3},{3,1},{5,7},{7,5},{8,10},{10,8},{12,... | collective-permute-start | bytes 786440 | tf_op jit(solution)/shard_map/ppermute | solution.py:48
  15.7 12.5 %collective-permute-start.14 = (bf16[128,1024]{1,0:T(8,128)(2,1)S(1)}, bf16[128,1024]{1,0:T(8,128)(2,1)S(1)}, u32[]{:S(2)}, u32[]{:S(2)}) collective-permute-start(bf16[128,1024]{1,0:T(8,128)(2,1)S(1)} %collective-permute-done.6.refs_0_), channel_id=1, source_target_pairs={{2,4},{4,2},{3,5},{5,3},{10,12},{12,10},{11,13},{13,11},{18,20},{2... | collective-permute-start | bytes 786440 | tf_op jit(solution)/shard_map/ppermute | solution.py:48
  16.4 13.9 %collective-permute-start.7 = (bf16[128,1024]{1,0:T(8,128)(2,1)S(1)}, bf16[128,1024]{1,0:T(8,128)(2,1)S(1)}, u32[]{:S(2)}, u32[]{:S(2)}) collective-permute-start(bf16[128,1024]{1,0:T(8,128)(2,1)S(1)} %collective-permute-done.6.refs_0_), channel_id=1, source_target_pairs={{0,1},{1,0},{2,3},{3,2},{4,5},{5,4},{6,7},{7,6},{8,9},{9,8},{10,11... | collective-permute-start | bytes 786440 | tf_op jit(solution)/shard_map/ppermute | solution.py:75
  18.1 14.2 %collective-permute-start.5 = (bf16[128,1024]{1,0:T(8,128)(2,1)S(1)}, bf16[128,1024]{1,0:T(8,128)(2,1)S(1)}, u32[]{:S(2)}, u32[]{:S(2)}) collective-permute-start(bf16[128,1024]{1,0:T(8,128)(2,1)S(1)} %collective-permute-done.4), channel_id=1, source_target_pairs={{0,2},{2,0},{4,6},{6,4},{1,3},{3,1},{5,7},{7,5},{8,10},{10,8},{12,... | collective-permute-start | bytes 786440 | tf_op jit(solution)/shard_map/ppermute | solution.py:48
  21.4 12.4 %collective-permute-start.11 = (bf16[128,1024]{1,0:T(8,128)(2,1)S(1)}, bf16[128,1024]{1,0:T(8,128)(2,1)S(1)}, u32[]{:S(2)}, u32[]{:S(2)}) collective-permute-start(bf16[128,1024]{1,0:T(8,128)(2,1)S(1)} %collective-permute-done.10.refs_1_), channel_id=1, source_target_pairs={{2,4},{4,2},{3,5},{5,3},{10,12},{12,10},{11,13},{13,11},{18,20},{2... | collective-permute-start | bytes 786440 | tf_op jit(solution)/shard_map/ppermute | solution.py:48
  22.1 0.7 copy-start.4
  22.8 7.5 %copy-start.6 = (s32[256,1]{0,1:T(1,128)S(1)}, s32[256,1]{0,1:T(1,128)}, u32[]{:S(2)}) copy-start(s32[256,1]{0,1:T(1,128)} %param.11) | copy-start | bytes 3076
  26.7 9.2 %collective-permute-start.1 = (bf16[128,1024]{1,0:T(8,128)(2,1)S(1)}, bf16[128,1024]{1,0:T(8,128)(2,1)S(1)}, u32[]{:S(2)}, u32[]{:S(2)}) collective-permute-start(bf16[128,1024]{1,0:T(8,128)(2,1)S(1)} %get-tuple-element.52.refs_1_), channel_id=1, source_target_pairs={{0,1},{1,0},{2,3},{3,2},{4,5},{5,4},{6,7},{7,6},{8,9},{9,8},{10,11... | collective-permute-start | bytes 786440 | tf_op jit(solution)/shard_map/ppermute | solution.py:75
  28.2 9.7 %collective-permute-start.15 = (bf16[128,1024]{1,0:T(8,128)(2,1)S(1)}, bf16[128,1024]{1,0:T(8,128)(2,1)S(1)}, u32[]{:S(2)}, u32[]{:S(2)}) collective-permute-start(bf16[128,1024]{1,0:T(8,128)(2,1)S(1)} %collective-permute-done.14), channel_id=1, source_target_pairs={{0,2},{2,0},{4,6},{6,4},{1,3},{3,1},{5,7},{7,5},{8,10},{10,8},{12,... | collective-permute-start | bytes 786440 | tf_op jit(solution)/shard_map/ppermute | solution.py:48
  30.3 23.3 %collective-permute-start.19 = (s32[256]{0:T(256)S(1)}, s32[256]{0:T(256)S(1)}, u32[]{:S(2)}, u32[]{:S(2)}) collective-permute-start(s32[256]{0:T(256)S(1)} %bitcast.32), channel_id=1, source_target_pairs={{0,1},{1,0},{2,3},{3,2},{4,5},{5,4},{6,7},{7,6},{8,9},{9,8},{10,11... | collective-permute-start | bytes 3080 | tf_op jit(solution)/shard_map/ppermute | solution.py:482
  32.3 11.7 %collective-permute-start.8 = (bf16[128,1024]{1,0:T(8,128)(2,1)S(1)}, bf16[128,1024]{1,0:T(8,128)(2,1)S(1)}, u32[]{:S(2)}, u32[]{:S(2)}) collective-permute-start(bf16[128,1024]{1,0:T(8,128)(2,1)S(1)} %broadcast_select_fusion.3.refs_4_), channel_id=1, source_target_pairs={{0,1},{1,0},{2,3},{3,2},{4,5},{5,4},{6,7},{7,6},{8,9},{9,8},{10,11... | collective-permute-start | bytes 786440 | tf_op jit(solution)/shard_map/ppermute | solution.py:75
  33.8 8.6 %collective-permute-start.12 = (bf16[128,1024]{1,0:T(8,128)(2,1)S(1)}, bf16[128,1024]{1,0:T(8,128)(2,1)S(1)}, u32[]{:S(2)}, u32[]{:S(2)}) collective-permute-start(bf16[128,1024]{1,0:T(8,128)(2,1)S(1)} %collective-permute-done.11), channel_id=1, source_target_pairs={{0,2},{2,0},{4,6},{6,4},{1,3},{3,1},{5,7},{7,5},{8,10},{10,8},{12,... | collective-permute-start | bytes 786440 | tf_op jit(solution)/shard_map/ppermute | solution.py:48
  35.9 11.2 %collective-permute-start.9 = (bf16[128,1024]{1,0:T(8,128)(2,1)S(1)}, bf16[128,1024]{1,0:T(8,128)(2,1)S(1)}, u32[]{:S(2)}, u32[]{:S(2)}) collective-permute-start(bf16[128,1024]{1,0:T(8,128)(2,1)S(1)} %broadcast_select_fusion.2.refs_5_), channel_id=1, source_target_pairs={{0,1},{1,0},{2,3},{3,2},{4,5},{5,4},{6,7},{7,6},{8,9},{9,8},{10,11... | collective-permute-start | bytes 786440 | tf_op jit(solution)/shard_map/ppermute | solution.py:75
  38.0 15.6 %collective-permute-start.16 = (bf16[128,1024]{1,0:T(8,128)(2,1)S(1)}, bf16[128,1024]{1,0:T(8,128)(2,1)S(1)}, u32[]{:S(2)}, u32[]{:S(2)}) collective-permute-start(bf16[128,1024]{1,0:T(8,128)(2,1)S(1)} %broadcast_select_fusion.1.refs_4_), channel_id=1, source_target_pairs={{0,1},{1,0},{2,3},{3,2},{4,5},{5,4},{6,7},{7,6},{8,9},{9,8},{10,11... | collective-permute-start | bytes 786440 | tf_op jit(solution)/shard_map/ppermute | solution.py:75
  42.5 13.1 %collective-permute-start.17 = (bf16[128,1024]{1,0:T(8,128)(2,1)S(1)}, bf16[128,1024]{1,0:T(8,128)(2,1)S(1)}, u32[]{:S(2)}, u32[]{:S(2)}) collective-permute-start(bf16[128,1024]{1,0:T(8,128)(2,1)S(1)} %broadcast_select_fusion.refs_5_), channel_id=1, source_target_pairs={{0,1},{1,0},{2,3},{3,2},{4,5},{5,4},{6,7},{7,6},{8,9},{9,8},{10,11... | collective-permute-start | bytes 786440 | tf_op jit(solution)/shard_map/ppermute | solution.py:75
  44.0 11.5 %collective-permute-start.13 = (bf16[128,1024]{1,0:T(8,128)(2,1)S(1)}, bf16[128,1024]{1,0:T(8,128)(2,1)S(1)}, u32[]{:S(2)}, u32[]{:S(2)}) collective-permute-start(bf16[128,1024]{1,0:T(8,128)(2,1)S(1)} %collective-permute-done.1.refs_3_), channel_id=1, source_target_pairs={{0,2},{2,0},{4,6},{6,4},{1,3},{3,1},{5,7},{7,5},{8,10},{10,8},{12,... | collective-permute-start | bytes 786440 | tf_op jit(solution)/shard_map/ppermute | solution.py:72
  47.1 3.4 %copy-start = (bf16[1,2,1024,2048]{3,2,1,0:T(8,128)(2,1)S(1)}, bf16[1,2,1024,2048]{3,2,1,0:T(8,128)(2,1)}, u32[]{:S(2)}) copy-start(bf16[1,2,1024,2048]{3,2,1,0:T(8,128)(2,1)} %param.7) | copy-start | bytes 25165828
  50.5 5.1 %copy-start.5 = (s32[1,16]{1,0:T(1,128)S(1)}, s32[1,16]{1,0:T(1,128)}, u32[]{:S(2)}) copy-start(s32[1,16]{1,0:T(1,128)} %param.10) | copy-start | bytes 196
  53.6 11.4 %copy-start.3 = (f32[2,16]{1,0:T(2,128)S(1)}, f32[2,16]{1,0:T(2,128)}, u32[]{:S(2)}) copy-start(f32[2,16]{1,0:T(2,128)} %table.3) | copy-start | bytes 388
  55.6 3.4 %copy-start.1 = (bf16[1,2,1024,2048]{3,2,1,0:T(8,128)(2,1)S(1)}, bf16[1,2,1024,2048]{3,2,1,0:T(8,128)(2,1)}, u32[]{:S(2)}) copy-start(bf16[1,2,1024,2048]{3,2,1,0:T(8,128)(2,1)} %param.7) | copy-start | bytes 25165828
  62.0 59.5 %collective-permute-start.18 = (bf16[4096,128]{1,0:T(8,128)(2,1)S(1)}, bf16[4096,128]{1,0:T(8,128)(2,1)S(1)}, u32[]{:S(2)}, u32[]{:S(2)}) collective-permute-start(bf16[4096,128]{1,0:T(8,128)(2,1)S(1)} %get-tuple-element.32), channel_id=1, source_target_pairs={{0,1},{1,0},{2,3},{3,2},{4,5},{5,4},{6,7},{7,6},{8,9},{9,8},{10,11... | collective-permute-start | bytes 3145736 | tf_op jit(solution)/shard_map/ppermute | solution.py:620
  65.0 45.4 %copy-start.2 = (f32[64,1,1,2,512]{4,3,2,1,0:T(2,128)S(1)}, f32[64,1,1,2,512]{4,3,2,1,0:T(2,128)}, u32[]{:S(2)}) copy-start(f32[64,1,1,2,512]{4,3,2,1,0:T(2,128)} %param.9) | copy-start | bytes 786436
  68.3 30.0 %collective-permute-start.20 = (bf16[4,72,1024]{2,1,0:T(8,128)(2,1)S(1)}, bf16[4,72,1024]{2,1,0:T(8,128)(2,1)S(1)}, u32[]{:S(2)}, u32[]{:S(2)}) collective-permute-start(bf16[4,72,1024]{2,1,0:T(8,128)(2,1)S(1)} %bitcast.30), channel_id=1, source_target_pairs={{0,1},{1,0},{2,3},{3,2},{4,5},{5,4},{6,7},{7,6},{8,9},{9,8},{10,11... | collective-permute-start | bytes 1769480 | tf_op jit(solution)/shard_map/ppermute | solution.py:571
  98.4 8.0 %collective-permute-start.21 = (bf16[72,1024]{1,0:T(8,128)(2,1)S(1)}, bf16[72,1024]{1,0:T(8,128)(2,1)S(1)}, u32[]{:S(2)}, u32[]{:S(2)}) collective-permute-start(bf16[72,1024]{1,0:T(8,128)(2,1)S(1)} %get-tuple-element.41), channel_id=1, source_target_pairs={{0,2},{2,4},{4,6},{6,0},{1,3},{3,5},{5,7},{7,1},{8,10},{10,12},{12... | collective-permute-start | bytes 442376 | tf_op jit(solution)/shard_map/ppermute | solution.py:584
  100.0 10.5 %collective-permute-start.22 = (bf16[72,1024]{1,0:T(8,128)(2,1)S(1)}, bf16[72,1024]{1,0:T(8,128)(2,1)S(1)}, u32[]{:S(2)}, u32[]{:S(2)}) collective-permute-start(bf16[72,1024]{1,0:T(8,128)(2,1)S(1)} %get-tuple-element.42), channel_id=1, source_target_pairs={{0,4},{2,6},{4,0},{6,2},{1,5},{3,7},{5,1},{7,3},{8,12},{10,14},{12... | collective-permute-start | bytes 442376 | tf_op jit(solution)/shard_map/ppermute | solution.py:584
  101.3 9.2 %collective-permute-start.23 = (bf16[72,1024]{1,0:T(8,128)(2,1)S(1)}, bf16[72,1024]{1,0:T(8,128)(2,1)S(1)}, u32[]{:S(2)}, u32[]{:S(2)}) collective-permute-start(bf16[72,1024]{1,0:T(8,128)(2,1)S(1)} %get-tuple-element.43), channel_id=1, source_target_pairs={{0,6},{2,0},{4,2},{6,4},{1,7},{3,1},{5,3},{7,5},{8,14},{10,8},{12,... | collective-permute-start | bytes 442376 | tf_op jit(solution)/shard_map/ppermute | solution.py:584
  111.8 1.9 %collective-permute-start.24 = (f32[288,128]{1,0:T(8,128)S(1)}, f32[288,128]{1,0:T(8,128)S(1)}, u32[]{:S(2)}, u32[]{:S(2)}) collective-permute-start(f32[288,128]{1,0:T(8,128)S(1)} %get-tuple-element.45.refs_0_), channel_id=1, source_target_pairs={{0,8},{8,0},{16,24},{24,16},{1,9},{9,1},{17,25},{25,17},{2,10},{10... | collective-permute-start | bytes 442376 | tf_op jit(solution)/shard_map/ppermute | solution.py:601
  111.8 6.7 %collective-permute-start.25 = (f32[288,128]{1,0:T(8,128)S(1)}, f32[288,128]{1,0:T(8,128)S(1)}, u32[]{:S(2)}, u32[]{:S(2)}) collective-permute-start(f32[288,128]{1,0:T(8,128)S(1)} %get-tuple-element.45.refs_0_), channel_id=1, source_target_pairs={{0,16},{8,24},{16,0},{24,8},{1,17},{9,25},{17,1},{25,9},{2,18},{10... | collective-permute-start | bytes 442376 | tf_op jit(solution)/shard_map/ppermute | solution.py:601
  113.3 7.5 %collective-permute-start.26 = (f32[288,128]{1,0:T(8,128)S(1)}, f32[288,128]{1,0:T(8,128)S(1)}, u32[]{:S(2)}, u32[]{:S(2)}) collective-permute-start(f32[288,128]{1,0:T(8,128)S(1)} %get-tuple-element.45.refs_0_), channel_id=1, source_target_pairs={{0,24},{8,16},{16,8},{24,0},{1,25},{9,17},{17,9},{25,1},{2,26},{10... | collective-permute-start | bytes 442376 | tf_op jit(solution)/shard_map/ppermute | solution.py:601

commit v8 on v7

--- a/solution.py
+++ b/solution.py
@@ -12,7 +12,6 @@
 BR = 8
 BC = 128
 MIB = 1 << 20
-SPLIT = (4,)
 
 
 def shift_pairs(rows, cols, step, valid):
@@ -232,27 +231,57 @@
 
 
 def last_kernel(sources, stages, rows, cols, ancestors, inverse, early, *refs):
-    keep, *sends, total, turned, full, acc, leaving = refs[-(6 + len(SPLIT)) :]
-    pieces = refs[: -(6 + len(SPLIT))]
+    total, turned, full, acc = refs[-4:]
+    pieces = refs[:-4]
     each = len(pieces) // len(stages)
     half = acc.shape[1] // 2
-    across = half // BC
-    row_blocks = early.shape[0]
-    own_blocks = row_blocks // cols
-    r = lax.axis_index("row")
-    c = lax.axis_index("col")
     for n, stage in enumerate(stages):
         fill(full, pieces[n * each : (n + 1) * each], sources, stage, cols)
     counts = counts_of(ancestors, inverse, rows, cols)
-    row_first = counts[4]
+
+    def store(i, real, imag):
+        total[i, :, :half] = real
+        total[i, :, half:] = imag
+
+    add_products(sources, stages, ancestors, inverse, early, full, acc, counts, store)
+    turn_blocks(sources, stages, ancestors, full, counts, turned)
+
+
+def lay_kernel(cols, ancestors, total, keep, send, leaving):
+    row_blocks, _, wide = total.shape
+    half = wide // 2
+    across = half // BC
+    own_blocks = row_blocks // cols
     size = BS * 2 * across
+    r = lax.axis_index("row")
+    c = lax.axis_index("col")
 
     for n in range(row_blocks):
+        slot = jnp.int32(0)
         listed = False
         for k in range(ancestors.shape[0]):
+            slot = slot + jnp.logical_and(
+                ancestors[k] >= r * row_blocks, ancestors[k] < r * row_blocks + n
+            ).astype(jnp.int32)
             listed = jnp.logical_or(listed, ancestors[k] == r * row_blocks + n)
         turn = lax.rem(n // own_blocks - c + cols, cols)
         within = n % own_blocks * size
+        start = pl.multiple_of((turn - 1) * keep.shape[0] + within, size)
+
+        def lay(target, start):
+            for j in range(across):
+                for m in range(2):
+                    first = m * half + j * BC
+                    rows_of = pl.ds(start + 2 * j + m, BS, stride=2 * across)
+                    target[rows_of, :] = -total[slot, :, first : first + BC]
+
+        @pl.when(jnp.logical_and(listed, turn == 0))
+        def _():
+            lay(keep, within)
+
+        @pl.when(jnp.logical_and(listed, turn > 0))
+        def _():
+            lay(leaving, start)
 
         @pl.when(jnp.logical_and(jnp.logical_not(listed), turn == 0))
         def _():
@@ -260,41 +289,9 @@
 
         @pl.when(jnp.logical_and(jnp.logical_not(listed), turn > 0))
         def _():
-            start = pl.multiple_of((turn - 1) * keep.shape[0] + within, size)
             leaving[pl.ds(start, size), :] = jnp.zeros((size, BC), jnp.float32)
 
-
-    def store(i, real, imag):
-        total[i, :, :half] = real
-        total[i, :, half:] = imag
-        block = ancestors[row_first + i] - r * row_blocks
-        within = lax.rem(block, own_blocks) * (BS * 2 * across)
-        turn = lax.rem(block // own_blocks - c + cols, cols)
-
-        def lay(target, start):
-            for j in range(across):
-                for n, value in enumerate((real, imag)):
-                    rows_of = pl.ds(start + 2 * j + n, BS, stride=2 * across)
-                    target[rows_of, :] = -value[:, j * BC : (j + 1) * BC]
-
-        @pl.when(turn == 0)
-        def _():
-            lay(keep, within)
-
-        @pl.when(turn > 0)
-        def _():
-            lay(leaving, (turn - 1) * keep.shape[0] + within)
-
-    add_products(sources, stages, ancestors, inverse, early, full, acc, counts, store)
-    turn_blocks(sources, stages, ancestors, full, counts, turned)
-    height = keep.shape[0]
-    for step in range(cols - 1):
-        first = 0
-        for send, share in zip(sends, SPLIT):
-            size = height * share // sum(SPLIT)
-            value = leaving[step * height + first : step * height + first + size, :]
-            send[step * size : (step + 1) * size, :] = value.astype(send.dtype)
-            first += size
+    send[...] = leaving[...].astype(send.dtype)
 
 
 def diag_kernel(
@@ -389,21 +386,12 @@
         out[...] = values[0]
 
 
-def join_kernel(steps, keep, *refs):
-    out = refs[-1]
-    block = pl.program_id(0)
-    first = 0
-    for n, share in enumerate(SPLIT):
-        arrived = refs[n * steps : (n + 1) * steps]
-
-        @pl.when(jnp.logical_and(block >= first, block < first + share))
-        def _():
-            value = keep[...]
-            for ref in arrived:
-                value = value + ref[...].astype(jnp.float32)
-            out[...] = value
-
-        first += share
+def join_kernel(keep, *refs):
+    *arrived, out = refs
+    value = keep[...]
+    for ref in arrived:
+        value = value + ref[...].astype(jnp.float32)
+    out[...] = value
 
 
 def halves(value):
@@ -532,16 +520,13 @@
     all_pieces = [piece for stage in last for piece in stages[stage]]
     others = max(1, cols - 1)
     laid_rows = rows_here * wide // BC
-    sizes = [laid_rows * share // sum(SPLIT) for share in SPLIT]
-    keep, *sends, total, turned = pl.pallas_call(
+    total, turned = pl.pallas_call(
         functools.partial(last_kernel, sources, last, rows, cols),
-        out_shape=(jax.ShapeDtypeStruct((laid_rows, BC), jnp.float32),)
-        + tuple(jax.ShapeDtypeStruct((others * size, BC), jnp.bfloat16) for size in sizes)
-        + (row_products, turned_blocks),
+        out_shape=(row_products, turned_blocks),
         in_specs=[smem] + [vmem] * (2 + len(all_pieces)),
-        out_specs=(vmem,) * (3 + len(SPLIT)),
-        scratch_shapes=scratch + [pltpu.VMEM((others * laid_rows, BC), jnp.float32)],
-        compiler_params=pltpu.CompilerParams(vmem_limit_bytes=28 * MIB),
+        out_specs=(vmem,) * 2,
+        scratch_shapes=scratch,
+        compiler_params=pltpu.CompilerParams(vmem_limit_bytes=24 * MIB),
         cost_estimate=pl.CostEstimate(
             flops=products // 2, bytes_accessed=8 * MIB, transcendentals=0
         ),
@@ -614,26 +599,29 @@
     )(*messages)
     density_diag = laid_density.reshape(part, 1, half)
 
-    parts = []
-    for send, size in zip(sends, sizes):
-        parts += [
-            lax.ppermute(send[(step - 1) * size : step * size], grid, everyone_pairs[step])
-            for step in range(1, cols)
-        ]
-    block = laid_rows // sum(SPLIT)
-    specs = [pl.BlockSpec((block, BC), lambda i: (i, 0))]
-    first = 0
-    for share in SPLIT:
-        spec = pl.BlockSpec(
-            (block, BC), lambda i, f=first, n=share: (jnp.clip(i - f, 0, n - 1), 0)
-        )
-        specs += [spec] * (cols - 1)
-        first += share
+    keep, send = pl.pallas_call(
+        functools.partial(lay_kernel, cols),
+        out_shape=(
+            jax.ShapeDtypeStruct((laid_rows, BC), jnp.float32),
+            jax.ShapeDtypeStruct((others * laid_rows, BC), jnp.bfloat16),
+        ),
+        in_specs=[smem, vmem],
+        out_specs=(vmem,) * 2,
+        scratch_shapes=[pltpu.VMEM((others * laid_rows, BC), jnp.float32)],
+        compiler_params=pltpu.CompilerParams(vmem_limit_bytes=20 * MIB),
+        cost_estimate=pl.CostEstimate(flops=0, bytes_accessed=8 * MIB, transcendentals=0),
+        name="lay_columns",
+    )(ancestors[0], total)
+    parts = [
+        lax.ppermute(send[(step - 1) * laid_rows : step * laid_rows], grid, everyone_pairs[step])
+        for step in range(1, cols)
+    ]
+    block = laid_rows // 4
     column = pl.pallas_call(
-        functools.partial(join_kernel, cols - 1),
-        grid=(sum(SPLIT),),
+        join_kernel,
+        grid=(4,),
         out_shape=jax.ShapeDtypeStruct((laid_rows, BC), jnp.float32),
-        in_specs=specs,
+        in_specs=[pl.BlockSpec((block, BC), lambda i: (i, 0))] * cols,
         out_specs=pl.BlockSpec((block, BC), lambda i: (i, 0)),
         compiler_params=pltpu.CompilerParams(vmem_limit_bytes=16 * MIB),
         name="join_columns",

time: 124 us -> 121 us (0.976)
  local copies, waits for them, and re-layouts: 8.5 us -> 5.11 us
    unnamed x14 -> x12, local copies, waits for them, and re-layouts: 7.43 us -> 4.05 us
    pallas_call x1 -> x2, Pallas kernels: 1.85 us -> 3.52 us  [the longest x1 1.85 us: compute(): pl.pallas_call(join_kernel, grid=(4,), out_shape=jax.ShapeDtypeStruct((la...]
where the time goes in v8:
time: 121 us
  waiting for transfers between devices  54.6 us (45%)
  starting transfers between devices  44.1 us (36%)
  Pallas kernels  15.3 us (13%)
  local copies, waits for them, and re-layouts  5.11 us (4%)
  between operations  1.48 us (1%)
    ppermute x1, waiting for transfers between devices, compute(): lax.ppermute(diag_send[step - 1], grid, everyone_pairs[step])  29.9 us
    ppermute x10, starting transfers between devices, hop(): return lax.ppermute(value, 'row', pairs)  21.2 us
    ppermute x7, starting transfers between devices, gather_stages(): last = lax.ppermute(leaving, grid, pairs)  9.98 us
    ppermute x10, waiting for transfers between devices, hop(): return lax.ppermute(value, 'row', pairs)  7.91 us
    ppermute x3, waiting for transfers between devices, compute(): lax.ppermute(message, 'pole', [(i, i ^ step) for i in range(poles)])  7.09 us
    ppermute x3, waiting for transfers between devices, compute(): lax.ppermute(rounded[step - 1], 'row', [(i, (i + step) % rows) for i in r...  6.43 us
    ppermute x3, starting transfers between devices, compute(): lax.ppermute(rounded[step - 1], 'row', [(i, (i + step) % rows) for i in r...  5.59 us
    unnamed x12, local copies, waits for them, and re-layouts  4.05 us
  transfers between devices with their start and end apart: 27, of which 11 were waited for; matrix products, arithmetic and copies ran while one was open for 0% of the time, Pallas kernels for 8%

profile of v8, /device:TPU:0, one launch (start us, length us, event | category | flops | bytes accessed | tf_op | source)
XLA Modules:
  0.0 120.8 jit_solution(6939350531635409039)
XLA Ops:
  0.6 1.1 slice_bitcast_fusion
  1.7 0.7 collective-permute-start.2
  2.4 5.9 %collective-permute-start.6 = (bf16[128,1024]{1,0:T(8,128)(2,1)S(1)}, bf16[128,1024]{1,0:T(8,128)(2,1)S(1)}, u32[]{:S(2)}, u32[]{:S(2)}) collective-permute-start(bf16[128,1024]{1,0:T(8,128)(2,1)S(1)} %get-tuple-element.53.refs_0_), channel_id=1, source_target_pairs={{0,2},{2,0},{4,6},{6,4},{1,3},{3,1},{5,7},{7,5},{8,10},{10,8},{12,... | collective-permute-start | bytes 786440 | tf_op jit(solution)/shard_map/ppermute | solution.py:47
  8.3 1.5 %collective-permute-start = (bf16[128,1024]{1,0:T(8,128)(2,1)S(1)}, bf16[128,1024]{1,0:T(8,128)(2,1)S(1)}, u32[]{:S(2)}, u32[]{:S(2)}) collective-permute-start(bf16[128,1024]{1,0:T(8,128)(2,1)S(1)} %get-tuple-element.53.refs_0_), channel_id=1, source_target_pairs={{0,1},{1,0},{2,3},{3,2},{4,5},{5,4},{6,7},{7,6},{8,9},{9,8},{10,11... | collective-permute-start | bytes 786440 | tf_op jit(solution)/shard_map/ppermute | solution.py:74
  9.8 0.7 collective-permute-start.4
  10.5 1.8 %collective-permute-start.10 = (bf16[128,1024]{1,0:T(8,128)(2,1)S(1)}, bf16[128,1024]{1,0:T(8,128)(2,1)S(1)}, u32[]{:S(2)}, u32[]{:S(2)}) collective-permute-start(bf16[128,1024]{1,0:T(8,128)(2,1)S(1)} %get-tuple-element.52.refs_1_), channel_id=1, source_target_pairs={{0,2},{2,0},{4,6},{6,4},{1,3},{3,1},{5,7},{7,5},{8,10},{10,8},{12,... | collective-permute-start | bytes 786440 | tf_op jit(solution)/shard_map/ppermute | solution.py:47
  12.3 3.4 %collective-permute-start.3 = (bf16[128,1024]{1,0:T(8,128)(2,1)S(1)}, bf16[128,1024]{1,0:T(8,128)(2,1)S(1)}, u32[]{:S(2)}, u32[]{:S(2)}) collective-permute-start(bf16[128,1024]{1,0:T(8,128)(2,1)S(1)} %collective-permute-done.2), channel_id=1, source_target_pairs={{0,2},{2,0},{4,6},{6,4},{1,3},{3,1},{5,7},{7,5},{8,10},{10,8},{12,... | collective-permute-start | bytes 786440 | tf_op jit(solution)/shard_map/ppermute | solution.py:47
  15.7 0.7 collective-permute-start.14
  16.4 1.7 %collective-permute-start.7 = (bf16[128,1024]{1,0:T(8,128)(2,1)S(1)}, bf16[128,1024]{1,0:T(8,128)(2,1)S(1)}, u32[]{:S(2)}, u32[]{:S(2)}) collective-permute-start(bf16[128,1024]{1,0:T(8,128)(2,1)S(1)} %collective-permute-done.6.refs_0_), channel_id=1, source_target_pairs={{0,1},{1,0},{2,3},{3,2},{4,5},{5,4},{6,7},{7,6},{8,9},{9,8},{10,11... | collective-permute-start | bytes 786440 | tf_op jit(solution)/shard_map/ppermute | solution.py:74
  18.1 3.3 %collective-permute-start.5 = (bf16[128,1024]{1,0:T(8,128)(2,1)S(1)}, bf16[128,1024]{1,0:T(8,128)(2,1)S(1)}, u32[]{:S(2)}, u32[]{:S(2)}) collective-permute-start(bf16[128,1024]{1,0:T(8,128)(2,1)S(1)} %collective-permute-done.4), channel_id=1, source_target_pairs={{0,2},{2,0},{4,6},{6,4},{1,3},{3,1},{5,7},{7,5},{8,10},{10,8},{12,... | collective-permute-start | bytes 786440 | tf_op jit(solution)/shard_map/ppermute | solution.py:47
  21.4 0.7 collective-permute-start.11
  22.1 0.6 copy-done.2
  22.8 1.1 list_blocks.1.ancestors
  24.6 2.1 %collective-permute-done.3 = bf16[128,1024]{1,0:T(8,128)(2,1)S(1)} collective-permute-done((bf16[128,1024]{1,0:T(8,128)(2,1)S(1)}, bf16[128,1024]{1,0:T(8,128)(2,1)S(1)}, u32[]{:S(2)}, u32[]{:S(2)}) %collective-permute-start.3) | collective-permute-done | bytes 262176 | tf_op jit(solution)/shard_map/ppermute | solution.py:47
  26.7 1.5 %collective-permute-start.1 = (bf16[128,1024]{1,0:T(8,128)(2,1)S(1)}, bf16[128,1024]{1,0:T(8,128)(2,1)S(1)}, u32[]{:S(2)}, u32[]{:S(2)}) collective-permute-start(bf16[128,1024]{1,0:T(8,128)(2,1)S(1)} %get-tuple-element.52.refs_1_), channel_id=1, source_target_pairs={{0,1},{1,0},{2,3},{3,2},{4,5},{5,4},{6,7},{7,6},{8,9},{9,8},{10,11... | collective-permute-start | bytes 786440 | tf_op jit(solution)/shard_map/ppermute | solution.py:74
  28.2 2.0 %collective-permute-start.15 = (bf16[128,1024]{1,0:T(8,128)(2,1)S(1)}, bf16[128,1024]{1,0:T(8,128)(2,1)S(1)}, u32[]{:S(2)}, u32[]{:S(2)}) collective-permute-start(bf16[128,1024]{1,0:T(8,128)(2,1)S(1)} %collective-permute-done.14), channel_id=1, source_target_pairs={{0,2},{2,0},{4,6},{6,4},{1,3},{3,1},{5,7},{7,5},{8,10},{10,8},{12,... | collective-permute-start | bytes 786440 | tf_op jit(solution)/shard_map/ppermute | solution.py:47
  30.3 0.6 collective-permute-start.19
  30.9 1.4 %collective-permute-done.5 = bf16[128,1024]{1,0:T(8,128)(2,1)S(1)} collective-permute-done((bf16[128,1024]{1,0:T(8,128)(2,1)S(1)}, bf16[128,1024]{1,0:T(8,128)(2,1)S(1)}, u32[]{:S(2)}, u32[]{:S(2)}) %collective-permute-start.5) | collective-permute-done | bytes 262176 | tf_op jit(solution)/shard_map/ppermute | solution.py:47
  32.3 1.5 %collective-permute-start.8 = (bf16[128,1024]{1,0:T(8,128)(2,1)S(1)}, bf16[128,1024]{1,0:T(8,128)(2,1)S(1)}, u32[]{:S(2)}, u32[]{:S(2)}) collective-permute-start(bf16[128,1024]{1,0:T(8,128)(2,1)S(1)} %broadcast_select_fusion.3.refs_4_), channel_id=1, source_target_pairs={{0,1},{1,0},{2,3},{3,2},{4,5},{5,4},{6,7},{7,6},{8,9},{9,8},{10,11... | collective-permute-start | bytes 786440 | tf_op jit(solution)/shard_map/ppermute | solution.py:74
  33.8 2.0 %collective-permute-start.12 = (bf16[128,1024]{1,0:T(8,128)(2,1)S(1)}, bf16[128,1024]{1,0:T(8,128)(2,1)S(1)}, u32[]{:S(2)}, u32[]{:S(2)}) collective-permute-start(bf16[128,1024]{1,0:T(8,128)(2,1)S(1)} %collective-permute-done.11), channel_id=1, source_target_pairs={{0,2},{2,0},{4,6},{6,4},{1,3},{3,1},{5,7},{7,5},{8,10},{10,8},{12,... | collective-permute-start | bytes 786440 | tf_op jit(solution)/shard_map/ppermute | solution.py:47
  35.9 0.6 collective-permute-start.9
  36.5 1.5 %collective-permute-done.15 = bf16[128,1024]{1,0:T(8,128)(2,1)S(1)} collective-permute-done((bf16[128,1024]{1,0:T(8,128)(2,1)S(1)}, bf16[128,1024]{1,0:T(8,128)(2,1)S(1)}, u32[]{:S(2)}, u32[]{:S(2)}) %collective-permute-start.15) | collective-permute-done | bytes 262176 | tf_op jit(solution)/shard_map/ppermute | solution.py:47
  38.0 1.6 %collective-permute-start.16 = (bf16[128,1024]{1,0:T(8,128)(2,1)S(1)}, bf16[128,1024]{1,0:T(8,128)(2,1)S(1)}, u32[]{:S(2)}, u32[]{:S(2)}) collective-permute-start(bf16[128,1024]{1,0:T(8,128)(2,1)S(1)} %broadcast_select_fusion.1.refs_4_), channel_id=1, source_target_pairs={{0,1},{1,0},{2,3},{3,2},{4,5},{5,4},{6,7},{7,6},{8,9},{9,8},{10,11... | collective-permute-start | bytes 786440 | tf_op jit(solution)/shard_map/ppermute | solution.py:74
  39.6 2.9 %collective-permute-done.12 = bf16[128,1024]{1,0:T(8,128)(2,1)S(1)} collective-permute-done((bf16[128,1024]{1,0:T(8,128)(2,1)S(1)}, bf16[128,1024]{1,0:T(8,128)(2,1)S(1)}, u32[]{:S(2)}, u32[]{:S(2)}) %collective-permute-start.12) | collective-permute-done | bytes 262176 | tf_op jit(solution)/shard_map/ppermute | solution.py:47
  42.5 1.6 %collective-permute-start.17 = (bf16[128,1024]{1,0:T(8,128)(2,1)S(1)}, bf16[128,1024]{1,0:T(8,128)(2,1)S(1)}, u32[]{:S(2)}, u32[]{:S(2)}) collective-permute-start(bf16[128,1024]{1,0:T(8,128)(2,1)S(1)} %broadcast_select_fusion.refs_5_), channel_id=1, source_target_pairs={{0,1},{1,0},{2,3},{3,2},{4,5},{5,4},{6,7},{7,6},{8,9},{9,8},{10,11... | collective-permute-start | bytes 786440 | tf_op jit(solution)/shard_map/ppermute | solution.py:74
  44.0 1.7 %collective-permute-start.13 = (bf16[128,1024]{1,0:T(8,128)(2,1)S(1)}, bf16[128,1024]{1,0:T(8,128)(2,1)S(1)}, u32[]{:S(2)}, u32[]{:S(2)}) collective-permute-start(bf16[128,1024]{1,0:T(8,128)(2,1)S(1)} %collective-permute-done.1.refs_3_), channel_id=1, source_target_pairs={{0,2},{2,0},{4,6},{6,4},{1,3},{3,1},{5,7},{7,5},{8,10},{10,8},{12,... | collective-permute-start | bytes 786440 | tf_op jit(solution)/shard_map/ppermute | solution.py:71
  45.8 1.3 %collective-permute-done.9.refs_7_ = bf16[128,1024]{1,0:T(8,128)(2,1)S(1)} collective-permute-done((bf16[128,1024]{1,0:T(8,128)(2,1)S(1)}, bf16[128,1024]{1,0:T(8,128)(2,1)S(1)}, u32[]{:S(2)}, u32[]{:S(2)}) %collective-permute-start.9) | collective-permute-done | bytes 262176 | tf_op jit(solution)/shard_map/ppermute | solution.py:74
  47.1 3.4 %copy-done = bf16[1,2,1024,2048]{3,2,1,0:T(8,128)(2,1)S(1)} copy-done((bf16[1,2,1024,2048]{3,2,1,0:T(8,128)(2,1)S(1)}, bf16[1,2,1024,2048]{3,2,1,0:T(8,128)(2,1)}, u32[]{:S(2)}) %copy-start) | copy-done | bytes 8388632
  50.5 3.0 %early_products.1 = (f32[8,128,1024]{2,1,0:T(8,128)S(1)}, bf16[8,512,256]{2,1,0:T(8,128)(2,1)S(1)}) custom-call(s32[16]{0:T(128)S(1)} %list_blocks.1.ancestors, bf16[2,1024,2048]{2,1,0:T(8,128)(2,1)S(1)} %bitcast.24, bf16[128,1024]{1,0:T(8,128)(2,1)S(1)} %get-tuple-element.53.refs_0_, bf16[128,1024]{1,0:T(8,128)(2,1)S(1)} %get-tuple-element.52.refs_1_, ...), custom_call_target="tpu_custom_call" | custom-call | flops 2147483648 | bytes 4194304 | tf_op jit(solution)/shard_map/early_products/pallas_call | solution.py:507
  53.6 2.0 %collective-permute-done.17.refs_7_ = bf16[128,1024]{1,0:T(8,128)(2,1)S(1)} collective-permute-done((bf16[128,1024]{1,0:T(8,128)(2,1)S(1)}, bf16[128,1024]{1,0:T(8,128)(2,1)S(1)}, u32[]{:S(2)}, u32[]{:S(2)}) %collective-permute-start.17) | collective-permute-done | bytes 262176 | tf_op jit(solution)/shard_map/ppermute | solution.py:74
  55.6 2.2 %last_products.1 = (f32[8,128,1024]{2,1,0:T(8,128)S(1)}, bf16[8,512,256]{2,1,0:T(8,128)(2,1)S(1)}) custom-call(s32[16]{0:T(128)S(1)} %bitcast.28, bf16[2,1024,2048]{2,1,0:T(8,128)(2,1)S(1)} %bitcast.25, f32[8,128,1024]{2,1,0:T(8,128)S(1)} %get-tuple-element.29.early, bf16[128,1024]{1,0:T(8,128)(2,1)S(1)} %collective-permute-done.6.refs_0_, ...), custom_call_target="tpu_custom_call" | custom-call | flops 2147483648 | bytes 8388608 | tf_op jit(solution)/shard_map/last_products/pallas_call | solution.py:523
  57.7 1.7 %lay_columns.1 = (f32[4096,128]{1,0:T(8,128)S(1)}, bf16[4096,128]{1,0:T(8,128)(2,1)S(1)}) custom-call(s32[16]{0:T(128)S(1)} %bitcast.29, f32[8,128,1024]{2,1,0:T(8,128)S(1)} %get-tuple-element.31.total.refs_0_), custom_call_target="tpu_custom_call" | custom-call | bytes 8388608 | tf_op jit(solution)/shard_map/lay_columns/pallas_call | solution.py:602
  59.4 3.0 %collective-permute-start.18 = (bf16[4096,128]{1,0:T(8,128)(2,1)S(1)}, bf16[4096,128]{1,0:T(8,128)(2,1)S(1)}, u32[]{:S(2)}, u32[]{:S(2)}) collective-permute-start(bf16[4096,128]{1,0:T(8,128)(2,1)S(1)} %get-tuple-element.33), channel_id=1, source_target_pairs={{0,1},{1,0},{2,3},{3,2},{4,5},{5,4},{6,7},{7,6},{8,9},{9,8},{10,11... | collective-permute-start | bytes 3145736 | tf_op jit(solution)/shard_map/ppermute | solution.py:616
  62.4 3.3 %diag_products.1 = (f32[4,72,1024]{2,1,0:T(8,128)S(1)}, bf16[1,4,72,1024]{3,2,1,0:T(8,128)(2,1)S(1)}) custom-call(s32[16]{0:T(128)S(1)} %bitcast.30, f32[2,16]{1,0:T(2,128)S(1)} %copy-done.4, s32[1]{0:T(128)S(6)} %copy.15.slot, s32[512]{0:T(512)S(1)} %pad_add_fusion.owner, f32[8,128,1024]{2,1,0:T(8,128)S(1)} %get-tuple-element.31.total.refs_0_, ...), custom_call_target="tpu_custom_call" | custom-call | flops 2147483648 | bytes 8388608 | tf_op jit(solution)/shard_map/diag_products/pallas_call | solution.py:535
  65.8 29.9 %collective-permute-done.20.refs_0_ = bf16[4,72,1024]{2,1,0:T(8,128)(2,1)S(1)} collective-permute-done((bf16[4,72,1024]{2,1,0:T(8,128)(2,1)S(1)}, bf16[4,72,1024]{2,1,0:T(8,128)(2,1)S(1)}, u32[]{:S(2)}, u32[]{:S(2)}) %collective-permute-start.20) | collective-permute-done | bytes 589856 | tf_op jit(solution)/shard_map/ppermute | solution.py:556
  95.7 0.1 regroup.1
  95.9 1.5 %collective-permute-start.21 = (bf16[72,1024]{1,0:T(8,128)(2,1)S(1)}, bf16[72,1024]{1,0:T(8,128)(2,1)S(1)}, u32[]{:S(2)}, u32[]{:S(2)}) collective-permute-start(bf16[72,1024]{1,0:T(8,128)(2,1)S(1)} %get-tuple-element.41), channel_id=1, source_target_pairs={{0,2},{2,4},{4,6},{6,0},{1,3},{3,5},{5,7},{7,1},{8,10},{10,12},{12... | collective-permute-start | bytes 442376 | tf_op jit(solution)/shard_map/ppermute | solution.py:569
  97.4 1.3 %collective-permute-start.22 = (bf16[72,1024]{1,0:T(8,128)(2,1)S(1)}, bf16[72,1024]{1,0:T(8,128)(2,1)S(1)}, u32[]{:S(2)}, u32[]{:S(2)}) collective-permute-start(bf16[72,1024]{1,0:T(8,128)(2,1)S(1)} %get-tuple-element.42), channel_id=1, source_target_pairs={{0,4},{2,6},{4,0},{6,2},{1,5},{3,7},{5,1},{7,3},{8,12},{10,14},{12... | collective-permute-start | bytes 442376 | tf_op jit(solution)/shard_map/ppermute | solution.py:569
  98.7 2.8 %collective-permute-start.23 = (bf16[72,1024]{1,0:T(8,128)(2,1)S(1)}, bf16[72,1024]{1,0:T(8,128)(2,1)S(1)}, u32[]{:S(2)}, u32[]{:S(2)}) collective-permute-start(bf16[72,1024]{1,0:T(8,128)(2,1)S(1)} %get-tuple-element.43), channel_id=1, source_target_pairs={{0,6},{2,0},{4,2},{6,4},{1,7},{3,1},{5,3},{7,5},{8,14},{10,8},{12,... | collective-permute-start | bytes 442376 | tf_op jit(solution)/shard_map/ppermute | solution.py:569
  101.5 2.4 %collective-permute-done.21.refs_0_ = bf16[72,1024]{1,0:T(8,128)(2,1)S(1)} collective-permute-done((bf16[72,1024]{1,0:T(8,128)(2,1)S(1)}, bf16[72,1024]{1,0:T(8,128)(2,1)S(1)}, u32[]{:S(2)}, u32[]{:S(2)}) %collective-permute-start.21) | collective-permute-done | bytes 147488 | tf_op jit(solution)/shard_map/ppermute | solution.py:569
  103.8 4.1 %collective-permute-done.22.refs_1_ = bf16[72,1024]{1,0:T(8,128)(2,1)S(1)} collective-permute-done((bf16[72,1024]{1,0:T(8,128)(2,1)S(1)}, bf16[72,1024]{1,0:T(8,128)(2,1)S(1)}, u32[]{:S(2)}, u32[]{:S(2)}) %collective-permute-start.22) | collective-permute-done | bytes 147488 | tf_op jit(solution)/shard_map/ppermute | solution.py:569
  107.9 1.4 %finish.1 = (f32[512,128]{1,0:T(8,128)}, f32[288,128]{1,0:T(8,128)S(1)}) custom-call(f32[2,16]{1,0:T(2,128)S(1)} %copy-done.4, s32[1]{0:T(128)S(6)} %copy.15.slot, f32[512,128]{1,0:T(8,128)S(1)} %bitcast.26, f32[72,1024]{1,0:T(8,128)S(1)} %get-tuple-element.40.own, bf16[72,1024]{1,0:T(8,128)(2,1)S(1)} %collective-permute-done.21.refs_0_, ...), custom_call_target="tpu_custom_call" | custom-call | tf_op jit(solution)/shard_map/finish/pallas_call | solution.py:572
  109.3 1.5 %collective-permute-start.25 = (f32[288,128]{1,0:T(8,128)S(1)}, f32[288,128]{1,0:T(8,128)S(1)}, u32[]{:S(2)}, u32[]{:S(2)}) collective-permute-start(f32[288,128]{1,0:T(8,128)S(1)} %get-tuple-element.45.refs_0_), channel_id=1, source_target_pairs={{0,16},{8,24},{16,0},{24,8},{1,17},{9,25},{17,1},{25,9},{2,18},{10... | collective-permute-start | bytes 442376 | tf_op jit(solution)/shard_map/ppermute | solution.py:586
  110.8 0.4 collective-permute-start.26
  111.1 4.9 %collective-permute-done.25.refs_2_ = f32[288,128]{1,0:T(8,128)S(1)} collective-permute-done((f32[288,128]{1,0:T(8,128)S(1)}, f32[288,128]{1,0:T(8,128)S(1)}, u32[]{:S(2)}, u32[]{:S(2)}) %collective-permute-start.25) | collective-permute-done | bytes 147488 | tf_op jit(solution)/shard_map/ppermute | solution.py:586
  116.0 2.2 %collective-permute-done.26.refs_3_ = f32[288,128]{1,0:T(8,128)S(1)} collective-permute-done((f32[288,128]{1,0:T(8,128)S(1)}, f32[288,128]{1,0:T(8,128)S(1)}, u32[]{:S(2)}, u32[]{:S(2)}) %collective-permute-start.26) | collective-permute-done | bytes 147488 | tf_op jit(solution)/shard_map/ppermute | solution.py:586
  118.2 0.7 density.1
  118.9 1.8 %join_columns.1 = f32[4096,128]{1,0:T(8,128)} custom-call(f32[4096,128]{1,0:T(8,128)S(1)} %get-tuple-element.32.keep, bf16[4096,128]{1,0:T(8,128)(2,1)S(1)} %collective-permute-done.18.refs_0_), custom_call_target="tpu_custom_call" | custom-call | tf_op jit(solution)/shard_map/join_columns/pallas_call | solution.py:620
  (33 shorter events, 0.3 us)
Async XLA Ops:
  1.7 10.6 %collective-permute-start.2 = (bf16[128,1024]{1,0:T(8,128)(2,1)S(1)}, bf16[128,1024]{1,0:T(8,128)(2,1)S(1)}, u32[]{:S(2)}, u32[]{:S(2)}) collective-permute-start(bf16[128,1024]{1,0:T(8,128)(2,1)S(1)} %get-tuple-element.53.refs_0_), channel_id=1, source_target_pairs={{2,4},{4,2},{3,5},{5,3},{10,12},{12,10},{11,13},{13,11},{18,20},{2... | collective-permute-start | bytes 786440 | tf_op jit(solution)/shard_map/ppermute | solution.py:47
  2.4 13.3 %collective-permute-start.6 = (bf16[128,1024]{1,0:T(8,128)(2,1)S(1)}, bf16[128,1024]{1,0:T(8,128)(2,1)S(1)}, u32[]{:S(2)}, u32[]{:S(2)}) collective-permute-start(bf16[128,1024]{1,0:T(8,128)(2,1)S(1)} %get-tuple-element.53.refs_0_), channel_id=1, source_target_pairs={{0,2},{2,0},{4,6},{6,4},{1,3},{3,1},{5,7},{7,5},{8,10},{10,8},{12,... | collective-permute-start | bytes 786440 | tf_op jit(solution)/shard_map/ppermute | solution.py:47
  8.3 8.1 %collective-permute-start = (bf16[128,1024]{1,0:T(8,128)(2,1)S(1)}, bf16[128,1024]{1,0:T(8,128)(2,1)S(1)}, u32[]{:S(2)}, u32[]{:S(2)}) collective-permute-start(bf16[128,1024]{1,0:T(8,128)(2,1)S(1)} %get-tuple-element.53.refs_0_), channel_id=1, source_target_pairs={{0,1},{1,0},{2,3},{3,2},{4,5},{5,4},{6,7},{7,6},{8,9},{9,8},{10,11... | collective-permute-start | bytes 786440 | tf_op jit(solution)/shard_map/ppermute | solution.py:74
  9.8 8.3 %collective-permute-start.4 = (bf16[128,1024]{1,0:T(8,128)(2,1)S(1)}, bf16[128,1024]{1,0:T(8,128)(2,1)S(1)}, u32[]{:S(2)}, u32[]{:S(2)}) collective-permute-start(bf16[128,1024]{1,0:T(8,128)(2,1)S(1)} %get-tuple-element.52.refs_1_), channel_id=1, source_target_pairs={{2,4},{4,2},{3,5},{5,3},{10,12},{12,10},{11,13},{13,11},{18,20},{2... | collective-permute-start | bytes 786440 | tf_op jit(solution)/shard_map/ppermute | solution.py:47
  10.5 10.9 %collective-permute-start.10 = (bf16[128,1024]{1,0:T(8,128)(2,1)S(1)}, bf16[128,1024]{1,0:T(8,128)(2,1)S(1)}, u32[]{:S(2)}, u32[]{:S(2)}) collective-permute-start(bf16[128,1024]{1,0:T(8,128)(2,1)S(1)} %get-tuple-element.52.refs_1_), channel_id=1, source_target_pairs={{0,2},{2,0},{4,6},{6,4},{1,3},{3,1},{5,7},{7,5},{8,10},{10,8},{12,... | collective-permute-start | bytes 786440 | tf_op jit(solution)/shard_map/ppermute | solution.py:47
  12.3 14.4 %collective-permute-start.3 = (bf16[128,1024]{1,0:T(8,128)(2,1)S(1)}, bf16[128,1024]{1,0:T(8,128)(2,1)S(1)}, u32[]{:S(2)}, u32[]{:S(2)}) collective-permute-start(bf16[128,1024]{1,0:T(8,128)(2,1)S(1)} %collective-permute-done.2), channel_id=1, source_target_pairs={{0,2},{2,0},{4,6},{6,4},{1,3},{3,1},{5,7},{7,5},{8,10},{10,8},{12,... | collective-permute-start | bytes 786440 | tf_op jit(solution)/shard_map/ppermute | solution.py:47
  15.7 12.5 %collective-permute-start.14 = (bf16[128,1024]{1,0:T(8,128)(2,1)S(1)}, bf16[128,1024]{1,0:T(8,128)(2,1)S(1)}, u32[]{:S(2)}, u32[]{:S(2)}) collective-permute-start(bf16[128,1024]{1,0:T(8,128)(2,1)S(1)} %collective-permute-done.6.refs_0_), channel_id=1, source_target_pairs={{2,4},{4,2},{3,5},{5,3},{10,12},{12,10},{11,13},{13,11},{18,20},{2... | collective-permute-start | bytes 786440 | tf_op jit(solution)/shard_map/ppermute | solution.py:47
  16.4 13.9 %collective-permute-start.7 = (bf16[128,1024]{1,0:T(8,128)(2,1)S(1)}, bf16[128,1024]{1,0:T(8,128)(2,1)S(1)}, u32[]{:S(2)}, u32[]{:S(2)}) collective-permute-start(bf16[128,1024]{1,0:T(8,128)(2,1)S(1)} %collective-permute-done.6.refs_0_), channel_id=1, source_target_pairs={{0,1},{1,0},{2,3},{3,2},{4,5},{5,4},{6,7},{7,6},{8,9},{9,8},{10,11... | collective-permute-start | bytes 786440 | tf_op jit(solution)/shard_map/ppermute | solution.py:74
  18.1 14.2 %collective-permute-start.5 = (bf16[128,1024]{1,0:T(8,128)(2,1)S(1)}, bf16[128,1024]{1,0:T(8,128)(2,1)S(1)}, u32[]{:S(2)}, u32[]{:S(2)}) collective-permute-start(bf16[128,1024]{1,0:T(8,128)(2,1)S(1)} %collective-permute-done.4), channel_id=1, source_target_pairs={{0,2},{2,0},{4,6},{6,4},{1,3},{3,1},{5,7},{7,5},{8,10},{10,8},{12,... | collective-permute-start | bytes 786440 | tf_op jit(solution)/shard_map/ppermute | solution.py:47
  21.4 12.4 %collective-permute-start.11 = (bf16[128,1024]{1,0:T(8,128)(2,1)S(1)}, bf16[128,1024]{1,0:T(8,128)(2,1)S(1)}, u32[]{:S(2)}, u32[]{:S(2)}) collective-permute-start(bf16[128,1024]{1,0:T(8,128)(2,1)S(1)} %collective-permute-done.10.refs_1_), channel_id=1, source_target_pairs={{2,4},{4,2},{3,5},{5,3},{10,12},{12,10},{11,13},{13,11},{18,20},{2... | collective-permute-start | bytes 786440 | tf_op jit(solution)/shard_map/ppermute | solution.py:47
  22.1 0.7 copy-start.2
  22.8 7.5 %copy-start.5 = (s32[256,1]{0,1:T(1,128)S(1)}, s32[256,1]{0,1:T(1,128)}, u32[]{:S(2)}) copy-start(s32[256,1]{0,1:T(1,128)} %param.11) | copy-start | bytes 3076
  26.7 9.2 %collective-permute-start.1 = (bf16[128,1024]{1,0:T(8,128)(2,1)S(1)}, bf16[128,1024]{1,0:T(8,128)(2,1)S(1)}, u32[]{:S(2)}, u32[]{:S(2)}) collective-permute-start(bf16[128,1024]{1,0:T(8,128)(2,1)S(1)} %get-tuple-element.52.refs_1_), channel_id=1, source_target_pairs={{0,1},{1,0},{2,3},{3,2},{4,5},{5,4},{6,7},{7,6},{8,9},{9,8},{10,11... | collective-permute-start | bytes 786440 | tf_op jit(solution)/shard_map/ppermute | solution.py:74
  28.2 9.7 %collective-permute-start.15 = (bf16[128,1024]{1,0:T(8,128)(2,1)S(1)}, bf16[128,1024]{1,0:T(8,128)(2,1)S(1)}, u32[]{:S(2)}, u32[]{:S(2)}) collective-permute-start(bf16[128,1024]{1,0:T(8,128)(2,1)S(1)} %collective-permute-done.14), channel_id=1, source_target_pairs={{0,2},{2,0},{4,6},{6,4},{1,3},{3,1},{5,7},{7,5},{8,10},{10,8},{12,... | collective-permute-start | bytes 786440 | tf_op jit(solution)/shard_map/ppermute | solution.py:47
  30.3 23.3 %collective-permute-start.19 = (s32[256]{0:T(256)S(1)}, s32[256]{0:T(256)S(1)}, u32[]{:S(2)}, u32[]{:S(2)}) collective-permute-start(s32[256]{0:T(256)S(1)} %bitcast.33), channel_id=1, source_target_pairs={{0,1},{1,0},{2,3},{3,2},{4,5},{5,4},{6,7},{7,6},{8,9},{9,8},{10,11... | collective-permute-start | bytes 3080 | tf_op jit(solution)/shard_map/ppermute | solution.py:470
  32.3 11.7 %collective-permute-start.8 = (bf16[128,1024]{1,0:T(8,128)(2,1)S(1)}, bf16[128,1024]{1,0:T(8,128)(2,1)S(1)}, u32[]{:S(2)}, u32[]{:S(2)}) collective-permute-start(bf16[128,1024]{1,0:T(8,128)(2,1)S(1)} %broadcast_select_fusion.3.refs_4_), channel_id=1, source_target_pairs={{0,1},{1,0},{2,3},{3,2},{4,5},{5,4},{6,7},{7,6},{8,9},{9,8},{10,11... | collective-permute-start | bytes 786440 | tf_op jit(solution)/shard_map/ppermute | solution.py:74
  33.8 8.6 %collective-permute-start.12 = (bf16[128,1024]{1,0:T(8,128)(2,1)S(1)}, bf16[128,1024]{1,0:T(8,128)(2,1)S(1)}, u32[]{:S(2)}, u32[]{:S(2)}) collective-permute-start(bf16[128,1024]{1,0:T(8,128)(2,1)S(1)} %collective-permute-done.11), channel_id=1, source_target_pairs={{0,2},{2,0},{4,6},{6,4},{1,3},{3,1},{5,7},{7,5},{8,10},{10,8},{12,... | collective-permute-start | bytes 786440 | tf_op jit(solution)/shard_map/ppermute | solution.py:47
  35.9 11.2 %collective-permute-start.9 = (bf16[128,1024]{1,0:T(8,128)(2,1)S(1)}, bf16[128,1024]{1,0:T(8,128)(2,1)S(1)}, u32[]{:S(2)}, u32[]{:S(2)}) collective-permute-start(bf16[128,1024]{1,0:T(8,128)(2,1)S(1)} %broadcast_select_fusion.2.refs_5_), channel_id=1, source_target_pairs={{0,1},{1,0},{2,3},{3,2},{4,5},{5,4},{6,7},{7,6},{8,9},{9,8},{10,11... | collective-permute-start | bytes 786440 | tf_op jit(solution)/shard_map/ppermute | solution.py:74
  38.0 15.6 %collective-permute-start.16 = (bf16[128,1024]{1,0:T(8,128)(2,1)S(1)}, bf16[128,1024]{1,0:T(8,128)(2,1)S(1)}, u32[]{:S(2)}, u32[]{:S(2)}) collective-permute-start(bf16[128,1024]{1,0:T(8,128)(2,1)S(1)} %broadcast_select_fusion.1.refs_4_), channel_id=1, source_target_pairs={{0,1},{1,0},{2,3},{3,2},{4,5},{5,4},{6,7},{7,6},{8,9},{9,8},{10,11... | collective-permute-start | bytes 786440 | tf_op jit(solution)/shard_map/ppermute | solution.py:74
  42.5 13.1 %collective-permute-start.17 = (bf16[128,1024]{1,0:T(8,128)(2,1)S(1)}, bf16[128,1024]{1,0:T(8,128)(2,1)S(1)}, u32[]{:S(2)}, u32[]{:S(2)}) collective-permute-start(bf16[128,1024]{1,0:T(8,128)(2,1)S(1)} %broadcast_select_fusion.refs_5_), channel_id=1, source_target_pairs={{0,1},{1,0},{2,3},{3,2},{4,5},{5,4},{6,7},{7,6},{8,9},{9,8},{10,11... | collective-permute-start | bytes 786440 | tf_op jit(solution)/shard_map/ppermute | solution.py:74
  44.0 11.5 %collective-permute-start.13 = (bf16[128,1024]{1,0:T(8,128)(2,1)S(1)}, bf16[128,1024]{1,0:T(8,128)(2,1)S(1)}, u32[]{:S(2)}, u32[]{:S(2)}) collective-permute-start(bf16[128,1024]{1,0:T(8,128)(2,1)S(1)} %collective-permute-done.1.refs_3_), channel_id=1, source_target_pairs={{0,2},{2,0},{4,6},{6,4},{1,3},{3,1},{5,7},{7,5},{8,10},{10,8},{12,... | collective-permute-start | bytes 786440 | tf_op jit(solution)/shard_map/ppermute | solution.py:71
  47.1 3.4 %copy-start = (bf16[1,2,1024,2048]{3,2,1,0:T(8,128)(2,1)S(1)}, bf16[1,2,1024,2048]{3,2,1,0:T(8,128)(2,1)}, u32[]{:S(2)}) copy-start(bf16[1,2,1024,2048]{3,2,1,0:T(8,128)(2,1)} %param.7) | copy-start | bytes 25165828
  50.5 5.1 %copy-start.3 = (s32[1,16]{1,0:T(1,128)S(1)}, s32[1,16]{1,0:T(1,128)}, u32[]{:S(2)}) copy-start(s32[1,16]{1,0:T(1,128)} %param.10) | copy-start | bytes 196
  57.7 4.7 %copy-start.4 = (f32[2,16]{1,0:T(2,128)S(1)}, f32[2,16]{1,0:T(2,128)}, u32[]{:S(2)}) copy-start(f32[2,16]{1,0:T(2,128)} %table.3) | copy-start | bytes 388
  59.4 59.5 %collective-permute-start.18 = (bf16[4096,128]{1,0:T(8,128)(2,1)S(1)}, bf16[4096,128]{1,0:T(8,128)(2,1)S(1)}, u32[]{:S(2)}, u32[]{:S(2)}) collective-permute-start(bf16[4096,128]{1,0:T(8,128)(2,1)S(1)} %get-tuple-element.33), channel_id=1, source_target_pairs={{0,1},{1,0},{2,3},{3,2},{4,5},{5,4},{6,7},{7,6},{8,9},{9,8},{10,11... | collective-permute-start | bytes 3145736 | tf_op jit(solution)/shard_map/ppermute | solution.py:616
  62.4 45.5 %copy-start.1 = (f32[64,1,1,2,512]{4,3,2,1,0:T(2,128)S(1)}, f32[64,1,1,2,512]{4,3,2,1,0:T(2,128)}, u32[]{:S(2)}) copy-start(f32[64,1,1,2,512]{4,3,2,1,0:T(2,128)} %param.9) | copy-start | bytes 786436
  65.7 30.0 %collective-permute-start.20 = (bf16[4,72,1024]{2,1,0:T(8,128)(2,1)S(1)}, bf16[4,72,1024]{2,1,0:T(8,128)(2,1)S(1)}, u32[]{:S(2)}, u32[]{:S(2)}) collective-permute-start(bf16[4,72,1024]{2,1,0:T(8,128)(2,1)S(1)} %bitcast.31), channel_id=1, source_target_pairs={{0,1},{1,0},{2,3},{3,2},{4,5},{5,4},{6,7},{7,6},{8,9},{9,8},{10,11... | collective-permute-start | bytes 1769480 | tf_op jit(solution)/shard_map/ppermute | solution.py:556
  95.9 8.0 %collective-permute-start.21 = (bf16[72,1024]{1,0:T(8,128)(2,1)S(1)}, bf16[72,1024]{1,0:T(8,128)(2,1)S(1)}, u32[]{:S(2)}, u32[]{:S(2)}) collective-permute-start(bf16[72,1024]{1,0:T(8,128)(2,1)S(1)} %get-tuple-element.41), channel_id=1, source_target_pairs={{0,2},{2,4},{4,6},{6,0},{1,3},{3,5},{5,7},{7,1},{8,10},{10,12},{12... | collective-permute-start | bytes 442376 | tf_op jit(solution)/shard_map/ppermute | solution.py:569
  97.4 10.5 %collective-permute-start.22 = (bf16[72,1024]{1,0:T(8,128)(2,1)S(1)}, bf16[72,1024]{1,0:T(8,128)(2,1)S(1)}, u32[]{:S(2)}, u32[]{:S(2)}) collective-permute-start(bf16[72,1024]{1,0:T(8,128)(2,1)S(1)} %get-tuple-element.42), channel_id=1, source_target_pairs={{0,4},{2,6},{4,0},{6,2},{1,5},{3,7},{5,1},{7,3},{8,12},{10,14},{12... | collective-permute-start | bytes 442376 | tf_op jit(solution)/shard_map/ppermute | solution.py:569
  98.7 9.2 %collective-permute-start.23 = (bf16[72,1024]{1,0:T(8,128)(2,1)S(1)}, bf16[72,1024]{1,0:T(8,128)(2,1)S(1)}, u32[]{:S(2)}, u32[]{:S(2)}) collective-permute-start(bf16[72,1024]{1,0:T(8,128)(2,1)S(1)} %get-tuple-element.43), channel_id=1, source_target_pairs={{0,6},{2,0},{4,2},{6,4},{1,7},{3,1},{5,3},{7,5},{8,14},{10,8},{12,... | collective-permute-start | bytes 442376 | tf_op jit(solution)/shard_map/ppermute | solution.py:569
  109.3 1.9 %collective-permute-start.24 = (f32[288,128]{1,0:T(8,128)S(1)}, f32[288,128]{1,0:T(8,128)S(1)}, u32[]{:S(2)}, u32[]{:S(2)}) collective-permute-start(f32[288,128]{1,0:T(8,128)S(1)} %get-tuple-element.45.refs_0_), channel_id=1, source_target_pairs={{0,8},{8,0},{16,24},{24,16},{1,9},{9,1},{17,25},{25,17},{2,10},{10... | collective-permute-start | bytes 442376 | tf_op jit(solution)/shard_map/ppermute | solution.py:586
  109.3 6.7 %collective-permute-start.25 = (f32[288,128]{1,0:T(8,128)S(1)}, f32[288,128]{1,0:T(8,128)S(1)}, u32[]{:S(2)}, u32[]{:S(2)}) collective-permute-start(f32[288,128]{1,0:T(8,128)S(1)} %get-tuple-element.45.refs_0_), channel_id=1, source_target_pairs={{0,16},{8,24},{16,0},{24,8},{1,17},{9,25},{17,1},{25,9},{2,18},{10... | collective-permute-start | bytes 442376 | tf_op jit(solution)/shard_map/ppermute | solution.py:586
  110.8 7.5 %collective-permute-start.26 = (f32[288,128]{1,0:T(8,128)S(1)}, f32[288,128]{1,0:T(8,128)S(1)}, u32[]{:S(2)}, u32[]{:S(2)}) collective-permute-start(f32[288,128]{1,0:T(8,128)S(1)} %get-tuple-element.45.refs_0_), channel_id=1, source_target_pairs={{0,24},{8,16},{16,8},{24,0},{1,25},{9,17},{17,9},{25,1},{2,26},{10... | collective-permute-start | bytes 442376 | tf_op jit(solution)/shard_map/ppermute | solution.py:586

commit v9 on v8

--- a/solution.py
+++ b/solution.py
@@ -295,10 +295,10 @@
 
 
 def diag_kernel(
-    sources, first_stages, poles, rows, cols, row_blocks, ancestors, table, slot, owner, *refs
+    imaginary, sources, first_stages, poles, rows, cols, row_blocks, ancestors, table, slot, owner, *refs
 ):
     total, first_turned, turned, diag_keep, diag_send, diag, tiles = refs
-    half, wide = diag.shape
+    half = diag.shape[1]
     across = half // BC
     own_blocks = row_blocks // cols
     r = lax.axis_index("row")
@@ -312,7 +312,8 @@
 
     row_first = below(r * row_blocks)
     diag[...] = jnp.zeros_like(diag)
-    tiles[...] = jnp.zeros_like(tiles)
+    if imaginary:
+        tiles[...] = jnp.zeros_like(tiles)
     weight_real = table[0, slot[0]]
     weight_imag = table[1, slot[0]]
 
@@ -322,27 +323,22 @@
         imag = total[i, :, half:]
         first = brought(sources, first_stages, rows, ancestors.shape[0], row_first + i)
 
-        @pl.when(first)
-        def _():
-            turned[i] = first_turned[i]
-
-        left = turned[i]
+        left = jnp.where(first, first_turned[i], turned[i])
         real_high = real.astype(jnp.bfloat16)
         imag_high = imag.astype(jnp.bfloat16)
         real_low = (real - real_high.astype(jnp.float32)).astype(jnp.bfloat16)
         imag_low = (imag - imag_high.astype(jnp.float32)).astype(jnp.bfloat16)
-        right = jnp.concatenate(
-            [
-                jnp.concatenate([real_high, imag_high], axis=1),
-                jnp.concatenate([-imag_high, real_high], axis=1),
-                jnp.concatenate([real_low, imag_low], axis=1),
-                jnp.concatenate([-imag_low, real_low], axis=1),
-            ],
-            axis=0,
+        if imaginary:
+            right = [imag_high, real_high, imag_low, real_low]
+        else:
+            right = [real_high, -imag_high, real_low, -imag_low]
+        diag[...] += jnp.dot(
+            jnp.concatenate([left, left], axis=1),
+            jnp.concatenate(right, axis=0),
+            preferred_element_type=jnp.float32,
         )
-        diag[...] += jnp.dot(
-            jnp.concatenate([left, left], axis=1), right, preferred_element_type=jnp.float32
-        )
+        if not imaginary:
+            return
         block = ancestors[row_first + i] - r * row_blocks
         place = block // own_blocks
         mixed = -(weight_real * imag + weight_imag * real)
@@ -362,18 +358,24 @@
             value = diag[pl.ds(pl.multiple_of(place * part, part), part), :]
             if step == 0:
                 diag_keep[row, :part] = value
-                diag_keep[row, part:] = jnp.zeros((BR, wide), jnp.float32)
             else:
                 diag_send[step - 1, row, :part] = value.astype(diag_send.dtype)
-                diag_send[step - 1, row, part:] = jnp.zeros((BR, wide), diag_send.dtype)
-            for pole in range(poles):
+            for pole in range(poles if imaginary else 0):
                 sum_of = tiles[0, pole * rows * cols + place]
                 for j in range(1, across):
                     sum_of = sum_of + tiles[j, pole * rows * cols + place]
+                start, first = band_of(pole, part, half)
                 if step == 0:
-                    diag_keep[row, part:, 2 * pole * BC : (2 * pole + 1) * BC] = sum_of
+                    both = jnp.concatenate([sum_of, jnp.zeros((BR, BC), jnp.float32)], axis=1)
+                    diag_keep[row, start : start + BR, first : first + 2 * BC] = both
                 else:
-                    diag_send[step - 1, row, part:, 2 * pole * BC : 2 * (pole + 1) * BC] = halves(sum_of)
+                    both = halves(sum_of)
+                    diag_send[step - 1, row, start : start + BR, first : first + 2 * BC] = both
+
+
+def band_of(pole, part, half):
+    across = half // (2 * BC)
+    return part + pole // across * BR, pole % across * 2 * BC
 
 
 def density_kernel(split, *refs):
@@ -400,27 +402,31 @@
     return jnp.concatenate([high, low], axis=1)
 
 
-def regroup_kernel(poles, rows, kept, *refs):
+def regroup_kernel(poles, rows, others, real_kept, imag_kept, *refs):
     *rounded, own = refs[-rows:]
-    arrived = refs[:-rows]
+    real_arrived, imag_arrived = refs[:others], refs[others:-rows]
     part = own.shape[0] - BR
+    half = own.shape[1] // 2
     r = lax.axis_index("row")
 
-    def total(row):
+    def total(kept, arrived, row):
         value = kept[row]
         for ref in arrived:
             value = value + ref[row].astype(jnp.float32)
         return value
 
-    own[...] = total(r)
-    for step in range(1, rows):
-        value = total(lax.rem(r + step, rows))
-        out = rounded[step - 1]
-        out[:part] = value[:part].astype(out.dtype)
+    for step in range(rows):
+        row = lax.rem(r + step, rows)
+        out = own if step == 0 else rounded[step - 1]
+        imag = total(imag_kept, imag_arrived, row)
+        out[:part, :half] = total(real_kept, real_arrived, row).astype(out.dtype)
+        out[:part, half:] = imag[:part].astype(out.dtype)
         for pole in range(poles):
-            first = 2 * pole * BC
-            band = value[part:, first : first + BC] + value[part:, first + BC : first + 2 * BC]
-            out[part:, first : first + 2 * BC] = halves(band)
+            start, first = band_of(pole, part, half)
+            band = imag[start : start + BR, first : first + 2 * BC]
+            if step > 0:
+                band = halves(band[:, :BC] + band[:, BC:])
+            out[part:, 2 * pole * BC : 2 * (pole + 1) * BC] = band
 
 
 def finish_kernel(poles, table, slot, laid_dinv, own, *refs):
@@ -532,39 +538,53 @@
         ),
         name="last_products",
     )(ancestors[0], here, early, *all_pieces)
-    diag_keep, diag_send = pl.pallas_call(
-        functools.partial(diag_kernel, sources, groups[0], poles, rows, cols, row_blocks),
-        out_shape=(
-            jax.ShapeDtypeStruct((rows, part + BR, wide), jnp.float32),
-            jax.ShapeDtypeStruct((others, rows, part + BR, wide), jnp.bfloat16),
-        ),
-        in_specs=[smem] * 4 + [vmem] * 3,
-        out_specs=(vmem,) * 2,
-        scratch_shapes=[
-            pltpu.VMEM((half, wide), jnp.float32),
-            pltpu.VMEM((half // BC, tile_count, BR, BC), jnp.float32),
-        ],
-        compiler_params=pltpu.CompilerParams(vmem_limit_bytes=20 * MIB),
-        cost_estimate=pl.CostEstimate(
-            flops=products // 2, bytes_accessed=8 * MIB, transcendentals=0
-        ),
-        name="diag_products",
-    )(ancestors[0], weight_table, pole_slot, jnp.concatenate(late_owners), total, first_turned, turned)
-
     everyone_pairs = [shift_pairs(rows, cols, step, everyone) for step in range(cols)]
-    arrived = [
-        lax.ppermute(diag_send[step - 1], grid, everyone_pairs[step])
-        for step in range(1, cols)
-    ]
+    band_rows = -(-poles * 2 * BC // half) * BR
+    kept, arrived = [], []
+    for imaginary, height in ((False, part), (True, part + band_rows)):
+        diag_keep, diag_send = pl.pallas_call(
+            functools.partial(
+                diag_kernel, imaginary, sources, groups[0], poles, rows, cols, row_blocks
+            ),
+            out_shape=(
+                jax.ShapeDtypeStruct((rows, height, half), jnp.float32),
+                jax.ShapeDtypeStruct((others, rows, height, half), jnp.bfloat16),
+            ),
+            in_specs=[smem] * 4 + [vmem] * 3,
+            out_specs=(vmem,) * 2,
+            scratch_shapes=[
+                pltpu.VMEM((half, half), jnp.float32),
+                pltpu.VMEM((half // BC, tile_count, BR, BC), jnp.float32),
+            ],
+            compiler_params=pltpu.CompilerParams(vmem_limit_bytes=20 * MIB),
+            cost_estimate=pl.CostEstimate(
+                flops=products // 4, bytes_accessed=4 * MIB, transcendentals=0
+            ),
+            name="diag_products",
+        )(
+            ancestors[0],
+            weight_table,
+            pole_slot,
+            jnp.concatenate(late_owners),
+            total,
+            first_turned,
+            turned,
+        )
+        kept.append(diag_keep)
+        arrived += [
+            lax.ppermute(diag_send[step - 1], grid, everyone_pairs[step])
+            for step in range(1, cols)
+        ]
+
     *rounded, own = pl.pallas_call(
-        functools.partial(regroup_kernel, poles, rows),
+        functools.partial(regroup_kernel, poles, rows, cols - 1),
         out_shape=(jax.ShapeDtypeStruct((part + BR, wide), jnp.bfloat16),) * (rows - 1)
         + (jax.ShapeDtypeStruct((part + BR, wide), jnp.float32),),
-        in_specs=[vmem] * (1 + len(arrived)),
+        in_specs=[vmem] * (2 + len(arrived)),
         out_specs=(vmem,) * rows,
         compiler_params=pltpu.CompilerParams(vmem_limit_bytes=16 * MIB),
         name="regroup",
-    )(diag_keep, *arrived)
+    )(*kept, *arrived)
     parts = [
         lax.ppermute(rounded[step - 1], "row", [(i, (i + step) % rows) for i in range(rows)])
         for step in range(1, rows)

time: 121 us -> 130 us (1.074)
  local copies, waits for them, and re-layouts: 5.11 us -> 9.23 us
  waiting for transfers between devices: 54.6 us -> 58.3 us
  Pallas kernels: 15.3 us -> 17.4 us
    ppermute x1 -> x2, waiting for transfers between devices: 29.9 us -> 7.4 us  [compute(): lax.ppermute(diag_send[step - 1], grid, everyone_pairs[step])]
    ppermute x1, waiting for transfers between devices: 0.01 us -> 19.9 us  [compute(): owners.append(lax.ppermute(owner[:, 0], grid, pairs))]
    unnamed x12 -> x27, local copies, waits for them, and re-layouts: 4.05 us -> 8.14 us
    ppermute x7, waiting for transfers between devices: 3.31 us -> 7.33 us  [gather_stages(): last = lax.ppermute(leaving, grid, pairs)]
    ppermute x1 -> x2, starting transfers between devices: 0.11 us -> 2.16 us  [compute(): lax.ppermute(diag_send[step - 1], grid, everyone_pairs[step])]
    ppermute x10, starting transfers between devices: 21.2 us -> 19.7 us  [hop(): return lax.ppermute(value, 'row', pairs)]
    pallas_call x2 -> x3, Pallas kernels: 3.41 us -> 4.43 us  [the longest x2 4.32 us: compute(): pl.pallas_call(functools.partial(diag_kernel, imaginary, sources, groups[...]
  transfers between devices with their start and end apart: 27 -> 28, of which waited for: 11 -> 16; matrix products, arithmetic and copies ran while one was open for 0% -> 0% of each run, Pallas kernels for 8% -> 8%
where the time goes in v9:
time: 130 us
  waiting for transfers between devices  58.3 us (45%)
  starting transfers between devices  43.6 us (34%)
  Pallas kernels  17.4 us (13%)
  local copies, waits for them, and re-layouts  9.23 us (7%)
  between operations  1.5 us (1%)
    ppermute x1, waiting for transfers between devices, compute(): owners.append(lax.ppermute(owner[:, 0], grid, pairs))  19.9 us
    ppermute x10, starting transfers between devices, hop(): return lax.ppermute(value, 'row', pairs)  19.7 us
    ppermute x7, starting transfers between devices, gather_stages(): last = lax.ppermute(leaving, grid, pairs)  9.71 us
    ppermute x10, waiting for transfers between devices, hop(): return lax.ppermute(value, 'row', pairs)  8.95 us
    unnamed x27, local copies, waits for them, and re-layouts  8.14 us
    ppermute x3, waiting for transfers between devices, compute(): lax.ppermute(rounded[step - 1], 'row', [(i, (i + step) % rows) for i in r...  7.57 us
    ppermute x2, waiting for transfers between devices, compute(): lax.ppermute(diag_send[step - 1], grid, everyone_pairs[step])  7.4 us
    ppermute x7, waiting for transfers between devices, gather_stages(): last = lax.ppermute(leaving, grid, pairs)  7.33 us
  transfers between devices with their start and end apart: 28, of which 16 were waited for; matrix products, arithmetic and copies ran while one was open for 0% of the time, Pallas kernels for 8%

profile of v9, /device:TPU:0, one launch (start us, length us, event | category | flops | bytes accessed | tf_op | source)
XLA Modules:
  0.0 130.1 jit_solution(7285207248539919106)
XLA Ops:
  0.6 1.1 slice_bitcast_fusion
  1.7 0.7 collective-permute-start.2
  2.4 5.9 %collective-permute-start.6 = (bf16[128,1024]{1,0:T(8,128)(2,1)S(1)}, bf16[128,1024]{1,0:T(8,128)(2,1)S(1)}, u32[]{:S(2)}, u32[]{:S(2)}) collective-permute-start(bf16[128,1024]{1,0:T(8,128)(2,1)S(1)} %get-tuple-element.57.refs_0_), channel_id=1, source_target_pairs={{0,2},{2,0},{4,6},{6,4},{1,3},{3,1},{5,7},{7,5},{8,10},{10,8},{12,... | collective-permute-start | bytes 786440 | tf_op jit(solution)/shard_map/ppermute | solution.py:47
  8.3 1.5 %collective-permute-start = (bf16[128,1024]{1,0:T(8,128)(2,1)S(1)}, bf16[128,1024]{1,0:T(8,128)(2,1)S(1)}, u32[]{:S(2)}, u32[]{:S(2)}) collective-permute-start(bf16[128,1024]{1,0:T(8,128)(2,1)S(1)} %get-tuple-element.57.refs_0_), channel_id=1, source_target_pairs={{0,1},{1,0},{2,3},{3,2},{4,5},{5,4},{6,7},{7,6},{8,9},{9,8},{10,11... | collective-permute-start | bytes 786440 | tf_op jit(solution)/shard_map/ppermute | solution.py:74
  10.6 4.1 %collective-permute-start.3 = (bf16[128,1024]{1,0:T(8,128)(2,1)S(1)}, bf16[128,1024]{1,0:T(8,128)(2,1)S(1)}, u32[]{:S(2)}, u32[]{:S(2)}) collective-permute-start(bf16[128,1024]{1,0:T(8,128)(2,1)S(1)} %collective-permute-done.2), channel_id=1, source_target_pairs={{0,2},{2,0},{4,6},{6,4},{1,3},{3,1},{5,7},{7,5},{8,10},{10,8},{12,... | collective-permute-start | bytes 786440 | tf_op jit(solution)/shard_map/ppermute | solution.py:47
  14.7 0.8 collective-permute-done.6.refs_0_
  16.2 0.7 copy-done.8
  16.9 1.5 %collective-permute-start.7 = (bf16[128,1024]{1,0:T(8,128)(2,1)S(1)}, bf16[128,1024]{1,0:T(8,128)(2,1)S(1)}, u32[]{:S(2)}, u32[]{:S(2)}) collective-permute-start(bf16[128,1024]{1,0:T(8,128)(2,1)S(1)} %collective-permute-done.6.refs_0_), channel_id=1, source_target_pairs={{0,1},{1,0},{2,3},{3,2},{4,5},{5,4},{6,7},{7,6},{8,9},{9,8},{10,11... | collective-permute-start | bytes 786440 | tf_op jit(solution)/shard_map/ppermute | solution.py:74
  18.4 2.7 %collective-permute-done.10.refs_1_ = bf16[128,1024]{1,0:T(8,128)(2,1)S(1)} collective-permute-done((bf16[128,1024]{1,0:T(8,128)(2,1)S(1)}, bf16[128,1024]{1,0:T(8,128)(2,1)S(1)}, u32[]{:S(2)}, u32[]{:S(2)}) %collective-permute-start.10) | collective-permute-done | bytes 262176 | tf_op jit(solution)/shard_map/ppermute | solution.py:47
  21.8 3.9 %collective-permute-start.5 = (bf16[128,1024]{1,0:T(8,128)(2,1)S(1)}, bf16[128,1024]{1,0:T(8,128)(2,1)S(1)}, u32[]{:S(2)}, u32[]{:S(2)}) collective-permute-start(bf16[128,1024]{1,0:T(8,128)(2,1)S(1)} %collective-permute-done.4), channel_id=1, source_target_pairs={{0,2},{2,0},{4,6},{6,4},{1,3},{3,1},{5,7},{7,5},{8,10},{10,8},{12,... | collective-permute-start | bytes 786440 | tf_op jit(solution)/shard_map/ppermute | solution.py:47
  25.7 1.1 collective-permute-done.3
  26.7 1.5 %collective-permute-start.1 = (bf16[128,1024]{1,0:T(8,128)(2,1)S(1)}, bf16[128,1024]{1,0:T(8,128)(2,1)S(1)}, u32[]{:S(2)}, u32[]{:S(2)}) collective-permute-start(bf16[128,1024]{1,0:T(8,128)(2,1)S(1)} %get-tuple-element.56.refs_1_), channel_id=1, source_target_pairs={{0,1},{1,0},{2,3},{3,2},{4,5},{5,4},{6,7},{7,6},{8,9},{9,8},{10,11... | collective-permute-start | bytes 786440 | tf_op jit(solution)/shard_map/ppermute | solution.py:74
  28.2 2.0 %collective-permute-start.15 = (bf16[128,1024]{1,0:T(8,128)(2,1)S(1)}, bf16[128,1024]{1,0:T(8,128)(2,1)S(1)}, u32[]{:S(2)}, u32[]{:S(2)}) collective-permute-start(bf16[128,1024]{1,0:T(8,128)(2,1)S(1)} %collective-permute-done.14), channel_id=1, source_target_pairs={{0,2},{2,0},{4,6},{6,4},{1,3},{3,1},{5,7},{7,5},{8,10},{10,8},{12,... | collective-permute-start | bytes 786440 | tf_op jit(solution)/shard_map/ppermute | solution.py:47
  30.9 1.0 collective-permute-start.12
  31.9 0.9 collective-permute-done.5
  32.8 3.0 %collective-permute-done.1.refs_3_ = bf16[128,1024]{1,0:T(8,128)(2,1)S(1)} collective-permute-done((bf16[128,1024]{1,0:T(8,128)(2,1)S(1)}, bf16[128,1024]{1,0:T(8,128)(2,1)S(1)}, u32[]{:S(2)}, u32[]{:S(2)}) %collective-permute-start.1) | collective-permute-done | bytes 262176 | tf_op jit(solution)/shard_map/ppermute | solution.py:74
  35.9 1.5 %collective-permute-start.9 = (bf16[128,1024]{1,0:T(8,128)(2,1)S(1)}, bf16[128,1024]{1,0:T(8,128)(2,1)S(1)}, u32[]{:S(2)}, u32[]{:S(2)}) collective-permute-start(bf16[128,1024]{1,0:T(8,128)(2,1)S(1)} %broadcast_select_fusion.2.refs_5_), channel_id=1, source_target_pairs={{0,1},{1,0},{2,3},{3,2},{4,5},{5,4},{6,7},{7,6},{8,9},{9,8},{10,11... | collective-permute-start | bytes 786440 | tf_op jit(solution)/shard_map/ppermute | solution.py:74
  37.4 1.0 collective-permute-done.15
  38.5 1.5 %collective-permute-start.16 = (bf16[128,1024]{1,0:T(8,128)(2,1)S(1)}, bf16[128,1024]{1,0:T(8,128)(2,1)S(1)}, u32[]{:S(2)}, u32[]{:S(2)}) collective-permute-start(bf16[128,1024]{1,0:T(8,128)(2,1)S(1)} %broadcast_select_fusion.1.refs_4_), channel_id=1, source_target_pairs={{0,1},{1,0},{2,3},{3,2},{4,5},{5,4},{6,7},{7,6},{8,9},{9,8},{10,11... | collective-permute-start | bytes 786440 | tf_op jit(solution)/shard_map/ppermute | solution.py:74
  40.0 2.5 %collective-permute-done.12 = bf16[128,1024]{1,0:T(8,128)(2,1)S(1)} collective-permute-done((bf16[128,1024]{1,0:T(8,128)(2,1)S(1)}, bf16[128,1024]{1,0:T(8,128)(2,1)S(1)}, u32[]{:S(2)}, u32[]{:S(2)}) %collective-permute-start.12) | collective-permute-done | bytes 262176 | tf_op jit(solution)/shard_map/ppermute | solution.py:47
  42.5 1.6 %collective-permute-start.17 = (bf16[128,1024]{1,0:T(8,128)(2,1)S(1)}, bf16[128,1024]{1,0:T(8,128)(2,1)S(1)}, u32[]{:S(2)}, u32[]{:S(2)}) collective-permute-start(bf16[128,1024]{1,0:T(8,128)(2,1)S(1)} %broadcast_select_fusion.refs_5_), channel_id=1, source_target_pairs={{0,1},{1,0},{2,3},{3,2},{4,5},{5,4},{6,7},{7,6},{8,9},{9,8},{10,11... | collective-permute-start | bytes 786440 | tf_op jit(solution)/shard_map/ppermute | solution.py:74
  44.1 1.7 %collective-permute-start.13 = (bf16[128,1024]{1,0:T(8,128)(2,1)S(1)}, bf16[128,1024]{1,0:T(8,128)(2,1)S(1)}, u32[]{:S(2)}, u32[]{:S(2)}) collective-permute-start(bf16[128,1024]{1,0:T(8,128)(2,1)S(1)} %collective-permute-done.1.refs_3_), channel_id=1, source_target_pairs={{0,2},{2,0},{4,6},{6,4},{1,3},{3,1},{5,7},{7,5},{8,10},{10,8},{12,... | collective-permute-start | bytes 786440 | tf_op jit(solution)/shard_map/ppermute | solution.py:71
  45.8 1.1 list_blocks.1.ancestors
  47.1 0.9 copy-done.9
  48.1 3.0 %early_products.1 = (f32[8,128,1024]{2,1,0:T(8,128)S(1)}, bf16[8,512,256]{2,1,0:T(8,128)(2,1)S(1)}) custom-call(s32[16]{0:T(128)S(1)} %list_blocks.1.ancestors, bf16[2,1024,2048]{2,1,0:T(8,128)(2,1)S(1)} %bitcast.25, bf16[128,1024]{1,0:T(8,128)(2,1)S(1)} %get-tuple-element.57.refs_0_, bf16[128,1024]{1,0:T(8,128)(2,1)S(1)} %get-tuple-element.56.refs_1_, ...), custom_call_target="tpu_custom_call" | custom-call | flops 2147483648 | bytes 4194304 | tf_op jit(solution)/shard_map/early_products/pallas_call | solution.py:513
  51.1 1.3 %collective-permute-done.16.refs_6_ = bf16[128,1024]{1,0:T(8,128)(2,1)S(1)} collective-permute-done((bf16[128,1024]{1,0:T(8,128)(2,1)S(1)}, bf16[128,1024]{1,0:T(8,128)(2,1)S(1)}, u32[]{:S(2)}, u32[]{:S(2)}) %collective-permute-start.16) | collective-permute-done | bytes 262176 | tf_op jit(solution)/shard_map/ppermute | solution.py:74
  52.4 2.8 %collective-permute-done.17.refs_7_ = bf16[128,1024]{1,0:T(8,128)(2,1)S(1)} collective-permute-done((bf16[128,1024]{1,0:T(8,128)(2,1)S(1)}, bf16[128,1024]{1,0:T(8,128)(2,1)S(1)}, u32[]{:S(2)}, u32[]{:S(2)}) %collective-permute-start.17) | collective-permute-done | bytes 262176 | tf_op jit(solution)/shard_map/ppermute | solution.py:74
  55.3 2.1 %last_products.1 = (f32[8,128,1024]{2,1,0:T(8,128)S(1)}, bf16[8,512,256]{2,1,0:T(8,128)(2,1)S(1)}) custom-call(s32[16]{0:T(128)S(1)} %bitcast.29, bf16[2,1024,2048]{2,1,0:T(8,128)(2,1)S(1)} %bitcast.26, f32[8,128,1024]{2,1,0:T(8,128)S(1)} %get-tuple-element.31.early, bf16[128,1024]{1,0:T(8,128)(2,1)S(1)} %collective-permute-done.6.refs_0_, ...), custom_call_target="tpu_custom_call" | custom-call | flops 2147483648 | bytes 8388608 | tf_op jit(solution)/shard_map/last_products/pallas_call | solution.py:529
  57.4 1.3 %copy-done.3 = bf16[8,512,256]{2,1,0:T(8,128)(2,1)} copy-done((bf16[8,512,256]{2,1,0:T(8,128)(2,1)}, bf16[8,512,256]{2,1,0:T(8,128)(2,1)S(1)}, u32[]{:S(2)}) %copy-start.3) | copy-done | bytes 2097176
  58.8 2.6 %lay_columns.1 = (f32[4096,128]{1,0:T(8,128)S(1)}, bf16[4096,128]{1,0:T(8,128)(2,1)}) custom-call(s32[16]{0:T(128)S(1)} %bitcast.30, f32[8,128,1024]{2,1,0:T(8,128)S(1)} %get-tuple-element.33.total.refs_0_), custom_call_target="tpu_custom_call" | custom-call | bytes 8388608 | tf_op jit(solution)/shard_map/lay_columns/pallas_call | solution.py:622
  61.4 1.3 %copy-done.5 = f32[4096,128]{1,0:T(8,128)} copy-done((f32[4096,128]{1,0:T(8,128)}, f32[4096,128]{1,0:T(8,128)S(1)}, u32[]{:S(2)}) %copy-start.5) | copy-done | bytes 2097176
  62.7 2.9 %collective-permute-start.18 = (bf16[4096,128]{1,0:T(8,128)(2,1)}, bf16[4096,128]{1,0:T(8,128)(2,1)S(1)}, u32[]{:S(2)}, u32[]{:S(2)}) collective-permute-start(bf16[4096,128]{1,0:T(8,128)(2,1)} %get-tuple-element.35), channel_id=1, source_target_pairs={{0,1},{1,0},{2,3},{3,2},{4,5},{5,4},{6,7},{7,6},{8,9},{9,8},{10,11... | collective-permute-start | bytes 3145736 | tf_op jit(solution)/shard_map/ppermute | solution.py:636
  66.4 19.9 %collective-permute-done.19 = s32[256]{0:T(256)S(1)} collective-permute-done((s32[256]{0:T(256)S(1)}, s32[256]{0:T(256)S(1)}, u32[]{:S(2)}, u32[]{:S(2)}) %collective-permute-start.19) | collective-permute-done | bytes 1056 | tf_op jit(solution)/shard_map/ppermute | solution.py:476
  86.3 2.2 %copy-done.1 = f32[8,128,1024]{2,1,0:T(8,128)S(1)} copy-done((f32[8,128,1024]{2,1,0:T(8,128)S(1)}, f32[8,128,1024]{2,1,0:T(8,128)}, u32[]{:S(2)}) %copy-start.1) | copy-done | bytes 4194328
  88.5 1.6 %copy-done.4 = bf16[8,512,256]{2,1,0:T(8,128)(2,1)S(1)} copy-done((bf16[8,512,256]{2,1,0:T(8,128)(2,1)S(1)}, bf16[8,512,256]{2,1,0:T(8,128)(2,1)}, u32[]{:S(2)}) %copy-start.4) | copy-done | bytes 2097176
  90.1 2.2 %diag_products.3 = (f32[4,80,512]{2,1,0:T(8,128)S(1)}, bf16[1,4,80,512]{3,2,1,0:T(8,128)(2,1)S(1)}) custom-call(s32[16]{0:T(128)S(1)} %bitcast.31, f32[2,16]{1,0:T(2,128)S(1)} %copy-done.10, s32[1]{0:T(128)S(6)} %copy.17.slot, s32[512]{0:T(512)S(1)} %constant_dynamic-update-slice_fusion.owner, f32[8,128,1024]{2,1,0:T(8,128)S(1)} %copy-done.1, ...), custom_call_target="tpu_custom_call" | custom-call | flops 1073741824 | bytes 4194304 | tf_op jit(solution)/shard_map/diag_products/pallas_call | solution.py:545
  92.3 1.8 %collective-permute-start.21 = (bf16[4,80,512]{2,1,0:T(8,128)(2,1)S(1)}, bf16[4,80,512]{2,1,0:T(8,128)(2,1)S(1)}, u32[]{:S(2)}, u32[]{:S(2)}) collective-permute-start(bf16[4,80,512]{2,1,0:T(8,128)(2,1)S(1)} %bitcast.33), channel_id=1, source_target_pairs={{0,1},{1,0},{2,3},{3,2},{4,5},{5,4},{6,7},{7,6},{8,9},{9,8},{10,11... | collective-permute-start | bytes 983048 | tf_op jit(solution)/shard_map/ppermute | solution.py:575
  94.2 2.1 %diag_products.2 = (f32[4,64,512]{2,1,0:T(8,128)S(1)}, bf16[1,4,64,512]{3,2,1,0:T(8,128)(2,1)S(1)}) custom-call(s32[16]{0:T(128)S(1)} %bitcast.32, f32[2,16]{1,0:T(2,128)S(1)} %copy-done.10, s32[1]{0:T(128)S(6)} %copy.17.slot, s32[512]{0:T(512)S(1)} %constant_dynamic-update-slice_fusion.owner, f32[8,128,1024]{2,1,0:T(8,128)S(1)} %copy-done.1, ...), custom_call_target="tpu_custom_call" | custom-call | flops 1073741824 | bytes 4194304 | tf_op jit(solution)/shard_map/diag_products/pallas_call | solution.py:545
  96.6 7.4 %collective-permute-done.20.refs_0_ = bf16[4,64,512]{2,1,0:T(8,128)(2,1)S(1)} collective-permute-done((bf16[4,64,512]{2,1,0:T(8,128)(2,1)S(1)}, bf16[4,64,512]{2,1,0:T(8,128)(2,1)S(1)}, u32[]{:S(2)}, u32[]{:S(2)}) %collective-permute-start.20) | collective-permute-done | bytes 262176 | tf_op jit(solution)/shard_map/ppermute | solution.py:575
  104.2 5.4 %collective-permute-start.23 = (bf16[72,1024]{1,0:T(8,128)(2,1)S(1)}, bf16[72,1024]{1,0:T(8,128)(2,1)S(1)}, u32[]{:S(2)}, u32[]{:S(2)}) collective-permute-start(bf16[72,1024]{1,0:T(8,128)(2,1)S(1)} %get-tuple-element.46), channel_id=1, source_target_pairs={{0,4},{2,6},{4,0},{6,2},{1,5},{3,7},{5,1},{7,3},{8,12},{10,14},{12... | collective-permute-start | bytes 442376 | tf_op jit(solution)/shard_map/ppermute | solution.py:589
  109.6 3.3 %collective-permute-done.22.refs_0_ = bf16[72,1024]{1,0:T(8,128)(2,1)S(1)} collective-permute-done((bf16[72,1024]{1,0:T(8,128)(2,1)S(1)}, bf16[72,1024]{1,0:T(8,128)(2,1)S(1)}, u32[]{:S(2)}, u32[]{:S(2)}) %collective-permute-start.22) | collective-permute-done | bytes 147488 | tf_op jit(solution)/shard_map/ppermute | solution.py:589
  112.9 4.3 %collective-permute-done.23.refs_1_ = bf16[72,1024]{1,0:T(8,128)(2,1)S(1)} collective-permute-done((bf16[72,1024]{1,0:T(8,128)(2,1)S(1)}, bf16[72,1024]{1,0:T(8,128)(2,1)S(1)}, u32[]{:S(2)}, u32[]{:S(2)}) %collective-permute-start.23) | collective-permute-done | bytes 147488 | tf_op jit(solution)/shard_map/ppermute | solution.py:589
  117.2 1.4 %finish.1 = (f32[512,128]{1,0:T(8,128)}, f32[288,128]{1,0:T(8,128)S(1)}) custom-call(f32[2,16]{1,0:T(2,128)S(1)} %copy-done.10, s32[1]{0:T(128)S(6)} %copy.17.slot, f32[512,128]{1,0:T(8,128)S(1)} %bitcast.27, f32[72,1024]{1,0:T(8,128)S(1)} %get-tuple-element.44.own, bf16[72,1024]{1,0:T(8,128)(2,1)S(1)} %collective-permute-done.22.refs_0_, ...), custom_call_target="tpu_custom_call" | custom-call | tf_op jit(solution)/shard_map/finish/pallas_call | solution.py:592
  118.6 1.5 %collective-permute-start.26 = (f32[288,128]{1,0:T(8,128)S(1)}, f32[288,128]{1,0:T(8,128)S(1)}, u32[]{:S(2)}, u32[]{:S(2)}) collective-permute-start(f32[288,128]{1,0:T(8,128)S(1)} %get-tuple-element.49.refs_0_), channel_id=1, source_target_pairs={{0,16},{8,24},{16,0},{24,8},{1,17},{9,25},{17,1},{25,9},{2,18},{10... | collective-permute-start | bytes 442376 | tf_op jit(solution)/shard_map/ppermute | solution.py:606
  120.4 4.9 %collective-permute-done.26.refs_2_ = f32[288,128]{1,0:T(8,128)S(1)} collective-permute-done((f32[288,128]{1,0:T(8,128)S(1)}, f32[288,128]{1,0:T(8,128)S(1)}, u32[]{:S(2)}, u32[]{:S(2)}) %collective-permute-start.26) | collective-permute-done | bytes 147488 | tf_op jit(solution)/shard_map/ppermute | solution.py:606
  125.3 2.2 %collective-permute-done.27.refs_3_ = f32[288,128]{1,0:T(8,128)S(1)} collective-permute-done((f32[288,128]{1,0:T(8,128)S(1)}, f32[288,128]{1,0:T(8,128)S(1)}, u32[]{:S(2)}, u32[]{:S(2)}) %collective-permute-start.27) | collective-permute-done | bytes 147488 | tf_op jit(solution)/shard_map/ppermute | solution.py:606
  127.5 0.7 density.1
  128.2 1.9 %join_columns.1 = f32[4096,128]{1,0:T(8,128)} custom-call(f32[4096,128]{1,0:T(8,128)S(1)} %copy-done.6, bf16[4096,128]{1,0:T(8,128)(2,1)S(1)} %collective-permute-done.18.refs_0_), custom_call_target="tpu_custom_call" | custom-call | tf_op jit(solution)/shard_map/join_columns/pallas_call | solution.py:640
  (52 shorter events, 4.0 us)
Async XLA Ops:
  0.6 45.2 %copy-start.11 = (s32[1,16]{1,0:T(1,128)S(1)}, s32[1,16]{1,0:T(1,128)}, u32[]{:S(2)}) copy-start(s32[1,16]{1,0:T(1,128)} %param.10) | copy-start | bytes 196
  1.7 8.9 %collective-permute-start.2 = (bf16[128,1024]{1,0:T(8,128)(2,1)S(1)}, bf16[128,1024]{1,0:T(8,128)(2,1)S(1)}, u32[]{:S(2)}, u32[]{:S(2)}) collective-permute-start(bf16[128,1024]{1,0:T(8,128)(2,1)S(1)} %get-tuple-element.57.refs_0_), channel_id=1, source_target_pairs={{2,4},{4,2},{3,5},{5,3},{10,12},{12,10},{11,13},{13,11},{18,20},{2... | collective-permute-start | bytes 786440 | tf_op jit(solution)/shard_map/ppermute | solution.py:47
  2.4 13.1 %collective-permute-start.6 = (bf16[128,1024]{1,0:T(8,128)(2,1)S(1)}, bf16[128,1024]{1,0:T(8,128)(2,1)S(1)}, u32[]{:S(2)}, u32[]{:S(2)}) collective-permute-start(bf16[128,1024]{1,0:T(8,128)(2,1)S(1)} %get-tuple-element.57.refs_0_), channel_id=1, source_target_pairs={{0,2},{2,0},{4,6},{6,4},{1,3},{3,1},{5,7},{7,5},{8,10},{10,8},{12,... | collective-permute-start | bytes 786440 | tf_op jit(solution)/shard_map/ppermute | solution.py:47
  8.3 7.8 %collective-permute-start = (bf16[128,1024]{1,0:T(8,128)(2,1)S(1)}, bf16[128,1024]{1,0:T(8,128)(2,1)S(1)}, u32[]{:S(2)}, u32[]{:S(2)}) collective-permute-start(bf16[128,1024]{1,0:T(8,128)(2,1)S(1)} %get-tuple-element.57.refs_0_), channel_id=1, source_target_pairs={{0,1},{1,0},{2,3},{3,2},{4,5},{5,4},{6,7},{7,6},{8,9},{9,8},{10,11... | collective-permute-start | bytes 786440 | tf_op jit(solution)/shard_map/ppermute | solution.py:74
  9.8 11.3 %collective-permute-start.10 = (bf16[128,1024]{1,0:T(8,128)(2,1)S(1)}, bf16[128,1024]{1,0:T(8,128)(2,1)S(1)}, u32[]{:S(2)}, u32[]{:S(2)}) collective-permute-start(bf16[128,1024]{1,0:T(8,128)(2,1)S(1)} %get-tuple-element.56.refs_1_), channel_id=1, source_target_pairs={{0,2},{2,0},{4,6},{6,4},{1,3},{3,1},{5,7},{7,5},{8,10},{10,8},{12,... | collective-permute-start | bytes 786440 | tf_op jit(solution)/shard_map/ppermute | solution.py:47
  9.9 11.9 %collective-permute-start.4 = (bf16[128,1024]{1,0:T(8,128)(2,1)S(1)}, bf16[128,1024]{1,0:T(8,128)(2,1)S(1)}, u32[]{:S(2)}, u32[]{:S(2)}) collective-permute-start(bf16[128,1024]{1,0:T(8,128)(2,1)S(1)} %get-tuple-element.56.refs_1_), channel_id=1, source_target_pairs={{2,4},{4,2},{3,5},{5,3},{10,12},{12,10},{11,13},{13,11},{18,20},{2... | collective-permute-start | bytes 786440 | tf_op jit(solution)/shard_map/ppermute | solution.py:47
  10.6 16.1 %collective-permute-start.3 = (bf16[128,1024]{1,0:T(8,128)(2,1)S(1)}, bf16[128,1024]{1,0:T(8,128)(2,1)S(1)}, u32[]{:S(2)}, u32[]{:S(2)}) collective-permute-start(bf16[128,1024]{1,0:T(8,128)(2,1)S(1)} %collective-permute-done.2), channel_id=1, source_target_pairs={{0,2},{2,0},{4,6},{6,4},{1,3},{3,1},{5,7},{7,5},{8,10},{10,8},{12,... | collective-permute-start | bytes 786440 | tf_op jit(solution)/shard_map/ppermute | solution.py:47
  15.5 12.8 %collective-permute-start.14 = (bf16[128,1024]{1,0:T(8,128)(2,1)S(1)}, bf16[128,1024]{1,0:T(8,128)(2,1)S(1)}, u32[]{:S(2)}, u32[]{:S(2)}) collective-permute-start(bf16[128,1024]{1,0:T(8,128)(2,1)S(1)} %collective-permute-done.6.refs_0_), channel_id=1, source_target_pairs={{2,4},{4,2},{3,5},{5,3},{10,12},{12,10},{11,13},{13,11},{18,20},{2... | collective-permute-start | bytes 786440 | tf_op jit(solution)/shard_map/ppermute | solution.py:47
  16.2 0.7 copy-start.8
  16.9 13.4 %collective-permute-start.7 = (bf16[128,1024]{1,0:T(8,128)(2,1)S(1)}, bf16[128,1024]{1,0:T(8,128)(2,1)S(1)}, u32[]{:S(2)}, u32[]{:S(2)}) collective-permute-start(bf16[128,1024]{1,0:T(8,128)(2,1)S(1)} %collective-permute-done.6.refs_0_), channel_id=1, source_target_pairs={{0,1},{1,0},{2,3},{3,2},{4,5},{5,4},{6,7},{7,6},{8,9},{9,8},{10,11... | collective-permute-start | bytes 786440 | tf_op jit(solution)/shard_map/ppermute | solution.py:74
  21.1 9.8 %collective-permute-start.11 = (bf16[128,1024]{1,0:T(8,128)(2,1)S(1)}, bf16[128,1024]{1,0:T(8,128)(2,1)S(1)}, u32[]{:S(2)}, u32[]{:S(2)}) collective-permute-start(bf16[128,1024]{1,0:T(8,128)(2,1)S(1)} %collective-permute-done.10.refs_1_), channel_id=1, source_target_pairs={{2,4},{4,2},{3,5},{5,3},{10,12},{12,10},{11,13},{13,11},{18,20},{2... | collective-permute-start | bytes 786440 | tf_op jit(solution)/shard_map/ppermute | solution.py:47
  21.8 11.0 %collective-permute-start.5 = (bf16[128,1024]{1,0:T(8,128)(2,1)S(1)}, bf16[128,1024]{1,0:T(8,128)(2,1)S(1)}, u32[]{:S(2)}, u32[]{:S(2)}) collective-permute-start(bf16[128,1024]{1,0:T(8,128)(2,1)S(1)} %collective-permute-done.4), channel_id=1, source_target_pairs={{0,2},{2,0},{4,6},{6,4},{1,3},{3,1},{5,7},{7,5},{8,10},{10,8},{12,... | collective-permute-start | bytes 786440 | tf_op jit(solution)/shard_map/ppermute | solution.py:47
  26.7 9.2 %collective-permute-start.1 = (bf16[128,1024]{1,0:T(8,128)(2,1)S(1)}, bf16[128,1024]{1,0:T(8,128)(2,1)S(1)}, u32[]{:S(2)}, u32[]{:S(2)}) collective-permute-start(bf16[128,1024]{1,0:T(8,128)(2,1)S(1)} %get-tuple-element.56.refs_1_), channel_id=1, source_target_pairs={{0,1},{1,0},{2,3},{3,2},{4,5},{5,4},{6,7},{7,6},{8,9},{9,8},{10,11... | collective-permute-start | bytes 786440 | tf_op jit(solution)/shard_map/ppermute | solution.py:74
  28.2 10.2 %collective-permute-start.15 = (bf16[128,1024]{1,0:T(8,128)(2,1)S(1)}, bf16[128,1024]{1,0:T(8,128)(2,1)S(1)}, u32[]{:S(2)}, u32[]{:S(2)}) collective-permute-start(bf16[128,1024]{1,0:T(8,128)(2,1)S(1)} %collective-permute-done.14), channel_id=1, source_target_pairs={{0,2},{2,0},{4,6},{6,4},{1,3},{3,1},{5,7},{7,5},{8,10},{10,8},{12,... | collective-permute-start | bytes 786440 | tf_op jit(solution)/shard_map/ppermute | solution.py:47
  30.3 16.9 %copy-start.2 = (bf16[1,2,1024,2048]{3,2,1,0:T(8,128)(2,1)S(1)}, bf16[1,2,1024,2048]{3,2,1,0:T(8,128)(2,1)}, u32[]{:S(2)}) copy-start(bf16[1,2,1024,2048]{3,2,1,0:T(8,128)(2,1)} %param.7) | copy-start | bytes 25165828
  30.3 16.7 %collective-permute-start.8 = (bf16[128,1024]{1,0:T(8,128)(2,1)S(1)}, bf16[128,1024]{1,0:T(8,128)(2,1)S(1)}, u32[]{:S(2)}, u32[]{:S(2)}) collective-permute-start(bf16[128,1024]{1,0:T(8,128)(2,1)S(1)} %broadcast_select_fusion.3.refs_4_), channel_id=1, source_target_pairs={{0,1},{1,0},{2,3},{3,2},{4,5},{5,4},{6,7},{7,6},{8,9},{9,8},{10,11... | collective-permute-start | bytes 786440 | tf_op jit(solution)/shard_map/ppermute | solution.py:74
  30.9 11.6 %collective-permute-start.12 = (bf16[128,1024]{1,0:T(8,128)(2,1)S(1)}, bf16[128,1024]{1,0:T(8,128)(2,1)S(1)}, u32[]{:S(2)}, u32[]{:S(2)}) collective-permute-start(bf16[128,1024]{1,0:T(8,128)(2,1)S(1)} %collective-permute-done.11), channel_id=1, source_target_pairs={{0,2},{2,0},{4,6},{6,4},{1,3},{3,1},{5,7},{7,5},{8,10},{10,8},{12,... | collective-permute-start | bytes 786440 | tf_op jit(solution)/shard_map/ppermute | solution.py:47
  35.9 11.2 %collective-permute-start.9 = (bf16[128,1024]{1,0:T(8,128)(2,1)S(1)}, bf16[128,1024]{1,0:T(8,128)(2,1)S(1)}, u32[]{:S(2)}, u32[]{:S(2)}) collective-permute-start(bf16[128,1024]{1,0:T(8,128)(2,1)S(1)} %broadcast_select_fusion.2.refs_5_), channel_id=1, source_target_pairs={{0,1},{1,0},{2,3},{3,2},{4,5},{5,4},{6,7},{7,6},{8,9},{9,8},{10,11... | collective-permute-start | bytes 786440 | tf_op jit(solution)/shard_map/ppermute | solution.py:74
  38.5 14.0 %collective-permute-start.16 = (bf16[128,1024]{1,0:T(8,128)(2,1)S(1)}, bf16[128,1024]{1,0:T(8,128)(2,1)S(1)}, u32[]{:S(2)}, u32[]{:S(2)}) collective-permute-start(bf16[128,1024]{1,0:T(8,128)(2,1)S(1)} %broadcast_select_fusion.1.refs_4_), channel_id=1, source_target_pairs={{0,1},{1,0},{2,3},{3,2},{4,5},{5,4},{6,7},{7,6},{8,9},{9,8},{10,11... | collective-permute-start | bytes 786440 | tf_op jit(solution)/shard_map/ppermute | solution.py:74
  42.5 12.8 %collective-permute-start.17 = (bf16[128,1024]{1,0:T(8,128)(2,1)S(1)}, bf16[128,1024]{1,0:T(8,128)(2,1)S(1)}, u32[]{:S(2)}, u32[]{:S(2)}) collective-permute-start(bf16[128,1024]{1,0:T(8,128)(2,1)S(1)} %broadcast_select_fusion.refs_5_), channel_id=1, source_target_pairs={{0,1},{1,0},{2,3},{3,2},{4,5},{5,4},{6,7},{7,6},{8,9},{9,8},{10,11... | collective-permute-start | bytes 786440 | tf_op jit(solution)/shard_map/ppermute | solution.py:74
  44.1 11.2 %collective-permute-start.13 = (bf16[128,1024]{1,0:T(8,128)(2,1)S(1)}, bf16[128,1024]{1,0:T(8,128)(2,1)S(1)}, u32[]{:S(2)}, u32[]{:S(2)}) collective-permute-start(bf16[128,1024]{1,0:T(8,128)(2,1)S(1)} %collective-permute-done.1.refs_3_), channel_id=1, source_target_pairs={{0,2},{2,0},{4,6},{6,4},{1,3},{3,1},{5,7},{7,5},{8,10},{10,8},{12,... | collective-permute-start | bytes 786440 | tf_op jit(solution)/shard_map/ppermute | solution.py:71
  47.1 1.0 copy-start.9
  57.4 1.4 %copy-start.3 = (bf16[8,512,256]{2,1,0:T(8,128)(2,1)}, bf16[8,512,256]{2,1,0:T(8,128)(2,1)S(1)}, u32[]{:S(2)}) copy-start(bf16[8,512,256]{2,1,0:T(8,128)(2,1)S(1)} %get-tuple-element.39.refs_2_) | copy-start | bytes 6291460
  58.8 2.7 %copy-start = (f32[8,128,1024]{2,1,0:T(8,128)}, f32[8,128,1024]{2,1,0:T(8,128)S(1)}, u32[]{:S(2)}) copy-start(f32[8,128,1024]{2,1,0:T(8,128)S(1)} %get-tuple-element.33.total.refs_0_) | copy-start | bytes 12582916
  58.8 6.9 %copy-start.12 = (s32[256,1]{0,1:T(1,128)S(1)}, s32[256,1]{0,1:T(1,128)}, u32[]{:S(2)}) copy-start(s32[256,1]{0,1:T(1,128)} %param.11) | copy-start | bytes 3076
  58.8 27.5 %copy-start.10 = (f32[2,16]{1,0:T(2,128)S(1)}, f32[2,16]{1,0:T(2,128)}, u32[]{:S(2)}) copy-start(f32[2,16]{1,0:T(2,128)} %table.5) | copy-start | bytes 388
  61.4 1.3 %copy-start.5 = (f32[4096,128]{1,0:T(8,128)}, f32[4096,128]{1,0:T(8,128)S(1)}, u32[]{:S(2)}) copy-start(f32[4096,128]{1,0:T(8,128)S(1)} %get-tuple-element.34.keep) | copy-start | bytes 6291460
  62.7 65.5 %collective-permute-start.18 = (bf16[4096,128]{1,0:T(8,128)(2,1)}, bf16[4096,128]{1,0:T(8,128)(2,1)S(1)}, u32[]{:S(2)}, u32[]{:S(2)}) collective-permute-start(bf16[4096,128]{1,0:T(8,128)(2,1)} %get-tuple-element.35), channel_id=1, source_target_pairs={{0,1},{1,0},{2,3},{3,2},{4,5},{5,4},{6,7},{7,6},{8,9},{9,8},{10,11... | collective-permute-start | bytes 3145736 | tf_op jit(solution)/shard_map/ppermute | solution.py:636
  65.7 20.6 %collective-permute-start.19 = (s32[256]{0:T(256)S(1)}, s32[256]{0:T(256)S(1)}, u32[]{:S(2)}, u32[]{:S(2)}) collective-permute-start(s32[256]{0:T(256)S(1)} %bitcast.36), channel_id=1, source_target_pairs={{0,1},{1,0},{2,3},{3,2},{4,5},{5,4},{6,7},{7,6},{8,9},{9,8},{10,11... | collective-permute-start | bytes 3080 | tf_op jit(solution)/shard_map/ppermute | solution.py:476
  86.3 2.2 %copy-start.1 = (f32[8,128,1024]{2,1,0:T(8,128)S(1)}, f32[8,128,1024]{2,1,0:T(8,128)}, u32[]{:S(2)}) copy-start(f32[8,128,1024]{2,1,0:T(8,128)} %copy-done) | copy-start | bytes 12582916
  88.5 1.6 %copy-start.4 = (bf16[8,512,256]{2,1,0:T(8,128)(2,1)S(1)}, bf16[8,512,256]{2,1,0:T(8,128)(2,1)}, u32[]{:S(2)}) copy-start(bf16[8,512,256]{2,1,0:T(8,128)(2,1)} %copy-done.3) | copy-start | bytes 6291460
  92.3 24.9 %copy-start.7 = (f32[64,1,1,2,512]{4,3,2,1,0:T(2,128)S(1)}, f32[64,1,1,2,512]{4,3,2,1,0:T(2,128)}, u32[]{:S(2)}) copy-start(f32[64,1,1,2,512]{4,3,2,1,0:T(2,128)} %param.9) | copy-start | bytes 786436
  92.3 11.7 %collective-permute-start.21 = (bf16[4,80,512]{2,1,0:T(8,128)(2,1)S(1)}, bf16[4,80,512]{2,1,0:T(8,128)(2,1)S(1)}, u32[]{:S(2)}, u32[]{:S(2)}) collective-permute-start(bf16[4,80,512]{2,1,0:T(8,128)(2,1)S(1)} %bitcast.33), channel_id=1, source_target_pairs={{0,1},{1,0},{2,3},{3,2},{4,5},{5,4},{6,7},{7,6},{8,9},{9,8},{10,11... | collective-permute-start | bytes 983048 | tf_op jit(solution)/shard_map/ppermute | solution.py:575
  96.3 32.0 %copy-start.6 = (f32[4096,128]{1,0:T(8,128)S(1)}, f32[4096,128]{1,0:T(8,128)}, u32[]{:S(2)}) copy-start(f32[4096,128]{1,0:T(8,128)} %copy-done.5) | copy-start | bytes 6291460
  96.3 7.7 %collective-permute-start.20 = (bf16[4,64,512]{2,1,0:T(8,128)(2,1)S(1)}, bf16[4,64,512]{2,1,0:T(8,128)(2,1)S(1)}, u32[]{:S(2)}, u32[]{:S(2)}) collective-permute-start(bf16[4,64,512]{2,1,0:T(8,128)(2,1)S(1)} %bitcast.34), channel_id=1, source_target_pairs={{0,1},{1,0},{2,3},{3,2},{4,5},{5,4},{6,7},{7,6},{8,9},{9,8},{10,11... | collective-permute-start | bytes 786440 | tf_op jit(solution)/shard_map/ppermute | solution.py:575
  104.1 8.7 %collective-permute-start.22 = (bf16[72,1024]{1,0:T(8,128)(2,1)S(1)}, bf16[72,1024]{1,0:T(8,128)(2,1)S(1)}, u32[]{:S(2)}, u32[]{:S(2)}) collective-permute-start(bf16[72,1024]{1,0:T(8,128)(2,1)S(1)} %get-tuple-element.45), channel_id=1, source_target_pairs={{0,2},{2,4},{4,6},{6,0},{1,3},{3,5},{5,7},{7,1},{8,10},{10,12},{12... | collective-permute-start | bytes 442376 | tf_op jit(solution)/shard_map/ppermute | solution.py:589
  104.2 13.0 %collective-permute-start.23 = (bf16[72,1024]{1,0:T(8,128)(2,1)S(1)}, bf16[72,1024]{1,0:T(8,128)(2,1)S(1)}, u32[]{:S(2)}, u32[]{:S(2)}) collective-permute-start(bf16[72,1024]{1,0:T(8,128)(2,1)S(1)} %get-tuple-element.46), channel_id=1, source_target_pairs={{0,4},{2,6},{4,0},{6,2},{1,5},{3,7},{5,1},{7,3},{8,12},{10,14},{12... | collective-permute-start | bytes 442376 | tf_op jit(solution)/shard_map/ppermute | solution.py:589
  109.6 7.6 %collective-permute-start.24 = (bf16[72,1024]{1,0:T(8,128)(2,1)S(1)}, bf16[72,1024]{1,0:T(8,128)(2,1)S(1)}, u32[]{:S(2)}, u32[]{:S(2)}) collective-permute-start(bf16[72,1024]{1,0:T(8,128)(2,1)S(1)} %get-tuple-element.47), channel_id=1, source_target_pairs={{0,6},{2,0},{4,2},{6,4},{1,7},{3,1},{5,3},{7,5},{8,14},{10,8},{12,... | collective-permute-start | bytes 442376 | tf_op jit(solution)/shard_map/ppermute | solution.py:589
  118.6 1.9 %collective-permute-start.25 = (f32[288,128]{1,0:T(8,128)S(1)}, f32[288,128]{1,0:T(8,128)S(1)}, u32[]{:S(2)}, u32[]{:S(2)}) collective-permute-start(f32[288,128]{1,0:T(8,128)S(1)} %get-tuple-element.49.refs_0_), channel_id=1, source_target_pairs={{0,8},{8,0},{16,24},{24,16},{1,9},{9,1},{17,25},{25,17},{2,10},{10... | collective-permute-start | bytes 442376 | tf_op jit(solution)/shard_map/ppermute | solution.py:606
  118.6 6.7 %collective-permute-start.26 = (f32[288,128]{1,0:T(8,128)S(1)}, f32[288,128]{1,0:T(8,128)S(1)}, u32[]{:S(2)}, u32[]{:S(2)}) collective-permute-start(f32[288,128]{1,0:T(8,128)S(1)} %get-tuple-element.49.refs_0_), channel_id=1, source_target_pairs={{0,16},{8,24},{16,0},{24,8},{1,17},{9,25},{17,1},{25,9},{2,18},{10... | collective-permute-start | bytes 442376 | tf_op jit(solution)/shard_map/ppermute | solution.py:606
  120.0 7.5 %collective-permute-start.27 = (f32[288,128]{1,0:T(8,128)S(1)}, f32[288,128]{1,0:T(8,128)S(1)}, u32[]{:S(2)}, u32[]{:S(2)}) collective-permute-start(f32[288,128]{1,0:T(8,128)S(1)} %get-tuple-element.49.refs_0_), channel_id=1, source_target_pairs={{0,24},{8,16},{16,8},{24,0},{1,25},{9,17},{17,9},{25,1},{2,26},{10... | collective-permute-start | bytes 442376 | tf_op jit(solution)/shard_map/ppermute | solution.py:606

commit v10 on v9

--- a/solution.py
+++ b/solution.py
@@ -378,6 +378,20 @@
     return part + pole // across * BR, pole % across * 2 * BC
 
 
+def settle_kernel(laid_dinv, own, *refs):
+    *arrived, diag_out = refs
+    part, wide = own.shape[0] - BR, own.shape[1]
+    across = wide // (2 * BC)
+    total = own[:part, :]
+    for ref in arrived:
+        total = total + ref[:part, :].astype(jnp.float32)
+    for j in range(across):
+        for n in range(2):
+            rows_of = pl.ds(2 * j + n, part, stride=2 * across)
+            first = (n * across + j) * BC
+            diag_out[rows_of, :] = laid_dinv[rows_of, :] + total[:, first : first + BC]
+
+
 def density_kernel(split, *refs):
     *messages, density, tile = refs
     start = pl.multiple_of(split + lax.axis_index("pole") * BR, BR)
@@ -430,8 +444,7 @@
 
 
 def finish_kernel(poles, table, slot, laid_dinv, own, *refs):
-    diag_out, message = refs[-2:]
-    arrived = refs[:-2]
+    *arrived, message = refs
     part, wide = own.shape[0] - BR, own.shape[1]
     across = wide // (2 * BC)
     total = own[...]
@@ -445,7 +458,6 @@
             rows_of = pl.ds(2 * j + n, part, stride=2 * across)
             first = (n * across + j) * BC
             values.append(laid_dinv[rows_of, :] + total[:part, first : first + BC])
-            diag_out[rows_of, :] = values[n]
         share = weight_real * values[1] + weight_imag * values[0]
         message[pl.ds(j, part, stride=across), :] = share
     for pole in range(poles):
@@ -589,17 +601,22 @@
         lax.ppermute(rounded[step - 1], "row", [(i, (i + step) % rows) for i in range(rows)])
         for step in range(1, rows)
     ]
-    laid_diag, message = pl.pallas_call(
+    message = pl.pallas_call(
         functools.partial(finish_kernel, poles),
-        out_shape=(
-            jax.ShapeDtypeStruct((part * 2 * across, BC), jnp.float32),
-            jax.ShapeDtypeStruct((part * across + poles * BR, BC), jnp.float32),
-        ),
+        out_shape=jax.ShapeDtypeStruct((part * across + poles * BR, BC), jnp.float32),
         in_specs=[smem] * 2 + [vmem] * (2 + len(parts)),
-        out_specs=(vmem,) * 2,
+        out_specs=vmem,
         compiler_params=pltpu.CompilerParams(vmem_limit_bytes=8 * MIB),
         name="finish",
     )(weight_table, pole_slot, laid(dinv), own, *parts)
+    laid_diag = pl.pallas_call(
+        settle_kernel,
+        out_shape=jax.ShapeDtypeStruct((part * 2 * across, BC), jnp.float32),
+        in_specs=[vmem] * (2 + len(parts)),
+        out_specs=vmem,
+        compiler_params=pltpu.CompilerParams(vmem_limit_bytes=8 * MIB),
+        name="settle",
+    )(laid(dinv), own, *parts)
     diag_inverse = plain(laid_diag, dinv.shape)
     messages = [message]
     for step in range(1, poles):

time: 130 us -> 130 us (level)
  no operation moved by 1% of the time
where the time goes in v10:
time: 130 us; the launch traced here: 129 us
  waiting for transfers between devices  57.4 us (44%)
  starting transfers between devices  43.6 us (34%)
  Pallas kernels  17.5 us (13%)
  local copies, waits for them, and re-layouts  9.23 us (7%)
  between operations  1.5 us (1%)
    ppermute x1, waiting for transfers between devices, compute(): owners.append(lax.ppermute(owner[:, 0], grid, pairs))  19.9 us
    ppermute x10, starting transfers between devices, hop(): return lax.ppermute(value, 'row', pairs)  19.7 us
    ppermute x7, starting transfers between devices, gather_stages(): last = lax.ppermute(leaving, grid, pairs)  9.71 us
    ppermute x10, waiting for transfers between devices, hop(): return lax.ppermute(value, 'row', pairs)  8.95 us
    unnamed x27, local copies, waits for them, and re-layouts  8.14 us
    ppermute x3, waiting for transfers between devices, compute(): lax.ppermute(rounded[step - 1], 'row', [(i, (i + step) % rows) for i in r...  7.57 us
    ppermute x2, waiting for transfers between devices, compute(): lax.ppermute(diag_send[step - 1], grid, everyone_pairs[step])  7.41 us
    ppermute x7, waiting for transfers between devices, gather_stages(): last = lax.ppermute(leaving, grid, pairs)  7.33 us
  transfers between devices with their start and end apart: 28, of which 16 were waited for; matrix products, arithmetic and copies ran while one was open for 0% of the time, Pallas kernels for 8%

profile of v10, /device:TPU:0, one launch (start us, length us, event | category | flops | bytes accessed | tf_op | source)
XLA Modules:
  0.0 129.3 jit_solution(4290219685544549502)
XLA Ops:
  0.6 1.1 slice_bitcast_fusion
  1.7 0.7 collective-permute-start.2
  2.4 5.9 %collective-permute-start.6 = (bf16[128,1024]{1,0:T(8,128)(2,1)S(1)}, bf16[128,1024]{1,0:T(8,128)(2,1)S(1)}, u32[]{:S(2)}, u32[]{:S(2)}) collective-permute-start(bf16[128,1024]{1,0:T(8,128)(2,1)S(1)} %get-tuple-element.53.refs_0_), channel_id=1, source_target_pairs={{0,2},{2,0},{4,6},{6,4},{1,3},{3,1},{5,7},{7,5},{8,10},{10,8},{12,... | collective-permute-start | bytes 786440 | tf_op jit(solution)/shard_map/ppermute | solution.py:47
  8.3 1.5 %collective-permute-start = (bf16[128,1024]{1,0:T(8,128)(2,1)S(1)}, bf16[128,1024]{1,0:T(8,128)(2,1)S(1)}, u32[]{:S(2)}, u32[]{:S(2)}) collective-permute-start(bf16[128,1024]{1,0:T(8,128)(2,1)S(1)} %get-tuple-element.53.refs_0_), channel_id=1, source_target_pairs={{0,1},{1,0},{2,3},{3,2},{4,5},{5,4},{6,7},{7,6},{8,9},{9,8},{10,11... | collective-permute-start | bytes 786440 | tf_op jit(solution)/shard_map/ppermute | solution.py:74
  10.6 4.1 %collective-permute-start.3 = (bf16[128,1024]{1,0:T(8,128)(2,1)S(1)}, bf16[128,1024]{1,0:T(8,128)(2,1)S(1)}, u32[]{:S(2)}, u32[]{:S(2)}) collective-permute-start(bf16[128,1024]{1,0:T(8,128)(2,1)S(1)} %collective-permute-done.2), channel_id=1, source_target_pairs={{0,2},{2,0},{4,6},{6,4},{1,3},{3,1},{5,7},{7,5},{8,10},{10,8},{12,... | collective-permute-start | bytes 786440 | tf_op jit(solution)/shard_map/ppermute | solution.py:47
  14.7 0.8 collective-permute-done.6.refs_0_
  16.2 0.7 copy-done.8
  16.9 1.5 %collective-permute-start.7 = (bf16[128,1024]{1,0:T(8,128)(2,1)S(1)}, bf16[128,1024]{1,0:T(8,128)(2,1)S(1)}, u32[]{:S(2)}, u32[]{:S(2)}) collective-permute-start(bf16[128,1024]{1,0:T(8,128)(2,1)S(1)} %collective-permute-done.6.refs_0_), channel_id=1, source_target_pairs={{0,1},{1,0},{2,3},{3,2},{4,5},{5,4},{6,7},{7,6},{8,9},{9,8},{10,11... | collective-permute-start | bytes 786440 | tf_op jit(solution)/shard_map/ppermute | solution.py:74
  18.4 2.7 %collective-permute-done.10.refs_1_ = bf16[128,1024]{1,0:T(8,128)(2,1)S(1)} collective-permute-done((bf16[128,1024]{1,0:T(8,128)(2,1)S(1)}, bf16[128,1024]{1,0:T(8,128)(2,1)S(1)}, u32[]{:S(2)}, u32[]{:S(2)}) %collective-permute-start.10) | collective-permute-done | bytes 262176 | tf_op jit(solution)/shard_map/ppermute | solution.py:47
  21.8 3.9 %collective-permute-start.5 = (bf16[128,1024]{1,0:T(8,128)(2,1)S(1)}, bf16[128,1024]{1,0:T(8,128)(2,1)S(1)}, u32[]{:S(2)}, u32[]{:S(2)}) collective-permute-start(bf16[128,1024]{1,0:T(8,128)(2,1)S(1)} %collective-permute-done.4), channel_id=1, source_target_pairs={{0,2},{2,0},{4,6},{6,4},{1,3},{3,1},{5,7},{7,5},{8,10},{10,8},{12,... | collective-permute-start | bytes 786440 | tf_op jit(solution)/shard_map/ppermute | solution.py:47
  25.7 1.1 collective-permute-done.3
  26.7 1.5 %collective-permute-start.1 = (bf16[128,1024]{1,0:T(8,128)(2,1)S(1)}, bf16[128,1024]{1,0:T(8,128)(2,1)S(1)}, u32[]{:S(2)}, u32[]{:S(2)}) collective-permute-start(bf16[128,1024]{1,0:T(8,128)(2,1)S(1)} %get-tuple-element.52.refs_1_), channel_id=1, source_target_pairs={{0,1},{1,0},{2,3},{3,2},{4,5},{5,4},{6,7},{7,6},{8,9},{9,8},{10,11... | collective-permute-start | bytes 786440 | tf_op jit(solution)/shard_map/ppermute | solution.py:74
  28.2 2.0 %collective-permute-start.15 = (bf16[128,1024]{1,0:T(8,128)(2,1)S(1)}, bf16[128,1024]{1,0:T(8,128)(2,1)S(1)}, u32[]{:S(2)}, u32[]{:S(2)}) collective-permute-start(bf16[128,1024]{1,0:T(8,128)(2,1)S(1)} %collective-permute-done.14), channel_id=1, source_target_pairs={{0,2},{2,0},{4,6},{6,4},{1,3},{3,1},{5,7},{7,5},{8,10},{10,8},{12,... | collective-permute-start | bytes 786440 | tf_op jit(solution)/shard_map/ppermute | solution.py:47
  30.9 1.0 collective-permute-start.12
  31.9 0.9 collective-permute-done.5
  32.8 3.0 %collective-permute-done.1.refs_3_ = bf16[128,1024]{1,0:T(8,128)(2,1)S(1)} collective-permute-done((bf16[128,1024]{1,0:T(8,128)(2,1)S(1)}, bf16[128,1024]{1,0:T(8,128)(2,1)S(1)}, u32[]{:S(2)}, u32[]{:S(2)}) %collective-permute-start.1) | collective-permute-done | bytes 262176 | tf_op jit(solution)/shard_map/ppermute | solution.py:74
  35.9 1.5 %collective-permute-start.9 = (bf16[128,1024]{1,0:T(8,128)(2,1)S(1)}, bf16[128,1024]{1,0:T(8,128)(2,1)S(1)}, u32[]{:S(2)}, u32[]{:S(2)}) collective-permute-start(bf16[128,1024]{1,0:T(8,128)(2,1)S(1)} %broadcast_select_fusion.2.refs_5_), channel_id=1, source_target_pairs={{0,1},{1,0},{2,3},{3,2},{4,5},{5,4},{6,7},{7,6},{8,9},{9,8},{10,11... | collective-permute-start | bytes 786440 | tf_op jit(solution)/shard_map/ppermute | solution.py:74
  37.4 1.0 collective-permute-done.15
  38.5 1.5 %collective-permute-start.16 = (bf16[128,1024]{1,0:T(8,128)(2,1)S(1)}, bf16[128,1024]{1,0:T(8,128)(2,1)S(1)}, u32[]{:S(2)}, u32[]{:S(2)}) collective-permute-start(bf16[128,1024]{1,0:T(8,128)(2,1)S(1)} %broadcast_select_fusion.1.refs_4_), channel_id=1, source_target_pairs={{0,1},{1,0},{2,3},{3,2},{4,5},{5,4},{6,7},{7,6},{8,9},{9,8},{10,11... | collective-permute-start | bytes 786440 | tf_op jit(solution)/shard_map/ppermute | solution.py:74
  40.0 2.5 %collective-permute-done.12 = bf16[128,1024]{1,0:T(8,128)(2,1)S(1)} collective-permute-done((bf16[128,1024]{1,0:T(8,128)(2,1)S(1)}, bf16[128,1024]{1,0:T(8,128)(2,1)S(1)}, u32[]{:S(2)}, u32[]{:S(2)}) %collective-permute-start.12) | collective-permute-done | bytes 262176 | tf_op jit(solution)/shard_map/ppermute | solution.py:47
  42.5 1.6 %collective-permute-start.17 = (bf16[128,1024]{1,0:T(8,128)(2,1)S(1)}, bf16[128,1024]{1,0:T(8,128)(2,1)S(1)}, u32[]{:S(2)}, u32[]{:S(2)}) collective-permute-start(bf16[128,1024]{1,0:T(8,128)(2,1)S(1)} %broadcast_select_fusion.refs_5_), channel_id=1, source_target_pairs={{0,1},{1,0},{2,3},{3,2},{4,5},{5,4},{6,7},{7,6},{8,9},{9,8},{10,11... | collective-permute-start | bytes 786440 | tf_op jit(solution)/shard_map/ppermute | solution.py:74
  44.1 1.7 %collective-permute-start.13 = (bf16[128,1024]{1,0:T(8,128)(2,1)S(1)}, bf16[128,1024]{1,0:T(8,128)(2,1)S(1)}, u32[]{:S(2)}, u32[]{:S(2)}) collective-permute-start(bf16[128,1024]{1,0:T(8,128)(2,1)S(1)} %collective-permute-done.1.refs_3_), channel_id=1, source_target_pairs={{0,2},{2,0},{4,6},{6,4},{1,3},{3,1},{5,7},{7,5},{8,10},{10,8},{12,... | collective-permute-start | bytes 786440 | tf_op jit(solution)/shard_map/ppermute | solution.py:71
  45.8 1.1 list_blocks.1.ancestors
  47.1 0.9 copy-done.9
  48.1 3.0 %early_products.1 = (f32[8,128,1024]{2,1,0:T(8,128)S(1)}, bf16[8,512,256]{2,1,0:T(8,128)(2,1)S(1)}) custom-call(s32[16]{0:T(128)S(1)} %list_blocks.1.ancestors, bf16[2,1024,2048]{2,1,0:T(8,128)(2,1)S(1)} %bitcast.25, bf16[128,1024]{1,0:T(8,128)(2,1)S(1)} %get-tuple-element.53.refs_0_, bf16[128,1024]{1,0:T(8,128)(2,1)S(1)} %get-tuple-element.52.refs_1_, ...), custom_call_target="tpu_custom_call" | custom-call | flops 2147483648 | bytes 4194304 | tf_op jit(solution)/shard_map/early_products/pallas_call | solution.py:525
  51.1 1.3 %collective-permute-done.16.refs_6_ = bf16[128,1024]{1,0:T(8,128)(2,1)S(1)} collective-permute-done((bf16[128,1024]{1,0:T(8,128)(2,1)S(1)}, bf16[128,1024]{1,0:T(8,128)(2,1)S(1)}, u32[]{:S(2)}, u32[]{:S(2)}) %collective-permute-start.16) | collective-permute-done | bytes 262176 | tf_op jit(solution)/shard_map/ppermute | solution.py:74
  52.4 2.8 %collective-permute-done.17.refs_7_ = bf16[128,1024]{1,0:T(8,128)(2,1)S(1)} collective-permute-done((bf16[128,1024]{1,0:T(8,128)(2,1)S(1)}, bf16[128,1024]{1,0:T(8,128)(2,1)S(1)}, u32[]{:S(2)}, u32[]{:S(2)}) %collective-permute-start.17) | collective-permute-done | bytes 262176 | tf_op jit(solution)/shard_map/ppermute | solution.py:74
  55.3 2.1 %last_products.1 = (f32[8,128,1024]{2,1,0:T(8,128)S(1)}, bf16[8,512,256]{2,1,0:T(8,128)(2,1)S(1)}) custom-call(s32[16]{0:T(128)S(1)} %bitcast.30, bf16[2,1024,2048]{2,1,0:T(8,128)(2,1)S(1)} %bitcast.26, f32[8,128,1024]{2,1,0:T(8,128)S(1)} %get-tuple-element.29.early, bf16[128,1024]{1,0:T(8,128)(2,1)S(1)} %collective-permute-done.6.refs_0_, ...), custom_call_target="tpu_custom_call" | custom-call | flops 2147483648 | bytes 8388608 | tf_op jit(solution)/shard_map/last_products/pallas_call | solution.py:541
  57.4 1.4 %copy-done.3 = bf16[8,512,256]{2,1,0:T(8,128)(2,1)} copy-done((bf16[8,512,256]{2,1,0:T(8,128)(2,1)}, bf16[8,512,256]{2,1,0:T(8,128)(2,1)S(1)}, u32[]{:S(2)}) %copy-start.3) | copy-done | bytes 2097176
  58.8 2.7 %lay_columns.1 = (f32[4096,128]{1,0:T(8,128)S(1)}, bf16[4096,128]{1,0:T(8,128)(2,1)}) custom-call(s32[16]{0:T(128)S(1)} %bitcast.31, f32[8,128,1024]{2,1,0:T(8,128)S(1)} %get-tuple-element.31.total.refs_0_), custom_call_target="tpu_custom_call" | custom-call | bytes 8388608 | tf_op jit(solution)/shard_map/lay_columns/pallas_call | solution.py:639
  61.4 1.3 %copy-done.5 = f32[4096,128]{1,0:T(8,128)} copy-done((f32[4096,128]{1,0:T(8,128)}, f32[4096,128]{1,0:T(8,128)S(1)}, u32[]{:S(2)}) %copy-start.5) | copy-done | bytes 2097176
  62.7 2.9 %collective-permute-start.18 = (bf16[4096,128]{1,0:T(8,128)(2,1)}, bf16[4096,128]{1,0:T(8,128)(2,1)S(1)}, u32[]{:S(2)}, u32[]{:S(2)}) collective-permute-start(bf16[4096,128]{1,0:T(8,128)(2,1)} %get-tuple-element.33), channel_id=1, source_target_pairs={{0,1},{1,0},{2,3},{3,2},{4,5},{5,4},{6,7},{7,6},{8,9},{9,8},{10,11... | collective-permute-start | bytes 3145736 | tf_op jit(solution)/shard_map/ppermute | solution.py:653
  66.4 19.9 %collective-permute-done.19 = s32[256]{0:T(256)S(1)} collective-permute-done((s32[256]{0:T(256)S(1)}, s32[256]{0:T(256)S(1)}, u32[]{:S(2)}, u32[]{:S(2)}) %collective-permute-start.19) | collective-permute-done | bytes 1056 | tf_op jit(solution)/shard_map/ppermute | solution.py:488
  86.3 2.2 %copy-done.1 = f32[8,128,1024]{2,1,0:T(8,128)S(1)} copy-done((f32[8,128,1024]{2,1,0:T(8,128)S(1)}, f32[8,128,1024]{2,1,0:T(8,128)}, u32[]{:S(2)}) %copy-start.1) | copy-done | bytes 4194328
  88.5 1.6 %copy-done.4 = bf16[8,512,256]{2,1,0:T(8,128)(2,1)S(1)} copy-done((bf16[8,512,256]{2,1,0:T(8,128)(2,1)S(1)}, bf16[8,512,256]{2,1,0:T(8,128)(2,1)}, u32[]{:S(2)}) %copy-start.4) | copy-done | bytes 2097176
  90.1 2.2 %diag_products.3 = (f32[4,80,512]{2,1,0:T(8,128)S(1)}, bf16[1,4,80,512]{3,2,1,0:T(8,128)(2,1)S(1)}) custom-call(s32[16]{0:T(128)S(1)} %bitcast.32, f32[2,16]{1,0:T(2,128)S(1)} %copy-done.10, s32[1]{0:T(128)S(6)} %copy.17.slot, s32[512]{0:T(512)S(1)} %constant_dynamic-update-slice_fusion.owner, f32[8,128,1024]{2,1,0:T(8,128)S(1)} %copy-done.1, ...), custom_call_target="tpu_custom_call" | custom-call | flops 1073741824 | bytes 4194304 | tf_op jit(solution)/shard_map/diag_products/pallas_call | solution.py:557
  92.3 1.8 %collective-permute-start.21 = (bf16[4,80,512]{2,1,0:T(8,128)(2,1)S(1)}, bf16[4,80,512]{2,1,0:T(8,128)(2,1)S(1)}, u32[]{:S(2)}, u32[]{:S(2)}) collective-permute-start(bf16[4,80,512]{2,1,0:T(8,128)(2,1)S(1)} %bitcast.34), channel_id=1, source_target_pairs={{0,1},{1,0},{2,3},{3,2},{4,5},{5,4},{6,7},{7,6},{8,9},{9,8},{10,11... | collective-permute-start | bytes 983048 | tf_op jit(solution)/shard_map/ppermute | solution.py:587
  94.2 2.1 %diag_products.2 = (f32[4,64,512]{2,1,0:T(8,128)S(1)}, bf16[1,4,64,512]{3,2,1,0:T(8,128)(2,1)S(1)}) custom-call(s32[16]{0:T(128)S(1)} %bitcast.33, f32[2,16]{1,0:T(2,128)S(1)} %copy-done.10, s32[1]{0:T(128)S(6)} %copy.17.slot, s32[512]{0:T(512)S(1)} %constant_dynamic-update-slice_fusion.owner, f32[8,128,1024]{2,1,0:T(8,128)S(1)} %copy-done.1, ...), custom_call_target="tpu_custom_call" | custom-call | flops 1073741824 | bytes 4194304 | tf_op jit(solution)/shard_map/diag_products/pallas_call | solution.py:557
  96.6 7.4 %collective-permute-done.20.refs_0_ = bf16[4,64,512]{2,1,0:T(8,128)(2,1)S(1)} collective-permute-done((bf16[4,64,512]{2,1,0:T(8,128)(2,1)S(1)}, bf16[4,64,512]{2,1,0:T(8,128)(2,1)S(1)}, u32[]{:S(2)}, u32[]{:S(2)}) %collective-permute-start.20) | collective-permute-done | bytes 262176 | tf_op jit(solution)/shard_map/ppermute | solution.py:587
  104.2 5.4 %collective-permute-start.23 = (bf16[72,1024]{1,0:T(8,128)(2,1)S(1)}, bf16[72,1024]{1,0:T(8,128)(2,1)S(1)}, u32[]{:S(2)}, u32[]{:S(2)}) collective-permute-start(bf16[72,1024]{1,0:T(8,128)(2,1)S(1)} %get-tuple-element.44), channel_id=1, source_target_pairs={{0,4},{2,6},{4,0},{6,2},{1,5},{3,7},{5,1},{7,3},{8,12},{10,14},{12... | collective-permute-start | bytes 442376 | tf_op jit(solution)/shard_map/ppermute | solution.py:601
  109.6 3.2 %collective-permute-done.22.refs_0_ = bf16[72,1024]{1,0:T(8,128)(2,1)S(1)} collective-permute-done((bf16[72,1024]{1,0:T(8,128)(2,1)S(1)}, bf16[72,1024]{1,0:T(8,128)(2,1)S(1)}, u32[]{:S(2)}, u32[]{:S(2)}) %collective-permute-start.22) | collective-permute-done | bytes 147488 | tf_op jit(solution)/shard_map/ppermute | solution.py:601
  112.8 4.3 %collective-permute-done.23.refs_1_ = bf16[72,1024]{1,0:T(8,128)(2,1)S(1)} collective-permute-done((bf16[72,1024]{1,0:T(8,128)(2,1)S(1)}, bf16[72,1024]{1,0:T(8,128)(2,1)S(1)}, u32[]{:S(2)}, u32[]{:S(2)}) %collective-permute-start.23) | collective-permute-done | bytes 147488 | tf_op jit(solution)/shard_map/ppermute | solution.py:601
  117.9 1.6 %collective-permute-start.26 = (f32[288,128]{1,0:T(8,128)S(1)}, f32[288,128]{1,0:T(8,128)S(1)}, u32[]{:S(2)}, u32[]{:S(2)}) collective-permute-start(f32[288,128]{1,0:T(8,128)S(1)} %finish.1.refs_0_), channel_id=1, source_target_pairs={{0,16},{8,24},{16,0},{24,8},{1,17},{9,25},{17,1},{25,9},{2,18},{10... | collective-permute-start | bytes 442376 | tf_op jit(solution)/shard_map/ppermute | solution.py:623
  119.8 0.8 settle.1
  120.6 4.1 %collective-permute-done.26.refs_2_ = f32[288,128]{1,0:T(8,128)S(1)} collective-permute-done((f32[288,128]{1,0:T(8,128)S(1)}, f32[288,128]{1,0:T(8,128)S(1)}, u32[]{:S(2)}, u32[]{:S(2)}) %collective-permute-start.26) | collective-permute-done | bytes 147488 | tf_op jit(solution)/shard_map/ppermute | solution.py:623
  124.7 2.1 %collective-permute-done.27.refs_3_ = f32[288,128]{1,0:T(8,128)S(1)} collective-permute-done((f32[288,128]{1,0:T(8,128)S(1)}, f32[288,128]{1,0:T(8,128)S(1)}, u32[]{:S(2)}, u32[]{:S(2)}) %collective-permute-start.27) | collective-permute-done | bytes 147488 | tf_op jit(solution)/shard_map/ppermute | solution.py:623
  126.8 0.7 density.1
  127.5 1.9 %join_columns.1 = f32[4096,128]{1,0:T(8,128)} custom-call(f32[4096,128]{1,0:T(8,128)S(1)} %copy-done.6, bf16[4096,128]{1,0:T(8,128)(2,1)S(1)} %collective-permute-done.18.refs_0_), custom_call_target="tpu_custom_call" | custom-call | tf_op jit(solution)/shard_map/join_columns/pallas_call | solution.py:657
  (53 shorter events, 4.6 us)
Async XLA Ops:
  0.6 45.2 %copy-start.11 = (s32[1,16]{1,0:T(1,128)S(1)}, s32[1,16]{1,0:T(1,128)}, u32[]{:S(2)}) copy-start(s32[1,16]{1,0:T(1,128)} %param.10) | copy-start | bytes 196
  1.7 8.9 %collective-permute-start.2 = (bf16[128,1024]{1,0:T(8,128)(2,1)S(1)}, bf16[128,1024]{1,0:T(8,128)(2,1)S(1)}, u32[]{:S(2)}, u32[]{:S(2)}) collective-permute-start(bf16[128,1024]{1,0:T(8,128)(2,1)S(1)} %get-tuple-element.53.refs_0_), channel_id=1, source_target_pairs={{2,4},{4,2},{3,5},{5,3},{10,12},{12,10},{11,13},{13,11},{18,20},{2... | collective-permute-start | bytes 786440 | tf_op jit(solution)/shard_map/ppermute | solution.py:47
  2.4 13.1 %collective-permute-start.6 = (bf16[128,1024]{1,0:T(8,128)(2,1)S(1)}, bf16[128,1024]{1,0:T(8,128)(2,1)S(1)}, u32[]{:S(2)}, u32[]{:S(2)}) collective-permute-start(bf16[128,1024]{1,0:T(8,128)(2,1)S(1)} %get-tuple-element.53.refs_0_), channel_id=1, source_target_pairs={{0,2},{2,0},{4,6},{6,4},{1,3},{3,1},{5,7},{7,5},{8,10},{10,8},{12,... | collective-permute-start | bytes 786440 | tf_op jit(solution)/shard_map/ppermute | solution.py:47
  8.3 7.8 %collective-permute-start = (bf16[128,1024]{1,0:T(8,128)(2,1)S(1)}, bf16[128,1024]{1,0:T(8,128)(2,1)S(1)}, u32[]{:S(2)}, u32[]{:S(2)}) collective-permute-start(bf16[128,1024]{1,0:T(8,128)(2,1)S(1)} %get-tuple-element.53.refs_0_), channel_id=1, source_target_pairs={{0,1},{1,0},{2,3},{3,2},{4,5},{5,4},{6,7},{7,6},{8,9},{9,8},{10,11... | collective-permute-start | bytes 786440 | tf_op jit(solution)/shard_map/ppermute | solution.py:74
  9.8 11.3 %collective-permute-start.10 = (bf16[128,1024]{1,0:T(8,128)(2,1)S(1)}, bf16[128,1024]{1,0:T(8,128)(2,1)S(1)}, u32[]{:S(2)}, u32[]{:S(2)}) collective-permute-start(bf16[128,1024]{1,0:T(8,128)(2,1)S(1)} %get-tuple-element.52.refs_1_), channel_id=1, source_target_pairs={{0,2},{2,0},{4,6},{6,4},{1,3},{3,1},{5,7},{7,5},{8,10},{10,8},{12,... | collective-permute-start | bytes 786440 | tf_op jit(solution)/shard_map/ppermute | solution.py:47
  9.9 11.9 %collective-permute-start.4 = (bf16[128,1024]{1,0:T(8,128)(2,1)S(1)}, bf16[128,1024]{1,0:T(8,128)(2,1)S(1)}, u32[]{:S(2)}, u32[]{:S(2)}) collective-permute-start(bf16[128,1024]{1,0:T(8,128)(2,1)S(1)} %get-tuple-element.52.refs_1_), channel_id=1, source_target_pairs={{2,4},{4,2},{3,5},{5,3},{10,12},{12,10},{11,13},{13,11},{18,20},{2... | collective-permute-start | bytes 786440 | tf_op jit(solution)/shard_map/ppermute | solution.py:47
  10.6 16.1 %collective-permute-start.3 = (bf16[128,1024]{1,0:T(8,128)(2,1)S(1)}, bf16[128,1024]{1,0:T(8,128)(2,1)S(1)}, u32[]{:S(2)}, u32[]{:S(2)}) collective-permute-start(bf16[128,1024]{1,0:T(8,128)(2,1)S(1)} %collective-permute-done.2), channel_id=1, source_target_pairs={{0,2},{2,0},{4,6},{6,4},{1,3},{3,1},{5,7},{7,5},{8,10},{10,8},{12,... | collective-permute-start | bytes 786440 | tf_op jit(solution)/shard_map/ppermute | solution.py:47
  15.5 12.8 %collective-permute-start.14 = (bf16[128,1024]{1,0:T(8,128)(2,1)S(1)}, bf16[128,1024]{1,0:T(8,128)(2,1)S(1)}, u32[]{:S(2)}, u32[]{:S(2)}) collective-permute-start(bf16[128,1024]{1,0:T(8,128)(2,1)S(1)} %collective-permute-done.6.refs_0_), channel_id=1, source_target_pairs={{2,4},{4,2},{3,5},{5,3},{10,12},{12,10},{11,13},{13,11},{18,20},{2... | collective-permute-start | bytes 786440 | tf_op jit(solution)/shard_map/ppermute | solution.py:47
  16.2 0.7 copy-start.8
  16.9 13.4 %collective-permute-start.7 = (bf16[128,1024]{1,0:T(8,128)(2,1)S(1)}, bf16[128,1024]{1,0:T(8,128)(2,1)S(1)}, u32[]{:S(2)}, u32[]{:S(2)}) collective-permute-start(bf16[128,1024]{1,0:T(8,128)(2,1)S(1)} %collective-permute-done.6.refs_0_), channel_id=1, source_target_pairs={{0,1},{1,0},{2,3},{3,2},{4,5},{5,4},{6,7},{7,6},{8,9},{9,8},{10,11... | collective-permute-start | bytes 786440 | tf_op jit(solution)/shard_map/ppermute | solution.py:74
  21.1 9.8 %collective-permute-start.11 = (bf16[128,1024]{1,0:T(8,128)(2,1)S(1)}, bf16[128,1024]{1,0:T(8,128)(2,1)S(1)}, u32[]{:S(2)}, u32[]{:S(2)}) collective-permute-start(bf16[128,1024]{1,0:T(8,128)(2,1)S(1)} %collective-permute-done.10.refs_1_), channel_id=1, source_target_pairs={{2,4},{4,2},{3,5},{5,3},{10,12},{12,10},{11,13},{13,11},{18,20},{2... | collective-permute-start | bytes 786440 | tf_op jit(solution)/shard_map/ppermute | solution.py:47
  21.8 11.0 %collective-permute-start.5 = (bf16[128,1024]{1,0:T(8,128)(2,1)S(1)}, bf16[128,1024]{1,0:T(8,128)(2,1)S(1)}, u32[]{:S(2)}, u32[]{:S(2)}) collective-permute-start(bf16[128,1024]{1,0:T(8,128)(2,1)S(1)} %collective-permute-done.4), channel_id=1, source_target_pairs={{0,2},{2,0},{4,6},{6,4},{1,3},{3,1},{5,7},{7,5},{8,10},{10,8},{12,... | collective-permute-start | bytes 786440 | tf_op jit(solution)/shard_map/ppermute | solution.py:47
  26.7 9.2 %collective-permute-start.1 = (bf16[128,1024]{1,0:T(8,128)(2,1)S(1)}, bf16[128,1024]{1,0:T(8,128)(2,1)S(1)}, u32[]{:S(2)}, u32[]{:S(2)}) collective-permute-start(bf16[128,1024]{1,0:T(8,128)(2,1)S(1)} %get-tuple-element.52.refs_1_), channel_id=1, source_target_pairs={{0,1},{1,0},{2,3},{3,2},{4,5},{5,4},{6,7},{7,6},{8,9},{9,8},{10,11... | collective-permute-start | bytes 786440 | tf_op jit(solution)/shard_map/ppermute | solution.py:74
  28.2 10.2 %collective-permute-start.15 = (bf16[128,1024]{1,0:T(8,128)(2,1)S(1)}, bf16[128,1024]{1,0:T(8,128)(2,1)S(1)}, u32[]{:S(2)}, u32[]{:S(2)}) collective-permute-start(bf16[128,1024]{1,0:T(8,128)(2,1)S(1)} %collective-permute-done.14), channel_id=1, source_target_pairs={{0,2},{2,0},{4,6},{6,4},{1,3},{3,1},{5,7},{7,5},{8,10},{10,8},{12,... | collective-permute-start | bytes 786440 | tf_op jit(solution)/shard_map/ppermute | solution.py:47
  30.3 16.9 %copy-start.2 = (bf16[1,2,1024,2048]{3,2,1,0:T(8,128)(2,1)S(1)}, bf16[1,2,1024,2048]{3,2,1,0:T(8,128)(2,1)}, u32[]{:S(2)}) copy-start(bf16[1,2,1024,2048]{3,2,1,0:T(8,128)(2,1)} %param.7) | copy-start | bytes 25165828
  30.3 16.7 %collective-permute-start.8 = (bf16[128,1024]{1,0:T(8,128)(2,1)S(1)}, bf16[128,1024]{1,0:T(8,128)(2,1)S(1)}, u32[]{:S(2)}, u32[]{:S(2)}) collective-permute-start(bf16[128,1024]{1,0:T(8,128)(2,1)S(1)} %broadcast_select_fusion.3.refs_4_), channel_id=1, source_target_pairs={{0,1},{1,0},{2,3},{3,2},{4,5},{5,4},{6,7},{7,6},{8,9},{9,8},{10,11... | collective-permute-start | bytes 786440 | tf_op jit(solution)/shard_map/ppermute | solution.py:74
  30.9 11.6 %collective-permute-start.12 = (bf16[128,1024]{1,0:T(8,128)(2,1)S(1)}, bf16[128,1024]{1,0:T(8,128)(2,1)S(1)}, u32[]{:S(2)}, u32[]{:S(2)}) collective-permute-start(bf16[128,1024]{1,0:T(8,128)(2,1)S(1)} %collective-permute-done.11), channel_id=1, source_target_pairs={{0,2},{2,0},{4,6},{6,4},{1,3},{3,1},{5,7},{7,5},{8,10},{10,8},{12,... | collective-permute-start | bytes 786440 | tf_op jit(solution)/shard_map/ppermute | solution.py:47
  35.9 11.2 %collective-permute-start.9 = (bf16[128,1024]{1,0:T(8,128)(2,1)S(1)}, bf16[128,1024]{1,0:T(8,128)(2,1)S(1)}, u32[]{:S(2)}, u32[]{:S(2)}) collective-permute-start(bf16[128,1024]{1,0:T(8,128)(2,1)S(1)} %broadcast_select_fusion.2.refs_5_), channel_id=1, source_target_pairs={{0,1},{1,0},{2,3},{3,2},{4,5},{5,4},{6,7},{7,6},{8,9},{9,8},{10,11... | collective-permute-start | bytes 786440 | tf_op jit(solution)/shard_map/ppermute | solution.py:74
  38.5 14.0 %collective-permute-start.16 = (bf16[128,1024]{1,0:T(8,128)(2,1)S(1)}, bf16[128,1024]{1,0:T(8,128)(2,1)S(1)}, u32[]{:S(2)}, u32[]{:S(2)}) collective-permute-start(bf16[128,1024]{1,0:T(8,128)(2,1)S(1)} %broadcast_select_fusion.1.refs_4_), channel_id=1, source_target_pairs={{0,1},{1,0},{2,3},{3,2},{4,5},{5,4},{6,7},{7,6},{8,9},{9,8},{10,11... | collective-permute-start | bytes 786440 | tf_op jit(solution)/shard_map/ppermute | solution.py:74
  42.5 12.8 %collective-permute-start.17 = (bf16[128,1024]{1,0:T(8,128)(2,1)S(1)}, bf16[128,1024]{1,0:T(8,128)(2,1)S(1)}, u32[]{:S(2)}, u32[]{:S(2)}) collective-permute-start(bf16[128,1024]{1,0:T(8,128)(2,1)S(1)} %broadcast_select_fusion.refs_5_), channel_id=1, source_target_pairs={{0,1},{1,0},{2,3},{3,2},{4,5},{5,4},{6,7},{7,6},{8,9},{9,8},{10,11... | collective-permute-start | bytes 786440 | tf_op jit(solution)/shard_map/ppermute | solution.py:74
  44.1 11.2 %collective-permute-start.13 = (bf16[128,1024]{1,0:T(8,128)(2,1)S(1)}, bf16[128,1024]{1,0:T(8,128)(2,1)S(1)}, u32[]{:S(2)}, u32[]{:S(2)}) collective-permute-start(bf16[128,1024]{1,0:T(8,128)(2,1)S(1)} %collective-permute-done.1.refs_3_), channel_id=1, source_target_pairs={{0,2},{2,0},{4,6},{6,4},{1,3},{3,1},{5,7},{7,5},{8,10},{10,8},{12,... | collective-permute-start | bytes 786440 | tf_op jit(solution)/shard_map/ppermute | solution.py:71
  47.1 1.0 copy-start.9
  57.4 1.4 %copy-start.3 = (bf16[8,512,256]{2,1,0:T(8,128)(2,1)}, bf16[8,512,256]{2,1,0:T(8,128)(2,1)S(1)}, u32[]{:S(2)}) copy-start(bf16[8,512,256]{2,1,0:T(8,128)(2,1)S(1)} %get-tuple-element.37.refs_2_) | copy-start | bytes 6291460
  58.8 2.7 %copy-start = (f32[8,128,1024]{2,1,0:T(8,128)}, f32[8,128,1024]{2,1,0:T(8,128)S(1)}, u32[]{:S(2)}) copy-start(f32[8,128,1024]{2,1,0:T(8,128)S(1)} %get-tuple-element.31.total.refs_0_) | copy-start | bytes 12582916
  58.8 6.9 %copy-start.12 = (s32[256,1]{0,1:T(1,128)S(1)}, s32[256,1]{0,1:T(1,128)}, u32[]{:S(2)}) copy-start(s32[256,1]{0,1:T(1,128)} %param.11) | copy-start | bytes 3076
  58.8 27.5 %copy-start.10 = (f32[2,16]{1,0:T(2,128)S(1)}, f32[2,16]{1,0:T(2,128)}, u32[]{:S(2)}) copy-start(f32[2,16]{1,0:T(2,128)} %table.5) | copy-start | bytes 388
  61.4 1.3 %copy-start.5 = (f32[4096,128]{1,0:T(8,128)}, f32[4096,128]{1,0:T(8,128)S(1)}, u32[]{:S(2)}) copy-start(f32[4096,128]{1,0:T(8,128)S(1)} %get-tuple-element.32.keep) | copy-start | bytes 6291460
  62.7 64.7 %collective-permute-start.18 = (bf16[4096,128]{1,0:T(8,128)(2,1)}, bf16[4096,128]{1,0:T(8,128)(2,1)S(1)}, u32[]{:S(2)}, u32[]{:S(2)}) collective-permute-start(bf16[4096,128]{1,0:T(8,128)(2,1)} %get-tuple-element.33), channel_id=1, source_target_pairs={{0,1},{1,0},{2,3},{3,2},{4,5},{5,4},{6,7},{7,6},{8,9},{9,8},{10,11... | collective-permute-start | bytes 3145736 | tf_op jit(solution)/shard_map/ppermute | solution.py:653
  65.7 20.6 %collective-permute-start.19 = (s32[256]{0:T(256)S(1)}, s32[256]{0:T(256)S(1)}, u32[]{:S(2)}, u32[]{:S(2)}) collective-permute-start(s32[256]{0:T(256)S(1)} %bitcast.38), channel_id=1, source_target_pairs={{0,1},{1,0},{2,3},{3,2},{4,5},{5,4},{6,7},{7,6},{8,9},{9,8},{10,11... | collective-permute-start | bytes 3080 | tf_op jit(solution)/shard_map/ppermute | solution.py:488
  86.3 2.2 %copy-start.1 = (f32[8,128,1024]{2,1,0:T(8,128)S(1)}, f32[8,128,1024]{2,1,0:T(8,128)}, u32[]{:S(2)}) copy-start(f32[8,128,1024]{2,1,0:T(8,128)} %copy-done) | copy-start | bytes 12582916
  88.5 1.6 %copy-start.4 = (bf16[8,512,256]{2,1,0:T(8,128)(2,1)S(1)}, bf16[8,512,256]{2,1,0:T(8,128)(2,1)}, u32[]{:S(2)}) copy-start(bf16[8,512,256]{2,1,0:T(8,128)(2,1)} %copy-done.3) | copy-start | bytes 6291460
  92.3 24.8 %copy-start.7 = (f32[64,1,1,2,512]{4,3,2,1,0:T(2,128)S(1)}, f32[64,1,1,2,512]{4,3,2,1,0:T(2,128)}, u32[]{:S(2)}) copy-start(f32[64,1,1,2,512]{4,3,2,1,0:T(2,128)} %param.9) | copy-start | bytes 786436
  92.3 11.7 %collective-permute-start.21 = (bf16[4,80,512]{2,1,0:T(8,128)(2,1)S(1)}, bf16[4,80,512]{2,1,0:T(8,128)(2,1)S(1)}, u32[]{:S(2)}, u32[]{:S(2)}) collective-permute-start(bf16[4,80,512]{2,1,0:T(8,128)(2,1)S(1)} %bitcast.34), channel_id=1, source_target_pairs={{0,1},{1,0},{2,3},{3,2},{4,5},{5,4},{6,7},{7,6},{8,9},{9,8},{10,11... | collective-permute-start | bytes 983048 | tf_op jit(solution)/shard_map/ppermute | solution.py:587
  96.3 7.7 %collective-permute-start.20 = (bf16[4,64,512]{2,1,0:T(8,128)(2,1)S(1)}, bf16[4,64,512]{2,1,0:T(8,128)(2,1)S(1)}, u32[]{:S(2)}, u32[]{:S(2)}) collective-permute-start(bf16[4,64,512]{2,1,0:T(8,128)(2,1)S(1)} %bitcast.35), channel_id=1, source_target_pairs={{0,1},{1,0},{2,3},{3,2},{4,5},{5,4},{6,7},{7,6},{8,9},{9,8},{10,11... | collective-permute-start | bytes 786440 | tf_op jit(solution)/shard_map/ppermute | solution.py:587
  104.0 23.5 %copy-start.6 = (f32[4096,128]{1,0:T(8,128)S(1)}, f32[4096,128]{1,0:T(8,128)}, u32[]{:S(2)}) copy-start(f32[4096,128]{1,0:T(8,128)} %copy-done.5) | copy-start | bytes 6291460
  104.1 8.7 %collective-permute-start.22 = (bf16[72,1024]{1,0:T(8,128)(2,1)S(1)}, bf16[72,1024]{1,0:T(8,128)(2,1)S(1)}, u32[]{:S(2)}, u32[]{:S(2)}) collective-permute-start(bf16[72,1024]{1,0:T(8,128)(2,1)S(1)} %get-tuple-element.43), channel_id=1, source_target_pairs={{0,2},{2,4},{4,6},{6,0},{1,3},{3,5},{5,7},{7,1},{8,10},{10,12},{12... | collective-permute-start | bytes 442376 | tf_op jit(solution)/shard_map/ppermute | solution.py:601
  104.2 13.0 %collective-permute-start.23 = (bf16[72,1024]{1,0:T(8,128)(2,1)S(1)}, bf16[72,1024]{1,0:T(8,128)(2,1)S(1)}, u32[]{:S(2)}, u32[]{:S(2)}) collective-permute-start(bf16[72,1024]{1,0:T(8,128)(2,1)S(1)} %get-tuple-element.44), channel_id=1, source_target_pairs={{0,4},{2,6},{4,0},{6,2},{1,5},{3,7},{5,1},{7,3},{8,12},{10,14},{12... | collective-permute-start | bytes 442376 | tf_op jit(solution)/shard_map/ppermute | solution.py:601
  109.6 7.6 %collective-permute-start.24 = (bf16[72,1024]{1,0:T(8,128)(2,1)S(1)}, bf16[72,1024]{1,0:T(8,128)(2,1)S(1)}, u32[]{:S(2)}, u32[]{:S(2)}) collective-permute-start(bf16[72,1024]{1,0:T(8,128)(2,1)S(1)} %get-tuple-element.45), channel_id=1, source_target_pairs={{0,6},{2,0},{4,2},{6,4},{1,7},{3,1},{5,3},{7,5},{8,14},{10,8},{12,... | collective-permute-start | bytes 442376 | tf_op jit(solution)/shard_map/ppermute | solution.py:601
  117.8 2.8 %collective-permute-start.25 = (f32[288,128]{1,0:T(8,128)S(1)}, f32[288,128]{1,0:T(8,128)S(1)}, u32[]{:S(2)}, u32[]{:S(2)}) collective-permute-start(f32[288,128]{1,0:T(8,128)S(1)} %finish.1.refs_0_), channel_id=1, source_target_pairs={{0,8},{8,0},{16,24},{24,16},{1,9},{9,1},{17,25},{25,17},{2,10},{10... | collective-permute-start | bytes 442376 | tf_op jit(solution)/shard_map/ppermute | solution.py:623
  117.9 6.8 %collective-permute-start.26 = (f32[288,128]{1,0:T(8,128)S(1)}, f32[288,128]{1,0:T(8,128)S(1)}, u32[]{:S(2)}, u32[]{:S(2)}) collective-permute-start(f32[288,128]{1,0:T(8,128)S(1)} %finish.1.refs_0_), channel_id=1, source_target_pairs={{0,16},{8,24},{16,0},{24,8},{1,17},{9,25},{17,1},{25,9},{2,18},{10... | collective-permute-start | bytes 442376 | tf_op jit(solution)/shard_map/ppermute | solution.py:623
  119.5 7.3 %collective-permute-start.27 = (f32[288,128]{1,0:T(8,128)S(1)}, f32[288,128]{1,0:T(8,128)S(1)}, u32[]{:S(2)}, u32[]{:S(2)}) collective-permute-start(f32[288,128]{1,0:T(8,128)S(1)} %finish.1.refs_0_), channel_id=1, source_target_pairs={{0,24},{8,16},{16,8},{24,0},{1,25},{9,17},{17,9},{25,1},{2,26},{10... | collective-permute-start | bytes 442376 | tf_op jit(solution)/shard_map/ppermute | solution.py:623
